TPU v7x, 512 devices: a whole 4x4x16 slice. The times are simulated.
512 devices in a mesh: lon: 32 (over z_lo, y), lat: 16 (over z_hi, x, core).
Axes of the slice: x: 4, y: 4, z: 16 (z_hi: 2, z_lo: 8; z = z_hi * 8 + z_lo), core: 2. Of those that a mesh axis runs over, the one named last changes fastest.
Arguments:
- fields: bfloat16 [16, 64, 32, 4096], P('lat', None, None, 'lon'), may hold values from -40 to 40
- ocean_mask: int32 [16, 32, 4096], P('lat', None, 'lon'), may hold values 0 or 1
- norm_gain: float32 [64], replicated, may hold values from 0.5 to 1.5
- w_vert: bfloat16 [5, 8, 8, 8], replicated, may hold values from -1 to 1
- b_vert: float32 [64], replicated, may hold values from -3 to 3
- w_horiz: bfloat16 [5, 64, 5, 64], replicated, may hold values from -0.15625 to 0.15625
- b_horiz: float32 [64], replicated, may hold values from -3 to 3
Outputs:
- updated: bfloat16 [16, 64, 32, 4096], P('lat', None, None, 'lon')
All inputs are finite; a program needn't handle non-finite values. No bound on the sum of `ocean_mask` on one device may be relied on, other than what follows from the above.
Results may differ from a plain program's by a relative error of at most 0.0023.
Values may be sent and summed in bfloat16 or wider, within the bound.
A program may use at most 64 MiB of HBM per device.

v0:
```python
import jax
import jax.numpy as jnp
from jax import lax
from jax.sharding import PartitionSpec as P


def extended_2(shard, sides, width):
    for axis, dim in sides:
        devices, length = (lax.axis_size(axis), shard.shape[dim])
        up = [(i, (i + 1) % devices) for i in range(devices)]
        down = [(j, i) for i, j in up]
        last = lax.slice_in_dim(shard, length - width, length, axis=dim)
        leading = lax.slice_in_dim(shard, 0, width, axis=dim)
        before = lax.ppermute(last, axis, up)
        after = lax.ppermute(leading, axis, down)
        shard = jnp.concatenate([before, shard, after], axis=dim)
    return shard


def normalize(block, norm_gain):
    values = block.astype(jnp.float32)
    center = jnp.mean(values, axis=1, keepdims=True)
    spread = jnp.mean((values - center) ** 2, axis=1, keepdims=True)
    return ((values - center) * lax.rsqrt(spread + 1e-05) * norm_gain[None, :, None, None]).astype(
        jnp.bfloat16
    )


def vertical(taps, w_vert, b_vert):
    count_lev, channels, rows_lat, cols_lon = taps[0].shape
    groups, width_in, width_out = (w_vert.shape[1], w_vert.shape[2], w_vert.shape[3])
    summed = jnp.zeros((count_lev, groups, width_out, rows_lat, cols_lon), jnp.float32)
    for tap_index in range(len(taps)):
        grouped = taps[tap_index].reshape(count_lev, groups, width_in, rows_lat, cols_lon)
        summed = summed + jnp.einsum(
            "gio,ngiab->ngoab", w_vert[tap_index], grouped, preferred_element_type=jnp.float32
        )
    summed = summed.reshape(count_lev, channels, rows_lat, cols_lon) + b_vert[None, :, None, None]
    return jax.nn.gelu(summed).astype(jnp.bfloat16)


def local(fields, ocean_mask, norm_gain, w_vert, b_vert, w_horiz, b_horiz):
    normed = normalize(fields, norm_gain)
    reach = w_vert.shape[0] // 2
    columns = lax.all_to_all(normed, "lat", split_axis=2, concat_axis=0, tiled=True)
    count_lev = columns.shape[0]
    padded = jnp.pad(columns, ((reach, reach), (0, 0), (0, 0), (0, 0)))
    taps = [padded[tap_index : tap_index + count_lev] for tap_index in range(w_vert.shape[0])]
    mixed = lax.all_to_all(
        vertical(taps, w_vert, b_vert), "lat", split_axis=0, concat_axis=2, tiled=True
    )
    masked = mixed * ocean_mask[:, None].astype(jnp.bfloat16)
    extended = extended_2(masked, (("lon", 3),), 2)
    extended = jnp.pad(extended, ((0, 0), (0, 0), (2, 2), (0, 0)))
    channels, rows_lat, cols_lon = (masked.shape[1], masked.shape[2], masked.shape[3])
    summed = jnp.zeros(masked.shape, jnp.float32)
    for row_tap in range(w_horiz.shape[0]):
        stacked = jnp.concatenate(
            [
                extended[:, :, row_tap : row_tap + rows_lat, col_tap : col_tap + cols_lon]
                for col_tap in range(w_horiz.shape[2])
            ],
            axis=1,
        )
        kernel = w_horiz[row_tap].reshape(channels, -1)
        summed = summed + jnp.einsum(
            "oj,njab->noab", kernel, stacked, preferred_element_type=jnp.float32
        )
    ocean = ocean_mask[:, None].astype(jnp.float32)
    return (fields.astype(jnp.float32) + ocean * (summed + b_horiz[None, :, None, None])).astype(
        jnp.bfloat16
    )


def solution(mesh):
    placed = (P("lat", None, None, "lon"), P("lat", None, "lon"), P(), P(), P(), P(), P())
    return jax.shard_map(
        local, mesh=mesh, in_specs=placed, out_specs=P("lat", None, None, "lon"), check_vma=False
    )
```

profile of v0, /device:TPU:71, one launch (start us, length us, event | category | flops | bytes accessed | tf_op | source)
XLA Modules:
  0.0 122.1 jit_solution(7292798042012247006)
XLA Ops:
  0.0 1.2 convert_reduce_fusion
  1.2 0.0 copy-start.2
  1.2 1.3 %fusion.48 = f32[32,128]{1,0:T(8,128)S(1)} fusion(f32[32,128]{1,0:T(8,128)S(1)} %broadcast_multiply_fusion, bf16[1,64,32,128]{3,2,1,0:T(8,128)(2,1)} %param.7), kind=kLoop, calls=%fused_computation.38 | loop fusion | flops 1044480 | bytes 557056 | tf_op jit(solution)/shard_map/reduce_sum | solution.py:23
  2.6 1.4 %fusion.67 = bf16[1,64,32,128]{3,1,0,2:T(8,128)(2,1)S(1)} fusion(f32[64]{0:T(128)} %param.9, f32[32,128]{1,0:T(8,128)S(1)} %add_rsqrt_fusion, f32[32,128]{1,0:T(8,128)S(1)} %broadcast_multiply_fusion, bf16[1,64,32,128]{3,2,1,0:T(8,128)(2,1)} %param.7), kind=kLoop, calls=%fused_computation.66 | loop fusion | flops 1310720 | bytes 1081600 | tf_op jit(solution)/shard_map/convert_element_type | solution.py:24
  3.9 43.2 %all_to_all.36 = bf16[1,64,32,128]{3,1,0,2:T(8,128)(2,1)S(1)} all-to-all(bf16[1,64,32,128]{3,1,0,2:T(8,128)(2,1)S(1)} %fusion.67), channel_id=1, replica_groups=mesh['lon'=32,'lat'=16] {'lat'}, dimensions={2} | all-to-all | bytes 1048576 | tf_op jit(solution)/shard_map/all_to_all | solution.py:45
  47.2 0.5 fusion.62
  47.7 0.0 copy-done.2
  47.7 0.3 fusion.74
  48.0 0.4 convolution_add_fusion.3
  48.4 0.4 convolution_add_fusion.2
  48.8 0.0 copy-start.7
  48.8 0.4 convolution_add_fusion.1
  49.1 0.0 copy-start.6
  49.1 0.4 fusion.26
  49.5 0.0 copy-done.7
  49.5 0.0 copy-start.1
  49.5 1.2 %fusion.58 = bf16[16,64,2,128]{3,1,2,0:T(8,128)(2,1)} fusion(f32[16,8,8,2,128]{4,2,3,0,1:T(8,128)S(1)} %fusion.26, f32[64]{0:T(128)S(1)} %copy-done.7), kind=kLoop, calls=%fused_computation.48 | loop fusion | flops 2621440 | bytes 1573120 | tf_op jit(solution)/shard_map/convert_element_type | solution.py:39
  50.8 5.5 %all-to-all-start.1 = ((bf16[16,64,2,128]{3,1,2,0:T(8,128)(2,1)}), bf16[16,64,2,128]{3,1,2,0:T(8,128)(2,1)S(1)}, u32[]{:S(2)}, u32[]{:S(2)}) async-start(bf16[16,64,2,128]{3,1,2,0:T(8,128)(2,1)} %fusion.58), calls=%async_computation.1 | async-start | bytes 1048576 | tf_op jit(solution)/shard_map/all_to_all | solution.py:49
  56.3 0.0 copy-done.6
  56.3 0.6 convert_bitcast_fusion
  56.9 0.0 copy-start.3
  56.9 38.6 %all-to-all-done.1 = bf16[16,64,2,128]{3,1,2,0:T(8,128)(2,1)S(1)} async-done(((bf16[16,64,2,128]{3,1,2,0:T(8,128)(2,1)}), bf16[16,64,2,128]{3,1,2,0:T(8,128)(2,1)S(1)}, u32[]{:S(2)}, u32[]{:S(2)}) %all-to-all-start.1) | async-done | bytes 524320 | tf_op jit(solution)/shard_map/all_to_all | solution.py:49
  95.5 0.2 fusion.86
  95.7 0.0 copy-done.3
  95.8 1.9 %collective-permute-start.1 = (bf16[1,64,32,2]{3,1,2,0:T(8,128)(2,1)S(1)}, bf16[1,64,32,2]{3,1,2,0:T(8,128)(2,1)S(1)}, u32[]{:S(2)}, u32[]{:S(2)}) collective-permute-start(bf16[1,64,32,2]{3,1,2,0:T(8,128)(2,1)S(1)} %get-tuple-element.25), channel_id=1, source_target_pairs={{16,0},{32,16},{48,32},{64,48},{80,64},{96,80},{112,96},{128,112},... | collective-permute-start | bytes 24584 | tf_op jit(solution)/shard_map/ppermute | solution.py:15
  97.7 3.5 %collective-permute-start = (bf16[1,64,32,2]{3,1,2,0:T(8,128)(2,1)S(1)}, bf16[1,64,32,2]{3,1,2,0:T(8,128)(2,1)S(1)}, u32[]{:S(2)}, u32[]{:S(2)}) collective-permute-start(bf16[1,64,32,2]{3,1,2,0:T(8,128)(2,1)S(1)} %get-tuple-element.24), channel_id=1, source_target_pairs={{0,16},{16,32},{32,48},{48,64},{64,80},{80,96},{96,112},{112,128},... | collective-permute-start | bytes 24584 | tf_op jit(solution)/shard_map/ppermute | solution.py:14
  101.2 0.0 copy-done.1
  101.2 0.8 fusion.87
  102.0 1.0 copy.64
  103.0 1.0 copy.62
  104.0 1.0 copy.58
  105.0 1.0 copy.56
  106.0 1.0 copy.60
  107.0 0.0 collective-permute-done.1
  107.0 3.3 %collective-permute-done = bf16[1,64,32,2]{3,1,2,0:T(8,128)(2,1)S(1)} collective-permute-done((bf16[1,64,32,2]{3,1,2,0:T(8,128)(2,1)S(1)}, bf16[1,64,32,2]{3,1,2,0:T(8,128)(2,1)S(1)}, u32[]{:S(2)}, u32[]{:S(2)}) %collective-permute-start) | collective-permute-done | bytes 8224 | tf_op jit(solution)/shard_map/ppermute | solution.py:14
  110.3 0.6 fusion.47
  111.0 0.4 slice_dynamic-update-slice_fusion.19
  111.4 0.8 slice_dynamic-update-slice_fusion.18
  112.2 0.9 slice_dynamic-update-slice_fusion.17
  113.1 0.9 slice_dynamic-update-slice_fusion.16
  114.0 0.9 slice_dynamic-update-slice_fusion.15
  114.8 0.3 slice_dynamic-update-slice_fusion
  115.1 0.7 fusion
  115.8 0.7 fusion.2
  116.5 0.0 copy-start.4
  116.5 0.7 fusion.6
  117.2 0.3 fusion.66
  117.5 0.5 fusion.69
  118.0 0.0 copy-done.4
  118.0 0.2 constant_dynamic-update-slice_fusion
  118.2 0.7 fusion.11
  118.9 0.0 copy-start
  118.9 0.0 copy-start.5
  118.9 0.0 copy-start.8
  118.9 0.5 fusion.64
  119.4 0.5 fusion.68
  119.9 0.0 copy-done
  119.9 0.0 copy-done.5
  119.9 0.0 copy-done.8
  119.9 1.0 fusion.41
  121.0 1.1 copy.66
  (3 shorter events, 0.1 us)
Async XLA Ops:
  1.2 46.4 %copy-start.2 = (bf16[5,8,8,8]{3,2,1,0:T(8,128)(2,1)S(1)}, bf16[5,8,8,8]{3,2,1,0:T(8,128)(2,1)}, u32[]{:S(2)}) copy-start(bf16[5,8,8,8]{3,2,1,0:T(8,128)(2,1)} %param.10) | copy-start | bytes 15364
  48.8 0.7 copy-start.7
  49.1 7.1 %copy-start.6 = (s32[1,32,128]{2,1,0:T(8,128)S(1)}, s32[1,32,128]{2,1,0:T(8,128)}, u32[]{:S(2)}) copy-start(s32[1,32,128]{2,1,0:T(8,128)} %param.8) | copy-start | bytes 49156
  49.5 51.7 %copy-start.1 = (bf16[5,64,5,64]{3,1,2,0:T(8,128)(2,1)S(1)}, bf16[5,64,5,64]{3,1,2,0:T(8,128)(2,1)}, u32[]{:S(2)}) copy-start(bf16[5,64,5,64]{3,1,2,0:T(8,128)(2,1)} %param.12) | copy-start | bytes 614404
  50.8 44.7 %all-to-all-start.1 = ((bf16[16,64,2,128]{3,1,2,0:T(8,128)(2,1)}), bf16[16,64,2,128]{3,1,2,0:T(8,128)(2,1)S(1)}, u32[]{:S(2)}, u32[]{:S(2)}) async-start(bf16[16,64,2,128]{3,1,2,0:T(8,128)(2,1)} %fusion.58), calls=%async_computation.1 | async-start | bytes 1048576 | tf_op jit(solution)/shard_map/all_to_all | solution.py:49
  56.9 38.9 %copy-start.3 = (bf16[32,128]{1,0:T(8,128)(2,1)}, bf16[32,128]{1,0:T(8,128)(2,1)S(1)}, u32[]{:S(2)}) copy-start(bf16[32,128]{1,0:T(8,128)(2,1)S(1)} %get-tuple-element.36) | copy-start | bytes 24580
  95.8 11.3 %collective-permute-start.1 = (bf16[1,64,32,2]{3,1,2,0:T(8,128)(2,1)S(1)}, bf16[1,64,32,2]{3,1,2,0:T(8,128)(2,1)S(1)}, u32[]{:S(2)}, u32[]{:S(2)}) collective-permute-start(bf16[1,64,32,2]{3,1,2,0:T(8,128)(2,1)S(1)} %get-tuple-element.25), channel_id=1, source_target_pairs={{16,0},{32,16},{48,32},{64,48},{80,64},{96,80},{112,96},{128,112},... | collective-permute-start | bytes 24584 | tf_op jit(solution)/shard_map/ppermute | solution.py:15
  97.7 12.7 %collective-permute-start = (bf16[1,64,32,2]{3,1,2,0:T(8,128)(2,1)S(1)}, bf16[1,64,32,2]{3,1,2,0:T(8,128)(2,1)S(1)}, u32[]{:S(2)}, u32[]{:S(2)}) collective-permute-start(bf16[1,64,32,2]{3,1,2,0:T(8,128)(2,1)S(1)} %get-tuple-element.24), channel_id=1, source_target_pairs={{0,16},{16,32},{32,48},{48,64},{64,80},{80,96},{96,112},{112,128},... | collective-permute-start | bytes 24584 | tf_op jit(solution)/shard_map/ppermute | solution.py:14
  116.5 1.5 %copy-start.4 = (bf16[32,128]{1,0:T(8,128)(2,1)S(1)}, bf16[32,128]{1,0:T(8,128)(2,1)}, u32[]{:S(2)}) copy-start(bf16[32,128]{1,0:T(8,128)(2,1)} %copy-done.3) | copy-start | bytes 24580
  118.9 1.1 copy-start
  118.9 1.0 copy-start.5
  118.9 1.0 copy-start.8
where the time goes:
time: 123 us; the launch traced here: 122 us
  blocking collectives  43.2 us (35%)
  waiting for transfers between devices  41.9 us (34%)
  local copies, waits for them, and re-layouts  11.8 us (10%)
  starting transfers between devices  11 us (9%)
  other arithmetic  8.36 us (7%)
  matrix products  5.52 us (4%)
    all_to_all x1, blocking collectives, local(): lax.all_to_all(normed, 'lat', split_axis=2, concat_axis=0, tiled=True)  43.2 us
    all_to_all x1, waiting for transfers between devices, local(): lax.all_to_all(vertical(taps, w_vert, b_vert), 'lat', split_axis=0, conca...  38.6 us
    slice x6, local copies, waits for them, and re-layouts, local(): kernel = w_horiz[row_tap].reshape(channels, -1)  5.78 us
    all_to_all x1, starting transfers between devices, local(): lax.all_to_all(vertical(taps, w_vert, b_vert), 'lat', split_axis=0, conca...  5.5 us
    dot_general x5, matrix products, local(): jnp.einsum('oj,njab->noab', kernel, stacked, preferred_element_type=jnp.f...  3.77 us
    ppermute x1, starting transfers between devices, extended_2(): before = lax.ppermute(last, axis, up)  3.54 us
    ppermute x1, waiting for transfers between devices, extended_2(): before = lax.ppermute(last, axis, up)  3.3 us
    unnamed x22, local copies, waits for them, and re-layouts  3 us
  transfers between devices with their start and end apart: 3, of which 2 were waited for; matrix products, arithmetic and copies ran while one was open for 5% of the time, Pallas kernels for 0%

commit v1 on v0

--- a/solution.py
+++ b/solution.py
@@ -42,12 +42,18 @@
 def local(fields, ocean_mask, norm_gain, w_vert, b_vert, w_horiz, b_horiz):
     normed = normalize(fields, norm_gain)
     reach = w_vert.shape[0] // 2
-    columns = lax.all_to_all(normed, "lat", split_axis=2, concat_axis=0, tiled=True)
+    columns = lax.all_to_all(normed, "lat_lo", split_axis=2, concat_axis=0, tiled=True)
     count_lev = columns.shape[0]
-    padded = jnp.pad(columns, ((reach, reach), (0, 0), (0, 0), (0, 0)))
+    upper = lax.axis_index("lat_hi") == 0
+    send = jnp.where(upper, columns[count_lev - reach :], columns[:reach])
+    recv = lax.ppermute(send, "lat_hi", [(0, 1), (1, 0)])
+    zeros = jnp.zeros_like(recv)
+    below = jnp.where(upper, zeros, recv)
+    above = jnp.where(upper, recv, zeros)
+    padded = jnp.concatenate([below, columns, above], axis=0)
     taps = [padded[tap_index : tap_index + count_lev] for tap_index in range(w_vert.shape[0])]
     mixed = lax.all_to_all(
-        vertical(taps, w_vert, b_vert), "lat", split_axis=0, concat_axis=2, tiled=True
+        vertical(taps, w_vert, b_vert), "lat_lo", split_axis=0, concat_axis=2, tiled=True
     )
     masked = mixed * ocean_mask[:, None].astype(jnp.bfloat16)
     extended = extended_2(masked, (("lon", 3),), 2)
@@ -73,7 +79,13 @@
 
 
 def solution(mesh):
-    placed = (P("lat", None, None, "lon"), P("lat", None, "lon"), P(), P(), P(), P(), P())
+    halves = 2
+    lon_count, lat_count = mesh.devices.shape
+    split = jax.sharding.Mesh(
+        mesh.devices.reshape(lon_count, halves, lat_count // halves), ("lon", "lat_hi", "lat_lo")
+    )
+    lat = ("lat_hi", "lat_lo")
+    placed = (P(lat, None, None, "lon"), P(lat, None, "lon"), P(), P(), P(), P(), P())
     return jax.shard_map(
-        local, mesh=mesh, in_specs=placed, out_specs=P("lat", None, None, "lon"), check_vma=False
+        local, mesh=split, in_specs=placed, out_specs=P(lat, None, None, "lon"), check_vma=False
     )

time: 123 us -> 104 us (0.85)
  the two profiles are of different devices: /device:TPU:71 before, /device:TPU:1 now
where the time goes in v1:
time: 104 us; the launch traced here: 103 us
  starting transfers between devices  39.1 us (38%)
  waiting for transfers between devices  37.6 us (36%)
  local copies, waits for them, and re-layouts  11.3 us (11%)
  other arithmetic  9.3 us (9%)
  matrix products  5.51 us (5%)
    ppermute x1, waiting for transfers between devices, extended_2(): before = lax.ppermute(last, axis, up)  12.5 us
    ppermute x1, starting transfers between devices, local(): recv = lax.ppermute(send, 'lat_hi', [(0, 1), (1, 0)])  10.9 us
    ppermute x1, starting transfers between devices, extended_2(): after = lax.ppermute(leading, axis, down)  10.7 us
    all_to_all x1, starting transfers between devices, local(): lax.all_to_all(normed, 'lat_lo', split_axis=2, concat_axis=0, tiled=True)  10.4 us
    all_to_all x1, waiting for transfers between devices, local(): lax.all_to_all(normed, 'lat_lo', split_axis=2, concat_axis=0, tiled=True)  9.5 us
    all_to_all x1, waiting for transfers between devices, local(): lax.all_to_all(vertical(taps, w_vert, b_vert), 'lat_lo', split_axis=0, co...  8.89 us
    slice x6, local copies, waits for them, and re-layouts, local(): kernel = w_horiz[row_tap].reshape(channels, -1)  5.77 us
    all_to_all x1, starting transfers between devices, local(): lax.all_to_all(vertical(taps, w_vert, b_vert), 'lat_lo', split_axis=0, co...  4.99 us
  transfers between devices with their start and end apart: 5, of which 5 were waited for; matrix products, arithmetic and copies ran while one was open for 6% of the time, Pallas kernels for 0%

profile of v1, /device:TPU:1, one launch (start us, length us, event | category | flops | bytes accessed | tf_op | source)
XLA Modules:
  0.0 103.2 jit_solution(13479347965897191853)
XLA Ops:
  0.0 1.2 %convert_reduce_fusion = f32[32,128]{1,0:T(8,128)S(1)} fusion(bf16[1,64,32,128]{3,2,1,0:T(8,128)(2,1)} %param.7), kind=kLoop, calls=%fused_computation.16 | loop fusion | flops 520192 | bytes 540672 | tf_op jit(solution)/shard_map/reduce_sum | solution.py:22
  1.2 1.3 %fusion.48 = f32[32,128]{1,0:T(8,128)S(1)} fusion(f32[32,128]{1,0:T(8,128)S(1)} %broadcast_multiply_fusion, bf16[1,64,32,128]{3,2,1,0:T(8,128)(2,1)} %param.7), kind=kLoop, calls=%fused_computation.38 | loop fusion | flops 1044480 | bytes 557056 | tf_op jit(solution)/shard_map/reduce_sum | solution.py:23
  2.5 2.2 %fusion.67 = bf16[1,64,32,128]{3,1,0,2:T(8,128)(2,1)} fusion(f32[64]{0:T(128)} %param.9, f32[32,128]{1,0:T(8,128)S(1)} %add_rsqrt_fusion, f32[32,128]{1,0:T(8,128)S(1)} %broadcast_multiply_fusion, bf16[1,64,32,128]{3,2,1,0:T(8,128)(2,1)} %param.7), kind=kLoop, calls=%fused_computation.66 | loop fusion | flops 1310720 | bytes 1081600 | tf_op jit(solution)/shard_map/convert_element_type | solution.py:24
  4.7 0.0 copy-start.2
  4.7 10.4 %all-to-all-start = ((bf16[1,64,32,128]{3,1,0,2:T(8,128)(2,1)}), bf16[1,64,32,128]{3,1,0,2:T(8,128)(2,1)S(1)}, u32[]{:S(2)}, u32[]{:S(2)}) async-start(bf16[1,64,32,128]{3,1,0,2:T(8,128)(2,1)} %fusion.67), calls=%async_computation | async-start | bytes 1048576 | tf_op jit(solution)/shard_map/all_to_all | solution.py:45
  15.1 9.5 %all-to-all-done = bf16[1,64,32,128]{3,1,0,2:T(8,128)(2,1)S(1)} async-done(((bf16[1,64,32,128]{3,1,0,2:T(8,128)(2,1)}), bf16[1,64,32,128]{3,1,0,2:T(8,128)(2,1)S(1)}, u32[]{:S(2)}, u32[]{:S(2)}) %all-to-all-start) | async-done | bytes 524320 | tf_op jit(solution)/shard_map/all_to_all | solution.py:45
  24.6 10.9 %collective-permute-start = (bf16[2,64,4,128]{3,1,2,0:T(8,128)(2,1)S(1)}, bf16[2,64,4,128]{3,1,2,0:T(8,128)(2,1)S(1)}, u32[]{:S(2)}, u32[]{:S(2)}) collective-permute-start(bf16[2,64,4,128]{3,1,2,0:T(8,128)(2,1)S(1)} %fusion.78), channel_id=1, source_target_pairs={{0,8},{8,0},{1,9},{9,1},{2,10},{10,2},{3,11},{11,3},{4,12},{12,4},... | collective-permute-start | bytes 393224 | tf_op jit(solution)/shard_map/ppermute | solution.py:49
  35.6 4.3 %collective-permute-done = bf16[2,64,4,128]{3,1,2,0:T(8,128)(2,1)S(1)} collective-permute-done((bf16[2,64,4,128]{3,1,2,0:T(8,128)(2,1)S(1)}, bf16[2,64,4,128]{3,1,2,0:T(8,128)(2,1)S(1)}, u32[]{:S(2)}, u32[]{:S(2)}) %collective-permute-start) | collective-permute-done | bytes 131104 | tf_op jit(solution)/shard_map/ppermute | solution.py:49
  39.9 0.1 fusion.70
  40.0 0.0 copy-done.2
  40.0 0.3 fusion.76
  40.4 0.4 convolution_add_fusion.3
  40.7 0.3 convolution_add_fusion.2
  41.1 0.0 copy-start.7
  41.1 0.4 convolution_add_fusion.1
  41.5 0.0 copy-start.6
  41.5 0.3 fusion.26
  41.8 0.0 copy-done.7
  41.9 0.0 copy-start.1
  41.9 1.2 %fusion.58 = bf16[8,64,4,128]{3,1,2,0:T(8,128)(2,1)} fusion(f32[8,8,8,4,128]{4,2,3,0,1:T(8,128)S(1)} %fusion.26, f32[64]{0:T(128)S(1)} %copy-done.7), kind=kLoop, calls=%fused_computation.48 | loop fusion | flops 2621440 | bytes 1573120 | tf_op jit(solution)/shard_map/convert_element_type | solution.py:39
  43.1 5.0 %all-to-all-start.1 = ((bf16[8,64,4,128]{3,1,2,0:T(8,128)(2,1)}), bf16[8,64,4,128]{3,1,2,0:T(8,128)(2,1)S(1)}, u32[]{:S(2)}, u32[]{:S(2)}) async-start(bf16[8,64,4,128]{3,1,2,0:T(8,128)(2,1)} %fusion.58), calls=%async_computation.1 | async-start | bytes 1048576 | tf_op jit(solution)/shard_map/all_to_all | solution.py:55
  48.1 0.0 copy-done.6
  48.1 0.6 convert_bitcast_fusion
  48.7 0.0 copy-start.3
  48.7 8.9 %all-to-all-done.1 = bf16[8,64,4,128]{3,1,2,0:T(8,128)(2,1)S(1)} async-done(((bf16[8,64,4,128]{3,1,2,0:T(8,128)(2,1)}), bf16[8,64,4,128]{3,1,2,0:T(8,128)(2,1)S(1)}, u32[]{:S(2)}, u32[]{:S(2)}) %all-to-all-start.1) | async-done | bytes 524320 | tf_op jit(solution)/shard_map/all_to_all | solution.py:55
  57.6 0.2 fusion.89
  57.9 0.0 copy-done.3
  57.9 10.7 %collective-permute-start.2 = (bf16[1,64,32,2]{3,1,2,0:T(8,128)(2,1)S(1)}, bf16[1,64,32,2]{3,1,2,0:T(8,128)(2,1)S(1)}, u32[]{:S(2)}, u32[]{:S(2)}) collective-permute-start(bf16[1,64,32,2]{3,1,2,0:T(8,128)(2,1)S(1)} %get-tuple-element.29), channel_id=1, source_target_pairs={{16,0},{32,16},{48,32},{64,48},{80,64},{96,80},{112,96},{128,112},... | collective-permute-start | bytes 24584 | tf_op jit(solution)/shard_map/ppermute | solution.py:15
  68.6 2.1 %collective-permute-start.1 = (bf16[1,64,32,2]{3,1,2,0:T(8,128)(2,1)S(1)}, bf16[1,64,32,2]{3,1,2,0:T(8,128)(2,1)S(1)}, u32[]{:S(2)}, u32[]{:S(2)}) collective-permute-start(bf16[1,64,32,2]{3,1,2,0:T(8,128)(2,1)S(1)} %get-tuple-element.28), channel_id=1, source_target_pairs={{0,16},{16,32},{32,48},{48,64},{64,80},{80,96},{96,112},{112,128},... | collective-permute-start | bytes 24584 | tf_op jit(solution)/shard_map/ppermute | solution.py:14
  70.7 0.0 copy-done.1
  70.7 0.8 fusion.90
  71.5 1.0 copy.64
  72.5 1.0 copy.62
  73.5 1.0 copy.58
  74.5 1.0 copy.56
  75.5 1.0 copy.60
  76.5 2.4 %collective-permute-done.2 = bf16[1,64,32,2]{3,1,2,0:T(8,128)(2,1)S(1)} collective-permute-done((bf16[1,64,32,2]{3,1,2,0:T(8,128)(2,1)S(1)}, bf16[1,64,32,2]{3,1,2,0:T(8,128)(2,1)S(1)}, u32[]{:S(2)}, u32[]{:S(2)}) %collective-permute-start.2) | collective-permute-done | bytes 8224 | tf_op jit(solution)/shard_map/ppermute | solution.py:15
  78.9 12.5 %collective-permute-done.1 = bf16[1,64,32,2]{3,1,2,0:T(8,128)(2,1)S(1)} collective-permute-done((bf16[1,64,32,2]{3,1,2,0:T(8,128)(2,1)S(1)}, bf16[1,64,32,2]{3,1,2,0:T(8,128)(2,1)S(1)}, u32[]{:S(2)}, u32[]{:S(2)}) %collective-permute-start.1) | collective-permute-done | bytes 8224 | tf_op jit(solution)/shard_map/ppermute | solution.py:14
  91.5 0.6 fusion.47
  92.1 0.4 slice_dynamic-update-slice_fusion.19
  92.5 0.8 slice_dynamic-update-slice_fusion.18
  93.3 0.9 slice_dynamic-update-slice_fusion.17
  94.2 0.9 slice_dynamic-update-slice_fusion.16
  95.1 0.9 slice_dynamic-update-slice_fusion.15
  95.9 0.3 slice_dynamic-update-slice_fusion
  96.2 0.7 fusion
  96.9 0.7 fusion.2
  97.6 0.0 copy-start.4
  97.6 0.7 fusion.6
  98.3 0.3 fusion.66
  98.6 0.5 fusion.69
  99.1 0.0 copy-done.4
  99.1 0.2 constant_dynamic-update-slice_fusion
  99.3 0.7 fusion.11
  100.0 0.0 copy-start
  100.0 0.0 copy-start.5
  100.0 0.0 copy-start.8
  100.0 0.5 fusion.64
  100.5 0.5 fusion.68
  101.0 0.0 copy-done
  101.0 0.0 copy-done.5
  101.0 0.0 copy-done.8
  101.1 1.0 fusion.41
  102.1 1.1 %copy.66 = bf16[1,64,32,128]{3,2,1,0:T(8,128)(2,1)} copy(bf16[1,64,32,128]{3,1,2,0:T(8,128)(2,1)S(1)} %fusion.41) | data formatting | bytes 1048576 | tf_op jit(solution)/shard_map/convert_element_type | solution.py:76
  (5 shorter events, 0.1 us)
Async XLA Ops:
  4.7 35.3 %copy-start.2 = (bf16[5,8,8,8]{3,2,1,0:T(8,128)(2,1)S(1)}, bf16[5,8,8,8]{3,2,1,0:T(8,128)(2,1)}, u32[]{:S(2)}) copy-start(bf16[5,8,8,8]{3,2,1,0:T(8,128)(2,1)} %param.10) | copy-start | bytes 15364
  4.7 19.9 %all-to-all-start = ((bf16[1,64,32,128]{3,1,0,2:T(8,128)(2,1)}), bf16[1,64,32,128]{3,1,0,2:T(8,128)(2,1)S(1)}, u32[]{:S(2)}, u32[]{:S(2)}) async-start(bf16[1,64,32,128]{3,1,0,2:T(8,128)(2,1)} %fusion.67), calls=%async_computation | async-start | bytes 1048576 | tf_op jit(solution)/shard_map/all_to_all | solution.py:45
  24.6 15.2 %collective-permute-start = (bf16[2,64,4,128]{3,1,2,0:T(8,128)(2,1)S(1)}, bf16[2,64,4,128]{3,1,2,0:T(8,128)(2,1)S(1)}, u32[]{:S(2)}, u32[]{:S(2)}) collective-permute-start(bf16[2,64,4,128]{3,1,2,0:T(8,128)(2,1)S(1)} %fusion.78), channel_id=1, source_target_pairs={{0,8},{8,0},{1,9},{9,1},{2,10},{10,2},{3,11},{11,3},{4,12},{12,4},... | collective-permute-start | bytes 393224 | tf_op jit(solution)/shard_map/ppermute | solution.py:49
  41.1 0.7 copy-start.7
  41.5 6.6 %copy-start.6 = (s32[1,32,128]{2,1,0:T(8,128)S(1)}, s32[1,32,128]{2,1,0:T(8,128)}, u32[]{:S(2)}) copy-start(s32[1,32,128]{2,1,0:T(8,128)} %param.8) | copy-start | bytes 49156
  41.9 28.8 %copy-start.1 = (bf16[5,64,5,64]{3,1,2,0:T(8,128)(2,1)S(1)}, bf16[5,64,5,64]{3,1,2,0:T(8,128)(2,1)}, u32[]{:S(2)}) copy-start(bf16[5,64,5,64]{3,1,2,0:T(8,128)(2,1)} %param.12) | copy-start | bytes 614404
  43.1 14.5 %all-to-all-start.1 = ((bf16[8,64,4,128]{3,1,2,0:T(8,128)(2,1)}), bf16[8,64,4,128]{3,1,2,0:T(8,128)(2,1)S(1)}, u32[]{:S(2)}, u32[]{:S(2)}) async-start(bf16[8,64,4,128]{3,1,2,0:T(8,128)(2,1)} %fusion.58), calls=%async_computation.1 | async-start | bytes 1048576 | tf_op jit(solution)/shard_map/all_to_all | solution.py:55
  48.7 9.2 %copy-start.3 = (bf16[32,128]{1,0:T(8,128)(2,1)}, bf16[32,128]{1,0:T(8,128)(2,1)S(1)}, u32[]{:S(2)}) copy-start(bf16[32,128]{1,0:T(8,128)(2,1)S(1)} %get-tuple-element.40) | copy-start | bytes 24580
  57.9 21.0 %collective-permute-start.2 = (bf16[1,64,32,2]{3,1,2,0:T(8,128)(2,1)S(1)}, bf16[1,64,32,2]{3,1,2,0:T(8,128)(2,1)S(1)}, u32[]{:S(2)}, u32[]{:S(2)}) collective-permute-start(bf16[1,64,32,2]{3,1,2,0:T(8,128)(2,1)S(1)} %get-tuple-element.29), channel_id=1, source_target_pairs={{16,0},{32,16},{48,32},{64,48},{80,64},{96,80},{112,96},{128,112},... | collective-permute-start | bytes 24584 | tf_op jit(solution)/shard_map/ppermute | solution.py:15
  68.6 22.9 %collective-permute-start.1 = (bf16[1,64,32,2]{3,1,2,0:T(8,128)(2,1)S(1)}, bf16[1,64,32,2]{3,1,2,0:T(8,128)(2,1)S(1)}, u32[]{:S(2)}, u32[]{:S(2)}) collective-permute-start(bf16[1,64,32,2]{3,1,2,0:T(8,128)(2,1)S(1)} %get-tuple-element.28), channel_id=1, source_target_pairs={{0,16},{16,32},{32,48},{48,64},{64,80},{80,96},{96,112},{112,128},... | collective-permute-start | bytes 24584 | tf_op jit(solution)/shard_map/ppermute | solution.py:14
  97.6 1.5 %copy-start.4 = (bf16[32,128]{1,0:T(8,128)(2,1)S(1)}, bf16[32,128]{1,0:T(8,128)(2,1)}, u32[]{:S(2)}) copy-start(bf16[32,128]{1,0:T(8,128)(2,1)} %copy-done.3) | copy-start | bytes 24580
  100.0 1.1 %copy-start = (bf16[1,64,32,128]{3,2,1,0:T(8,128)(2,1)S(1)}, bf16[1,64,32,128]{3,2,1,0:T(8,128)(2,1)}, u32[]{:S(2)}) copy-start(bf16[1,64,32,128]{3,2,1,0:T(8,128)(2,1)} %param.7) | copy-start | bytes 1572868
  100.0 1.0 %copy-start.5 = (f32[32,128]{1,0:T(8,128)S(1)}, f32[32,128]{1,0:T(8,128)}, u32[]{:S(2)}) copy-start(f32[32,128]{1,0:T(8,128)} %get-tuple-element.39) | copy-start | bytes 49156
  100.0 1.0 %copy-start.8 = (f32[64]{0:T(128)S(1)}, f32[64]{0:T(128)}, u32[]{:S(2)}) copy-start(f32[64]{0:T(128)} %param.13) | copy-start | bytes 772

commit v2 on v1

--- a/solution.py
+++ b/solution.py
@@ -39,9 +39,37 @@
     return jax.nn.gelu(summed).astype(jnp.bfloat16)
 
 
+def shifted(block, axis, offset):
+    devices = lax.axis_size(axis)
+    pairs = [(i, i - offset) for i in range(devices) if 0 <= i - offset < devices]
+    return lax.ppermute(block, axis, pairs)
+
+
+def lon_halo(block, width):
+    devices = lax.axis_size("lon")
+    length = block.shape[-1]
+    up = [(i, (i + 1) % devices) for i in range(devices)]
+    down = [(j, i) for i, j in up]
+    before = lax.ppermute(block[..., length - width :], "lon", up)
+    after = lax.ppermute(block[..., :width], "lon", down)
+    return before, after
+
+
 def local(fields, ocean_mask, norm_gain, w_vert, b_vert, w_horiz, b_horiz):
+    reach = w_vert.shape[0] // 2
+    lat = ("lat_hi", "lat_lo")
+    field_before, field_after = lon_halo(fields, reach)
+    mask_before, mask_after = lon_halo(ocean_mask, reach)
+    halo = jnp.concatenate([field_before, field_after], axis=3)
+    halo_normed = normalize(halo, norm_gain)
+    halo_taps = [
+        halo_normed if tap == reach else shifted(halo_normed, lat, tap - reach)
+        for tap in range(w_vert.shape[0])
+    ]
+    halo_mask = jnp.concatenate([mask_before, mask_after], axis=2)
+    halo_masked = vertical(halo_taps, w_vert, b_vert) * halo_mask[:, None].astype(jnp.bfloat16)
+
     normed = normalize(fields, norm_gain)
-    reach = w_vert.shape[0] // 2
     columns = lax.all_to_all(normed, "lat_lo", split_axis=2, concat_axis=0, tiled=True)
     count_lev = columns.shape[0]
     upper = lax.axis_index("lat_hi") == 0
@@ -56,7 +84,9 @@
         vertical(taps, w_vert, b_vert), "lat_lo", split_axis=0, concat_axis=2, tiled=True
     )
     masked = mixed * ocean_mask[:, None].astype(jnp.bfloat16)
-    extended = extended_2(masked, (("lon", 3),), 2)
+    extended = jnp.concatenate(
+        [halo_masked[..., :reach], masked, halo_masked[..., reach:]], axis=3
+    )
     extended = jnp.pad(extended, ((0, 0), (0, 0), (2, 2), (0, 0)))
     channels, rows_lat, cols_lon = (masked.shape[1], masked.shape[2], masked.shape[3])
     summed = jnp.zeros(masked.shape, jnp.float32)

time: 104 us -> 130 us (1.25)
  starting transfers between devices: 39.1 us -> 79.3 us
  waiting for transfers between devices: 37.6 us -> 24.5 us
  local copies, waits for them, and re-layouts: 11.3 us -> 8.99 us
    ppermute x2 -> x8, starting transfers between devices: 12.8 us -> 43.6 us  [the longest x2 28.5 us: lon_halo(): after = lax.ppermute(block[..., :width], 'lon', down)]
    ppermute x1, starting transfers between devices: 10.9 us -> 26.1 us  [local(): recv = lax.ppermute(send, 'lat_hi', [(0, 1), (1, 0)])]
    all_to_all x1, waiting for transfers between devices: 9.5 us -> 0.01 us  [local(): lax.all_to_all(normed, 'lat_lo', split_axis=2, concat_axis=0, tiled=True)]
    all_to_all x1, starting transfers between devices: 10.4 us -> 5.25 us  [local(): lax.all_to_all(normed, 'lat_lo', split_axis=2, concat_axis=0, tiled=True)]
    slice x6, local copies, waits for them, and re-layouts: 5.77 us -> 0.66 us  [local(): kernel = w_horiz[row_tap].reshape(channels, -1)]
    ppermute x2 -> x8, waiting for transfers between devices: 15 us -> 12.8 us  [the longest x2 12 us: lon_halo(): before = lax.ppermute(block[..., length - width:], 'lon', up)]
    slice x1 -> x5, local copies, waits for them, and re-layouts: 0.24 us -> 1.76 us  [the longest x2 1.08 us: lon_halo(): before = lax.ppermute(block[..., length - width:], 'lon', up)]
    dot_general x5 -> x10, matrix products: 1.75 us -> 2.81 us  [vertical(): jnp.einsum('gio,ngiab->ngoab', w_vert[tap_index], grouped, preferred_elem...]
  transfers between devices with their start and end apart: 5 -> 11, of which waited for: 5 -> 4; matrix products, arithmetic and copies ran while one was open for 6% -> 9% of each run, Pallas kernels for 0% -> 0%
where the time goes in v2:
time: 130 us; the launch traced here: 129 us
  starting transfers between devices  79.3 us (61%)
  waiting for transfers between devices  24.5 us (19%)
  other arithmetic  9.11 us (7%)
  local copies, waits for them, and re-layouts  8.99 us (7%)
  matrix products  6.58 us (5%)
    ppermute x2, starting transfers between devices, lon_halo(): after = lax.ppermute(block[..., :width], 'lon', down)  28.5 us
    ppermute x1, starting transfers between devices, local(): recv = lax.ppermute(send, 'lat_hi', [(0, 1), (1, 0)])  26.1 us
    ppermute x2, waiting for transfers between devices, lon_halo(): before = lax.ppermute(block[..., length - width:], 'lon', up)  12 us
    ppermute x4, starting transfers between devices, shifted(): return lax.ppermute(block, axis, pairs)  11.3 us
    all_to_all x1, waiting for transfers between devices, local(): lax.all_to_all(vertical(taps, w_vert, b_vert), 'lat_lo', split_axis=0, co...  8.39 us
    all_to_all x1, starting transfers between devices, local(): lax.all_to_all(normed, 'lat_lo', split_axis=2, concat_axis=0, tiled=True)  5.25 us
    all_to_all x1, starting transfers between devices, local(): lax.all_to_all(vertical(taps, w_vert, b_vert), 'lat_lo', split_axis=0, co...  4.31 us
    unnamed x22, local copies, waits for them, and re-layouts  4.11 us
  transfers between devices with their start and end apart: 11, of which 4 were waited for; matrix products, arithmetic and copies ran while one was open for 9% of the time, Pallas kernels for 0%

profile of v2, /device:TPU:1, one launch (start us, length us, event | category | flops | bytes accessed | tf_op | source)
XLA Modules:
  0.0 129.0 jit_solution(12597623093102594426)
XLA Ops:
  0.0 0.9 fusion.130
  0.9 16.2 %collective-permute-start.7 = (s32[1,32,2]{1,2,0:T(2,128)S(1)}, s32[1,32,2]{1,2,0:T(2,128)S(1)}, u32[]{:S(2)}, u32[]{:S(2)}) collective-permute-start(s32[1,32,2]{1,2,0:T(2,128)S(1)} %copy.167), channel_id=1, source_target_pairs={{16,0},{32,16},{48,32},{64,48},{80,64},{96,80},{112,96},{128,112},... | collective-permute-start | bytes 776 | tf_op jit(solution)/shard_map/ppermute | solution.py:54
  17.1 0.1 copy.166
  17.2 1.9 %collective-permute-start.6 = (s32[1,32,2]{1,2,0:T(2,128)S(1)}, s32[1,32,2]{1,2,0:T(2,128)S(1)}, u32[]{:S(2)}, u32[]{:S(2)}) collective-permute-start(s32[1,32,2]{1,2,0:T(2,128)S(1)} %copy.166), channel_id=1, source_target_pairs={{0,16},{16,32},{32,48},{48,64},{64,80},{80,96},{96,112},{112,128},... | collective-permute-start | bytes 776 | tf_op jit(solution)/shard_map/ppermute | solution.py:53
  19.1 1.2 convert_reduce_fusion
  20.3 1.3 fusion.51
  21.7 2.2 %fusion.70 = bf16[1,64,32,128]{3,1,0,2:T(8,128)(2,1)} fusion(f32[64]{0:T(128)} %param.9, f32[32,128]{1,0:T(8,128)S(1)} %add_rsqrt_fusion, f32[32,128]{1,0:T(8,128)S(1)} %broadcast_multiply_fusion, bf16[1,64,32,128]{3,2,1,0:T(8,128)(2,1)} %param.7), kind=kLoop, calls=%fused_computation.71 | loop fusion | flops 1310720 | bytes 1081600 | tf_op jit(solution)/shard_map/convert_element_type | solution.py:24
  23.9 5.3 %all-to-all-start = ((bf16[1,64,32,128]{3,1,0,2:T(8,128)(2,1)}), bf16[1,64,32,128]{3,1,0,2:T(8,128)(2,1)S(1)}, u32[]{:S(2)}, u32[]{:S(2)}) async-start(bf16[1,64,32,128]{3,1,0,2:T(8,128)(2,1)} %fusion.70), calls=%async_computation | async-start | bytes 1048576 | tf_op jit(solution)/shard_map/all_to_all | solution.py:73
  29.1 0.2 fusion.127
  29.4 0.5 copy.160
  29.8 12.4 %collective-permute-start.1 = (bf16[1,64,32,2]{2,1,3,0:T(8,128)(2,1)S(1)}, bf16[1,64,32,2]{2,1,3,0:T(8,128)(2,1)S(1)}, u32[]{:S(2)}, u32[]{:S(2)}) collective-permute-start(bf16[1,64,32,2]{2,1,3,0:T(8,128)(2,1)S(1)} %copy.160), channel_id=1, source_target_pairs={{16,0},{32,16},{48,32},{64,48},{80,64},{96,80},{112,96},{128,112},... | collective-permute-start | bytes 24584 | tf_op jit(solution)/shard_map/ppermute | solution.py:54
  42.2 0.5 copy.159
  42.7 1.9 %collective-permute-start = (bf16[1,64,32,2]{2,1,3,0:T(8,128)(2,1)S(1)}, bf16[1,64,32,2]{2,1,3,0:T(8,128)(2,1)S(1)}, u32[]{:S(2)}, u32[]{:S(2)}) collective-permute-start(bf16[1,64,32,2]{2,1,3,0:T(8,128)(2,1)S(1)} %copy.159), channel_id=1, source_target_pairs={{0,16},{16,32},{32,48},{48,64},{64,80},{80,96},{96,112},{112,128},... | collective-permute-start | bytes 24584 | tf_op jit(solution)/shard_map/ppermute | solution.py:53
  44.6 0.1 mul.183
  44.8 0.1 copy.125
  44.9 0.1 copy.131
  45.0 0.1 copy.127
  45.2 0.1 copy.135
  45.3 0.1 copy.133
  45.5 12.0 %collective-permute-done = bf16[1,64,32,2]{2,1,3,0:T(8,128)(2,1)S(1)} collective-permute-done((bf16[1,64,32,2]{2,1,3,0:T(8,128)(2,1)S(1)}, bf16[1,64,32,2]{2,1,3,0:T(8,128)(2,1)S(1)}, u32[]{:S(2)}, u32[]{:S(2)}) %collective-permute-start) | collective-permute-done | bytes 8224 | tf_op jit(solution)/shard_map/ppermute | solution.py:53
  57.5 0.1 fusion.85
  57.6 1.3 %collective-permute-start.5 = (bf16[1,64,32,4]{2,1,3,0:T(8,128)(2,1)S(1)}, bf16[1,64,32,4]{2,1,3,0:T(8,128)(2,1)S(1)}, u32[]{:S(2)}, u32[]{:S(2)}) collective-permute-start(bf16[1,64,32,4]{2,1,3,0:T(8,128)(2,1)S(1)} %fusion.85), channel_id=1, source_target_pairs={{2,0},{3,1},{4,2},{5,3},{6,4},{7,5},{8,6},{9,7},{10,8},{11,9},{12,... | collective-permute-start | bytes 49160 | tf_op jit(solution)/shard_map/ppermute | solution.py:45
  58.9 3.8 %collective-permute-start.4 = (bf16[1,64,32,4]{2,1,3,0:T(8,128)(2,1)S(1)}, bf16[1,64,32,4]{2,1,3,0:T(8,128)(2,1)S(1)}, u32[]{:S(2)}, u32[]{:S(2)}) collective-permute-start(bf16[1,64,32,4]{2,1,3,0:T(8,128)(2,1)S(1)} %fusion.85), channel_id=1, source_target_pairs={{1,0},{2,1},{3,2},{4,3},{5,4},{6,5},{7,6},{8,7},{9,8},{10,9},{11,1... | collective-permute-start | bytes 49160 | tf_op jit(solution)/shard_map/ppermute | solution.py:45
  62.7 4.2 %collective-permute-start.3 = (bf16[1,64,32,4]{2,1,3,0:T(8,128)(2,1)S(1)}, bf16[1,64,32,4]{2,1,3,0:T(8,128)(2,1)S(1)}, u32[]{:S(2)}, u32[]{:S(2)}) collective-permute-start(bf16[1,64,32,4]{2,1,3,0:T(8,128)(2,1)S(1)} %fusion.85), channel_id=1, source_target_pairs={{0,1},{1,2},{2,3},{3,4},{4,5},{5,6},{6,7},{7,8},{8,9},{9,10},{10,1... | collective-permute-start | bytes 49160 | tf_op jit(solution)/shard_map/ppermute | solution.py:45
  66.9 2.0 %collective-permute-start.2 = (bf16[1,64,32,4]{2,1,3,0:T(8,128)(2,1)S(1)}, bf16[1,64,32,4]{2,1,3,0:T(8,128)(2,1)S(1)}, u32[]{:S(2)}, u32[]{:S(2)}) collective-permute-start(bf16[1,64,32,4]{2,1,3,0:T(8,128)(2,1)S(1)} %fusion.85), channel_id=1, source_target_pairs={{0,2},{1,3},{2,4},{3,5},{4,6},{5,7},{6,8},{7,9},{8,10},{9,11},{10,... | collective-permute-start | bytes 49160 | tf_op jit(solution)/shard_map/ppermute | solution.py:45
  68.9 0.2 fusion.95
  69.2 0.2 fusion.100
  69.4 0.9 collective-permute-done.2
  70.2 0.2 fusion.50
  70.5 26.1 %collective-permute-start.8 = (bf16[2,64,4,128]{3,1,2,0:T(8,128)(2,1)S(1)}, bf16[2,64,4,128]{3,1,2,0:T(8,128)(2,1)S(1)}, u32[]{:S(2)}, u32[]{:S(2)}) collective-permute-start(bf16[2,64,4,128]{3,1,2,0:T(8,128)(2,1)S(1)} %fusion.86), channel_id=1, source_target_pairs={{0,8},{8,0},{1,9},{9,1},{2,10},{10,2},{3,11},{11,3},{4,12},{12,4},... | collective-permute-start | bytes 393224 | tf_op jit(solution)/shard_map/ppermute | solution.py:77
  96.6 0.2 fusion.97
  96.8 3.3 %collective-permute-done.8 = bf16[2,64,4,128]{3,1,2,0:T(8,128)(2,1)S(1)} collective-permute-done((bf16[2,64,4,128]{3,1,2,0:T(8,128)(2,1)S(1)}, bf16[2,64,4,128]{3,1,2,0:T(8,128)(2,1)S(1)}, u32[]{:S(2)}, u32[]{:S(2)}) %collective-permute-start.8) | collective-permute-done | bytes 131104 | tf_op jit(solution)/shard_map/ppermute | solution.py:77
  100.1 0.1 fusion.73
  100.3 0.3 fusion.79
  100.6 0.4 convolution_add_fusion.3
  101.0 0.3 convolution_add_fusion.2
  101.4 0.4 convolution_add_fusion.1
  101.7 0.4 fusion.26
  102.1 1.2 fusion.61
  103.3 4.3 %all-to-all-start.1 = ((bf16[8,64,4,128]{3,1,2,0:T(8,128)(2,1)}), bf16[8,64,4,128]{3,1,2,0:T(8,128)(2,1)S(1)}, u32[]{:S(2)}, u32[]{:S(2)}) async-start(bf16[8,64,4,128]{3,1,2,0:T(8,128)(2,1)} %fusion.61), calls=%async_computation.1 | async-start | bytes 1048576 | tf_op jit(solution)/shard_map/all_to_all | solution.py:83
  107.7 0.2 fusion.49
  107.9 0.1 copy.113
  108.0 0.1 fusion.106
  108.1 0.3 copy.123
  108.4 0.3 copy.124
  108.8 8.4 %all-to-all-done.1 = bf16[8,64,4,128]{3,1,2,0:T(8,128)(2,1)S(1)} async-done(((bf16[8,64,4,128]{3,1,2,0:T(8,128)(2,1)}), bf16[8,64,4,128]{3,1,2,0:T(8,128)(2,1)S(1)}, u32[]{:S(2)}, u32[]{:S(2)}) %all-to-all-start.1) | async-done | bytes 524320 | tf_op jit(solution)/shard_map/all_to_all | solution.py:83
  117.2 0.3 fusion.69
  117.5 0.6 fusion.47
  118.1 0.5 fusion.72
  118.6 0.2 constant_dynamic-update-slice_fusion
  118.8 0.5 fusion.67
  119.3 0.5 fusion.71
  119.9 0.4 slice_dynamic-update-slice_fusion.19
  120.3 0.8 slice_dynamic-update-slice_fusion.18
  121.1 0.9 slice_dynamic-update-slice_fusion.17
  122.0 0.9 slice_dynamic-update-slice_fusion.16
  122.8 0.9 slice_dynamic-update-slice_fusion.15
  123.7 0.3 slice_dynamic-update-slice_fusion
  124.0 0.7 fusion.4
  124.7 0.7 fusion.2
  125.4 0.7 fusion.6
  126.1 0.7 fusion
  126.8 1.0 fusion.41
  127.8 1.1 copy.137
  (38 shorter events, 0.4 us)
Async XLA Ops:
  0.0 29.1 %copy-start = (bf16[1,64,32,128]{3,2,1,0:T(8,128)(2,1)S(1)}, bf16[1,64,32,128]{3,2,1,0:T(8,128)(2,1)}, u32[]{:S(2)}) copy-start(bf16[1,64,32,128]{3,2,1,0:T(8,128)(2,1)} %param.7) | copy-start | bytes 1572868
  0.9 44.5 %collective-permute-start.7 = (s32[1,32,2]{1,2,0:T(2,128)S(1)}, s32[1,32,2]{1,2,0:T(2,128)S(1)}, u32[]{:S(2)}, u32[]{:S(2)}) collective-permute-start(s32[1,32,2]{1,2,0:T(2,128)S(1)} %copy.167), channel_id=1, source_target_pairs={{16,0},{32,16},{48,32},{64,48},{80,64},{96,80},{112,96},{128,112},... | collective-permute-start | bytes 776 | tf_op jit(solution)/shard_map/ppermute | solution.py:54
  17.2 28.3 %collective-permute-start.6 = (s32[1,32,2]{1,2,0:T(2,128)S(1)}, s32[1,32,2]{1,2,0:T(2,128)S(1)}, u32[]{:S(2)}, u32[]{:S(2)}) collective-permute-start(s32[1,32,2]{1,2,0:T(2,128)S(1)} %copy.166), channel_id=1, source_target_pairs={{0,16},{16,32},{32,48},{48,64},{64,80},{80,96},{96,112},{112,128},... | collective-permute-start | bytes 776 | tf_op jit(solution)/shard_map/ppermute | solution.py:53
  21.6 23.0 %copy-start.4 = (f32[64]{0:T(128)S(1)}, f32[64]{0:T(128)}, u32[]{:S(2)}) copy-start(f32[64]{0:T(128)} %param.9) | copy-start | bytes 772
  21.7 23.1 %copy-start.3 = (s32[1,32,128]{2,1,0:T(8,128)S(1)}, s32[1,32,128]{2,1,0:T(8,128)}, u32[]{:S(2)}) copy-start(s32[1,32,128]{2,1,0:T(8,128)} %param.8) | copy-start | bytes 49156
  21.7 23.1 %copy-start.1 = (bf16[5,64,5,64]{3,1,2,0:T(8,128)(2,1)S(1)}, bf16[5,64,5,64]{3,1,2,0:T(8,128)(2,1)}, u32[]{:S(2)}) copy-start(bf16[5,64,5,64]{3,1,2,0:T(8,128)(2,1)} %param.12) | copy-start | bytes 614404
  23.9 46.6 %all-to-all-start = ((bf16[1,64,32,128]{3,1,0,2:T(8,128)(2,1)}), bf16[1,64,32,128]{3,1,0,2:T(8,128)(2,1)S(1)}, u32[]{:S(2)}, u32[]{:S(2)}) async-start(bf16[1,64,32,128]{3,1,0,2:T(8,128)(2,1)} %fusion.70), calls=%async_computation | async-start | bytes 1048576 | tf_op jit(solution)/shard_map/all_to_all | solution.py:73
  29.1 39.8 %copy-start.2 = (bf16[5,8,8,8]{3,2,1,0:T(8,128)(2,1)S(1)}, bf16[5,8,8,8]{3,2,1,0:T(8,128)(2,1)}, u32[]{:S(2)}) copy-start(bf16[5,8,8,8]{3,2,1,0:T(8,128)(2,1)} %param.10) | copy-start | bytes 15364
  29.8 15.6 %collective-permute-start.1 = (bf16[1,64,32,2]{2,1,3,0:T(8,128)(2,1)S(1)}, bf16[1,64,32,2]{2,1,3,0:T(8,128)(2,1)S(1)}, u32[]{:S(2)}, u32[]{:S(2)}) collective-permute-start(bf16[1,64,32,2]{2,1,3,0:T(8,128)(2,1)S(1)} %copy.160), channel_id=1, source_target_pairs={{16,0},{32,16},{48,32},{64,48},{80,64},{96,80},{112,96},{128,112},... | collective-permute-start | bytes 24584 | tf_op jit(solution)/shard_map/ppermute | solution.py:54
  42.7 14.8 %collective-permute-start = (bf16[1,64,32,2]{2,1,3,0:T(8,128)(2,1)S(1)}, bf16[1,64,32,2]{2,1,3,0:T(8,128)(2,1)S(1)}, u32[]{:S(2)}, u32[]{:S(2)}) collective-permute-start(bf16[1,64,32,2]{2,1,3,0:T(8,128)(2,1)S(1)} %copy.159), channel_id=1, source_target_pairs={{0,16},{16,32},{32,48},{48,64},{64,80},{80,96},{96,112},{112,128},... | collective-permute-start | bytes 24584 | tf_op jit(solution)/shard_map/ppermute | solution.py:53
  57.6 39.0 %collective-permute-start.5 = (bf16[1,64,32,4]{2,1,3,0:T(8,128)(2,1)S(1)}, bf16[1,64,32,4]{2,1,3,0:T(8,128)(2,1)S(1)}, u32[]{:S(2)}, u32[]{:S(2)}) collective-permute-start(bf16[1,64,32,4]{2,1,3,0:T(8,128)(2,1)S(1)} %fusion.85), channel_id=1, source_target_pairs={{2,0},{3,1},{4,2},{5,3},{6,4},{7,5},{8,6},{9,7},{10,8},{11,9},{12,... | collective-permute-start | bytes 49160 | tf_op jit(solution)/shard_map/ppermute | solution.py:45
  58.9 48.7 %collective-permute-start.4 = (bf16[1,64,32,4]{2,1,3,0:T(8,128)(2,1)S(1)}, bf16[1,64,32,4]{2,1,3,0:T(8,128)(2,1)S(1)}, u32[]{:S(2)}, u32[]{:S(2)}) collective-permute-start(bf16[1,64,32,4]{2,1,3,0:T(8,128)(2,1)S(1)} %fusion.85), channel_id=1, source_target_pairs={{1,0},{2,1},{3,2},{4,3},{5,4},{6,5},{7,6},{8,7},{9,8},{10,9},{11,1... | collective-permute-start | bytes 49160 | tf_op jit(solution)/shard_map/ppermute | solution.py:45
  62.7 6.5 %collective-permute-start.3 = (bf16[1,64,32,4]{2,1,3,0:T(8,128)(2,1)S(1)}, bf16[1,64,32,4]{2,1,3,0:T(8,128)(2,1)S(1)}, u32[]{:S(2)}, u32[]{:S(2)}) collective-permute-start(bf16[1,64,32,4]{2,1,3,0:T(8,128)(2,1)S(1)} %fusion.85), channel_id=1, source_target_pairs={{0,1},{1,2},{2,3},{3,4},{4,5},{5,6},{6,7},{7,8},{8,9},{9,10},{10,1... | collective-permute-start | bytes 49160 | tf_op jit(solution)/shard_map/ppermute | solution.py:45
  66.9 3.3 %collective-permute-start.2 = (bf16[1,64,32,4]{2,1,3,0:T(8,128)(2,1)S(1)}, bf16[1,64,32,4]{2,1,3,0:T(8,128)(2,1)S(1)}, u32[]{:S(2)}, u32[]{:S(2)}) collective-permute-start(bf16[1,64,32,4]{2,1,3,0:T(8,128)(2,1)S(1)} %fusion.85), channel_id=1, source_target_pairs={{0,2},{1,3},{2,4},{3,5},{4,6},{5,7},{6,8},{7,9},{8,10},{9,11},{10,... | collective-permute-start | bytes 49160 | tf_op jit(solution)/shard_map/ppermute | solution.py:45
  70.5 29.6 %collective-permute-start.8 = (bf16[2,64,4,128]{3,1,2,0:T(8,128)(2,1)S(1)}, bf16[2,64,4,128]{3,1,2,0:T(8,128)(2,1)S(1)}, u32[]{:S(2)}, u32[]{:S(2)}) collective-permute-start(bf16[2,64,4,128]{3,1,2,0:T(8,128)(2,1)S(1)} %fusion.86), channel_id=1, source_target_pairs={{0,8},{8,0},{1,9},{9,1},{2,10},{10,2},{3,11},{11,3},{4,12},{12,4},... | collective-permute-start | bytes 393224 | tf_op jit(solution)/shard_map/ppermute | solution.py:77
  101.4 0.7 copy-start.5
  103.3 13.8 %all-to-all-start.1 = ((bf16[8,64,4,128]{3,1,2,0:T(8,128)(2,1)}), bf16[8,64,4,128]{3,1,2,0:T(8,128)(2,1)S(1)}, u32[]{:S(2)}, u32[]{:S(2)}) async-start(bf16[8,64,4,128]{3,1,2,0:T(8,128)(2,1)} %fusion.61), calls=%async_computation.1 | async-start | bytes 1048576 | tf_op jit(solution)/shard_map/all_to_all | solution.py:83
  126.1 0.7 copy-start.6

commit v3 on v1

--- a/solution.py
+++ b/solution.py
@@ -1,20 +1,9 @@
 import jax
+from jax.experimental import pallas as pl
+from jax.experimental.pallas import tpu as pltpu
 import jax.numpy as jnp
 from jax import lax
 from jax.sharding import PartitionSpec as P
-
-
-def extended_2(shard, sides, width):
-    for axis, dim in sides:
-        devices, length = (lax.axis_size(axis), shard.shape[dim])
-        up = [(i, (i + 1) % devices) for i in range(devices)]
-        down = [(j, i) for i, j in up]
-        last = lax.slice_in_dim(shard, length - width, length, axis=dim)
-        leading = lax.slice_in_dim(shard, 0, width, axis=dim)
-        before = lax.ppermute(last, axis, up)
-        after = lax.ppermute(leading, axis, down)
-        shard = jnp.concatenate([before, shard, after], axis=dim)
-    return shard
 
 
 def normalize(block, norm_gain):
@@ -56,26 +45,65 @@
         vertical(taps, w_vert, b_vert), "lat_lo", split_axis=0, concat_axis=2, tiled=True
     )
     masked = mixed * ocean_mask[:, None].astype(jnp.bfloat16)
-    extended = extended_2(masked, (("lon", 3),), 2)
-    extended = jnp.pad(extended, ((0, 0), (0, 0), (2, 2), (0, 0)))
-    channels, rows_lat, cols_lon = (masked.shape[1], masked.shape[2], masked.shape[3])
-    summed = jnp.zeros(masked.shape, jnp.float32)
-    for row_tap in range(w_horiz.shape[0]):
-        stacked = jnp.concatenate(
-            [
-                extended[:, :, row_tap : row_tap + rows_lat, col_tap : col_tap + cols_lon]
-                for col_tap in range(w_horiz.shape[2])
-            ],
-            axis=1,
-        )
-        kernel = w_horiz[row_tap].reshape(channels, -1)
-        summed = summed + jnp.einsum(
-            "oj,njab->noab", kernel, stacked, preferred_element_type=jnp.float32
-        )
+    conv = horizontal(masked, w_horiz)
     ocean = ocean_mask[:, None].astype(jnp.float32)
-    return (fields.astype(jnp.float32) + ocean * (summed + b_horiz[None, :, None, None])).astype(
+    return (fields.astype(jnp.float32) + ocean * (conv + b_horiz[None, :, None, None])).astype(
         jnp.bfloat16
     )
+
+
+def horizontal_kernel(x_ref, w_ref, o_ref):
+    taps, channels, rows = (w_ref.shape[0] // o_ref.shape[1], o_ref.shape[1], o_ref.shape[0])
+    lanes = x_ref.shape[2]
+    reach = taps // 2
+    weights = w_ref[...]
+
+    def row(a, carry):
+        window = x_ref[pl.ds(a, taps)].reshape(taps * x_ref.shape[1], lanes)
+        partial = jnp.dot(weights, window, preferred_element_type=jnp.float32)
+        total = jnp.zeros((channels, lanes), jnp.float32)
+        for col_tap in range(taps):
+            piece = partial[col_tap * channels : (col_tap + 1) * channels]
+            total = total + pltpu.roll(piece, (reach - col_tap) % lanes, 1)
+        o_ref[a] = total[:, : o_ref.shape[2]]
+        return carry
+
+    lax.fori_loop(0, rows, row, 0)
+
+
+def horizontal(masked, w_horiz):
+    row_taps, channels, col_taps, _ = w_horiz.shape
+    reach_row, reach_col = row_taps // 2, col_taps // 2
+    _, _, rows_lat, cols_lon = masked.shape
+    before, after = lon_halo(masked, reach_col)
+    lanes = 2 * cols_lon
+    gap = jnp.zeros(masked.shape[:3] + (lanes - cols_lon - 2 * reach_col,), masked.dtype)
+    wide = jnp.concatenate([masked, after, gap, before], axis=3)[0]
+    wide = jnp.transpose(wide, (1, 0, 2))
+    wide = jnp.pad(wide, ((reach_row, reach_row), (0, 0), (0, 0)))
+    weights = jnp.transpose(w_horiz, (2, 1, 0, 3)).reshape(col_taps * channels, row_taps * channels)
+    conv = pl.pallas_call(
+        horizontal_kernel,
+        out_shape=jax.ShapeDtypeStruct((rows_lat, channels, cols_lon), jnp.float32),
+        in_specs=[pl.BlockSpec(memory_space=pltpu.VMEM)] * 2,
+        out_specs=pl.BlockSpec(memory_space=pltpu.VMEM),
+        cost_estimate=pl.CostEstimate(
+            flops=2 * rows_lat * lanes * weights.shape[0] * weights.shape[1],
+            bytes_accessed=wide.size * 2 + weights.size * 2 + rows_lat * channels * cols_lon * 4,
+            transcendentals=0,
+        ),
+    )(wide, weights)
+    return jnp.transpose(conv, (1, 0, 2))[None]
+
+
+def lon_halo(block, width):
+    devices = lax.axis_size("lon")
+    length = block.shape[-1]
+    up = [(i, (i + 1) % devices) for i in range(devices)]
+    down = [(j, i) for i, j in up]
+    before = lax.ppermute(block[..., length - width :], "lon", up)
+    after = lax.ppermute(block[..., :width], "lon", down)
+    return before, after
 
 
 def solution(mesh):

time: 104 us -> 110 us (1.058)
  Pallas kernels: 0 us -> 12.3 us
  local copies, waits for them, and re-layouts: 11.3 us -> 5.84 us
  waiting for transfers between devices: 37.6 us -> 42.7 us
  matrix products: 5.51 us -> 1.75 us
  other arithmetic: 9.3 us -> 7.7 us
    pallas_call x0 -> x1, Pallas kernels: none -> 12.3 us  [horizontal(): pl.pallas_call(horizontal_kernel, out_shape=jax.ShapeDtypeStruct((rows_la...]
    slice x7 -> x1, local copies, waits for them, and re-layouts: 6.02 us -> 1 us  [lon_halo(): after = lax.ppermute(block[..., :width], 'lon', down)]
    ppermute x2, waiting for transfers between devices: 15 us -> 19.5 us  [the longest x1 12.2 us: lon_halo(): before = lax.ppermute(block[..., length - width:], 'lon', up)]
    dot_general x5 -> x0, matrix products: 3.77 us -> none  [local(): jnp.einsum('oj,njab->noab', kernel, stacked, preferred_element_type=jnp.f...]
    unnamed x22 -> x12, local copies, waits for them, and re-layouts: 2.99 us -> 1.04 us
    convert_element_type x0 -> x1, other arithmetic: none -> 1.51 us  [local(): (fields.astype(jnp.float32) + ocean * (conv + b_horiz[None, :, None, None...]
    unnamed x4 -> x0, other arithmetic: 1.43 us -> none
    pad x0 -> x1, local copies, waits for them, and re-layouts: none -> 1.19 us  [horizontal(): wide = jnp.pad(wide, ((reach_row, reach_row), (0, 0), (0, 0)))]
  transfers between devices with their start and end apart: 5 -> 5, of which waited for: 5 -> 5; matrix products, arithmetic and copies ran while one was open for 6% -> 1% of each run, Pallas kernels for 0% -> 0%
where the time goes in v3:
time: 110 us; the launch traced here: 109 us
  waiting for transfers between devices  42.7 us (39%)
  starting transfers between devices  38.8 us (35%)
  Pallas kernels  12.3 us (11%)
  other arithmetic  7.7 us (7%)
  local copies, waits for them, and re-layouts  5.84 us (5%)
  matrix products  1.75 us (2%)
    pallas_call x1, Pallas kernels, horizontal(): pl.pallas_call(horizontal_kernel, out_shape=jax.ShapeDtypeStruct((rows_la...  12.3 us
    ppermute x1, waiting for transfers between devices, lon_halo(): before = lax.ppermute(block[..., length - width:], 'lon', up)  12.2 us
    ppermute x1, starting transfers between devices, local(): recv = lax.ppermute(send, 'lat_hi', [(0, 1), (1, 0)])  10.9 us
    ppermute x1, starting transfers between devices, lon_halo(): after = lax.ppermute(block[..., :width], 'lon', down)  10.7 us
    all_to_all x1, starting transfers between devices, local(): lax.all_to_all(normed, 'lat_lo', split_axis=2, concat_axis=0, tiled=True)  10.3 us
    all_to_all x1, waiting for transfers between devices, local(): lax.all_to_all(normed, 'lat_lo', split_axis=2, concat_axis=0, tiled=True)  9.5 us
    all_to_all x1, waiting for transfers between devices, local(): lax.all_to_all(vertical(taps, w_vert, b_vert), 'lat_lo', split_axis=0, co...  9.49 us
    ppermute x1, waiting for transfers between devices, lon_halo(): after = lax.ppermute(block[..., :width], 'lon', down)  7.25 us
  transfers between devices with their start and end apart: 5, of which 5 were waited for; matrix products, arithmetic and copies ran while one was open for 1% of the time, Pallas kernels for 0%

profile of v3, /device:TPU:1, one launch (start us, length us, event | category | flops | bytes accessed | tf_op | source)
XLA Modules:
  0.0 109.3 jit_solution(13043550375090307170)
XLA Ops:
  0.0 0.0 copy-start
  0.0 1.3 %convert_reduce_fusion = f32[32,128]{1,0:T(8,128)S(1)} fusion(bf16[1,64,32,128]{3,2,1,0:T(8,128)(2,1)} %param.7), kind=kLoop, calls=%fused_computation.3 | loop fusion | flops 520192 | bytes 540672 | tf_op jit(solution)/shard_map/reduce_sum | solution.py:11
  1.3 1.3 %fusion.3 = f32[32,128]{1,0:T(8,128)S(1)} fusion(f32[32,128]{1,0:T(8,128)S(1)} %broadcast_multiply_fusion, bf16[1,64,32,128]{3,2,1,0:T(8,128)(2,1)} %param.7), kind=kLoop, calls=%fused_computation.11 | loop fusion | flops 1044480 | bytes 557056 | tf_op jit(solution)/shard_map/reduce_sum | solution.py:12
  2.6 0.0 copy-done
  2.6 1.7 %fusion.19 = bf16[1,64,32,128]{3,1,0,2:T(8,128)(2,1)} fusion(f32[64]{0:T(128)} %param.9, f32[32,128]{1,0:T(8,128)S(1)} %add_rsqrt_fusion, f32[32,128]{1,0:T(8,128)S(1)} %broadcast_multiply_fusion, bf16[1,64,32,128]{3,2,1,0:T(8,128)(2,1)S(1)} %copy-done), kind=kLoop, calls=%fused_computation.33 | loop fusion | flops 1310720 | bytes 1081600 | tf_op jit(solution)/shard_map/convert_element_type | solution.py:13
  4.4 10.3 %all-to-all-start = ((bf16[1,64,32,128]{3,1,0,2:T(8,128)(2,1)}), bf16[1,64,32,128]{3,1,0,2:T(8,128)(2,1)S(1)}, u32[]{:S(2)}, u32[]{:S(2)}) async-start(bf16[1,64,32,128]{3,1,0,2:T(8,128)(2,1)} %fusion.19), calls=%async_computation | async-start | bytes 1048576 | tf_op jit(solution)/shard_map/all_to_all | solution.py:34
  14.6 9.5 %all-to-all-done = bf16[1,64,32,128]{3,1,0,2:T(8,128)(2,1)S(1)} async-done(((bf16[1,64,32,128]{3,1,0,2:T(8,128)(2,1)}), bf16[1,64,32,128]{3,1,0,2:T(8,128)(2,1)S(1)}, u32[]{:S(2)}, u32[]{:S(2)}) %all-to-all-start) | async-done | bytes 524320 | tf_op jit(solution)/shard_map/all_to_all | solution.py:34
  24.2 10.9 %collective-permute-start = (bf16[2,64,4,128]{3,1,2,0:T(8,128)(2,1)S(1)}, bf16[2,64,4,128]{3,1,2,0:T(8,128)(2,1)S(1)}, u32[]{:S(2)}, u32[]{:S(2)}) collective-permute-start(bf16[2,64,4,128]{3,1,2,0:T(8,128)(2,1)S(1)} %fusion.28), channel_id=1, source_target_pairs={{0,8},{8,0},{1,9},{9,1},{2,10},{10,2},{3,11},{11,3},{4,12},{12,4},... | collective-permute-start | bytes 393224 | tf_op jit(solution)/shard_map/ppermute | solution.py:38
  35.1 4.3 %collective-permute-done = bf16[2,64,4,128]{3,1,2,0:T(8,128)(2,1)S(1)} collective-permute-done((bf16[2,64,4,128]{3,1,2,0:T(8,128)(2,1)S(1)}, bf16[2,64,4,128]{3,1,2,0:T(8,128)(2,1)S(1)}, u32[]{:S(2)}, u32[]{:S(2)}) %collective-permute-start) | collective-permute-done | bytes 131104 | tf_op jit(solution)/shard_map/ppermute | solution.py:38
  39.4 0.0 copy-start.2
  39.4 0.1 fusion.20
  39.6 0.7 copy-done.2
  40.3 0.3 fusion.26
  40.7 0.4 convolution_add_fusion.3
  41.0 0.3 convolution_add_fusion.2
  41.4 0.4 convolution_add_fusion.1
  41.7 0.0 copy-start.4
  41.8 0.4 fusion
  42.1 0.3 copy-done.4
  42.4 0.0 copy-start.3
  42.4 1.2 %fusion.14 = bf16[8,64,4,128]{3,1,2,0:T(8,128)(2,1)} fusion(f32[8,8,8,4,128]{4,2,3,0,1:T(8,128)S(1)} %fusion, f32[64]{0:T(128)S(1)} %copy-done.4), kind=kLoop, calls=%fused_computation.22 | loop fusion | flops 2621440 | bytes 1573120 | tf_op jit(solution)/shard_map/convert_element_type | solution.py:28
  43.6 5.0 %all-to-all-start.1 = ((bf16[8,64,4,128]{3,1,2,0:T(8,128)(2,1)}), bf16[8,64,4,128]{3,1,2,0:T(8,128)(2,1)S(1)}, u32[]{:S(2)}, u32[]{:S(2)}) async-start(bf16[8,64,4,128]{3,1,2,0:T(8,128)(2,1)} %fusion.14), calls=%async_computation.1 | async-start | bytes 1048576 | tf_op jit(solution)/shard_map/all_to_all | solution.py:44
  48.6 0.0 copy-done.3
  48.6 9.5 %all-to-all-done.1 = bf16[8,64,4,128]{3,1,2,0:T(8,128)(2,1)S(1)} async-done(((bf16[8,64,4,128]{3,1,2,0:T(8,128)(2,1)}), bf16[8,64,4,128]{3,1,2,0:T(8,128)(2,1)S(1)}, u32[]{:S(2)}, u32[]{:S(2)}) %all-to-all-start.1) | async-done | bytes 524320 | tf_op jit(solution)/shard_map/all_to_all | solution.py:44
  58.2 0.0 copy-start.1
  58.2 1.0 fusion.39
  59.2 10.7 %collective-permute-start.1 = (bf16[1,64,32,2]{3,1,2,0:T(8,128)(2,1)}, bf16[1,64,32,2]{3,1,2,0:T(8,128)(2,1)S(1)}, u32[]{:S(2)}, u32[]{:S(2)}) collective-permute-start(bf16[1,64,32,2]{3,1,2,0:T(8,128)(2,1)} %get-tuple-element.9), channel_id=1, source_target_pairs={{16,0},{32,16},{48,32},{64,48},{80,64},{96,80},{112,96},{128,112},... | collective-permute-start | bytes 24584 | tf_op jit(solution)/shard_map/ppermute | solution.py:105
  69.9 1.9 %collective-permute-start.2 = (bf16[1,64,32,2]{3,1,2,0:T(8,128)(2,1)S(1)}, bf16[1,64,32,2]{3,1,2,0:T(8,128)(2,1)S(1)}, u32[]{:S(2)}, u32[]{:S(2)}) collective-permute-start(bf16[1,64,32,2]{3,1,2,0:T(8,128)(2,1)S(1)} %get-tuple-element.10), channel_id=1, source_target_pairs={{0,16},{16,32},{32,48},{48,64},{64,80},{80,96},{96,112},{112,128},... | collective-permute-start | bytes 24584 | tf_op jit(solution)/shard_map/ppermute | solution.py:104
  71.8 0.0 copy-done.1
  71.8 0.3 copy.43
  72.1 1.1 reshape.95.w_ref
  73.2 0.1 pad.7.clone
  73.3 7.2 %collective-permute-done.1 = bf16[1,64,32,2]{3,1,2,0:T(8,128)(2,1)S(1)} collective-permute-done((bf16[1,64,32,2]{3,1,2,0:T(8,128)(2,1)}, bf16[1,64,32,2]{3,1,2,0:T(8,128)(2,1)S(1)}, u32[]{:S(2)}, u32[]{:S(2)}) %collective-permute-start.1) | collective-permute-done | bytes 8224 | tf_op jit(solution)/shard_map/ppermute | solution.py:105
  80.5 12.2 %collective-permute-done.2 = bf16[1,64,32,2]{3,1,2,0:T(8,128)(2,1)S(1)} collective-permute-done((bf16[1,64,32,2]{3,1,2,0:T(8,128)(2,1)S(1)}, bf16[1,64,32,2]{3,1,2,0:T(8,128)(2,1)S(1)}, u32[]{:S(2)}, u32[]{:S(2)}) %collective-permute-start.2) | collective-permute-done | bytes 8224 | tf_op jit(solution)/shard_map/ppermute | solution.py:104
  92.7 0.4 maximum_bitcast_fusion
  93.1 1.2 %pad.4.x_ref = bf16[36,64,256]{2,1,0:T(8,128)(2,1)} pad(bf16[32,64,256]{2,1,0:T(8,128)(2,1)S(1)} %maximum_bitcast_fusion, bf16[]{:T(256)} %constant.7.clone.1), padding=2_2x0_0x0_0 | pad | bytes 2228226 | tf_op jit(solution)/shard_map/jit(_pad)/pad | solution.py:83
  94.3 0.0 copy-start.5
  94.3 12.3 %shard_map.73 = f32[32,64,128]{2,1,0:T(8,128)} custom-call(bf16[36,64,256]{2,1,0:T(8,128)(2,1)} %pad.4.x_ref, bf16[320,320]{1,0:T(8,128)(2,1)} %reshape.95.w_ref), custom_call_target="tpu_custom_call" | custom-call | flops 1677721600 | bytes 2433024 | tf_op jit(solution)/shard_map/pallas_call | solution.py:85
  106.6 0.0 copy-done.5
  106.6 1.5 %fusion.6 = bf16[1,64,32,128]{3,1,2,0:T(8,128)(2,1)S(1)} fusion(f32[32,64,128]{2,1,0:T(8,128)} %shard_map.73, f32[64]{0:T(128)S(1)} %copy-done.5, f32[32,128]{1,0:T(8,128)S(1)} %get-tuple-element.15, bf16[1,64,32,128]{3,2,1,0:T(8,128)(2,1)S(1)} %copy-done), kind=kLoop, calls=%fused_computation.14 | loop fusion | flops 1310720 | bytes 2113792 | tf_op jit(solution)/shard_map/convert_element_type | solution.py:50
  108.1 1.1 %copy.44 = bf16[1,64,32,128]{3,2,1,0:T(8,128)(2,1)} copy(bf16[1,64,32,128]{3,1,2,0:T(8,128)(2,1)S(1)} %fusion.6) | data formatting | bytes 1048576 | tf_op jit(solution)/shard_map/convert_element_type | solution.py:50
  (7 shorter events, 0.1 us)
Async XLA Ops:
  0.0 2.6 %copy-start = (bf16[1,64,32,128]{3,2,1,0:T(8,128)(2,1)S(1)}, bf16[1,64,32,128]{3,2,1,0:T(8,128)(2,1)}, u32[]{:S(2)}) copy-start(bf16[1,64,32,128]{3,2,1,0:T(8,128)(2,1)} %param.7) | copy-start | bytes 1572868
  4.4 19.8 %all-to-all-start = ((bf16[1,64,32,128]{3,1,0,2:T(8,128)(2,1)}), bf16[1,64,32,128]{3,1,0,2:T(8,128)(2,1)S(1)}, u32[]{:S(2)}, u32[]{:S(2)}) async-start(bf16[1,64,32,128]{3,1,0,2:T(8,128)(2,1)} %fusion.19), calls=%async_computation | async-start | bytes 1048576 | tf_op jit(solution)/shard_map/all_to_all | solution.py:34
  24.2 15.2 %collective-permute-start = (bf16[2,64,4,128]{3,1,2,0:T(8,128)(2,1)S(1)}, bf16[2,64,4,128]{3,1,2,0:T(8,128)(2,1)S(1)}, u32[]{:S(2)}, u32[]{:S(2)}) collective-permute-start(bf16[2,64,4,128]{3,1,2,0:T(8,128)(2,1)S(1)} %fusion.28), channel_id=1, source_target_pairs={{0,8},{8,0},{1,9},{9,1},{2,10},{10,2},{3,11},{11,3},{4,12},{12,4},... | collective-permute-start | bytes 393224 | tf_op jit(solution)/shard_map/ppermute | solution.py:38
  39.4 0.9 copy-start.2
  41.7 0.7 copy-start.4
  42.4 6.2 %copy-start.3 = (s32[1,32,128]{2,1,0:T(8,128)S(1)}, s32[1,32,128]{2,1,0:T(8,128)}, u32[]{:S(2)}) copy-start(s32[1,32,128]{2,1,0:T(8,128)} %param.8) | copy-start | bytes 49156
  43.6 14.5 %all-to-all-start.1 = ((bf16[8,64,4,128]{3,1,2,0:T(8,128)(2,1)}), bf16[8,64,4,128]{3,1,2,0:T(8,128)(2,1)S(1)}, u32[]{:S(2)}, u32[]{:S(2)}) async-start(bf16[8,64,4,128]{3,1,2,0:T(8,128)(2,1)} %fusion.14), calls=%async_computation.1 | async-start | bytes 1048576 | tf_op jit(solution)/shard_map/all_to_all | solution.py:44
  58.2 13.6 %copy-start.1 = (bf16[5,64,5,64]{3,1,2,0:T(8,128)(2,1)S(1)}, bf16[5,64,5,64]{3,1,2,0:T(8,128)(2,1)}, u32[]{:S(2)}) copy-start(bf16[5,64,5,64]{3,1,2,0:T(8,128)(2,1)} %param.12) | copy-start | bytes 614404
  59.2 21.3 %collective-permute-start.1 = (bf16[1,64,32,2]{3,1,2,0:T(8,128)(2,1)}, bf16[1,64,32,2]{3,1,2,0:T(8,128)(2,1)S(1)}, u32[]{:S(2)}, u32[]{:S(2)}) collective-permute-start(bf16[1,64,32,2]{3,1,2,0:T(8,128)(2,1)} %get-tuple-element.9), channel_id=1, source_target_pairs={{16,0},{32,16},{48,32},{64,48},{80,64},{96,80},{112,96},{128,112},... | collective-permute-start | bytes 24584 | tf_op jit(solution)/shard_map/ppermute | solution.py:105
  69.9 22.9 %collective-permute-start.2 = (bf16[1,64,32,2]{3,1,2,0:T(8,128)(2,1)S(1)}, bf16[1,64,32,2]{3,1,2,0:T(8,128)(2,1)S(1)}, u32[]{:S(2)}, u32[]{:S(2)}) collective-permute-start(bf16[1,64,32,2]{3,1,2,0:T(8,128)(2,1)S(1)} %get-tuple-element.10), channel_id=1, source_target_pairs={{0,16},{16,32},{32,48},{48,64},{64,80},{80,96},{96,112},{112,128},... | collective-permute-start | bytes 24584 | tf_op jit(solution)/shard_map/ppermute | solution.py:104
  94.3 12.3 %copy-start.5 = (f32[64]{0:T(128)S(1)}, f32[64]{0:T(128)}, u32[]{:S(2)}) copy-start(f32[64]{0:T(128)} %param.13) | copy-start | bytes 772

commit v4 on v3

--- a/solution.py
+++ b/solution.py
@@ -53,22 +53,26 @@
 
 
 def horizontal_kernel(x_ref, w_ref, o_ref):
-    taps, channels, rows = (w_ref.shape[0] // o_ref.shape[1], o_ref.shape[1], o_ref.shape[0])
-    lanes = x_ref.shape[2]
-    reach = taps // 2
+    rows, channels, cols_lon = o_ref.shape
+    taps = w_ref.shape[0] // channels
+    segment = x_ref.shape[1] // (rows + taps - 1)
+    chunk = 8
     weights = w_ref[...]
-
-    def row(a, carry):
-        window = x_ref[pl.ds(a, taps)].reshape(taps * x_ref.shape[1], lanes)
+    for start in range(0, rows, chunk):
+        window = jnp.concatenate(
+            [
+                x_ref[:, (start + row_tap) * segment : (start + row_tap + chunk) * segment]
+                for row_tap in range(taps)
+            ],
+            axis=0,
+        )
         partial = jnp.dot(weights, window, preferred_element_type=jnp.float32)
-        total = jnp.zeros((channels, lanes), jnp.float32)
-        for col_tap in range(taps):
+        total = partial[:channels]
+        for col_tap in range(1, taps):
             piece = partial[col_tap * channels : (col_tap + 1) * channels]
-            total = total + pltpu.roll(piece, (reach - col_tap) % lanes, 1)
-        o_ref[a] = total[:, : o_ref.shape[2]]
-        return carry
-
-    lax.fori_loop(0, rows, row, 0)
+            total = total + pltpu.roll(piece, chunk * segment - col_tap, 1)
+        for row in range(chunk):
+            o_ref[start + row] = total[:, row * segment : row * segment + cols_lon]
 
 
 def horizontal(masked, w_horiz):
@@ -76,11 +80,11 @@
     reach_row, reach_col = row_taps // 2, col_taps // 2
     _, _, rows_lat, cols_lon = masked.shape
     before, after = lon_halo(masked, reach_col)
-    lanes = 2 * cols_lon
-    gap = jnp.zeros(masked.shape[:3] + (lanes - cols_lon - 2 * reach_col,), masked.dtype)
-    wide = jnp.concatenate([masked, after, gap, before], axis=3)[0]
-    wide = jnp.transpose(wide, (1, 0, 2))
-    wide = jnp.pad(wide, ((reach_row, reach_row), (0, 0), (0, 0)))
+    segment = 2 * cols_lon
+    gap = jnp.zeros(masked.shape[:3] + (segment - cols_lon - 2 * reach_col,), masked.dtype)
+    wide = jnp.concatenate([before, masked, after, gap], axis=3)[0]
+    wide = jnp.pad(wide, ((0, 0), (reach_row, reach_row), (0, 0)))
+    wide = wide.reshape(channels, (rows_lat + 2 * reach_row) * segment)
     weights = jnp.transpose(w_horiz, (2, 1, 0, 3)).reshape(col_taps * channels, row_taps * channels)
     conv = pl.pallas_call(
         horizontal_kernel,
@@ -88,7 +92,7 @@
         in_specs=[pl.BlockSpec(memory_space=pltpu.VMEM)] * 2,
         out_specs=pl.BlockSpec(memory_space=pltpu.VMEM),
         cost_estimate=pl.CostEstimate(
-            flops=2 * rows_lat * lanes * weights.shape[0] * weights.shape[1],
+            flops=2 * rows_lat * segment * weights.shape[0] * weights.shape[1],
             bytes_accessed=wide.size * 2 + weights.size * 2 + rows_lat * channels * cols_lon * 4,
             transcendentals=0,
         ),

time: 110 us -> 96.9 us (0.88)
  the two profiles are of different devices: /device:TPU:1 before, /device:TPU:24 now
where the time goes in v4:
time: 96.9 us; the launch traced here: 96.4 us
  waiting for transfers between devices  38 us (39%)
  starting transfers between devices  36.3 us (37%)
  other arithmetic  8.28 us (9%)
  local copies, waits for them, and re-layouts  6.63 us (7%)
  Pallas kernels  5.31 us (5%)
  matrix products  1.75 us (2%)
    ppermute x1, starting transfers between devices, local(): recv = lax.ppermute(send, 'lat_hi', [(0, 1), (1, 0)])  15.7 us
    ppermute x1, starting transfers between devices, lon_halo(): before = lax.ppermute(block[..., length - width:], 'lon', up)  10.8 us
    all_to_all x1, waiting for transfers between devices, local(): lax.all_to_all(normed, 'lat_lo', split_axis=2, concat_axis=0, tiled=True)  10.3 us
    all_to_all x1, waiting for transfers between devices, local(): lax.all_to_all(vertical(taps, w_vert, b_vert), 'lat_lo', split_axis=0, co...  10.2 us
    ppermute x1, waiting for transfers between devices, lon_halo(): before = lax.ppermute(block[..., length - width:], 'lon', up)  7.87 us
    ppermute x1, waiting for transfers between devices, lon_halo(): after = lax.ppermute(block[..., :width], 'lon', down)  5.91 us
    pallas_call x1, Pallas kernels, horizontal(): pl.pallas_call(horizontal_kernel, out_shape=jax.ShapeDtypeStruct((rows_la...  5.31 us
    all_to_all x1, starting transfers between devices, local(): lax.all_to_all(normed, 'lat_lo', split_axis=2, concat_axis=0, tiled=True)  4.3 us
  transfers between devices with their start and end apart: 5, of which 5 were waited for; matrix products, arithmetic and copies ran while one was open for 2% of the time, Pallas kernels for 0%

profile of v4, /device:TPU:24, one launch (start us, length us, event | category | flops | bytes accessed | tf_op | source)
XLA Modules:
  0.0 96.4 jit_solution(1702350878703658605)
XLA Ops:
  0.0 0.0 copy-start
  0.0 1.3 %convert_reduce_fusion = f32[32,128]{1,0:T(8,128)S(1)} fusion(bf16[1,64,32,128]{3,2,1,0:T(8,128)(2,1)} %param.7), kind=kLoop, calls=%fused_computation.3 | loop fusion | flops 520192 | bytes 540672 | tf_op jit(solution)/shard_map/reduce_sum | solution.py:11
  1.3 1.3 %fusion.3 = f32[32,128]{1,0:T(8,128)S(1)} fusion(f32[32,128]{1,0:T(8,128)S(1)} %broadcast_multiply_fusion, bf16[1,64,32,128]{3,2,1,0:T(8,128)(2,1)} %param.7), kind=kLoop, calls=%fused_computation.11 | loop fusion | flops 1044480 | bytes 557056 | tf_op jit(solution)/shard_map/reduce_sum | solution.py:12
  2.6 0.0 copy-done
  2.6 1.7 %fusion.19 = bf16[1,64,32,128]{3,1,0,2:T(8,128)(2,1)} fusion(f32[64]{0:T(128)} %param.9, f32[32,128]{1,0:T(8,128)S(1)} %add_rsqrt_fusion, f32[32,128]{1,0:T(8,128)S(1)} %broadcast_multiply_fusion, bf16[1,64,32,128]{3,2,1,0:T(8,128)(2,1)S(1)} %copy-done), kind=kLoop, calls=%fused_computation.33 | loop fusion | flops 1310720 | bytes 1081600 | tf_op jit(solution)/shard_map/convert_element_type | solution.py:13
  4.4 4.3 %all-to-all-start = ((bf16[1,64,32,128]{3,1,0,2:T(8,128)(2,1)}), bf16[1,64,32,128]{3,1,0,2:T(8,128)(2,1)S(1)}, u32[]{:S(2)}, u32[]{:S(2)}) async-start(bf16[1,64,32,128]{3,1,0,2:T(8,128)(2,1)} %fusion.19), calls=%async_computation | async-start | bytes 1048576 | tf_op jit(solution)/shard_map/all_to_all | solution.py:34
  8.7 10.3 %all-to-all-done = bf16[1,64,32,128]{3,1,0,2:T(8,128)(2,1)S(1)} async-done(((bf16[1,64,32,128]{3,1,0,2:T(8,128)(2,1)}), bf16[1,64,32,128]{3,1,0,2:T(8,128)(2,1)S(1)}, u32[]{:S(2)}, u32[]{:S(2)}) %all-to-all-start) | async-done | bytes 524320 | tf_op jit(solution)/shard_map/all_to_all | solution.py:34
  19.0 15.7 %collective-permute-start = (bf16[2,64,4,128]{3,1,2,0:T(8,128)(2,1)S(1)}, bf16[2,64,4,128]{3,1,2,0:T(8,128)(2,1)S(1)}, u32[]{:S(2)}, u32[]{:S(2)}) collective-permute-start(bf16[2,64,4,128]{3,1,2,0:T(8,128)(2,1)S(1)} %fusion.28), channel_id=1, source_target_pairs={{0,8},{8,0},{1,9},{9,1},{2,10},{10,2},{3,11},{11,3},{4,12},{12,4},... | collective-permute-start | bytes 393224 | tf_op jit(solution)/shard_map/ppermute | solution.py:38
  34.8 3.6 %collective-permute-done = bf16[2,64,4,128]{3,1,2,0:T(8,128)(2,1)S(1)} collective-permute-done((bf16[2,64,4,128]{3,1,2,0:T(8,128)(2,1)S(1)}, bf16[2,64,4,128]{3,1,2,0:T(8,128)(2,1)S(1)}, u32[]{:S(2)}, u32[]{:S(2)}) %collective-permute-start) | collective-permute-done | bytes 131104 | tf_op jit(solution)/shard_map/ppermute | solution.py:38
  38.4 0.0 copy-start.2
  38.4 0.1 fusion.20
  38.5 0.7 copy-done.2
  39.3 0.3 fusion.26
  39.6 0.4 convolution_add_fusion.3
  40.0 0.3 convolution_add_fusion.2
  40.3 0.4 convolution_add_fusion.1
  40.7 0.0 copy-start.4
  40.7 0.4 fusion
  41.1 0.3 copy-done.4
  41.4 0.0 copy-start.3
  41.4 1.2 %fusion.14 = bf16[8,64,4,128]{3,1,2,0:T(8,128)(2,1)} fusion(f32[8,8,8,4,128]{4,2,3,0,1:T(8,128)S(1)} %fusion, f32[64]{0:T(128)S(1)} %copy-done.4), kind=kLoop, calls=%fused_computation.22 | loop fusion | flops 2621440 | bytes 1573120 | tf_op jit(solution)/shard_map/convert_element_type | solution.py:28
  42.6 3.5 %all-to-all-start.1 = ((bf16[8,64,4,128]{3,1,2,0:T(8,128)(2,1)}), bf16[8,64,4,128]{3,1,2,0:T(8,128)(2,1)S(1)}, u32[]{:S(2)}, u32[]{:S(2)}) async-start(bf16[8,64,4,128]{3,1,2,0:T(8,128)(2,1)} %fusion.14), calls=%async_computation.1 | async-start | bytes 1048576 | tf_op jit(solution)/shard_map/all_to_all | solution.py:44
  46.1 0.0 copy-done.3
  46.1 10.2 %all-to-all-done.1 = bf16[8,64,4,128]{3,1,2,0:T(8,128)(2,1)S(1)} async-done(((bf16[8,64,4,128]{3,1,2,0:T(8,128)(2,1)}), bf16[8,64,4,128]{3,1,2,0:T(8,128)(2,1)S(1)}, u32[]{:S(2)}, u32[]{:S(2)}) %all-to-all-start.1) | async-done | bytes 524320 | tf_op jit(solution)/shard_map/all_to_all | solution.py:44
  56.4 0.3 copy_multiply_fusion
  56.7 0.0 copy-start.1
  56.7 1.0 %fusion.39 = (bf16[1,64,32,2]{3,2,1,0:T(8,128)(2,1)}, bf16[1,64,32,2]{3,2,1,0:T(8,128)(2,1)S(1)}) fusion(bf16[1,64,32,128]{3,2,1,0:T(8,128)(2,1)S(1)} %copy_multiply_fusion), kind=kLoop, calls=%fused_computation.63 | loop fusion | bytes 32768 | tf_op jit(solution)/shard_map/slice | solution.py:108
  57.7 10.8 %collective-permute-start.1 = (bf16[1,64,32,2]{3,2,1,0:T(8,128)(2,1)}, bf16[1,64,32,2]{3,2,1,0:T(8,128)(2,1)S(1)}, u32[]{:S(2)}, u32[]{:S(2)}) collective-permute-start(bf16[1,64,32,2]{3,2,1,0:T(8,128)(2,1)} %get-tuple-element.9), channel_id=1, source_target_pairs={{0,16},{16,32},{32,48},{48,64},{64,80},{80,96},{96,112},{112,128},... | collective-permute-start | bytes 24584 | tf_op jit(solution)/shard_map/ppermute | solution.py:108
  68.5 1.9 %collective-permute-start.2 = (bf16[1,64,32,2]{3,2,1,0:T(8,128)(2,1)S(1)}, bf16[1,64,32,2]{3,2,1,0:T(8,128)(2,1)S(1)}, u32[]{:S(2)}, u32[]{:S(2)}) collective-permute-start(bf16[1,64,32,2]{3,2,1,0:T(8,128)(2,1)S(1)} %get-tuple-element.10), channel_id=1, source_target_pairs={{16,0},{32,16},{48,32},{64,48},{80,64},{96,80},{112,96},{128,112},... | collective-permute-start | bytes 24584 | tf_op jit(solution)/shard_map/ppermute | solution.py:109
  70.5 0.0 copy-done.1
  70.5 0.3 copy.45
  70.8 1.1 %reshape.99.w_ref = bf16[320,320]{1,0:T(8,128)(2,1)} reshape(bf16[5,64,5,64]{3,2,1,0:T(8,128)(2,1)S(1)} %copy.45) | data formatting | bytes 409600 | tf_op jit(solution)/shard_map/reshape | solution.py:88
  71.9 0.1 pad.8.clone
  72.0 7.9 %collective-permute-done.1 = bf16[1,64,32,2]{3,2,1,0:T(8,128)(2,1)S(1)} collective-permute-done((bf16[1,64,32,2]{3,2,1,0:T(8,128)(2,1)}, bf16[1,64,32,2]{3,2,1,0:T(8,128)(2,1)S(1)}, u32[]{:S(2)}, u32[]{:S(2)}) %collective-permute-start.1) | collective-permute-done | bytes 8224 | tf_op jit(solution)/shard_map/ppermute | solution.py:108
  79.8 5.9 %collective-permute-done.2 = bf16[1,64,32,2]{3,2,1,0:T(8,128)(2,1)S(1)} collective-permute-done((bf16[1,64,32,2]{3,2,1,0:T(8,128)(2,1)S(1)}, bf16[1,64,32,2]{3,2,1,0:T(8,128)(2,1)S(1)}, u32[]{:S(2)}, u32[]{:S(2)}) %collective-permute-start.2) | collective-permute-done | bytes 8224 | tf_op jit(solution)/shard_map/ppermute | solution.py:109
  85.7 0.7 maximum_bitcast_fusion
  86.4 0.7 pad.4
  87.2 1.3 %copy.57 = bf16[8,8,36,256]{3,1,2,0:T(8,128)(2,1)} copy(bf16[8,8,36,256]{3,2,1,0:T(8,128)(2,1)S(1)} %bitcast.86) | data formatting | bytes 2359296
  88.4 0.0 copy-start.5
  88.4 5.3 %shard_map.73 = f32[32,64,128]{2,1,0:T(8,128)} custom-call(bf16[64,9216]{1,0:T(8,128)(2,1)} %bitcast.88, bf16[320,320]{1,0:T(8,128)(2,1)} %reshape.99.w_ref), custom_call_target="tpu_custom_call" | custom-call | flops 1677721600 | bytes 2433024 | tf_op jit(solution)/shard_map/pallas_call | solution.py:89
  93.7 0.0 copy-done.5
  93.7 1.5 %fusion.6 = bf16[1,64,32,128]{3,1,2,0:T(8,128)(2,1)S(1)} fusion(f32[32,64,128]{2,1,0:T(8,128)} %shard_map.73, f32[64]{0:T(128)S(1)} %copy-done.5, f32[32,128]{1,0:T(8,128)S(1)} %get-tuple-element.15, bf16[1,64,32,128]{3,2,1,0:T(8,128)(2,1)S(1)} %copy-done), kind=kLoop, calls=%fused_computation.14 | loop fusion | flops 1310720 | bytes 2113792 | tf_op jit(solution)/shard_map/convert_element_type | solution.py:50
  95.3 1.1 %copy.46 = bf16[1,64,32,128]{3,2,1,0:T(8,128)(2,1)} copy(bf16[1,64,32,128]{3,1,2,0:T(8,128)(2,1)S(1)} %fusion.6) | data formatting | bytes 1048576 | tf_op jit(solution)/shard_map/convert_element_type | solution.py:50
  (6 shorter events, 0.1 us)
Async XLA Ops:
  0.0 2.6 %copy-start = (bf16[1,64,32,128]{3,2,1,0:T(8,128)(2,1)S(1)}, bf16[1,64,32,128]{3,2,1,0:T(8,128)(2,1)}, u32[]{:S(2)}) copy-start(bf16[1,64,32,128]{3,2,1,0:T(8,128)(2,1)} %param.7) | copy-start | bytes 1572868
  4.4 14.6 %all-to-all-start = ((bf16[1,64,32,128]{3,1,0,2:T(8,128)(2,1)}), bf16[1,64,32,128]{3,1,0,2:T(8,128)(2,1)S(1)}, u32[]{:S(2)}, u32[]{:S(2)}) async-start(bf16[1,64,32,128]{3,1,0,2:T(8,128)(2,1)} %fusion.19), calls=%async_computation | async-start | bytes 1048576 | tf_op jit(solution)/shard_map/all_to_all | solution.py:34
  19.0 19.3 %collective-permute-start = (bf16[2,64,4,128]{3,1,2,0:T(8,128)(2,1)S(1)}, bf16[2,64,4,128]{3,1,2,0:T(8,128)(2,1)S(1)}, u32[]{:S(2)}, u32[]{:S(2)}) collective-permute-start(bf16[2,64,4,128]{3,1,2,0:T(8,128)(2,1)S(1)} %fusion.28), channel_id=1, source_target_pairs={{0,8},{8,0},{1,9},{9,1},{2,10},{10,2},{3,11},{11,3},{4,12},{12,4},... | collective-permute-start | bytes 393224 | tf_op jit(solution)/shard_map/ppermute | solution.py:38
  38.4 0.9 copy-start.2
  40.7 0.7 copy-start.4
  41.4 4.7 %copy-start.3 = (s32[1,32,128]{2,1,0:T(8,128)S(1)}, s32[1,32,128]{2,1,0:T(8,128)}, u32[]{:S(2)}) copy-start(s32[1,32,128]{2,1,0:T(8,128)} %param.8) | copy-start | bytes 49156
  42.6 13.8 %all-to-all-start.1 = ((bf16[8,64,4,128]{3,1,2,0:T(8,128)(2,1)}), bf16[8,64,4,128]{3,1,2,0:T(8,128)(2,1)S(1)}, u32[]{:S(2)}, u32[]{:S(2)}) async-start(bf16[8,64,4,128]{3,1,2,0:T(8,128)(2,1)} %fusion.14), calls=%async_computation.1 | async-start | bytes 1048576 | tf_op jit(solution)/shard_map/all_to_all | solution.py:44
  56.7 13.8 %copy-start.1 = (bf16[5,64,5,64]{3,1,2,0:T(8,128)(2,1)S(1)}, bf16[5,64,5,64]{3,1,2,0:T(8,128)(2,1)}, u32[]{:S(2)}) copy-start(bf16[5,64,5,64]{3,1,2,0:T(8,128)(2,1)} %param.12) | copy-start | bytes 614404
  57.7 22.1 %collective-permute-start.1 = (bf16[1,64,32,2]{3,2,1,0:T(8,128)(2,1)}, bf16[1,64,32,2]{3,2,1,0:T(8,128)(2,1)S(1)}, u32[]{:S(2)}, u32[]{:S(2)}) collective-permute-start(bf16[1,64,32,2]{3,2,1,0:T(8,128)(2,1)} %get-tuple-element.9), channel_id=1, source_target_pairs={{0,16},{16,32},{32,48},{48,64},{64,80},{80,96},{96,112},{112,128},... | collective-permute-start | bytes 24584 | tf_op jit(solution)/shard_map/ppermute | solution.py:108
  68.5 17.2 %collective-permute-start.2 = (bf16[1,64,32,2]{3,2,1,0:T(8,128)(2,1)S(1)}, bf16[1,64,32,2]{3,2,1,0:T(8,128)(2,1)S(1)}, u32[]{:S(2)}, u32[]{:S(2)}) collective-permute-start(bf16[1,64,32,2]{3,2,1,0:T(8,128)(2,1)S(1)} %get-tuple-element.10), channel_id=1, source_target_pairs={{16,0},{32,16},{48,32},{64,48},{80,64},{96,80},{112,96},{128,112},... | collective-permute-start | bytes 24584 | tf_op jit(solution)/shard_map/ppermute | solution.py:109
  88.4 5.3 %copy-start.5 = (f32[64]{0:T(128)S(1)}, f32[64]{0:T(128)}, u32[]{:S(2)}) copy-start(f32[64]{0:T(128)} %param.13) | copy-start | bytes 772

commit v5 on v4

--- a/solution.py
+++ b/solution.py
@@ -1,3 +1,5 @@
+import functools
+
 import jax
 from jax.experimental import pallas as pl
 from jax.experimental.pallas import tpu as pltpu
@@ -100,14 +102,54 @@
     return jnp.transpose(conv, (1, 0, 2))[None]
 
 
+def halo_kernel(count, left_edge, right_edge, from_left, from_right, send_sems, recv_sems):
+    me = lax.axis_index("lon")
+    right, left = lax.rem(me + 1, count), lax.rem(me + count - 1, count)
+    rest = (lax.axis_index("lat_hi"), lax.axis_index("lat_lo"))
+    mesh_ids = pl.DeviceIdType.MESH
+    barrier = pltpu.get_barrier_semaphore()
+    for neighbour in (left, right):
+        pl.semaphore_signal(barrier, inc=1, device_id=(neighbour,) + rest, device_id_type=mesh_ids)
+    pl.semaphore_wait(barrier, 2)
+    to_right = pltpu.make_async_remote_copy(
+        src_ref=right_edge,
+        dst_ref=from_left,
+        send_sem=send_sems.at[0],
+        recv_sem=recv_sems.at[0],
+        device_id=(right,) + rest,
+        device_id_type=mesh_ids,
+    )
+    to_left = pltpu.make_async_remote_copy(
+        src_ref=left_edge,
+        dst_ref=from_right,
+        send_sem=send_sems.at[1],
+        recv_sem=recv_sems.at[1],
+        device_id=(left,) + rest,
+        device_id_type=mesh_ids,
+    )
+    to_right.start()
+    to_left.start()
+    to_right.wait()
+    to_left.wait()
+
+
 def lon_halo(block, width):
-    devices = lax.axis_size("lon")
+    count = lax.axis_size("lon")
     length = block.shape[-1]
-    up = [(i, (i + 1) % devices) for i in range(devices)]
-    down = [(j, i) for i, j in up]
-    before = lax.ppermute(block[..., length - width :], "lon", up)
-    after = lax.ppermute(block[..., :width], "lon", down)
-    return before, after
+    edge_shape = block.shape[:-1] + (width,)
+    flat = (block.shape[1], block.shape[2] * width)
+    left_edge = block[..., :width].reshape(flat)
+    right_edge = block[..., length - width :].reshape(flat)
+    any_spec = pl.BlockSpec(memory_space=pl.ANY)
+    from_left, from_right = pl.pallas_call(
+        functools.partial(halo_kernel, count),
+        out_shape=(jax.ShapeDtypeStruct(flat, block.dtype),) * 2,
+        in_specs=[any_spec] * 2,
+        out_specs=(any_spec,) * 2,
+        scratch_shapes=[pltpu.SemaphoreType.DMA((2,)), pltpu.SemaphoreType.DMA((2,))],
+        compiler_params=pltpu.CompilerParams(collective_id=0, has_side_effects=True),
+    )(left_edge, right_edge)
+    return from_left.reshape(edge_shape), from_right.reshape(edge_shape)
 
 
 def solution(mesh):

time: 96.9 us -> 88.8 us (0.916)
  the two profiles are of different devices: /device:TPU:24 before, /device:TPU:1 now
where the time goes in v5:
time: 88.8 us; the launch traced here: 88 us
  starting transfers between devices  26.3 us (30%)
  waiting for transfers between devices  21.8 us (25%)
  Pallas kernels  17.7 us (20%)
  local copies, waits for them, and re-layouts  12 us (14%)
  other arithmetic  8.28 us (9%)
  matrix products  1.75 us (2%)
    pallas_call x1, Pallas kernels, lon_halo(): pl.pallas_call(functools.partial(halo_kernel, count), out_shape=(jax.Shap...  12.4 us
    ppermute x1, starting transfers between devices, local(): recv = lax.ppermute(send, 'lat_hi', [(0, 1), (1, 0)])  10.9 us
    all_to_all x1, starting transfers between devices, local(): lax.all_to_all(normed, 'lat_lo', split_axis=2, concat_axis=0, tiled=True)  10.3 us
    all_to_all x1, waiting for transfers between devices, local(): lax.all_to_all(normed, 'lat_lo', split_axis=2, concat_axis=0, tiled=True)  9.5 us
    all_to_all x1, waiting for transfers between devices, local(): lax.all_to_all(vertical(taps, w_vert, b_vert), 'lat_lo', split_axis=0, co...  8.01 us
    pallas_call x1, Pallas kernels, horizontal(): pl.pallas_call(horizontal_kernel, out_shape=jax.ShapeDtypeStruct((rows_la...  5.32 us
    all_to_all x1, starting transfers between devices, local(): lax.all_to_all(vertical(taps, w_vert, b_vert), 'lat_lo', split_axis=0, co...  5.12 us
    ppermute x1, waiting for transfers between devices, local(): recv = lax.ppermute(send, 'lat_hi', [(0, 1), (1, 0)])  4.28 us
  transfers between devices with their start and end apart: 3, of which 3 were waited for; matrix products, arithmetic and copies ran while one was open for 2% of the time, Pallas kernels for 0%

profile of v5, /device:TPU:1, one launch (start us, length us, event | category | flops | bytes accessed | tf_op | source)
XLA Modules:
  0.0 88.0 jit_solution(12458224834839484056)
XLA Ops:
  0.0 0.0 copy-start
  0.0 1.3 %convert_reduce_fusion = f32[32,128]{1,0:T(8,128)S(1)} fusion(bf16[1,64,32,128]{3,2,1,0:T(8,128)(2,1)} %param.7), kind=kLoop, calls=%fused_computation.3 | loop fusion | flops 520192 | bytes 540672 | tf_op jit(solution)/shard_map/reduce_sum | solution.py:13
  1.3 1.3 %fusion.3 = f32[32,128]{1,0:T(8,128)S(1)} fusion(f32[32,128]{1,0:T(8,128)S(1)} %broadcast_multiply_fusion, bf16[1,64,32,128]{3,2,1,0:T(8,128)(2,1)} %param.7), kind=kLoop, calls=%fused_computation.11 | loop fusion | flops 1044480 | bytes 557056 | tf_op jit(solution)/shard_map/reduce_sum | solution.py:14
  2.6 0.0 copy-done
  2.6 1.7 %fusion.19 = bf16[1,64,32,128]{3,1,0,2:T(8,128)(2,1)} fusion(f32[64]{0:T(128)} %param.9, f32[32,128]{1,0:T(8,128)S(1)} %add_rsqrt_fusion, f32[32,128]{1,0:T(8,128)S(1)} %broadcast_multiply_fusion, bf16[1,64,32,128]{3,2,1,0:T(8,128)(2,1)S(1)} %copy-done), kind=kLoop, calls=%fused_computation.33 | loop fusion | flops 1310720 | bytes 1081600 | tf_op jit(solution)/shard_map/convert_element_type | solution.py:15
  4.4 10.3 %all-to-all-start = ((bf16[1,64,32,128]{3,1,0,2:T(8,128)(2,1)}), bf16[1,64,32,128]{3,1,0,2:T(8,128)(2,1)S(1)}, u32[]{:S(2)}, u32[]{:S(2)}) async-start(bf16[1,64,32,128]{3,1,0,2:T(8,128)(2,1)} %fusion.19), calls=%async_computation | async-start | bytes 1048576 | tf_op jit(solution)/shard_map/all_to_all | solution.py:36
  14.6 9.5 %all-to-all-done = bf16[1,64,32,128]{3,1,0,2:T(8,128)(2,1)S(1)} async-done(((bf16[1,64,32,128]{3,1,0,2:T(8,128)(2,1)}), bf16[1,64,32,128]{3,1,0,2:T(8,128)(2,1)S(1)}, u32[]{:S(2)}, u32[]{:S(2)}) %all-to-all-start) | async-done | bytes 524320 | tf_op jit(solution)/shard_map/all_to_all | solution.py:36
  24.2 10.9 %collective-permute-start = (bf16[2,64,4,128]{3,1,2,0:T(8,128)(2,1)S(1)}, bf16[2,64,4,128]{3,1,2,0:T(8,128)(2,1)S(1)}, u32[]{:S(2)}, u32[]{:S(2)}) collective-permute-start(bf16[2,64,4,128]{3,1,2,0:T(8,128)(2,1)S(1)} %fusion.28), channel_id=1, source_target_pairs={{0,8},{8,0},{1,9},{9,1},{2,10},{10,2},{3,11},{11,3},{4,12},{12,4},... | collective-permute-start | bytes 393224 | tf_op jit(solution)/shard_map/ppermute | solution.py:40
  35.1 4.3 %collective-permute-done = bf16[2,64,4,128]{3,1,2,0:T(8,128)(2,1)S(1)} collective-permute-done((bf16[2,64,4,128]{3,1,2,0:T(8,128)(2,1)S(1)}, bf16[2,64,4,128]{3,1,2,0:T(8,128)(2,1)S(1)}, u32[]{:S(2)}, u32[]{:S(2)}) %collective-permute-start) | collective-permute-done | bytes 131104 | tf_op jit(solution)/shard_map/ppermute | solution.py:40
  39.4 0.0 copy-start.2
  39.4 0.1 fusion.20
  39.6 0.7 copy-done.2
  40.3 0.3 fusion.26
  40.7 0.4 convolution_add_fusion.3
  41.0 0.3 convolution_add_fusion.2
  41.4 0.4 convolution_add_fusion.1
  41.7 0.0 copy-start.4
  41.8 0.4 fusion
  42.1 0.3 copy-done.4
  42.4 0.0 copy-start.1
  42.4 1.2 %fusion.14 = bf16[8,64,4,128]{3,1,2,0:T(8,128)(2,1)} fusion(f32[8,8,8,4,128]{4,2,3,0,1:T(8,128)S(1)} %fusion, f32[64]{0:T(128)S(1)} %copy-done.4), kind=kLoop, calls=%fused_computation.22 | loop fusion | flops 2621440 | bytes 1573120 | tf_op jit(solution)/shard_map/convert_element_type | solution.py:30
  43.6 0.0 copy-start.3
  43.6 5.1 %all-to-all-start.1 = ((bf16[8,64,4,128]{3,1,2,0:T(8,128)(2,1)}), bf16[8,64,4,128]{3,1,2,0:T(8,128)(2,1)S(1)}, u32[]{:S(2)}, u32[]{:S(2)}) async-start(bf16[8,64,4,128]{3,1,2,0:T(8,128)(2,1)} %fusion.14), calls=%async_computation.1 | async-start | bytes 1048576 | tf_op jit(solution)/shard_map/all_to_all | solution.py:46
  48.8 0.0 copy-done.1
  48.8 0.3 copy.61
  49.1 1.1 %reshape.115.w_ref = bf16[320,320]{1,0:T(8,128)(2,1)} reshape(bf16[5,64,5,64]{3,2,1,0:T(8,128)(2,1)S(1)} %copy.61) | data formatting | bytes 409600 | tf_op jit(solution)/shard_map/reshape | solution.py:90
  50.2 0.1 pad.8.clone
  50.2 0.0 copy-done.3
  50.2 8.0 %all-to-all-done.1 = bf16[8,64,4,128]{3,1,2,0:T(8,128)(2,1)S(1)} async-done(((bf16[8,64,4,128]{3,1,2,0:T(8,128)(2,1)}), bf16[8,64,4,128]{3,1,2,0:T(8,128)(2,1)S(1)}, u32[]{:S(2)}, u32[]{:S(2)}) %all-to-all-start.1) | async-done | bytes 524320 | tf_op jit(solution)/shard_map/all_to_all | solution.py:46
  58.3 0.3 copy_multiply_fusion
  58.6 0.2 fusion.39
  58.8 0.6 copy.53
  59.4 0.7 copy.55.left_edge
  60.1 0.6 copy.54
  60.7 0.7 copy.56.right_edge
  61.4 12.4 %shard_map.73 = (bf16[64,64]{1,0:T(8,128)(2,1)}, bf16[64,64]{1,0:T(8,128)(2,1)}) custom-call(bf16[64,64]{1,0:T(8,128)(2,1)} %copy.55.left_edge, bf16[64,64]{1,0:T(8,128)(2,1)} %copy.56.right_edge), custom_call_target="tpu_custom_call" | custom-call | tf_op jit(solution)/shard_map/pallas_call | solution.py:144
  73.8 0.8 copy.57
  74.6 0.9 %copy.59 = bf16[1,64,32,2]{3,2,1,0:T(8,128)(2,1)S(1)} copy(bf16[1,64,32,2]{1,3,2,0:T(2,128)(2,1)S(1)} %bitcast.96) | data formatting | bytes 16384 | tf_op jit(solution)/shard_map/reshape | solution.py:152
  75.5 0.8 copy.58
  76.3 0.9 %copy.60 = bf16[1,64,32,2]{3,2,1,0:T(8,128)(2,1)S(1)} copy(bf16[1,64,32,2]{1,3,2,0:T(2,128)(2,1)S(1)} %bitcast.97) | data formatting | bytes 16384 | tf_op jit(solution)/shard_map/reshape | solution.py:152
  77.3 0.7 maximum_bitcast_fusion
  78.0 0.7 pad.4
  78.7 1.3 %copy.73 = bf16[8,8,36,256]{3,1,2,0:T(8,128)(2,1)} copy(bf16[8,8,36,256]{3,2,1,0:T(8,128)(2,1)S(1)} %bitcast.90) | data formatting | bytes 2359296
  80.0 0.0 copy-start.5
  80.0 5.3 %shard_map.74 = f32[32,64,128]{2,1,0:T(8,128)} custom-call(bf16[64,9216]{1,0:T(8,128)(2,1)} %bitcast.92, bf16[320,320]{1,0:T(8,128)(2,1)} %reshape.115.w_ref), custom_call_target="tpu_custom_call" | custom-call | flops 1677721600 | bytes 2433024 | tf_op jit(solution)/shard_map/pallas_call | solution.py:91
  85.3 0.0 copy-done.5
  85.3 1.5 %fusion.6 = bf16[1,64,32,128]{3,1,2,0:T(8,128)(2,1)S(1)} fusion(f32[32,64,128]{2,1,0:T(8,128)} %shard_map.74, f32[64]{0:T(128)S(1)} %copy-done.5, f32[32,128]{1,0:T(8,128)S(1)} %get-tuple-element.19, bf16[1,64,32,128]{3,2,1,0:T(8,128)(2,1)S(1)} %copy-done), kind=kLoop, calls=%fused_computation.14 | loop fusion | flops 1310720 | bytes 2113792 | tf_op jit(solution)/shard_map/convert_element_type | solution.py:52
  86.8 1.1 %copy.62 = bf16[1,64,32,128]{3,2,1,0:T(8,128)(2,1)} copy(bf16[1,64,32,128]{3,1,2,0:T(8,128)(2,1)S(1)} %fusion.6) | data formatting | bytes 1048576 | tf_op jit(solution)/shard_map/convert_element_type | solution.py:52
  (6 shorter events, 0.1 us)
Async XLA Ops:
  0.0 2.6 %copy-start = (bf16[1,64,32,128]{3,2,1,0:T(8,128)(2,1)S(1)}, bf16[1,64,32,128]{3,2,1,0:T(8,128)(2,1)}, u32[]{:S(2)}) copy-start(bf16[1,64,32,128]{3,2,1,0:T(8,128)(2,1)} %param.7) | copy-start | bytes 1572868
  4.4 19.8 %all-to-all-start = ((bf16[1,64,32,128]{3,1,0,2:T(8,128)(2,1)}), bf16[1,64,32,128]{3,1,0,2:T(8,128)(2,1)S(1)}, u32[]{:S(2)}, u32[]{:S(2)}) async-start(bf16[1,64,32,128]{3,1,0,2:T(8,128)(2,1)} %fusion.19), calls=%async_computation | async-start | bytes 1048576 | tf_op jit(solution)/shard_map/all_to_all | solution.py:36
  24.2 15.2 %collective-permute-start = (bf16[2,64,4,128]{3,1,2,0:T(8,128)(2,1)S(1)}, bf16[2,64,4,128]{3,1,2,0:T(8,128)(2,1)S(1)}, u32[]{:S(2)}, u32[]{:S(2)}) collective-permute-start(bf16[2,64,4,128]{3,1,2,0:T(8,128)(2,1)S(1)} %fusion.28), channel_id=1, source_target_pairs={{0,8},{8,0},{1,9},{9,1},{2,10},{10,2},{3,11},{11,3},{4,12},{12,4},... | collective-permute-start | bytes 393224 | tf_op jit(solution)/shard_map/ppermute | solution.py:40
  39.4 0.9 %copy-start.2 = (bf16[5,8,8,8]{3,2,1,0:T(8,128)(2,1)S(1)}, bf16[5,8,8,8]{3,2,1,0:T(8,128)(2,1)}, u32[]{:S(2)}) copy-start(bf16[5,8,8,8]{3,2,1,0:T(8,128)(2,1)} %param.10) | copy-start | bytes 15364
  41.7 0.7 copy-start.4
  42.4 6.4 %copy-start.1 = (bf16[5,64,5,64]{3,1,2,0:T(8,128)(2,1)S(1)}, bf16[5,64,5,64]{3,1,2,0:T(8,128)(2,1)}, u32[]{:S(2)}) copy-start(bf16[5,64,5,64]{3,1,2,0:T(8,128)(2,1)} %param.12) | copy-start | bytes 614404
  43.6 6.6 %copy-start.3 = (s32[1,32,128]{2,1,0:T(8,128)S(1)}, s32[1,32,128]{2,1,0:T(8,128)}, u32[]{:S(2)}) copy-start(s32[1,32,128]{2,1,0:T(8,128)} %param.8) | copy-start | bytes 49156
  43.6 14.6 %all-to-all-start.1 = ((bf16[8,64,4,128]{3,1,2,0:T(8,128)(2,1)}), bf16[8,64,4,128]{3,1,2,0:T(8,128)(2,1)S(1)}, u32[]{:S(2)}, u32[]{:S(2)}) async-start(bf16[8,64,4,128]{3,1,2,0:T(8,128)(2,1)} %fusion.14), calls=%async_computation.1 | async-start | bytes 1048576 | tf_op jit(solution)/shard_map/all_to_all | solution.py:46
  80.0 5.3 %copy-start.5 = (f32[64]{0:T(128)S(1)}, f32[64]{0:T(128)}, u32[]{:S(2)}) copy-start(f32[64]{0:T(128)} %param.13) | copy-start | bytes 772

commit v6 on v4

--- a/solution.py
+++ b/solution.py
@@ -1,3 +1,5 @@
+import functools
+
 import jax
 from jax.experimental import pallas as pl
 from jax.experimental.pallas import tpu as pltpu
@@ -52,7 +54,18 @@
     )
 
 
-def horizontal_kernel(x_ref, w_ref, o_ref):
+def horizontal_kernel(
+    count, x_ref, w_ref, right_ref, left_ref, o_ref, yl_ref, yr_ref,
+    from_left, from_right, send_sems, recv_sems,
+):
+    me = lax.axis_index("lon")
+    right, left = lax.rem(me + 1, count), lax.rem(me + count - 1, count)
+    rest = (lax.axis_index("lat_hi"), lax.axis_index("lat_lo"))
+    mesh_ids = pl.DeviceIdType.MESH
+    barrier = pltpu.get_barrier_semaphore()
+    for neighbour in (left, right):
+        pl.semaphore_signal(barrier, inc=1, device_id=(neighbour,) + rest, device_id_type=mesh_ids)
+
     rows, channels, cols_lon = o_ref.shape
     taps = w_ref.shape[0] // channels
     segment = x_ref.shape[1] // (rows + taps - 1)
@@ -74,40 +87,93 @@
         for row in range(chunk):
             o_ref[start + row] = total[:, row * segment : row * segment + cols_lon]
 
+    pl.semaphore_wait(barrier, 2)
+    to_right = pltpu.make_async_remote_copy(
+        src_ref=right_ref,
+        dst_ref=from_left,
+        send_sem=send_sems.at[0],
+        recv_sem=recv_sems.at[0],
+        device_id=(right,) + rest,
+        device_id_type=mesh_ids,
+    )
+    to_left = pltpu.make_async_remote_copy(
+        src_ref=left_ref,
+        dst_ref=from_right,
+        send_sem=send_sems.at[1],
+        recv_sem=recv_sems.at[1],
+        device_id=(left,) + rest,
+        device_id_type=mesh_ids,
+    )
+    to_right.start()
+    to_left.start()
+    to_right.wait()
+    to_left.wait()
+    yl_ref[...] = jnp.dot(weights, from_left[...], preferred_element_type=jnp.float32)
+    yr_ref[...] = jnp.dot(weights, from_right[...], preferred_element_type=jnp.float32)
+
+
+def stacked_edge(edge, reach_row):
+    channels, rows_lat, width = edge.shape
+    padded = jnp.pad(edge, ((0, 0), (reach_row, reach_row), (0, 0)))
+    return jnp.concatenate(
+        [
+            padded[:, row_tap : row_tap + rows_lat].reshape(channels, rows_lat * width)
+            for row_tap in range(2 * reach_row + 1)
+        ],
+        axis=0,
+    )
+
 
 def horizontal(masked, w_horiz):
     row_taps, channels, col_taps, _ = w_horiz.shape
     reach_row, reach_col = row_taps // 2, col_taps // 2
     _, _, rows_lat, cols_lon = masked.shape
-    before, after = lon_halo(masked, reach_col)
+    count = lax.axis_size("lon")
     segment = 2 * cols_lon
-    gap = jnp.zeros(masked.shape[:3] + (segment - cols_lon - 2 * reach_col,), masked.dtype)
-    wide = jnp.concatenate([before, masked, after, gap], axis=3)[0]
+    block = masked[0]
+    side = jnp.zeros((channels, rows_lat, reach_col), masked.dtype)
+    gap = jnp.zeros((channels, rows_lat, segment - cols_lon - 2 * reach_col), masked.dtype)
+    wide = jnp.concatenate([side, block, side, gap], axis=2)
     wide = jnp.pad(wide, ((0, 0), (reach_row, reach_row), (0, 0)))
     wide = wide.reshape(channels, (rows_lat + 2 * reach_row) * segment)
     weights = jnp.transpose(w_horiz, (2, 1, 0, 3)).reshape(col_taps * channels, row_taps * channels)
-    conv = pl.pallas_call(
-        horizontal_kernel,
-        out_shape=jax.ShapeDtypeStruct((rows_lat, channels, cols_lon), jnp.float32),
-        in_specs=[pl.BlockSpec(memory_space=pltpu.VMEM)] * 2,
-        out_specs=pl.BlockSpec(memory_space=pltpu.VMEM),
+    right_edge = stacked_edge(block[:, :, cols_lon - reach_col :], reach_row)
+    left_edge = stacked_edge(block[:, :, :reach_col], reach_row)
+    vmem = pl.BlockSpec(memory_space=pltpu.VMEM)
+    edge_out = jax.ShapeDtypeStruct((weights.shape[0], right_edge.shape[1]), jnp.float32)
+    conv, from_left, from_right = pl.pallas_call(
+        functools.partial(horizontal_kernel, count),
+        out_shape=(
+            jax.ShapeDtypeStruct((rows_lat, channels, cols_lon), jnp.float32),
+            edge_out,
+            edge_out,
+        ),
+        in_specs=[vmem] * 4,
+        out_specs=(vmem,) * 3,
+        scratch_shapes=[
+            pltpu.VMEM(right_edge.shape, right_edge.dtype),
+            pltpu.VMEM(left_edge.shape, left_edge.dtype),
+            pltpu.SemaphoreType.DMA((2,)),
+            pltpu.SemaphoreType.DMA((2,)),
+        ],
+        compiler_params=pltpu.CompilerParams(collective_id=0, has_side_effects=True),
         cost_estimate=pl.CostEstimate(
             flops=2 * rows_lat * segment * weights.shape[0] * weights.shape[1],
             bytes_accessed=wide.size * 2 + weights.size * 2 + rows_lat * channels * cols_lon * 4,
             transcendentals=0,
         ),
-    )(wide, weights)
-    return jnp.transpose(conv, (1, 0, 2))[None]
-
-
-def lon_halo(block, width):
-    devices = lax.axis_size("lon")
-    length = block.shape[-1]
-    up = [(i, (i + 1) % devices) for i in range(devices)]
-    down = [(j, i) for i, j in up]
-    before = lax.ppermute(block[..., length - width :], "lon", up)
-    after = lax.ppermute(block[..., :width], "lon", down)
-    return before, after
+    )(wide, weights, right_edge, left_edge)
+    conv = jnp.transpose(conv, (1, 0, 2))
+    lanes = lambda y, tap, col: y[tap * channels : (tap + 1) * channels, col::reach_col]
+    first = lanes(from_left, 0, 0) + lanes(from_left, 1, 1)
+    second = lanes(from_left, 0, 1)
+    before_last = lanes(from_right, col_taps - 1, 0)
+    last = lanes(from_right, col_taps - 2, 0) + lanes(from_right, col_taps - 1, 1)
+    middle = jnp.zeros((channels, rows_lat, cols_lon - 2 * reach_col), jnp.float32)
+    fix = jnp.concatenate(
+        [first[..., None], second[..., None], middle, before_last[..., None], last[..., None]], axis=2
+    )
+    return (conv + fix)[None]
 
 
 def solution(mesh):

time: 96.9 us -> 104 us (1.073)
  the two profiles are of different devices: /device:TPU:24 before, /device:TPU:1 now
where the time goes in v6:
time: 104 us; the launch traced here: 103 us
  starting transfers between devices  26.3 us (25%)
  local copies, waits for them, and re-layouts  26 us (25%)
  waiting for transfers between devices  21.8 us (21%)
  Pallas kernels  16.9 us (16%)
  other arithmetic  9.45 us (9%)
  matrix products  1.75 us (2%)
    pallas_call x1, Pallas kernels, horizontal(): pl.pallas_call(functools.partial(horizontal_kernel, count), out_shape=(ja...  16.9 us
    ppermute x1, starting transfers between devices, local(): recv = lax.ppermute(send, 'lat_hi', [(0, 1), (1, 0)])  10.9 us
    all_to_all x1, starting transfers between devices, local(): lax.all_to_all(normed, 'lat_lo', split_axis=2, concat_axis=0, tiled=True)  10.4 us
    all_to_all x1, waiting for transfers between devices, local(): lax.all_to_all(normed, 'lat_lo', split_axis=2, concat_axis=0, tiled=True)  9.5 us
    all_to_all x1, waiting for transfers between devices, local(): lax.all_to_all(vertical(taps, w_vert, b_vert), 'lat_lo', split_axis=0, co...  8.03 us
    slice x6, local copies, waits for them, and re-layouts, horizontal(): y[tap * channels:(tap + 1) * channels, col::reach_col]  6.54 us
    all_to_all x1, starting transfers between devices, local(): lax.all_to_all(vertical(taps, w_vert, b_vert), 'lat_lo', split_axis=0, co...  4.99 us
    concatenate x1, local copies, waits for them, and re-layouts, horizontal(): jnp.concatenate([first[..., None], second[..., None], middle, before_last...  4.44 us
  transfers between devices with their start and end apart: 3, of which 3 were waited for; matrix products, arithmetic and copies ran while one was open for 1% of the time, Pallas kernels for 0%

profile of v6, /device:TPU:1, one launch (start us, length us, event | category | flops | bytes accessed | tf_op | source)
XLA Modules:
  0.0 102.6 jit_solution(12654028556524999087)
XLA Ops:
  0.0 1.2 %convert_reduce_fusion = f32[32,128]{1,0:T(8,128)S(1)} fusion(bf16[1,64,32,128]{3,2,1,0:T(8,128)(2,1)} %param.7), kind=kLoop, calls=%fused_computation.4 | loop fusion | flops 520192 | bytes 540672 | tf_op jit(solution)/shard_map/reduce_sum | solution.py:13
  1.2 1.3 %fusion.3 = f32[32,128]{1,0:T(8,128)S(1)} fusion(f32[32,128]{1,0:T(8,128)S(1)} %broadcast_multiply_fusion.1, bf16[1,64,32,128]{3,2,1,0:T(8,128)(2,1)} %param.7), kind=kLoop, calls=%fused_computation.12 | loop fusion | flops 1044480 | bytes 557056 | tf_op jit(solution)/shard_map/reduce_sum | solution.py:14
  2.5 2.2 %fusion.21 = bf16[1,64,32,128]{3,1,0,2:T(8,128)(2,1)} fusion(f32[64]{0:T(128)} %param.9, f32[32,128]{1,0:T(8,128)S(1)} %add_rsqrt_fusion, f32[32,128]{1,0:T(8,128)S(1)} %broadcast_multiply_fusion.1, bf16[1,64,32,128]{3,2,1,0:T(8,128)(2,1)} %param.7), kind=kLoop, calls=%fused_computation.36 | loop fusion | flops 1310720 | bytes 1081600 | tf_op jit(solution)/shard_map/convert_element_type | solution.py:15
  4.7 0.0 copy-start.2
  4.7 10.4 %all-to-all-start = ((bf16[1,64,32,128]{3,1,0,2:T(8,128)(2,1)}), bf16[1,64,32,128]{3,1,0,2:T(8,128)(2,1)S(1)}, u32[]{:S(2)}, u32[]{:S(2)}) async-start(bf16[1,64,32,128]{3,1,0,2:T(8,128)(2,1)} %fusion.21), calls=%async_computation | async-start | bytes 1048576 | tf_op jit(solution)/shard_map/all_to_all | solution.py:36
  15.1 9.5 %all-to-all-done = bf16[1,64,32,128]{3,1,0,2:T(8,128)(2,1)S(1)} async-done(((bf16[1,64,32,128]{3,1,0,2:T(8,128)(2,1)}), bf16[1,64,32,128]{3,1,0,2:T(8,128)(2,1)S(1)}, u32[]{:S(2)}, u32[]{:S(2)}) %all-to-all-start) | async-done | bytes 524320 | tf_op jit(solution)/shard_map/all_to_all | solution.py:36
  24.6 10.9 %collective-permute-start = (bf16[2,64,4,128]{3,1,2,0:T(8,128)(2,1)S(1)}, bf16[2,64,4,128]{3,1,2,0:T(8,128)(2,1)S(1)}, u32[]{:S(2)}, u32[]{:S(2)}) collective-permute-start(bf16[2,64,4,128]{3,1,2,0:T(8,128)(2,1)S(1)} %fusion.30), channel_id=1, source_target_pairs={{0,8},{8,0},{1,9},{9,1},{2,10},{10,2},{3,11},{11,3},{4,12},{12,4},... | collective-permute-start | bytes 393224 | tf_op jit(solution)/shard_map/ppermute | solution.py:40
  35.6 4.3 %collective-permute-done = bf16[2,64,4,128]{3,1,2,0:T(8,128)(2,1)S(1)} collective-permute-done((bf16[2,64,4,128]{3,1,2,0:T(8,128)(2,1)S(1)}, bf16[2,64,4,128]{3,1,2,0:T(8,128)(2,1)S(1)}, u32[]{:S(2)}, u32[]{:S(2)}) %collective-permute-start) | collective-permute-done | bytes 131104 | tf_op jit(solution)/shard_map/ppermute | solution.py:40
  39.9 0.1 fusion.22
  40.0 0.0 copy-done.2
  40.0 0.3 fusion.28
  40.4 0.4 convolution_add_fusion.3
  40.7 0.3 convolution_add_fusion.2
  41.1 0.0 copy-start.6
  41.1 0.4 convolution_add_fusion.1
  41.5 0.0 copy-start.1
  41.5 0.4 fusion
  41.8 0.0 copy-done.6
  41.9 0.0 copy-start.3
  41.9 1.2 %fusion.14 = bf16[8,64,4,128]{3,1,2,0:T(8,128)(2,1)} fusion(f32[8,8,8,4,128]{4,2,3,0,1:T(8,128)S(1)} %fusion, f32[64]{0:T(128)S(1)} %copy-done.6), kind=kLoop, calls=%fused_computation.23 | loop fusion | flops 2621440 | bytes 1573120 | tf_op jit(solution)/shard_map/convert_element_type | solution.py:30
  43.1 5.0 %all-to-all-start.1 = ((bf16[8,64,4,128]{3,1,2,0:T(8,128)(2,1)}), bf16[8,64,4,128]{3,1,2,0:T(8,128)(2,1)S(1)}, u32[]{:S(2)}, u32[]{:S(2)}) async-start(bf16[8,64,4,128]{3,1,2,0:T(8,128)(2,1)} %fusion.14), calls=%async_computation.1 | async-start | bytes 1048576 | tf_op jit(solution)/shard_map/all_to_all | solution.py:46
  48.1 0.0 copy-done.1
  48.1 0.3 copy.65
  48.4 1.1 %reshape.121.w_ref = bf16[320,320]{1,0:T(8,128)(2,1)} reshape(bf16[5,64,5,64]{3,2,1,0:T(8,128)(2,1)S(1)} %copy.65) | data formatting | bytes 409600 | tf_op jit(solution)/shard_map/reshape | solution.py:139
  49.5 0.1 pad.17.clone
  49.6 0.0 copy-done.3
  49.6 8.0 %all-to-all-done.1 = bf16[8,64,4,128]{3,1,2,0:T(8,128)(2,1)S(1)} async-done(((bf16[8,64,4,128]{3,1,2,0:T(8,128)(2,1)}), bf16[8,64,4,128]{3,1,2,0:T(8,128)(2,1)S(1)}, u32[]{:S(2)}, u32[]{:S(2)}) %all-to-all-start.1) | async-done | bytes 524320 | tf_op jit(solution)/shard_map/all_to_all | solution.py:46
  57.6 0.5 copy.63
  58.1 0.7 broadcast_multiply_fusion
  58.8 0.1 copy.68
  58.9 0.1 pad_slice_fusion.4
  59.0 0.1 copy.73
  59.1 0.1 copy.75
  59.2 0.1 copy.72
  59.3 0.1 copy.74
  59.4 0.1 copy.71
  59.5 0.1 copy.66
  59.6 0.1 copy.69
  59.7 0.1 copy.67
  59.8 0.1 copy.70
  60.0 0.7 maximum_maximum_fusion
  60.7 0.6 pad.11
  61.3 2.2 %copy.86.x_ref = bf16[64,9216]{1,0:T(8,128)(2,1)} copy(bf16[64,9216]{0,1:T(8,128)(2,1)S(1)} %bitcast.102) | data formatting | bytes 2359296 | tf_op jit(solution)/shard_map/reshape | solution.py:138
  63.5 0.0 copy-start.5
  63.6 0.6 copy-done.5
  64.2 0.0 copy-start.4
  64.2 0.6 copy-done.4
  64.8 16.9 %shard_map.73 = (f32[32,64,128]{2,1,0:T(8,128)}, f32[320,64]{1,0:T(8,128)}, f32[320,64]{1,0:T(8,128)}) custom-call(bf16[64,9216]{1,0:T(8,128)(2,1)} %copy.86.x_ref, bf16[320,320]{1,0:T(8,128)(2,1)} %reshape.121.w_ref, bf16[320,64]{1,0:T(8,128)(2,1)} %copy-done.5, bf16[320,64]{1,0:T(8,128)(2,1)} %copy-done.4), custom_call_target="tpu_custom_call" | custom-call | flops 1677721600 | bytes 2433024 | tf_op jit(solution)/shard_map/pallas_call | solution.py:144
  81.7 1.1 %slice.112 = f32[64,32]{1,0:T(8,128)S(1)} slice(f32[320,64]{1,0:T(8,128)} %get-tuple-element.9), slice={[0:64:1], [1:64:2]} | slice | bytes 16384 | tf_op jit(solution)/shard_map/slice | solution.py:167
  82.8 1.1 %slice.111 = f32[64,32]{1,0:T(8,128)S(1)} slice(f32[320,64]{1,0:T(8,128)} %get-tuple-element.9), slice={[64:128:1], [1:64:2]} | slice | bytes 16384 | tf_op jit(solution)/shard_map/slice | solution.py:167
  83.9 1.1 %slice.110 = f32[64,32]{1,0:T(8,128)S(1)} slice(f32[320,64]{1,0:T(8,128)} %get-tuple-element.9), slice={[0:64:1], [0:64:2]} | slice | bytes 16384 | tf_op jit(solution)/shard_map/slice | solution.py:167
  85.0 1.1 %slice.115 = f32[64,32]{1,0:T(8,128)S(1)} slice(f32[320,64]{1,0:T(8,128)} %get-tuple-element.10), slice={[256:320:1], [1:64:2]} | slice | bytes 16384 | tf_op jit(solution)/shard_map/slice | solution.py:167
  86.1 1.1 %slice.114 = f32[64,32]{1,0:T(8,128)S(1)} slice(f32[320,64]{1,0:T(8,128)} %get-tuple-element.10), slice={[192:256:1], [0:64:2]} | slice | bytes 16384 | tf_op jit(solution)/shard_map/slice | solution.py:167
  87.2 1.1 %slice.113 = f32[64,32]{1,0:T(8,128)S(1)} slice(f32[320,64]{1,0:T(8,128)} %get-tuple-element.10), slice={[256:320:1], [0:64:2]} | slice | bytes 16384 | tf_op jit(solution)/shard_map/slice | solution.py:167
  88.3 1.0 copy.78
  89.3 1.0 copy.79
  90.3 1.8 %copy.76 = f32[64,32,1]{2,0,1:T(8,128)} copy(f32[64,32,1]{1,0,2:T(8,128)S(1)} %add_bitcast_fusion.1) | data formatting | bytes 16384 | tf_op jit(solution)/shard_map/broadcast_in_dim | solution.py:174
  92.1 1.8 %copy.77 = f32[64,32,1]{2,0,1:T(8,128)} copy(f32[64,32,1]{1,0,2:T(8,128)S(1)} %bitcast.110) | data formatting | bytes 16384 | tf_op jit(solution)/shard_map/broadcast_in_dim | solution.py:174
  94.0 1.1 %broadcast_in_dim.37 = f32[64,32,124]{2,0,1:T(8,128)} broadcast(f32[]{:T(128)} %constant.6.clone.1), dimensions={} | broadcast | bytes 1015812 | tf_op jit(solution)/shard_map/broadcast_in_dim | solution.py:172
  95.1 4.4 %concatenate.26 = f32[64,32,128]{2,0,1:T(8,128)} concatenate(f32[64,32,1]{2,0,1:T(8,128)} %copy.76, f32[64,32,1]{2,0,1:T(8,128)} %copy.77, f32[64,32,124]{2,0,1:T(8,128)} %broadcast_in_dim.37, f32[64,32,1]{2,0,1:T(8,128)S(1)} %copy.78, f32[64,32,1]{2,0,1:T(8,128)S(1)} %copy.79), dimensions={2} | concatenate | bytes 2097152 | tf_op jit(solution)/shard_map/concatenate | solution.py:173
  99.5 0.0 copy-done
  99.5 0.0 copy-done.7
  99.5 1.9 %fusion.6 = bf16[1,64,32,128]{3,1,2,0:T(8,128)(2,1)S(1)} fusion(f32[64,32,128]{2,0,1:T(8,128)} %concatenate.26, f32[32,64,128]{2,1,0:T(8,128)} %get-tuple-element.8, f32[64]{0:T(128)S(1)} %copy-done.7, f32[32,128]{1,0:T(8,128)S(1)} %get-tuple-element.21, bf16[1,64,32,128]{3,2,1,0:T(8,128)(2,1)S(1)} %copy-done), kind=kLoop, calls=%fused_computation.15 | loop fusion | flops 1572864 | bytes 3162368 | tf_op jit(solution)/shard_map/convert_element_type | solution.py:52
  101.4 1.1 %copy.80 = bf16[1,64,32,128]{3,2,1,0:T(8,128)(2,1)} copy(bf16[1,64,32,128]{3,1,2,0:T(8,128)(2,1)S(1)} %fusion.6) | data formatting | bytes 1048576 | tf_op jit(solution)/shard_map/convert_element_type | solution.py:52
  (22 shorter events, 0.2 us)
Async XLA Ops:
  4.7 35.3 %copy-start.2 = (bf16[5,8,8,8]{3,2,1,0:T(8,128)(2,1)S(1)}, bf16[5,8,8,8]{3,2,1,0:T(8,128)(2,1)}, u32[]{:S(2)}) copy-start(bf16[5,8,8,8]{3,2,1,0:T(8,128)(2,1)} %param.10) | copy-start | bytes 15364
  4.7 19.9 %all-to-all-start = ((bf16[1,64,32,128]{3,1,0,2:T(8,128)(2,1)}), bf16[1,64,32,128]{3,1,0,2:T(8,128)(2,1)S(1)}, u32[]{:S(2)}, u32[]{:S(2)}) async-start(bf16[1,64,32,128]{3,1,0,2:T(8,128)(2,1)} %fusion.21), calls=%async_computation | async-start | bytes 1048576 | tf_op jit(solution)/shard_map/all_to_all | solution.py:36
  24.6 15.2 %collective-permute-start = (bf16[2,64,4,128]{3,1,2,0:T(8,128)(2,1)S(1)}, bf16[2,64,4,128]{3,1,2,0:T(8,128)(2,1)S(1)}, u32[]{:S(2)}, u32[]{:S(2)}) collective-permute-start(bf16[2,64,4,128]{3,1,2,0:T(8,128)(2,1)S(1)} %fusion.30), channel_id=1, source_target_pairs={{0,8},{8,0},{1,9},{9,1},{2,10},{10,2},{3,11},{11,3},{4,12},{12,4},... | collective-permute-start | bytes 393224 | tf_op jit(solution)/shard_map/ppermute | solution.py:40
  41.1 0.7 copy-start.6
  41.5 6.6 %copy-start.1 = (bf16[5,64,5,64]{3,1,2,0:T(8,128)(2,1)S(1)}, bf16[5,64,5,64]{3,1,2,0:T(8,128)(2,1)}, u32[]{:S(2)}) copy-start(bf16[5,64,5,64]{3,1,2,0:T(8,128)(2,1)} %param.12) | copy-start | bytes 614404
  41.9 7.7 %copy-start.3 = (s32[1,32,128]{2,1,0:T(8,128)S(1)}, s32[1,32,128]{2,1,0:T(8,128)}, u32[]{:S(2)}) copy-start(s32[1,32,128]{2,1,0:T(8,128)} %param.8) | copy-start | bytes 49156
  43.1 14.5 %all-to-all-start.1 = ((bf16[8,64,4,128]{3,1,2,0:T(8,128)(2,1)}), bf16[8,64,4,128]{3,1,2,0:T(8,128)(2,1)S(1)}, u32[]{:S(2)}, u32[]{:S(2)}) async-start(bf16[8,64,4,128]{3,1,2,0:T(8,128)(2,1)} %fusion.14), calls=%async_computation.1 | async-start | bytes 1048576 | tf_op jit(solution)/shard_map/all_to_all | solution.py:46
  63.5 0.6 copy-start.5
  64.2 0.6 copy-start.4
  95.1 4.4 %copy-start = (bf16[1,64,32,128]{3,2,1,0:T(8,128)(2,1)S(1)}, bf16[1,64,32,128]{3,2,1,0:T(8,128)(2,1)}, u32[]{:S(2)}) copy-start(bf16[1,64,32,128]{3,2,1,0:T(8,128)(2,1)} %param.7) | copy-start | bytes 1572868
  95.1 4.5 %copy-start.7 = (f32[64]{0:T(128)S(1)}, f32[64]{0:T(128)}, u32[]{:S(2)}) copy-start(f32[64]{0:T(128)} %param.13) | copy-start | bytes 772

commit v7 on v6

--- a/solution.py
+++ b/solution.py
@@ -55,8 +55,7 @@
 
 
 def horizontal_kernel(
-    count, x_ref, w_ref, right_ref, left_ref, o_ref, yl_ref, yr_ref,
-    from_left, from_right, send_sems, recv_sems,
+    count, x_ref, w_ref, right_ref, left_ref, o_ref, fix_ref, from_left, from_right, send_sems, recv_sems,
 ):
     me = lax.axis_index("lon")
     right, left = lax.rem(me + 1, count), lax.rem(me + count - 1, count)
@@ -108,19 +107,27 @@
     to_left.start()
     to_right.wait()
     to_left.wait()
-    yl_ref[...] = jnp.dot(weights, from_left[...], preferred_element_type=jnp.float32)
-    yr_ref[...] = jnp.dot(weights, from_right[...], preferred_element_type=jnp.float32)
+    mix = lambda edge: jnp.dot(weights, edge, preferred_element_type=jnp.float32)
+    near_left, far_left = mix(from_left[0]), mix(from_left[1])
+    near_right, far_right = mix(from_right[0]), mix(from_right[1])
+    tap = lambda y, col_tap: y[col_tap * channels : (col_tap + 1) * channels]
+    fix_ref[0] = tap(near_left, 0) + tap(far_left, 1)
+    fix_ref[1] = tap(far_left, 0)
+    fix_ref[2] = tap(near_right, taps - 1)
+    fix_ref[3] = tap(near_right, taps - 2) + tap(far_right, taps - 1)
 
 
 def stacked_edge(edge, reach_row):
     channels, rows_lat, width = edge.shape
     padded = jnp.pad(edge, ((0, 0), (reach_row, reach_row), (0, 0)))
-    return jnp.concatenate(
+    return jnp.stack(
         [
-            padded[:, row_tap : row_tap + rows_lat].reshape(channels, rows_lat * width)
-            for row_tap in range(2 * reach_row + 1)
-        ],
-        axis=0,
+            jnp.concatenate(
+                [padded[:, row_tap : row_tap + rows_lat, col] for row_tap in range(2 * reach_row + 1)],
+                axis=0,
+            )
+            for col in range(width)
+        ]
     )
 
 
@@ -140,16 +147,14 @@
     right_edge = stacked_edge(block[:, :, cols_lon - reach_col :], reach_row)
     left_edge = stacked_edge(block[:, :, :reach_col], reach_row)
     vmem = pl.BlockSpec(memory_space=pltpu.VMEM)
-    edge_out = jax.ShapeDtypeStruct((weights.shape[0], right_edge.shape[1]), jnp.float32)
-    conv, from_left, from_right = pl.pallas_call(
+    conv, fix = pl.pallas_call(
         functools.partial(horizontal_kernel, count),
         out_shape=(
             jax.ShapeDtypeStruct((rows_lat, channels, cols_lon), jnp.float32),
-            edge_out,
-            edge_out,
+            jax.ShapeDtypeStruct((2 * reach_col, channels, rows_lat), jnp.float32),
         ),
         in_specs=[vmem] * 4,
-        out_specs=(vmem,) * 3,
+        out_specs=(vmem,) * 2,
         scratch_shapes=[
             pltpu.VMEM(right_edge.shape, right_edge.dtype),
             pltpu.VMEM(left_edge.shape, left_edge.dtype),
@@ -164,16 +169,11 @@
         ),
     )(wide, weights, right_edge, left_edge)
     conv = jnp.transpose(conv, (1, 0, 2))
-    lanes = lambda y, tap, col: y[tap * channels : (tap + 1) * channels, col::reach_col]
-    first = lanes(from_left, 0, 0) + lanes(from_left, 1, 1)
-    second = lanes(from_left, 0, 1)
-    before_last = lanes(from_right, col_taps - 1, 0)
-    last = lanes(from_right, col_taps - 2, 0) + lanes(from_right, col_taps - 1, 1)
-    middle = jnp.zeros((channels, rows_lat, cols_lon - 2 * reach_col), jnp.float32)
-    fix = jnp.concatenate(
-        [first[..., None], second[..., None], middle, before_last[..., None], last[..., None]], axis=2
-    )
-    return (conv + fix)[None]
+    column = lax.broadcasted_iota(jnp.int32, conv.shape, 2)
+    edge_cols = (0, 1, cols_lon - 2, cols_lon - 1)
+    for index, col in enumerate(edge_cols):
+        conv = conv + jnp.where(column == col, fix[index][..., None], 0.0)
+    return conv[None]
 
 
 def solution(mesh):

time: 104 us -> 95.2 us (0.915)
  local copies, waits for them, and re-layouts: 26 us -> 16.8 us
  Pallas kernels: 16.9 us -> 18.8 us
    broadcast_in_dim x5, local copies, waits for them, and re-layouts: 6.75 us -> 1.1 us  [horizontal(): conv = conv + jnp.where(column == col, fix[index][..., None], 0.0)]
    concatenate x3 -> x4, local copies, waits for them, and re-layouts: 4.46 us -> 0.37 us  [stacked_edge(): jnp.concatenate([padded[:, row_tap:row_tap + rows_lat, col] for row_tap i...]
    reshape x11 -> x0, local copies, waits for them, and re-layouts: 3.1 us -> none  [the longest x1 2.16 us: horizontal(): wide = wide.reshape(channels, (rows_lat + 2 * reach_row) * segment)]
    pallas_call x1, Pallas kernels: 16.9 us -> 18.8 us  [horizontal(): pl.pallas_call(functools.partial(horizontal_kernel, count), out_shape=(ja...]
    another operation x0 -> x2, local copies, waits for them, and re-layouts: none -> 1.63 us  [stacked_edge(): jnp.stack([jnp.concatenate([padded[:, row_tap:row_tap + rows_lat, col] fo...]
    unnamed x24 -> x13, local copies, waits for them, and re-layouts: 1.3 us -> 2.29 us
    slice x7 -> x2, local copies, waits for them, and re-layouts: 6.62 us -> 7.42 us  [stacked_edge(): padded[:, row_tap:row_tap + rows_lat, col]]
  transfers between devices with their start and end apart: 3 -> 3, of which waited for: 3 -> 3; matrix products, arithmetic and copies ran while one was open for 1% -> 2% of each run, Pallas kernels for 0% -> 0%
where the time goes in v7:
time: 95.2 us; the launch traced here: 94.6 us
  starting transfers between devices  26.3 us (28%)
  waiting for transfers between devices  21.8 us (23%)
  Pallas kernels  18.8 us (20%)
  local copies, waits for them, and re-layouts  16.8 us (18%)
  other arithmetic  8.95 us (9%)
  matrix products  1.75 us (2%)
    pallas_call x1, Pallas kernels, horizontal(): pl.pallas_call(functools.partial(horizontal_kernel, count), out_shape=(ja...  18.8 us
    ppermute x1, starting transfers between devices, local(): recv = lax.ppermute(send, 'lat_hi', [(0, 1), (1, 0)])  10.9 us
    all_to_all x1, starting transfers between devices, local(): lax.all_to_all(normed, 'lat_lo', split_axis=2, concat_axis=0, tiled=True)  10.3 us
    all_to_all x1, waiting for transfers between devices, local(): lax.all_to_all(normed, 'lat_lo', split_axis=2, concat_axis=0, tiled=True)  9.5 us
    all_to_all x1, waiting for transfers between devices, local(): lax.all_to_all(vertical(taps, w_vert, b_vert), 'lat_lo', split_axis=0, co...  8 us
    slice x2, local copies, waits for them, and re-layouts, stacked_edge(): padded[:, row_tap:row_tap + rows_lat, col]  7.42 us
    all_to_all x1, starting transfers between devices, local(): lax.all_to_all(vertical(taps, w_vert, b_vert), 'lat_lo', split_axis=0, co...  5.12 us
    ppermute x1, waiting for transfers between devices, local(): recv = lax.ppermute(send, 'lat_hi', [(0, 1), (1, 0)])  4.28 us
  transfers between devices with their start and end apart: 3, of which 3 were waited for; matrix products, arithmetic and copies ran while one was open for 2% of the time, Pallas kernels for 0%

profile of v7, /device:TPU:1, one launch (start us, length us, event | category | flops | bytes accessed | tf_op | source)
XLA Modules:
  0.0 94.6 jit_solution(10536847474213341223)
XLA Ops:
  0.0 0.0 copy-start
  0.0 1.3 %convert_reduce_fusion = f32[32,128]{1,0:T(8,128)S(1)} fusion(bf16[1,64,32,128]{3,2,1,0:T(8,128)(2,1)} %param.7), kind=kLoop, calls=%fused_computation.3 | loop fusion | flops 520192 | bytes 540672 | tf_op jit(solution)/shard_map/reduce_sum | solution.py:13
  1.3 1.3 %fusion.3 = f32[32,128]{1,0:T(8,128)S(1)} fusion(f32[32,128]{1,0:T(8,128)S(1)} %broadcast_multiply_fusion.1, bf16[1,64,32,128]{3,2,1,0:T(8,128)(2,1)} %param.7), kind=kLoop, calls=%fused_computation.11 | loop fusion | flops 1044480 | bytes 557056 | tf_op jit(solution)/shard_map/reduce_sum | solution.py:14
  2.6 0.0 copy-done
  2.6 1.7 %fusion.24 = bf16[1,64,32,128]{3,1,0,2:T(8,128)(2,1)} fusion(f32[64]{0:T(128)} %param.9, f32[32,128]{1,0:T(8,128)S(1)} %add_rsqrt_fusion, f32[32,128]{1,0:T(8,128)S(1)} %broadcast_multiply_fusion.1, bf16[1,64,32,128]{3,2,1,0:T(8,128)(2,1)S(1)} %copy-done), kind=kLoop, calls=%fused_computation.39 | loop fusion | flops 1310720 | bytes 1081600 | tf_op jit(solution)/shard_map/convert_element_type | solution.py:15
  4.4 10.3 %all-to-all-start = ((bf16[1,64,32,128]{3,1,0,2:T(8,128)(2,1)}), bf16[1,64,32,128]{3,1,0,2:T(8,128)(2,1)S(1)}, u32[]{:S(2)}, u32[]{:S(2)}) async-start(bf16[1,64,32,128]{3,1,0,2:T(8,128)(2,1)} %fusion.24), calls=%async_computation | async-start | bytes 1048576 | tf_op jit(solution)/shard_map/all_to_all | solution.py:36
  14.6 9.5 %all-to-all-done = bf16[1,64,32,128]{3,1,0,2:T(8,128)(2,1)S(1)} async-done(((bf16[1,64,32,128]{3,1,0,2:T(8,128)(2,1)}), bf16[1,64,32,128]{3,1,0,2:T(8,128)(2,1)S(1)}, u32[]{:S(2)}, u32[]{:S(2)}) %all-to-all-start) | async-done | bytes 524320 | tf_op jit(solution)/shard_map/all_to_all | solution.py:36
  24.2 10.9 %collective-permute-start = (bf16[2,64,4,128]{3,1,2,0:T(8,128)(2,1)S(1)}, bf16[2,64,4,128]{3,1,2,0:T(8,128)(2,1)S(1)}, u32[]{:S(2)}, u32[]{:S(2)}) collective-permute-start(bf16[2,64,4,128]{3,1,2,0:T(8,128)(2,1)S(1)} %fusion.33), channel_id=1, source_target_pairs={{0,8},{8,0},{1,9},{9,1},{2,10},{10,2},{3,11},{11,3},{4,12},{12,4},... | collective-permute-start | bytes 393224 | tf_op jit(solution)/shard_map/ppermute | solution.py:40
  35.1 4.3 %collective-permute-done = bf16[2,64,4,128]{3,1,2,0:T(8,128)(2,1)S(1)} collective-permute-done((bf16[2,64,4,128]{3,1,2,0:T(8,128)(2,1)S(1)}, bf16[2,64,4,128]{3,1,2,0:T(8,128)(2,1)S(1)}, u32[]{:S(2)}, u32[]{:S(2)}) %collective-permute-start) | collective-permute-done | bytes 131104 | tf_op jit(solution)/shard_map/ppermute | solution.py:40
  39.4 0.0 copy-start.2
  39.4 0.1 fusion.25
  39.6 0.7 copy-done.2
  40.3 0.3 fusion.31
  40.7 0.4 convolution_add_fusion.3
  41.0 0.3 convolution_add_fusion.2
  41.4 0.4 convolution_add_fusion.1
  41.7 0.0 copy-start.4
  41.8 0.4 fusion
  42.1 0.3 copy-done.4
  42.4 0.0 copy-start.1
  42.4 1.2 %fusion.14 = bf16[8,64,4,128]{3,1,2,0:T(8,128)(2,1)} fusion(f32[8,8,8,4,128]{4,2,3,0,1:T(8,128)S(1)} %fusion, f32[64]{0:T(128)S(1)} %copy-done.4), kind=kLoop, calls=%fused_computation.22 | loop fusion | flops 2621440 | bytes 1573120 | tf_op jit(solution)/shard_map/convert_element_type | solution.py:30
  43.6 0.0 copy-start.3
  43.6 5.1 %all-to-all-start.1 = ((bf16[8,64,4,128]{3,1,2,0:T(8,128)(2,1)}), bf16[8,64,4,128]{3,1,2,0:T(8,128)(2,1)S(1)}, u32[]{:S(2)}, u32[]{:S(2)}) async-start(bf16[8,64,4,128]{3,1,2,0:T(8,128)(2,1)} %fusion.14), calls=%async_computation.1 | async-start | bytes 1048576 | tf_op jit(solution)/shard_map/all_to_all | solution.py:46
  48.8 0.0 copy-done.1
  48.8 0.3 copy.78
  49.1 1.1 %reshape.95.w_ref = bf16[320,320]{1,0:T(8,128)(2,1)} reshape(bf16[5,64,5,64]{3,2,1,0:T(8,128)(2,1)S(1)} %copy.78) | data formatting | bytes 409600 | tf_op jit(solution)/shard_map/reshape | solution.py:146
  50.1 0.1 pad.21.clone
  50.2 0.0 copy-done.3
  50.3 8.0 %all-to-all-done.1 = bf16[8,64,4,128]{3,1,2,0:T(8,128)(2,1)S(1)} async-done(((bf16[8,64,4,128]{3,1,2,0:T(8,128)(2,1)}), bf16[8,64,4,128]{3,1,2,0:T(8,128)(2,1)S(1)}, u32[]{:S(2)}, u32[]{:S(2)}) %all-to-all-start.1) | async-done | bytes 524320 | tf_op jit(solution)/shard_map/all_to_all | solution.py:46
  58.3 0.1 broadcast_multiply_fusion
  58.3 0.2 fusion.44
  58.6 1.6 %slice_reduce_fusion.1 = (bf16[64,32]{0,1:T(8,128)(2,1)S(1)}, bf16[64,32]{0,1:T(8,128)(2,1)S(1)}, bf16[64,32]{0,1:T(8,128)(2,1)S(1)}, bf16[64,32]{0,1:T(8,128)(2,1)S(1)}) fusion(bf16[64,32,128]{2,0,1:T(8,128)(2,1)S(1)} %broadcast_multiply_fusion), kind=kLoop, calls=%fused_computation.41 | loop fusion | bytes 32768 | tf_op jit(solution)/shard_map/slice | solution.py:126
  60.2 0.3 copy.77
  60.5 5.8 %slice_reduce_fusion.8 = (bf16[64,32]{0,1:T(8,128)(2,1)S(1)}, bf16[64,32]{0,1:T(8,128)(2,1)S(1)}, bf16[64,32]{0,1:T(8,128)(2,1)S(1)}, bf16[64,32]{0,1:T(8,128)(2...) fusion(bf16[64,32,2]{2,0,1:T(8,128)(2,1)S(1)} %get-tuple-elemen, ...), kind=kLoop, calls=%fused_computation.58 | loop fusion | bytes 81920 | tf_op jit(solution)/shard_map/slice | solution.py:126
  66.4 0.1 concatenate.29
  66.5 0.1 concatenate.30
  66.6 0.8 copy.80.left_ref
  67.4 0.1 concatenate.27
  67.5 0.1 concatenate.28
  67.6 0.8 copy.79.right_ref
  68.4 0.1 broadcast_in_dim.55
  68.5 0.7 maximum_maximum_fusion
  69.2 0.7 pad.11
  69.9 1.3 %copy.96 = bf16[8,8,36,256]{3,1,2,0:T(8,128)(2,1)} copy(bf16[8,8,36,256]{3,2,1,0:T(8,128)(2,1)S(1)} %bitcast.109) | data formatting | bytes 2359296
  71.2 0.0 copy-start.5
  71.2 18.8 %shard_map.73 = (f32[32,64,128]{2,1,0:T(8,128)}, f32[4,64,32]{2,1,0:T(8,128)}) custom-call(bf16[64,9216]{1,0:T(8,128)(2,1)} %bitcast.110, bf16[320,320]{1,0:T(8,128)(2,1)} %reshape.95.w_ref, bf16[2,320,32]{2,1,0:T(8,128)(2,1)} %copy.79.right_ref, bf16[2,320,32]{2,1,0:T(8,128)(2,1)} %copy.80.left_ref), custom_call_target="tpu_custom_call" | custom-call | flops 1677721600 | bytes 2433024 | tf_op jit(solution)/shard_map/pallas_call | solution.py:150
  90.0 0.8 slice_bitcast_fusion.3
  90.9 0.1 copy.81
  90.9 0.1 copy.82
  91.0 0.1 copy.83
  91.1 0.1 copy.84
  91.1 0.0 copy-done.5
  91.1 2.3 %fusion.6 = bf16[1,64,32,128]{3,1,2,0:T(8,128)(2,1)S(1)} fusion(f32[32,64,128]{2,1,0:T(8,128)} %get-tuple-element.7, f32[64]{0:T(128)S(1)} %copy-done.5, f32[64,32]{0,1:T(8,128)S(1)} %copy.84, f32[64,32]{0,1:T(8,128)S(1)} %copy.83, f32[64,32]{0,1:T(8,128)S(1)} %copy.82, f32[64,32]{0,1:T(8,128)S(1)} %copy.81, f32[32,128]{1,0:T(8,128)S(1)} %get-tuple-element.43, ...), kind=kLoop, calls=%fused_computation.14 | loop fusion | flops 3407872 | bytes 2147072 | tf_op jit(solution)/shard_map/convert_element_type | solution.py:52
  93.5 1.1 %copy.85 = bf16[1,64,32,128]{3,2,1,0:T(8,128)(2,1)} copy(bf16[1,64,32,128]{3,1,2,0:T(8,128)(2,1)S(1)} %fusion.6) | data formatting | bytes 1048576 | tf_op jit(solution)/shard_map/convert_element_type | solution.py:52
  (10 shorter events, 0.1 us)
Async XLA Ops:
  0.0 2.6 %copy-start = (bf16[1,64,32,128]{3,2,1,0:T(8,128)(2,1)S(1)}, bf16[1,64,32,128]{3,2,1,0:T(8,128)(2,1)}, u32[]{:S(2)}) copy-start(bf16[1,64,32,128]{3,2,1,0:T(8,128)(2,1)} %param.7) | copy-start | bytes 1572868
  4.4 19.8 %all-to-all-start = ((bf16[1,64,32,128]{3,1,0,2:T(8,128)(2,1)}), bf16[1,64,32,128]{3,1,0,2:T(8,128)(2,1)S(1)}, u32[]{:S(2)}, u32[]{:S(2)}) async-start(bf16[1,64,32,128]{3,1,0,2:T(8,128)(2,1)} %fusion.24), calls=%async_computation | async-start | bytes 1048576 | tf_op jit(solution)/shard_map/all_to_all | solution.py:36
  24.2 15.2 %collective-permute-start = (bf16[2,64,4,128]{3,1,2,0:T(8,128)(2,1)S(1)}, bf16[2,64,4,128]{3,1,2,0:T(8,128)(2,1)S(1)}, u32[]{:S(2)}, u32[]{:S(2)}) collective-permute-start(bf16[2,64,4,128]{3,1,2,0:T(8,128)(2,1)S(1)} %fusion.33), channel_id=1, source_target_pairs={{0,8},{8,0},{1,9},{9,1},{2,10},{10,2},{3,11},{11,3},{4,12},{12,4},... | collective-permute-start | bytes 393224 | tf_op jit(solution)/shard_map/ppermute | solution.py:40
  39.4 0.9 copy-start.2
  41.7 0.7 copy-start.4
  42.4 6.4 %copy-start.1 = (bf16[5,64,5,64]{3,1,2,0:T(8,128)(2,1)S(1)}, bf16[5,64,5,64]{3,1,2,0:T(8,128)(2,1)}, u32[]{:S(2)}) copy-start(bf16[5,64,5,64]{3,1,2,0:T(8,128)(2,1)} %param.12) | copy-start | bytes 614404
  43.6 6.6 %copy-start.3 = (s32[1,32,128]{2,1,0:T(8,128)S(1)}, s32[1,32,128]{2,1,0:T(8,128)}, u32[]{:S(2)}) copy-start(s32[1,32,128]{2,1,0:T(8,128)} %param.8) | copy-start | bytes 49156
  43.6 14.6 %all-to-all-start.1 = ((bf16[8,64,4,128]{3,1,2,0:T(8,128)(2,1)}), bf16[8,64,4,128]{3,1,2,0:T(8,128)(2,1)S(1)}, u32[]{:S(2)}, u32[]{:S(2)}) async-start(bf16[8,64,4,128]{3,1,2,0:T(8,128)(2,1)} %fusion.14), calls=%async_computation.1 | async-start | bytes 1048576 | tf_op jit(solution)/shard_map/all_to_all | solution.py:46
  71.2 20.0 %copy-start.5 = (f32[64]{0:T(128)S(1)}, f32[64]{0:T(128)}, u32[]{:S(2)}) copy-start(f32[64]{0:T(128)} %param.13) | copy-start | bytes 772

commit v8 on v5

--- a/solution.py
+++ b/solution.py
@@ -8,13 +8,24 @@
 from jax.sharding import PartitionSpec as P
 
 
+def normalize_kernel(x_ref, g_ref, o_ref):
+    values = x_ref[...].astype(jnp.float32)
+    channels = values.shape[1]
+    center = jnp.sum(values, axis=1, keepdims=True) / channels
+    spread = jnp.sum((values - center) ** 2, axis=1, keepdims=True) / channels
+    scale = lax.rsqrt(spread + 1e-05)
+    o_ref[...] = ((values - center) * scale * g_ref[...]).astype(o_ref.dtype)
+
+
 def normalize(block, norm_gain):
-    values = block.astype(jnp.float32)
-    center = jnp.mean(values, axis=1, keepdims=True)
-    spread = jnp.mean((values - center) ** 2, axis=1, keepdims=True)
-    return ((values - center) * lax.rsqrt(spread + 1e-05) * norm_gain[None, :, None, None]).astype(
-        jnp.bfloat16
-    )
+    vmem = pl.BlockSpec(memory_space=pltpu.VMEM)
+    gain = jnp.broadcast_to(norm_gain[None, :, None, None], (1, norm_gain.shape[0], 1, block.shape[3]))
+    return pl.pallas_call(
+        normalize_kernel,
+        out_shape=jax.ShapeDtypeStruct(block.shape, jnp.bfloat16),
+        in_specs=[vmem, vmem],
+        out_specs=vmem,
+    )(block, gain)
 
 
 def vertical(taps, w_vert, b_vert):

time: 88.8 us -> 90.1 us (1.015)
  other arithmetic: 8.28 us -> 3.95 us
  local copies, waits for them, and re-layouts: 12 us -> 15.4 us
  Pallas kernels: 17.7 us -> 19.9 us
    reduce_sum x2 -> x0, other arithmetic: 2.57 us -> none  [the longest x1 1.29 us: normalize(): center = jnp.mean(values, axis=1, keepdims=True)]
    pallas_call x0 -> x1, Pallas kernels: none -> 2.19 us  [normalize(): pl.pallas_call(normalize_kernel, out_shape=jax.ShapeDtypeStruct(block.sha...]
    pallas_call x0 -> x1, local copies, waits for them, and re-layouts: none -> 2.03 us  [normalize(): pl.pallas_call(normalize_kernel, out_shape=jax.ShapeDtypeStruct(block.sha...]
    convert_element_type x1 -> x0, other arithmetic: 1.75 us -> none  [normalize(): ((values - center) * lax.rsqrt(spread + 1e-05) * norm_gain[None, :, None,...]
    broadcast_in_dim x0 -> x1, local copies, waits for them, and re-layouts: none -> 1.39 us  [normalize(): jnp.broadcast_to(norm_gain[None, :, None, None], (1, norm_gain.shape[0],...]
where the time goes in v8:
time: 90.1 us; the launch traced here: 89.2 us
  starting transfers between devices  26.3 us (29%)
  waiting for transfers between devices  21.8 us (24%)
  Pallas kernels  19.9 us (22%)
  local copies, waits for them, and re-layouts  15.4 us (17%)
  other arithmetic  3.95 us (4%)
  matrix products  1.75 us (2%)
    pallas_call x1, Pallas kernels, lon_halo(): pl.pallas_call(functools.partial(halo_kernel, count), out_shape=(jax.Shap...  12.4 us
    ppermute x1, starting transfers between devices, local(): recv = lax.ppermute(send, 'lat_hi', [(0, 1), (1, 0)])  11 us
    all_to_all x1, starting transfers between devices, local(): lax.all_to_all(normed, 'lat_lo', split_axis=2, concat_axis=0, tiled=True)  10.3 us
    all_to_all x1, waiting for transfers between devices, local(): lax.all_to_all(normed, 'lat_lo', split_axis=2, concat_axis=0, tiled=True)  9.5 us
    all_to_all x1, waiting for transfers between devices, local(): lax.all_to_all(vertical(taps, w_vert, b_vert), 'lat_lo', split_axis=0, co...  8.01 us
    pallas_call x1, Pallas kernels, horizontal(): pl.pallas_call(horizontal_kernel, out_shape=jax.ShapeDtypeStruct((rows_la...  5.34 us
    all_to_all x1, starting transfers between devices, local(): lax.all_to_all(vertical(taps, w_vert, b_vert), 'lat_lo', split_axis=0, co...  5.12 us
    ppermute x1, waiting for transfers between devices, local(): recv = lax.ppermute(send, 'lat_hi', [(0, 1), (1, 0)])  4.27 us
  transfers between devices with their start and end apart: 3, of which 3 were waited for; matrix products, arithmetic and copies ran while one was open for 2% of the time, Pallas kernels for 0%

profile of v8, /device:TPU:1, one launch (start us, length us, event | category | flops | bytes accessed | tf_op | source)
XLA Modules:
  0.0 89.2 jit_solution(12524844953629153061)
XLA Ops:
  0.0 1.4 %broadcast_in_dim.7.g_ref = f32[1,64,1,128]{3,2,1,0:T(1,128)} broadcast(f32[64]{0:T(128)} %param.9), dimensions={1} | broadcast | bytes 33024 | tf_op jit(solution)/shard_map/broadcast_in_dim | solution.py:22
  1.4 2.2 %shard_map.73 = bf16[1,64,32,128]{3,2,1,0:T(8,128)(2,1)} custom-call(bf16[1,64,32,128]{3,2,1,0:T(8,128)(2,1)} %x_ref.1, f32[1,64,1,128]{3,2,1,0:T(1,128)} %broadcast_in_dim.7.g_ref), custom_call_target="tpu_custom_call" | custom-call | tf_op jit(solution)/shard_map/pallas_call | solution.py:23
  3.6 2.0 %copy.41 = bf16[1,64,32,128]{3,1,0,2:T(8,128)(2,1)} copy(bf16[1,64,32,128]{3,2,1,0:T(8,128)(2,1)} %shard_map.73) | data formatting | bytes 1048576 | tf_op jit(solution)/shard_map/pallas_call | solution.py:23
  5.6 10.3 %all-to-all-start = ((bf16[1,64,32,128]{3,1,0,2:T(8,128)(2,1)}), bf16[1,64,32,128]{3,1,0,2:T(8,128)(2,1)S(1)}, u32[]{:S(2)}, u32[]{:S(2)}) async-start(bf16[1,64,32,128]{3,1,0,2:T(8,128)(2,1)} %copy.41), calls=%async_computation | async-start | bytes 1048576 | tf_op jit(solution)/shard_map/all_to_all | solution.py:47
  15.9 9.5 %all-to-all-done = bf16[1,64,32,128]{3,1,0,2:T(8,128)(2,1)S(1)} async-done(((bf16[1,64,32,128]{3,1,0,2:T(8,128)(2,1)}), bf16[1,64,32,128]{3,1,0,2:T(8,128)(2,1)S(1)}, u32[]{:S(2)}, u32[]{:S(2)}) %all-to-all-start) | async-done | bytes 524320 | tf_op jit(solution)/shard_map/all_to_all | solution.py:47
  25.4 11.0 %collective-permute-start = (bf16[2,64,4,128]{3,1,2,0:T(8,128)(2,1)S(1)}, bf16[2,64,4,128]{3,1,2,0:T(8,128)(2,1)S(1)}, u32[]{:S(2)}, u32[]{:S(2)}) collective-permute-start(bf16[2,64,4,128]{3,1,2,0:T(8,128)(2,1)S(1)} %fusion.22), channel_id=1, source_target_pairs={{0,8},{8,0},{1,9},{9,1},{2,10},{10,2},{3,11},{11,3},{4,12},{12,4},... | collective-permute-start | bytes 393224 | tf_op jit(solution)/shard_map/ppermute | solution.py:51
  36.4 4.3 %collective-permute-done = bf16[2,64,4,128]{3,1,2,0:T(8,128)(2,1)S(1)} collective-permute-done((bf16[2,64,4,128]{3,1,2,0:T(8,128)(2,1)S(1)}, bf16[2,64,4,128]{3,1,2,0:T(8,128)(2,1)S(1)}, u32[]{:S(2)}, u32[]{:S(2)}) %collective-permute-start) | collective-permute-done | bytes 131104 | tf_op jit(solution)/shard_map/ppermute | solution.py:51
  40.7 0.0 copy-start.2
  40.7 0.1 fusion.14
  40.8 0.7 copy-done.2
  41.6 0.3 fusion.20
  41.9 0.4 convolution_add_fusion.3
  42.3 0.3 convolution_add_fusion.2
  42.6 0.4 convolution_add_fusion.1
  43.0 0.0 copy-start.4
  43.0 0.4 fusion
  43.3 0.3 copy-done.4
  43.6 0.0 copy-start.1
  43.6 1.2 %fusion.8 = bf16[8,64,4,128]{3,1,2,0:T(8,128)(2,1)} fusion(f32[8,8,8,4,128]{4,2,3,0,1:T(8,128)S(1)} %fusion, f32[64]{0:T(128)S(1)} %copy-done.4), kind=kLoop, calls=%fused_computation.13 | loop fusion | flops 2621440 | bytes 1573120 | tf_op jit(solution)/shard_map/convert_element_type | solution.py:41
  44.9 0.0 copy-start.3
  44.9 5.1 %all-to-all-start.1 = ((bf16[8,64,4,128]{3,1,2,0:T(8,128)(2,1)}), bf16[8,64,4,128]{3,1,2,0:T(8,128)(2,1)S(1)}, u32[]{:S(2)}, u32[]{:S(2)}) async-start(bf16[8,64,4,128]{3,1,2,0:T(8,128)(2,1)} %fusion.8), calls=%async_computation.1 | async-start | bytes 1048576 | tf_op jit(solution)/shard_map/all_to_all | solution.py:57
  50.0 0.0 copy-done.1
  50.0 0.3 copy.62
  50.3 1.1 %reshape.93.w_ref = bf16[320,320]{1,0:T(8,128)(2,1)} reshape(bf16[5,64,5,64]{3,2,1,0:T(8,128)(2,1)S(1)} %copy.62) | data formatting | bytes 409600 | tf_op jit(solution)/shard_map/reshape | solution.py:101
  51.4 0.1 pad.8.clone
  51.5 0.0 copy-done.3
  51.5 8.0 %all-to-all-done.1 = bf16[8,64,4,128]{3,1,2,0:T(8,128)(2,1)S(1)} async-done(((bf16[8,64,4,128]{3,1,2,0:T(8,128)(2,1)}), bf16[8,64,4,128]{3,1,2,0:T(8,128)(2,1)S(1)}, u32[]{:S(2)}, u32[]{:S(2)}) %all-to-all-start.1) | async-done | bytes 524320 | tf_op jit(solution)/shard_map/all_to_all | solution.py:57
  59.5 0.3 copy_multiply_fusion
  59.8 0.2 fusion.33
  60.0 0.6 copy.54
  60.6 0.7 copy.56.left_edge
  61.4 0.6 copy.55
  62.0 0.7 copy.57.right_edge
  62.7 12.4 %shard_map.74 = (bf16[64,64]{1,0:T(8,128)(2,1)}, bf16[64,64]{1,0:T(8,128)(2,1)}) custom-call(bf16[64,64]{1,0:T(8,128)(2,1)} %copy.56.left_edge, bf16[64,64]{1,0:T(8,128)(2,1)} %copy.57.right_edge), custom_call_target="tpu_custom_call" | custom-call | tf_op jit(solution)/shard_map/pallas_call | solution.py:155
  75.0 0.8 copy.58
  75.8 0.9 %copy.60 = bf16[1,64,32,2]{3,2,1,0:T(8,128)(2,1)S(1)} copy(bf16[1,64,32,2]{1,3,2,0:T(2,128)(2,1)S(1)} %bitcast.96) | data formatting | bytes 16384 | tf_op jit(solution)/shard_map/reshape | solution.py:163
  76.8 0.8 copy.59
  77.6 0.9 %copy.61 = bf16[1,64,32,2]{3,2,1,0:T(8,128)(2,1)S(1)} copy(bf16[1,64,32,2]{1,3,2,0:T(2,128)(2,1)S(1)} %bitcast.97) | data formatting | bytes 16384 | tf_op jit(solution)/shard_map/reshape | solution.py:163
  78.5 0.7 maximum_bitcast_fusion
  79.2 0.7 pad.4
  79.9 1.3 %copy.74 = bf16[8,8,36,256]{3,1,2,0:T(8,128)(2,1)} copy(bf16[8,8,36,256]{3,2,1,0:T(8,128)(2,1)S(1)} %bitcast.90) | data formatting | bytes 2359296
  81.2 0.0 copy-start
  81.2 0.0 copy-start.5
  81.2 5.3 %shard_map.75 = f32[32,64,128]{2,1,0:T(8,128)} custom-call(bf16[64,9216]{1,0:T(8,128)(2,1)} %bitcast.92, bf16[320,320]{1,0:T(8,128)(2,1)} %reshape.93.w_ref), custom_call_target="tpu_custom_call" | custom-call | flops 1677721600 | bytes 2433024 | tf_op jit(solution)/shard_map/pallas_call | solution.py:102
  86.6 0.0 copy-done
  86.6 0.0 copy-done.5
  86.6 1.5 %fusion.9 = bf16[1,64,32,128]{3,1,2,0:T(8,128)(2,1)S(1)} fusion(f32[32,64,128]{2,1,0:T(8,128)} %shard_map.75, bf16[1,64,32,128]{3,2,1,0:T(8,128)(2,1)S(1)} %copy-done, f32[64]{0:T(128)S(1)} %copy-done.5, f32[32,128]{1,0:T(8,128)S(1)} %get-tuple-element.19), kind=kLoop, calls=%fused_computation.16 | loop fusion | flops 1310720 | bytes 2113792 | tf_op jit(solution)/shard_map/convert_element_type | solution.py:63
  88.1 1.1 %copy.63 = bf16[1,64,32,128]{3,2,1,0:T(8,128)(2,1)} copy(bf16[1,64,32,128]{3,1,2,0:T(8,128)(2,1)S(1)} %fusion.9) | data formatting | bytes 1048576 | tf_op jit(solution)/shard_map/convert_element_type | solution.py:63
  (4 shorter events, 0.0 us)
Async XLA Ops:
  5.6 19.8 %all-to-all-start = ((bf16[1,64,32,128]{3,1,0,2:T(8,128)(2,1)}), bf16[1,64,32,128]{3,1,0,2:T(8,128)(2,1)S(1)}, u32[]{:S(2)}, u32[]{:S(2)}) async-start(bf16[1,64,32,128]{3,1,0,2:T(8,128)(2,1)} %copy.41), calls=%async_computation | async-start | bytes 1048576 | tf_op jit(solution)/shard_map/all_to_all | solution.py:47
  25.4 15.2 %collective-permute-start = (bf16[2,64,4,128]{3,1,2,0:T(8,128)(2,1)S(1)}, bf16[2,64,4,128]{3,1,2,0:T(8,128)(2,1)S(1)}, u32[]{:S(2)}, u32[]{:S(2)}) collective-permute-start(bf16[2,64,4,128]{3,1,2,0:T(8,128)(2,1)S(1)} %fusion.22), channel_id=1, source_target_pairs={{0,8},{8,0},{1,9},{9,1},{2,10},{10,2},{3,11},{11,3},{4,12},{12,4},... | collective-permute-start | bytes 393224 | tf_op jit(solution)/shard_map/ppermute | solution.py:51
  40.7 0.9 copy-start.2
  43.0 0.7 copy-start.4
  43.6 6.4 %copy-start.1 = (bf16[5,64,5,64]{3,1,2,0:T(8,128)(2,1)S(1)}, bf16[5,64,5,64]{3,1,2,0:T(8,128)(2,1)}, u32[]{:S(2)}) copy-start(bf16[5,64,5,64]{3,1,2,0:T(8,128)(2,1)} %param.12) | copy-start | bytes 614404
  44.9 6.6 %copy-start.3 = (s32[1,32,128]{2,1,0:T(8,128)S(1)}, s32[1,32,128]{2,1,0:T(8,128)}, u32[]{:S(2)}) copy-start(s32[1,32,128]{2,1,0:T(8,128)} %param.8) | copy-start | bytes 49156
  44.9 14.6 %all-to-all-start.1 = ((bf16[8,64,4,128]{3,1,2,0:T(8,128)(2,1)}), bf16[8,64,4,128]{3,1,2,0:T(8,128)(2,1)S(1)}, u32[]{:S(2)}, u32[]{:S(2)}) async-start(bf16[8,64,4,128]{3,1,2,0:T(8,128)(2,1)} %fusion.8), calls=%async_computation.1 | async-start | bytes 1048576 | tf_op jit(solution)/shard_map/all_to_all | solution.py:57
  81.2 5.3 %copy-start = (bf16[1,64,32,128]{3,2,1,0:T(8,128)(2,1)S(1)}, bf16[1,64,32,128]{3,2,1,0:T(8,128)(2,1)}, u32[]{:S(2)}) copy-start(bf16[1,64,32,128]{3,2,1,0:T(8,128)(2,1)} %x_ref.1) | copy-start | bytes 1572868
  81.2 5.3 %copy-start.5 = (f32[64]{0:T(128)S(1)}, f32[64]{0:T(128)}, u32[]{:S(2)}) copy-start(f32[64]{0:T(128)} %param.13) | copy-start | bytes 772

commit v9 on v5

--- a/solution.py
+++ b/solution.py
@@ -30,18 +30,129 @@
     return jax.nn.gelu(summed).astype(jnp.bfloat16)
 
 
+def column_kernel(halves, group, reach, blocks_ref, out_ref, send_sems, recv_sems, own_sem):
+    lon = lax.axis_index("lon")
+    half, place = lax.axis_index("lat_hi"), lax.axis_index("lat_lo")
+    upper = halves - 1 - half
+    mesh_ids = pl.DeviceIdType.MESH
+    partner = (lon, upper, place)
+    barrier = pltpu.get_barrier_semaphore()
+    for other in range(group):
+
+        @pl.when(place != other)
+        def _():
+            pl.semaphore_signal(barrier, inc=1, device_id=(lon, half, other), device_id_type=mesh_ids)
+
+    pl.semaphore_signal(barrier, inc=1, device_id=partner, device_id_type=mesh_ids)
+    pl.semaphore_wait(barrier, group)
+
+    own = pltpu.make_async_copy(blocks_ref.at[place], out_ref.at[reach + place], own_sem.at[0])
+    own.start()
+
+    def inward(other):
+        return pltpu.make_async_remote_copy(
+            src_ref=blocks_ref.at[other],
+            dst_ref=out_ref.at[reach + place],
+            send_sem=send_sems.at[other],
+            recv_sem=recv_sems.at[reach + place],
+            device_id=(lon, half, other),
+            device_id_type=mesh_ids,
+        )
+
+    def arrival(slot):
+        return pltpu.make_async_remote_copy(
+            src_ref=blocks_ref.at[0],
+            dst_ref=out_ref.at[slot],
+            send_sem=send_sems.at[group],
+            recv_sem=recv_sems.at[slot],
+            device_id=partner,
+            device_id_type=mesh_ids,
+        )
+
+    for other in range(group):
+
+        @pl.when(place != other)
+        def _():
+            inward(other).start()
+
+    edge = (group - reach) * upper
+    mine = jnp.logical_and(place >= edge, place < edge + reach)
+    forwards = []
+    for level in range(reach):
+        source = edge + level
+
+        @pl.when(place != source)
+        def _():
+            arrival(reach + source).wait_recv()
+
+        @pl.when(place == source)
+        def _():
+            own.wait()
+
+        forward = pltpu.make_async_remote_copy(
+            src_ref=out_ref.at[reach + source],
+            dst_ref=out_ref.at[(group + reach) * half + level],
+            send_sem=send_sems.at[group + level],
+            recv_sem=recv_sems.at[(group + reach) * half + level],
+            device_id=partner,
+            device_id_type=mesh_ids,
+        )
+        forward.start()
+        forwards.append(forward)
+
+    for other in range(group):
+        boundary = jnp.logical_and(other >= edge, other < edge + reach)
+
+        @pl.when(jnp.logical_and(place != other, jnp.logical_not(boundary)))
+        def _():
+            arrival(reach + other).wait_recv()
+
+    @pl.when(jnp.logical_not(mine))
+    def _():
+        own.wait()
+
+    for level in range(reach):
+        arrival((group + reach) * upper + level).wait_recv()
+    for other in range(group):
+
+        @pl.when(place != other)
+        def _():
+            inward(other).wait_send()
+
+    for forward in forwards:
+        forward.wait_send()
+
+
+def columns_of(normed, reach):
+    halves, group = lax.axis_size("lat_hi"), lax.axis_size("lat_lo")
+    _, channels, rows_lat, cols_lon = normed.shape
+    rows = rows_lat // group
+    blocks = normed[0].reshape(channels, group, rows, cols_lon).transpose(1, 0, 2, 3)
+    any_spec = pl.BlockSpec(memory_space=pl.ANY)
+    slots = group + 2 * reach
+    out = pl.pallas_call(
+        functools.partial(column_kernel, halves, group, reach),
+        out_shape=jax.ShapeDtypeStruct((slots, channels, rows, cols_lon), normed.dtype),
+        in_specs=[any_spec],
+        out_specs=any_spec,
+        scratch_shapes=[
+            pltpu.SemaphoreType.DMA((group + reach,)),
+            pltpu.SemaphoreType.DMA((slots,)),
+            pltpu.SemaphoreType.DMA((1,)),
+        ],
+        compiler_params=pltpu.CompilerParams(collective_id=1, has_side_effects=True),
+    )(blocks)
+    half = lax.axis_index("lat_hi")
+    slot = lax.broadcasted_iota(jnp.int32, (slots, 1, 1, 1), 0)
+    real = jnp.logical_and(slot >= reach * (1 - half), slot < slots - reach * half)
+    return jnp.where(real, out, jnp.zeros_like(out))
+
+
 def local(fields, ocean_mask, norm_gain, w_vert, b_vert, w_horiz, b_horiz):
     normed = normalize(fields, norm_gain)
     reach = w_vert.shape[0] // 2
-    columns = lax.all_to_all(normed, "lat_lo", split_axis=2, concat_axis=0, tiled=True)
-    count_lev = columns.shape[0]
-    upper = lax.axis_index("lat_hi") == 0
-    send = jnp.where(upper, columns[count_lev - reach :], columns[:reach])
-    recv = lax.ppermute(send, "lat_hi", [(0, 1), (1, 0)])
-    zeros = jnp.zeros_like(recv)
-    below = jnp.where(upper, zeros, recv)
-    above = jnp.where(upper, recv, zeros)
-    padded = jnp.concatenate([below, columns, above], axis=0)
+    padded = columns_of(normed, reach)
+    count_lev = padded.shape[0] - 2 * reach
     taps = [padded[tap_index : tap_index + count_lev] for tap_index in range(w_vert.shape[0])]
     mixed = lax.all_to_all(
         vertical(taps, w_vert, b_vert), "lat_lo", split_axis=0, concat_axis=2, tiled=True

time: 88.8 us -> 89.6 us (level)
  Pallas kernels: 17.7 us -> 49.1 us
  starting transfers between devices: 26.3 us -> 7.59 us
  waiting for transfers between devices: 21.8 us -> 8.01 us
  local copies, waits for them, and re-layouts: 12 us -> 13.6 us
    pallas_call x0 -> x1, Pallas kernels: none -> 31.4 us  [columns_of(): pl.pallas_call(functools.partial(column_kernel, halves, group, reach), ou...]
    ppermute x1 -> x0, starting transfers between devices: 10.9 us -> none  [local(): recv = lax.ppermute(send, 'lat_hi', [(0, 1), (1, 0)])]
    all_to_all x1 -> x0, starting transfers between devices: 10.3 us -> none  [local(): lax.all_to_all(normed, 'lat_lo', split_axis=2, concat_axis=0, tiled=True)]
    all_to_all x1 -> x0, waiting for transfers between devices: 9.5 us -> none  [local(): lax.all_to_all(normed, 'lat_lo', split_axis=2, concat_axis=0, tiled=True)]
    ppermute x1 -> x0, waiting for transfers between devices: 4.28 us -> none  [local(): recv = lax.ppermute(send, 'lat_hi', [(0, 1), (1, 0)])]
    all_to_all x1, starting transfers between devices: 5.12 us -> 7.59 us  [local(): lax.all_to_all(vertical(taps, w_vert, b_vert), 'lat_lo', split_axis=0, co...]
    select_n x2 -> x1, other arithmetic: 0.04 us -> 1.54 us  [columns_of(): return jnp.where(real, out, jnp.zeros_like(out))]
    slice x0 -> x1, local copies, waits for them, and re-layouts: none -> 1.21 us  [local(): padded[tap_index:tap_index + count_lev]]
  transfers between devices with their start and end apart: 3 -> 1, of which waited for: 3 -> 1; matrix products, arithmetic and copies ran while one was open for 2% -> 2% of each run, Pallas kernels for 0% -> 0%
where the time goes in v9:
time: 89.6 us; the launch traced here: 89.1 us
  Pallas kernels  49.1 us (55%)
  local copies, waits for them, and re-layouts  13.6 us (15%)
  other arithmetic  8.85 us (10%)
  waiting for transfers between devices  8.01 us (9%)
  starting transfers between devices  7.59 us (8%)
  matrix products  1.74 us (2%)
    pallas_call x1, Pallas kernels, columns_of(): pl.pallas_call(functools.partial(column_kernel, halves, group, reach), ou...  31.4 us
    pallas_call x1, Pallas kernels, lon_halo(): pl.pallas_call(functools.partial(halo_kernel, count), out_shape=(jax.Shap...  12.4 us
    all_to_all x1, waiting for transfers between devices, local(): lax.all_to_all(vertical(taps, w_vert, b_vert), 'lat_lo', split_axis=0, co...  8.01 us
    all_to_all x1, starting transfers between devices, local(): lax.all_to_all(vertical(taps, w_vert, b_vert), 'lat_lo', split_axis=0, co...  7.59 us
    pallas_call x1, Pallas kernels, horizontal(): pl.pallas_call(horizontal_kernel, out_shape=jax.ShapeDtypeStruct((rows_la...  5.33 us
    reshape x2, local copies, waits for them, and re-layouts, lon_halo(): return (from_left.reshape(edge_shape), from_right.reshape(edge_shape))  1.86 us
  transfers between devices with their start and end apart: 1, of which 1 were waited for; matrix products, arithmetic and copies ran while one was open for 2% of the time, Pallas kernels for 0%

profile of v9, /device:TPU:1, one launch (start us, length us, event | category | flops | bytes accessed | tf_op | source)
XLA Modules:
  0.0 89.1 jit_solution(16687840131218068035)
XLA Ops:
  0.0 0.0 copy-start
  0.0 1.3 %convert_reduce_fusion = f32[32,128]{1,0:T(8,128)S(1)} fusion(bf16[1,64,32,128]{3,2,1,0:T(8,128)(2,1)} %param.7), kind=kLoop, calls=%fused_computation.3 | loop fusion | flops 520192 | bytes 540672 | tf_op jit(solution)/shard_map/reduce_sum | solution.py:13
  1.3 1.3 %fusion.3 = f32[32,128]{1,0:T(8,128)S(1)} fusion(f32[32,128]{1,0:T(8,128)S(1)} %broadcast_multiply_fusion, bf16[1,64,32,128]{3,2,1,0:T(8,128)(2,1)} %param.7), kind=kLoop, calls=%fused_computation.11 | loop fusion | flops 1044480 | bytes 557056 | tf_op jit(solution)/shard_map/reduce_sum | solution.py:14
  2.6 0.0 copy-done
  2.6 1.0 %fusion.5 = bf16[1,64,32,128]{3,1,2,0:T(8,128)(2,1)S(1)} fusion(f32[64]{0:T(128)} %param.9, f32[32,128]{1,0:T(8,128)S(1)} %add_rsqrt_fusion, f32[32,128]{1,0:T(8,128)S(1)} %broadcast_multiply_fusion, bf16[1,64,32,128]{3,2,1,0:T(8,128)(2,1)S(1)} %copy-done), kind=kLoop, calls=%fused_computation.13 | loop fusion | flops 1310720 | bytes 1081600 | tf_op jit(solution)/shard_map/convert_element_type | solution.py:15
  3.6 1.2 %copy.74 = bf16[64,8,4,128]{3,2,0,1:T(4,128)(2,1)} copy(bf16[64,8,4,128]{3,0,2,1:T(8,128)(2,1)S(1)} %bitcast.84) | data formatting | bytes 1048576 | tf_op jit(solution)/shard_map/reshape;squeeze | solution.py:130
  4.8 31.4 %shard_map.73 = bf16[12,64,4,128]{3,2,1,0:T(4,128)(2,1)} custom-call(bf16[8,64,4,128]{3,2,1,0:T(4,128)(2,1)} %bitcast.85), custom_call_target="tpu_custom_call" | custom-call | tf_op jit(solution)/shard_map/pallas_call | solution.py:133
  36.2 1.5 %broadcast_select_fusion = bf16[12,64,4,128]{3,2,1,0:T(4,128)(2,1)S(1)} fusion(bf16[12,64,4,128]{3,2,1,0:T(4,128)(2,1)} %shard_map.73, pred[12]{0:T(512)(128)(4,1)S(1)} %compare_and_fusion), kind=kLoop, calls=%fused_computation.25 | loop fusion | flops 393216 | bytes 1572876 | tf_op jit(solution)/shard_map/jit(_where)/select_n | solution.py:148
  37.7 0.0 copy-start.2
  37.8 1.2 %fusion.31 = (bf16[8,64,4,128]{3,2,1,0:T(4,128)(2,1)S(1)}, bf16[8,64,4,128]{3,2,1,0:T(4,128)(2,1)S(1)}, bf16[8,64,4,128]{3,2,1,0:T(4,128)(2,1)S(1)}, bf16[8,64,4...) fusion(bf16[12,64,4,128]{3,2,1,0:T(4,128)(2,1)S(1)} %broadcast_select_fusion), kind=kLoop, calls=%fused_computation.49 | loop fusion | bytes 5242880 | tf_op jit(solution)/shard_map/slice | solution.py:156
  39.0 0.0 copy-done.2
  39.0 0.3 fusion.19
  39.3 0.3 convolution_add_fusion.3
  39.7 0.3 convolution_add_fusion.2
  40.0 0.3 convolution_add_fusion.1
  40.4 0.0 copy-start.4
  40.4 0.3 fusion
  40.8 0.3 copy-done.4
  41.1 0.0 copy-start.1
  41.1 1.2 %fusion.14 = bf16[8,64,4,128]{3,1,2,0:T(8,128)(2,1)} fusion(f32[8,8,8,4,128]{4,2,3,0,1:T(8,128)S(1)} %fusion, f32[64]{0:T(128)S(1)} %copy-done.4), kind=kLoop, calls=%fused_computation.22 | loop fusion | flops 2621440 | bytes 1573120 | tf_op jit(solution)/shard_map/convert_element_type | solution.py:30
  42.3 0.0 copy-start.3
  42.3 7.6 %all-to-all-start = ((bf16[8,64,4,128]{3,1,2,0:T(8,128)(2,1)}), bf16[8,64,4,128]{3,1,2,0:T(8,128)(2,1)S(1)}, u32[]{:S(2)}, u32[]{:S(2)}) async-start(bf16[8,64,4,128]{3,1,2,0:T(8,128)(2,1)} %fusion.14), calls=%async_computation | async-start | bytes 1048576 | tf_op jit(solution)/shard_map/all_to_all | solution.py:157
  49.9 0.0 copy-done.1
  49.9 0.3 copy.44
  50.2 1.1 %reshape.121.w_ref = bf16[320,320]{1,0:T(8,128)(2,1)} reshape(bf16[5,64,5,64]{3,2,1,0:T(8,128)(2,1)S(1)} %copy.44) | data formatting | bytes 409600 | tf_op jit(solution)/shard_map/reshape | solution.py:201
  51.3 0.1 pad.8.clone
  51.4 0.0 copy-done.3
  51.4 8.0 %all-to-all-done = bf16[8,64,4,128]{3,1,2,0:T(8,128)(2,1)S(1)} async-done(((bf16[8,64,4,128]{3,1,2,0:T(8,128)(2,1)}), bf16[8,64,4,128]{3,1,2,0:T(8,128)(2,1)S(1)}, u32[]{:S(2)}, u32[]{:S(2)}) %all-to-all-start) | async-done | bytes 524320 | tf_op jit(solution)/shard_map/all_to_all | solution.py:157
  59.4 0.3 copy_multiply_fusion
  59.7 0.2 fusion.32
  59.9 0.6 copy.36
  60.5 0.7 copy.38.left_edge
  61.2 0.6 copy.37
  61.8 0.7 copy.39.right_edge
  62.5 12.4 %shard_map.74 = (bf16[64,64]{1,0:T(8,128)(2,1)}, bf16[64,64]{1,0:T(8,128)(2,1)}) custom-call(bf16[64,64]{1,0:T(8,128)(2,1)} %copy.38.left_edge, bf16[64,64]{1,0:T(8,128)(2,1)} %copy.39.right_edge), custom_call_target="tpu_custom_call" | custom-call | tf_op jit(solution)/shard_map/pallas_call | solution.py:255
  74.9 0.8 copy.40
  75.7 0.9 %copy.42 = bf16[1,64,32,2]{3,2,1,0:T(8,128)(2,1)S(1)} copy(bf16[1,64,32,2]{1,3,2,0:T(2,128)(2,1)S(1)} %bitcast.90) | data formatting | bytes 16384 | tf_op jit(solution)/shard_map/reshape | solution.py:263
  76.7 0.8 copy.41
  77.5 0.9 %copy.43 = bf16[1,64,32,2]{3,2,1,0:T(8,128)(2,1)S(1)} copy(bf16[1,64,32,2]{1,3,2,0:T(2,128)(2,1)S(1)} %bitcast.91) | data formatting | bytes 16384 | tf_op jit(solution)/shard_map/reshape | solution.py:263
  78.4 0.7 maximum_bitcast_fusion
  79.1 0.7 pad.4
  79.8 1.3 %copy.56 = bf16[8,8,36,256]{3,1,2,0:T(8,128)(2,1)} copy(bf16[8,8,36,256]{3,2,1,0:T(8,128)(2,1)S(1)} %bitcast.77) | data formatting | bytes 2359296
  81.1 0.0 copy-start.5
  81.1 5.3 %shard_map.75 = f32[32,64,128]{2,1,0:T(8,128)} custom-call(bf16[64,9216]{1,0:T(8,128)(2,1)} %bitcast.86, bf16[320,320]{1,0:T(8,128)(2,1)} %reshape.121.w_ref), custom_call_target="tpu_custom_call" | custom-call | flops 1677721600 | bytes 2433024 | tf_op jit(solution)/shard_map/pallas_call | solution.py:202
  86.4 0.0 copy-done.5
  86.4 1.5 %fusion.6 = bf16[1,64,32,128]{3,1,2,0:T(8,128)(2,1)S(1)} fusion(f32[32,64,128]{2,1,0:T(8,128)} %shard_map.75, f32[64]{0:T(128)S(1)} %copy-done.5, f32[32,128]{1,0:T(8,128)S(1)} %get-tuple-element.16, bf16[1,64,32,128]{3,2,1,0:T(8,128)(2,1)S(1)} %copy-done), kind=kLoop, calls=%fused_computation.14 | loop fusion | flops 1310720 | bytes 2113792 | tf_op jit(solution)/shard_map/convert_element_type | solution.py:163
  87.9 1.1 %copy.45 = bf16[1,64,32,128]{3,2,1,0:T(8,128)(2,1)} copy(bf16[1,64,32,128]{3,1,2,0:T(8,128)(2,1)S(1)} %fusion.6) | data formatting | bytes 1048576 | tf_op jit(solution)/shard_map/convert_element_type | solution.py:163
  (5 shorter events, 0.0 us)
Async XLA Ops:
  0.0 2.6 %copy-start = (bf16[1,64,32,128]{3,2,1,0:T(8,128)(2,1)S(1)}, bf16[1,64,32,128]{3,2,1,0:T(8,128)(2,1)}, u32[]{:S(2)}) copy-start(bf16[1,64,32,128]{3,2,1,0:T(8,128)(2,1)} %param.7) | copy-start | bytes 1572868
  37.7 1.2 %copy-start.2 = (bf16[5,8,8,8]{3,2,1,0:T(8,128)(2,1)S(1)}, bf16[5,8,8,8]{3,2,1,0:T(8,128)(2,1)}, u32[]{:S(2)}) copy-start(bf16[5,8,8,8]{3,2,1,0:T(8,128)(2,1)} %param.10) | copy-start | bytes 15364
  40.4 0.7 copy-start.4
  41.1 8.8 %copy-start.1 = (bf16[5,64,5,64]{3,1,2,0:T(8,128)(2,1)S(1)}, bf16[5,64,5,64]{3,1,2,0:T(8,128)(2,1)}, u32[]{:S(2)}) copy-start(bf16[5,64,5,64]{3,1,2,0:T(8,128)(2,1)} %param.12) | copy-start | bytes 614404
  42.3 9.1 %copy-start.3 = (s32[1,32,128]{2,1,0:T(8,128)S(1)}, s32[1,32,128]{2,1,0:T(8,128)}, u32[]{:S(2)}) copy-start(s32[1,32,128]{2,1,0:T(8,128)} %param.8) | copy-start | bytes 49156
  42.3 17.1 %all-to-all-start = ((bf16[8,64,4,128]{3,1,2,0:T(8,128)(2,1)}), bf16[8,64,4,128]{3,1,2,0:T(8,128)(2,1)S(1)}, u32[]{:S(2)}, u32[]{:S(2)}) async-start(bf16[8,64,4,128]{3,1,2,0:T(8,128)(2,1)} %fusion.14), calls=%async_computation | async-start | bytes 1048576 | tf_op jit(solution)/shard_map/all_to_all | solution.py:157
  81.1 5.3 %copy-start.5 = (f32[64]{0:T(128)S(1)}, f32[64]{0:T(128)}, u32[]{:S(2)}) copy-start(f32[64]{0:T(128)} %param.13) | copy-start | bytes 772

commit v10 on v9

--- a/solution.py
+++ b/solution.py
@@ -31,6 +31,7 @@
 
 
 def column_kernel(halves, group, reach, blocks_ref, out_ref, send_sems, recv_sems, own_sem):
+    cross = reach > 0
     lon = lax.axis_index("lon")
     half, place = lax.axis_index("lat_hi"), lax.axis_index("lat_lo")
     upper = halves - 1 - half
@@ -43,8 +44,9 @@
         def _():
             pl.semaphore_signal(barrier, inc=1, device_id=(lon, half, other), device_id_type=mesh_ids)
 
-    pl.semaphore_signal(barrier, inc=1, device_id=partner, device_id_type=mesh_ids)
-    pl.semaphore_wait(barrier, group)
+    if cross:
+        pl.semaphore_signal(barrier, inc=1, device_id=partner, device_id_type=mesh_ids)
+    pl.semaphore_wait(barrier, group - 1 + cross)
 
     own = pltpu.make_async_copy(blocks_ref.at[place], out_ref.at[reach + place], own_sem.at[0])
     own.start()
@@ -123,16 +125,13 @@
         forward.wait_send()
 
 
-def columns_of(normed, reach):
+def exchange(blocks, reach, collective):
     halves, group = lax.axis_size("lat_hi"), lax.axis_size("lat_lo")
-    _, channels, rows_lat, cols_lon = normed.shape
-    rows = rows_lat // group
-    blocks = normed[0].reshape(channels, group, rows, cols_lon).transpose(1, 0, 2, 3)
     any_spec = pl.BlockSpec(memory_space=pl.ANY)
     slots = group + 2 * reach
-    out = pl.pallas_call(
+    return pl.pallas_call(
         functools.partial(column_kernel, halves, group, reach),
-        out_shape=jax.ShapeDtypeStruct((slots, channels, rows, cols_lon), normed.dtype),
+        out_shape=jax.ShapeDtypeStruct((slots,) + blocks.shape[1:], blocks.dtype),
         in_specs=[any_spec],
         out_specs=any_spec,
         scratch_shapes=[
@@ -140,12 +139,27 @@
             pltpu.SemaphoreType.DMA((slots,)),
             pltpu.SemaphoreType.DMA((1,)),
         ],
-        compiler_params=pltpu.CompilerParams(collective_id=1, has_side_effects=True),
+        compiler_params=pltpu.CompilerParams(collective_id=collective, has_side_effects=True),
     )(blocks)
+
+
+def columns_of(normed, reach):
+    group = lax.axis_size("lat_lo")
+    _, channels, rows_lat, cols_lon = normed.shape
+    rows = rows_lat // group
+    blocks = normed[0].reshape(channels, group, rows, cols_lon).transpose(1, 0, 2, 3)
+    out = exchange(blocks, reach, 1)
+    slots = out.shape[0]
     half = lax.axis_index("lat_hi")
     slot = lax.broadcasted_iota(jnp.int32, (slots, 1, 1, 1), 0)
     real = jnp.logical_and(slot >= reach * (1 - half), slot < slots - reach * half)
     return jnp.where(real, out, jnp.zeros_like(out))
+
+
+def rows_of(mixed):
+    group, channels, rows, cols_lon = mixed.shape
+    back = exchange(mixed, 0, 2)
+    return back.transpose(1, 0, 2, 3).reshape(1, channels, group * rows, cols_lon)
 
 
 def local(fields, ocean_mask, norm_gain, w_vert, b_vert, w_horiz, b_horiz):
@@ -154,9 +168,7 @@
     padded = columns_of(normed, reach)
     count_lev = padded.shape[0] - 2 * reach
     taps = [padded[tap_index : tap_index + count_lev] for tap_index in range(w_vert.shape[0])]
-    mixed = lax.all_to_all(
-        vertical(taps, w_vert, b_vert), "lat_lo", split_axis=0, concat_axis=2, tiled=True
-    )
+    mixed = rows_of(vertical(taps, w_vert, b_vert))
     masked = mixed * ocean_mask[:, None].astype(jnp.bfloat16)
     conv = horizontal(masked, w_horiz)
     ocean = ocean_mask[:, None].astype(jnp.float32)

time: 89.6 us -> 88.4 us (0.987)
  Pallas kernels: 49.1 us -> 63 us
  waiting for transfers between devices: 8.01 us -> 0 us
  starting transfers between devices: 7.59 us -> 0 us
    pallas_call x1 -> x2, Pallas kernels: 31.4 us -> 45.3 us  [exchange(): pl.pallas_call(functools.partial(column_kernel, halves, group, reach), ou...]
    all_to_all x1 -> x0, waiting for transfers between devices: 8.01 us -> none  [local(): lax.all_to_all(vertical(taps, w_vert, b_vert), 'lat_lo', split_axis=0, co...]
    all_to_all x1 -> x0, starting transfers between devices: 7.59 us -> none  [local(): lax.all_to_all(vertical(taps, w_vert, b_vert), 'lat_lo', split_axis=0, co...]
    reshape x2, local copies, waits for them, and re-layouts: 1.86 us -> 0.68 us  [lon_halo(): return (from_left.reshape(edge_shape), from_right.reshape(edge_shape))]
    transpose x0 -> x1, local copies, waits for them, and re-layouts: none -> 1.16 us  [rows_of(): back.transpose(1, 0, 2, 3).reshape(1, channels, group * rows, cols_lon)]
    unnamed x13 -> x14, local copies, waits for them, and re-layouts: 1.58 us -> 2.21 us
  transfers between devices with their start and end apart: 1 -> 0, of which waited for: 1 -> 0; matrix products, arithmetic and copies ran while one was open for 2% -> 0% of each run, Pallas kernels for 0% -> 0%
where the time goes in v10:
time: 88.4 us; the launch traced here: 87.9 us
  Pallas kernels  63 us (71%)
  local copies, waits for them, and re-layouts  13.9 us (16%)
  other arithmetic  9.01 us (10%)
  matrix products  1.74 us (2%)
    pallas_call x2, Pallas kernels, exchange(): pl.pallas_call(functools.partial(column_kernel, halves, group, reach), ou...  45.3 us
    pallas_call x1, Pallas kernels, lon_halo(): pl.pallas_call(functools.partial(halo_kernel, count), out_shape=(jax.Shap...  12.4 us
    pallas_call x1, Pallas kernels, horizontal(): pl.pallas_call(horizontal_kernel, out_shape=jax.ShapeDtypeStruct((rows_la...  5.33 us
    unnamed x14, local copies, waits for them, and re-layouts  2.21 us

profile of v10, /device:TPU:1, one launch (start us, length us, event | category | flops | bytes accessed | tf_op | source)
XLA Modules:
  0.0 87.9 jit_solution(11933618206613156363)
XLA Ops:
  0.0 0.0 copy-start
  0.0 1.3 %convert_reduce_fusion = f32[32,128]{1,0:T(8,128)S(1)} fusion(bf16[1,64,32,128]{3,2,1,0:T(8,128)(2,1)} %param.7), kind=kLoop, calls=%fused_computation.3 | loop fusion | flops 520192 | bytes 540672 | tf_op jit(solution)/shard_map/reduce_sum | solution.py:13
  1.3 1.3 %fusion.3 = f32[32,128]{1,0:T(8,128)S(1)} fusion(f32[32,128]{1,0:T(8,128)S(1)} %broadcast_multiply_fusion, bf16[1,64,32,128]{3,2,1,0:T(8,128)(2,1)} %param.7), kind=kLoop, calls=%fused_computation.11 | loop fusion | flops 1044480 | bytes 557056 | tf_op jit(solution)/shard_map/reduce_sum | solution.py:14
  2.6 0.0 copy-done
  2.6 1.0 %fusion.5 = bf16[1,64,32,128]{3,1,2,0:T(8,128)(2,1)S(1)} fusion(f32[64]{0:T(128)} %param.9, f32[32,128]{1,0:T(8,128)S(1)} %add_rsqrt_fusion, f32[32,128]{1,0:T(8,128)S(1)} %broadcast_multiply_fusion, bf16[1,64,32,128]{3,2,1,0:T(8,128)(2,1)S(1)} %copy-done), kind=kLoop, calls=%fused_computation.13 | loop fusion | flops 1310720 | bytes 1081600 | tf_op jit(solution)/shard_map/convert_element_type | solution.py:15
  3.6 1.2 %copy.101 = bf16[64,8,4,128]{3,2,0,1:T(4,128)(2,1)} copy(bf16[64,8,4,128]{3,0,2,1:T(8,128)(2,1)S(1)} %bitcast.79) | data formatting | bytes 1048576 | tf_op jit(solution)/shard_map/reshape;squeeze | solution.py:150
  4.8 31.4 %shard_map.73 = bf16[12,64,4,128]{3,2,1,0:T(4,128)(2,1)} custom-call(bf16[8,64,4,128]{3,2,1,0:T(4,128)(2,1)} %bitcast.80), custom_call_target="tpu_custom_call" | custom-call | tf_op jit(solution)/shard_map/pallas_call | solution.py:132
  36.2 1.5 %broadcast_select_fusion = bf16[12,64,4,128]{3,2,1,0:T(4,128)(2,1)S(1)} fusion(bf16[12,64,4,128]{3,2,1,0:T(4,128)(2,1)} %shard_map.73, pred[12]{0:T(512)(128)(4,1)S(1)} %compare_and_fusion), kind=kLoop, calls=%fused_computation.24 | loop fusion | flops 393216 | bytes 1572876 | tf_op jit(solution)/shard_map/jit(_where)/select_n | solution.py:156
  37.7 0.0 copy-start.2
  37.8 1.2 %fusion.31 = (bf16[8,64,4,128]{3,2,1,0:T(4,128)(2,1)S(1)}, bf16[8,64,4,128]{3,2,1,0:T(4,128)(2,1)S(1)}, bf16[8,64,4,128]{3,2,1,0:T(4,128)(2,1)S(1)}, bf16[8,64,4...) fusion(bf16[12,64,4,128]{3,2,1,0:T(4,128)(2,1)S(1)} %broadcast_select_fusion), kind=kLoop, calls=%fused_computation.48 | loop fusion | bytes 5242880 | tf_op jit(solution)/shard_map/slice | solution.py:170
  39.0 0.0 copy-done.2
  39.0 0.3 fusion.19
  39.3 0.3 convolution_add_fusion.3
  39.7 0.3 convolution_add_fusion.2
  40.0 0.3 convolution_add_fusion.1
  40.4 0.3 fusion
  40.8 0.0 copy-start.4
  40.8 0.3 copy.60
  41.1 0.3 copy-done.4
  41.4 1.6 %fusion.14.blocks_ref = bf16[8,64,4,128]{3,2,1,0:T(4,128)(2,1)} fusion(f32[8,64,4,128]{3,2,1,0:T(4,128)S(1)} %bitcast.73, f32[64]{0:T(128)S(1)} %copy-done.4), kind=kLoop, calls=%fused_computation.23 | loop fusion | flops 2621440 | bytes 1573120 | tf_op jit(solution)/shard_map/convert_element_type | solution.py:30
  43.0 0.0 copy-start.3
  43.0 13.9 %shard_map.74 = bf16[8,64,4,128]{3,2,1,0:T(4,128)(2,1)} custom-call(bf16[8,64,4,128]{3,2,1,0:T(4,128)(2,1)} %fusion.14.blocks_ref), custom_call_target="tpu_custom_call" | custom-call | tf_op jit(solution)/shard_map/pallas_call | solution.py:132
  57.0 1.2 %copy.62 = bf16[64,8,4,128]{3,0,2,1:T(8,128)(2,1)S(1)} copy(bf16[64,8,4,128]{3,2,0,1:T(4,128)(2,1)} %bitcast.81) | data formatting | bytes 1048576 | tf_op jit(solution)/shard_map/transpose | solution.py:162
  58.1 0.0 copy-done.3
  58.2 0.1 bitcast_multiply_fusion
  58.2 0.2 fusion.32
  58.5 0.3 copy.63
  58.8 0.7 copy.65.left_edge
  59.5 0.3 copy.64
  59.7 0.7 copy.66.right_edge
  60.4 12.4 %shard_map.75 = (bf16[64,64]{1,0:T(8,128)(2,1)}, bf16[64,64]{1,0:T(8,128)(2,1)}) custom-call(bf16[64,64]{1,0:T(8,128)(2,1)} %copy.65.left_edge, bf16[64,64]{1,0:T(8,128)(2,1)} %copy.66.right_edge), custom_call_target="tpu_custom_call" | custom-call | tf_op jit(solution)/shard_map/pallas_call | solution.py:267
  72.8 0.8 copy.67
  73.6 0.3 copy.69
  74.0 0.8 copy.68
  74.8 0.3 copy.70
  75.1 0.1 pad.8.clone
  75.2 0.7 maximum_bitcast_fusion
  75.9 0.6 copy.84
  76.5 0.7 pad.4.clone
  77.2 0.0 copy-start.1
  77.2 1.3 %copy.85 = bf16[8,8,36,256]{3,1,2,0:T(8,128)(2,1)} copy(bf16[8,8,36,256]{3,2,1,0:T(8,128)(2,1)S(1)} %bitcast.72) | data formatting | bytes 2359296
  78.5 0.0 copy-done.1
  78.5 0.3 copy.72
  78.8 1.1 %reshape.125.w_ref = bf16[320,320]{1,0:T(8,128)(2,1)} reshape(bf16[5,64,5,64]{3,2,1,0:T(8,128)(2,1)S(1)} %copy.72) | data formatting | bytes 409600 | tf_op jit(solution)/shard_map/reshape | solution.py:213
  79.9 0.0 copy-start.5
  79.9 5.3 %shard_map.76 = f32[32,64,128]{2,1,0:T(8,128)} custom-call(bf16[64,9216]{1,0:T(8,128)(2,1)} %bitcast.82, bf16[320,320]{1,0:T(8,128)(2,1)} %reshape.125.w_ref), custom_call_target="tpu_custom_call" | custom-call | flops 1677721600 | bytes 2433024 | tf_op jit(solution)/shard_map/pallas_call | solution.py:214
  85.2 0.0 copy-done.5
  85.2 1.5 %fusion.6 = bf16[1,64,32,128]{3,1,2,0:T(8,128)(2,1)S(1)} fusion(f32[32,64,128]{2,1,0:T(8,128)} %shard_map.76, f32[64]{0:T(128)S(1)} %copy-done.5, f32[32,128]{1,0:T(8,128)S(1)} %get-tuple-element.16, bf16[1,64,32,128]{3,2,1,0:T(8,128)(2,1)S(1)} %copy-done), kind=kLoop, calls=%fused_computation.14 | loop fusion | flops 1310720 | bytes 2113792 | tf_op jit(solution)/shard_map/convert_element_type | solution.py:175
  86.7 1.1 %copy.73 = bf16[1,64,32,128]{3,2,1,0:T(8,128)(2,1)} copy(bf16[1,64,32,128]{3,1,2,0:T(8,128)(2,1)S(1)} %fusion.6) | data formatting | bytes 1048576 | tf_op jit(solution)/shard_map/convert_element_type | solution.py:175
  (5 shorter events, 0.0 us)
Async XLA Ops:
  0.0 2.6 %copy-start = (bf16[1,64,32,128]{3,2,1,0:T(8,128)(2,1)S(1)}, bf16[1,64,32,128]{3,2,1,0:T(8,128)(2,1)}, u32[]{:S(2)}) copy-start(bf16[1,64,32,128]{3,2,1,0:T(8,128)(2,1)} %param.7) | copy-start | bytes 1572868
  37.7 1.2 %copy-start.2 = (bf16[5,8,8,8]{3,2,1,0:T(8,128)(2,1)S(1)}, bf16[5,8,8,8]{3,2,1,0:T(8,128)(2,1)}, u32[]{:S(2)}) copy-start(bf16[5,8,8,8]{3,2,1,0:T(8,128)(2,1)} %param.10) | copy-start | bytes 15364
  40.8 0.7 copy-start.4
  43.0 15.1 %copy-start.3 = (s32[1,32,128]{2,1,0:T(8,128)S(1)}, s32[1,32,128]{2,1,0:T(8,128)}, u32[]{:S(2)}) copy-start(s32[1,32,128]{2,1,0:T(8,128)} %param.8) | copy-start | bytes 49156
  77.2 1.3 %copy-start.1 = (bf16[5,64,5,64]{3,1,2,0:T(8,128)(2,1)S(1)}, bf16[5,64,5,64]{3,1,2,0:T(8,128)(2,1)}, u32[]{:S(2)}) copy-start(bf16[5,64,5,64]{3,1,2,0:T(8,128)(2,1)} %param.12) | copy-start | bytes 614404
  79.9 5.3 %copy-start.5 = (f32[64]{0:T(128)S(1)}, f32[64]{0:T(128)}, u32[]{:S(2)}) copy-start(f32[64]{0:T(128)} %param.13) | copy-start | bytes 772

commit v11 on v10

--- a/solution.py
+++ b/solution.py
@@ -30,7 +30,9 @@
     return jax.nn.gelu(summed).astype(jnp.bfloat16)
 
 
-def column_kernel(halves, group, reach, blocks_ref, out_ref, send_sems, recv_sems, own_sem):
+def column_kernel(
+    halves, group, reach, blocks_ref, out_ref, send_sems, recv_sems, own_sem, zero_ref, zero_sems
+):
     cross = reach > 0
     lon = lax.axis_index("lon")
     half, place = lax.axis_index("lat_hi"), lax.axis_index("lat_lo")
@@ -50,6 +52,13 @@
 
     own = pltpu.make_async_copy(blocks_ref.at[place], out_ref.at[reach + place], own_sem.at[0])
     own.start()
+    zero_ref[...] = jnp.zeros(zero_ref.shape, zero_ref.dtype)
+    blanks = [
+        pltpu.make_async_copy(zero_ref, out_ref.at[(group + reach) * half + level], zero_sems.at[level])
+        for level in range(reach)
+    ]
+    for blank in blanks:
+        blank.start()
 
     def inward(other):
         return pltpu.make_async_remote_copy(
@@ -123,6 +132,8 @@
 
     for forward in forwards:
         forward.wait_send()
+    for blank in blanks:
+        blank.wait()
 
 
 def exchange(blocks, reach, collective):
@@ -138,6 +149,8 @@
             pltpu.SemaphoreType.DMA((group + reach,)),
             pltpu.SemaphoreType.DMA((slots,)),
             pltpu.SemaphoreType.DMA((1,)),
+            pltpu.VMEM(blocks.shape[1:], blocks.dtype),
+            pltpu.SemaphoreType.DMA((max(reach, 1),)),
         ],
         compiler_params=pltpu.CompilerParams(collective_id=collective, has_side_effects=True),
     )(blocks)
@@ -148,12 +161,7 @@
     _, channels, rows_lat, cols_lon = normed.shape
     rows = rows_lat // group
     blocks = normed[0].reshape(channels, group, rows, cols_lon).transpose(1, 0, 2, 3)
-    out = exchange(blocks, reach, 1)
-    slots = out.shape[0]
-    half = lax.axis_index("lat_hi")
-    slot = lax.broadcasted_iota(jnp.int32, (slots, 1, 1, 1), 0)
-    real = jnp.logical_and(slot >= reach * (1 - half), slot < slots - reach * half)
-    return jnp.where(real, out, jnp.zeros_like(out))
+    return exchange(blocks, reach, 1)
 
 
 def rows_of(mixed):

time: 88.4 us -> 88.8 us (level)
  local copies, waits for them, and re-layouts: 13.9 us -> 15.8 us
  other arithmetic: 9.01 us -> 7.46 us
    slice x1, local copies, waits for them, and re-layouts: 1.21 us -> 3.14 us  [local(): padded[tap_index:tap_index + count_lev]]
    select_n x1 -> x0, other arithmetic: 1.54 us -> none  [columns_of(): return jnp.where(real, out, jnp.zeros_like(out))]
where the time goes in v11:
time: 88.8 us; the launch traced here: 88.3 us
  Pallas kernels  63 us (71%)
  local copies, waits for them, and re-layouts  15.8 us (18%)
  other arithmetic  7.46 us (8%)
  matrix products  1.75 us (2%)
    pallas_call x2, Pallas kernels, exchange(): pl.pallas_call(functools.partial(column_kernel, halves, group, reach), ou...  45.3 us
    pallas_call x1, Pallas kernels, lon_halo(): pl.pallas_call(functools.partial(halo_kernel, count), out_shape=(jax.Shap...  12.4 us
    pallas_call x1, Pallas kernels, horizontal(): pl.pallas_call(horizontal_kernel, out_shape=jax.ShapeDtypeStruct((rows_la...  5.33 us
    slice x1, local copies, waits for them, and re-layouts, local(): padded[tap_index:tap_index + count_lev]  3.14 us
    unnamed x14, local copies, waits for them, and re-layouts  2.21 us

profile of v11, /device:TPU:1, one launch (start us, length us, event | category | flops | bytes accessed | tf_op | source)
XLA Modules:
  0.0 88.3 jit_solution(8802616400629135731)
XLA Ops:
  0.0 0.0 copy-start
  0.0 1.3 %convert_reduce_fusion = f32[32,128]{1,0:T(8,128)S(1)} fusion(bf16[1,64,32,128]{3,2,1,0:T(8,128)(2,1)} %param.7), kind=kLoop, calls=%fused_computation.3 | loop fusion | flops 520192 | bytes 540672 | tf_op jit(solution)/shard_map/reduce_sum | solution.py:13
  1.3 1.3 %fusion.3 = f32[32,128]{1,0:T(8,128)S(1)} fusion(f32[32,128]{1,0:T(8,128)S(1)} %broadcast_multiply_fusion, bf16[1,64,32,128]{3,2,1,0:T(8,128)(2,1)} %param.7), kind=kLoop, calls=%fused_computation.11 | loop fusion | flops 1044480 | bytes 557056 | tf_op jit(solution)/shard_map/reduce_sum | solution.py:14
  2.6 0.0 copy-done
  2.6 1.0 %fusion.5 = bf16[1,64,32,128]{3,1,2,0:T(8,128)(2,1)S(1)} fusion(f32[64]{0:T(128)} %param.9, f32[32,128]{1,0:T(8,128)S(1)} %add_rsqrt_fusion, f32[32,128]{1,0:T(8,128)S(1)} %broadcast_multiply_fusion, bf16[1,64,32,128]{3,2,1,0:T(8,128)(2,1)S(1)} %copy-done), kind=kLoop, calls=%fused_computation.13 | loop fusion | flops 1310720 | bytes 1081600 | tf_op jit(solution)/shard_map/convert_element_type | solution.py:15
  3.6 1.2 %copy.101 = bf16[64,8,4,128]{3,2,0,1:T(4,128)(2,1)} copy(bf16[64,8,4,128]{3,0,2,1:T(8,128)(2,1)S(1)} %bitcast.79) | data formatting | bytes 1048576 | tf_op jit(solution)/shard_map/reshape;squeeze | solution.py:163
  4.8 31.4 %shard_map.73 = bf16[12,64,4,128]{3,2,1,0:T(4,128)(2,1)} custom-call(bf16[8,64,4,128]{3,2,1,0:T(4,128)(2,1)} %bitcast.80), custom_call_target="tpu_custom_call" | custom-call | tf_op jit(solution)/shard_map/pallas_call | solution.py:143
  36.2 0.0 copy-start.2
  36.2 3.1 %fusion.31 = (bf16[8,64,4,128]{3,2,1,0:T(4,128)(2,1)S(1)}, bf16[8,64,4,128]{3,2,1,0:T(4,128)(2,1)S(1)}, bf16[8,64,4,128]{3,2,1,0:T(4,128)(2,1)S(1)}, bf16[8,64,4...) fusion(bf16[12,64,4,128]{3,2,1,0:T(4,128)(2,1)} %shard_map.73), kind=kLoop, calls=%fused_computation.46 | loop fusion | bytes 5242880 | tf_op jit(solution)/shard_map/slice | solution.py:178
  39.4 0.0 copy-done.2
  39.4 0.3 fusion.19
  39.7 0.3 convolution_add_fusion.3
  40.1 0.3 convolution_add_fusion.2
  40.5 0.3 convolution_add_fusion.1
  40.8 0.3 fusion
  41.2 0.0 copy-start.4
  41.2 0.3 copy.60
  41.5 0.3 copy-done.4
  41.8 1.6 %fusion.14.blocks_ref = bf16[8,64,4,128]{3,2,1,0:T(4,128)(2,1)} fusion(f32[8,64,4,128]{3,2,1,0:T(4,128)S(1)} %bitcast.73, f32[64]{0:T(128)S(1)} %copy-done.4), kind=kLoop, calls=%fused_computation.23 | loop fusion | flops 2621440 | bytes 1573120 | tf_op jit(solution)/shard_map/convert_element_type | solution.py:30
  43.4 0.0 copy-start.3
  43.4 13.9 %shard_map.74 = bf16[8,64,4,128]{3,2,1,0:T(4,128)(2,1)} custom-call(bf16[8,64,4,128]{3,2,1,0:T(4,128)(2,1)} %fusion.14.blocks_ref), custom_call_target="tpu_custom_call" | custom-call | tf_op jit(solution)/shard_map/pallas_call | solution.py:143
  57.4 1.2 %copy.62 = bf16[64,8,4,128]{3,0,2,1:T(8,128)(2,1)S(1)} copy(bf16[64,8,4,128]{3,2,0,1:T(4,128)(2,1)} %bitcast.81) | data formatting | bytes 1048576 | tf_op jit(solution)/shard_map/transpose | solution.py:170
  58.5 0.0 copy-done.3
  58.6 0.1 bitcast_multiply_fusion
  58.6 0.2 fusion.32
  58.9 0.3 copy.63
  59.2 0.7 copy.65.left_edge
  59.9 0.3 copy.64
  60.1 0.7 copy.66.right_edge
  60.8 12.4 %shard_map.75 = (bf16[64,64]{1,0:T(8,128)(2,1)}, bf16[64,64]{1,0:T(8,128)(2,1)}) custom-call(bf16[64,64]{1,0:T(8,128)(2,1)} %copy.65.left_edge, bf16[64,64]{1,0:T(8,128)(2,1)} %copy.66.right_edge), custom_call_target="tpu_custom_call" | custom-call | tf_op jit(solution)/shard_map/pallas_call | solution.py:275
  73.2 0.8 copy.67
  74.0 0.3 copy.69
  74.3 0.8 copy.68
  75.2 0.3 copy.70
  75.5 0.1 pad.8.clone
  75.6 0.7 maximum_bitcast_fusion
  76.3 0.6 copy.84
  76.9 0.7 pad.4.clone
  77.6 0.0 copy-start.1
  77.6 1.3 %copy.85 = bf16[8,8,36,256]{3,1,2,0:T(8,128)(2,1)} copy(bf16[8,8,36,256]{3,2,1,0:T(8,128)(2,1)S(1)} %bitcast.72) | data formatting | bytes 2359296
  78.9 0.0 copy-done.1
  78.9 0.3 copy.72
  79.2 1.1 %reshape.114.w_ref = bf16[320,320]{1,0:T(8,128)(2,1)} reshape(bf16[5,64,5,64]{3,2,1,0:T(8,128)(2,1)S(1)} %copy.72) | data formatting | bytes 409600 | tf_op jit(solution)/shard_map/reshape | solution.py:221
  80.3 0.0 copy-start.5
  80.3 5.3 %shard_map.76 = f32[32,64,128]{2,1,0:T(8,128)} custom-call(bf16[64,9216]{1,0:T(8,128)(2,1)} %bitcast.82, bf16[320,320]{1,0:T(8,128)(2,1)} %reshape.114.w_ref), custom_call_target="tpu_custom_call" | custom-call | flops 1677721600 | bytes 2433024 | tf_op jit(solution)/shard_map/pallas_call | solution.py:222
  85.6 0.0 copy-done.5
  85.6 1.5 %fusion.6 = bf16[1,64,32,128]{3,1,2,0:T(8,128)(2,1)S(1)} fusion(f32[32,64,128]{2,1,0:T(8,128)} %shard_map.76, f32[64]{0:T(128)S(1)} %copy-done.5, f32[32,128]{1,0:T(8,128)S(1)} %get-tuple-element.16, bf16[1,64,32,128]{3,2,1,0:T(8,128)(2,1)S(1)} %copy-done), kind=kLoop, calls=%fused_computation.14 | loop fusion | flops 1310720 | bytes 2113792 | tf_op jit(solution)/shard_map/convert_element_type | solution.py:183
  87.1 1.1 %copy.73 = bf16[1,64,32,128]{3,2,1,0:T(8,128)(2,1)} copy(bf16[1,64,32,128]{3,1,2,0:T(8,128)(2,1)S(1)} %fusion.6) | data formatting | bytes 1048576 | tf_op jit(solution)/shard_map/convert_element_type | solution.py:183
  (4 shorter events, 0.0 us)
Async XLA Ops:
  0.0 2.6 %copy-start = (bf16[1,64,32,128]{3,2,1,0:T(8,128)(2,1)S(1)}, bf16[1,64,32,128]{3,2,1,0:T(8,128)(2,1)}, u32[]{:S(2)}) copy-start(bf16[1,64,32,128]{3,2,1,0:T(8,128)(2,1)} %param.7) | copy-start | bytes 1572868
  36.2 3.2 %copy-start.2 = (bf16[5,8,8,8]{3,2,1,0:T(8,128)(2,1)S(1)}, bf16[5,8,8,8]{3,2,1,0:T(8,128)(2,1)}, u32[]{:S(2)}) copy-start(bf16[5,8,8,8]{3,2,1,0:T(8,128)(2,1)} %param.10) | copy-start | bytes 15364
  41.2 0.7 copy-start.4
  43.4 15.1 %copy-start.3 = (s32[1,32,128]{2,1,0:T(8,128)S(1)}, s32[1,32,128]{2,1,0:T(8,128)}, u32[]{:S(2)}) copy-start(s32[1,32,128]{2,1,0:T(8,128)} %param.8) | copy-start | bytes 49156
  77.6 1.3 %copy-start.1 = (bf16[5,64,5,64]{3,1,2,0:T(8,128)(2,1)S(1)}, bf16[5,64,5,64]{3,1,2,0:T(8,128)(2,1)}, u32[]{:S(2)}) copy-start(bf16[5,64,5,64]{3,1,2,0:T(8,128)(2,1)} %param.12) | copy-start | bytes 614404
  80.3 5.3 %copy-start.5 = (f32[64]{0:T(128)S(1)}, f32[64]{0:T(128)}, u32[]{:S(2)}) copy-start(f32[64]{0:T(128)} %param.13) | copy-start | bytes 772

commit v12 on v5

--- a/solution.py
+++ b/solution.py
@@ -102,7 +102,7 @@
     return jnp.transpose(conv, (1, 0, 2))[None]
 
 
-def halo_kernel(count, left_edge, right_edge, from_left, from_right, send_sems, recv_sems):
+def halo_kernel(count, edges, halos, send_sems, recv_sems):
     me = lax.axis_index("lon")
     right, left = lax.rem(me + 1, count), lax.rem(me + count - 1, count)
     rest = (lax.axis_index("lat_hi"), lax.axis_index("lat_lo"))
@@ -112,16 +112,16 @@
         pl.semaphore_signal(barrier, inc=1, device_id=(neighbour,) + rest, device_id_type=mesh_ids)
     pl.semaphore_wait(barrier, 2)
     to_right = pltpu.make_async_remote_copy(
-        src_ref=right_edge,
-        dst_ref=from_left,
+        src_ref=edges.at[1],
+        dst_ref=halos.at[0],
         send_sem=send_sems.at[0],
         recv_sem=recv_sems.at[0],
         device_id=(right,) + rest,
         device_id_type=mesh_ids,
     )
     to_left = pltpu.make_async_remote_copy(
-        src_ref=left_edge,
-        dst_ref=from_right,
+        src_ref=edges.at[0],
+        dst_ref=halos.at[1],
         send_sem=send_sems.at[1],
         recv_sem=recv_sems.at[1],
         device_id=(left,) + rest,
@@ -136,20 +136,19 @@
 def lon_halo(block, width):
     count = lax.axis_size("lon")
     length = block.shape[-1]
-    edge_shape = block.shape[:-1] + (width,)
-    flat = (block.shape[1], block.shape[2] * width)
-    left_edge = block[..., :width].reshape(flat)
-    right_edge = block[..., length - width :].reshape(flat)
+    edges = jnp.stack([block[0, :, :, :width], block[0, :, :, length - width :]])
+    edges = jnp.transpose(edges, (0, 1, 3, 2))
     any_spec = pl.BlockSpec(memory_space=pl.ANY)
-    from_left, from_right = pl.pallas_call(
+    halos = pl.pallas_call(
         functools.partial(halo_kernel, count),
-        out_shape=(jax.ShapeDtypeStruct(flat, block.dtype),) * 2,
-        in_specs=[any_spec] * 2,
-        out_specs=(any_spec,) * 2,
+        out_shape=jax.ShapeDtypeStruct(edges.shape, block.dtype),
+        in_specs=[any_spec],
+        out_specs=any_spec,
         scratch_shapes=[pltpu.SemaphoreType.DMA((2,)), pltpu.SemaphoreType.DMA((2,))],
         compiler_params=pltpu.CompilerParams(collective_id=0, has_side_effects=True),
-    )(left_edge, right_edge)
-    return from_left.reshape(edge_shape), from_right.reshape(edge_shape)
+    )(edges)
+    halos = jnp.transpose(halos, (0, 1, 3, 2))[:, None]
+    return halos[0], halos[1]
 
 
 def solution(mesh):

time: 88.8 us -> 88.6 us (level)
  local copies, waits for them, and re-layouts: 12 us -> 9.37 us
  other arithmetic: 8.28 us -> 10.8 us
    reshape x4 -> x0, local copies, waits for them, and re-layouts: 3.27 us -> none  [the longest x2 1.86 us: lon_halo(): return (from_left.reshape(edge_shape), from_right.reshape(edge_shape))]
    all_to_all x0 -> x1, local copies, waits for them, and re-layouts: none -> 1.9 us  [local(): lax.all_to_all(vertical(taps, w_vert, b_vert), 'lat_lo', split_axis=0, co...]
    pallas_call x2 -> x0, local copies, waits for them, and re-layouts: 1.6 us -> none  [lon_halo(): pl.pallas_call(functools.partial(halo_kernel, count), out_shape=(jax.Shap...]
    mul x1, other arithmetic: 0.3 us -> 1.73 us  [local(): masked = mixed * ocean_mask[:, None].astype(jnp.bfloat16)]
    unnamed x13, local copies, waits for them, and re-layouts: 2.3 us -> 1.29 us
    slice x3 -> x4, local copies, waits for them, and re-layouts: 1.45 us -> 1.86 us  [the longest x3 1.8 us: lon_halo(): return (halos[0], halos[1])]
where the time goes in v12:
time: 88.6 us; the launch traced here: 87.9 us
  starting transfers between devices  26.2 us (30%)
  waiting for transfers between devices  21.7 us (24%)
  Pallas kernels  17.9 us (20%)
  other arithmetic  10.8 us (12%)
  local copies, waits for them, and re-layouts  9.37 us (11%)
  matrix products  1.75 us (2%)
    pallas_call x1, Pallas kernels, lon_halo(): pl.pallas_call(functools.partial(halo_kernel, count), out_shape=jax.Shape...  12.5 us
    ppermute x1, starting transfers between devices, local(): recv = lax.ppermute(send, 'lat_hi', [(0, 1), (1, 0)])  10.9 us
    all_to_all x1, starting transfers between devices, local(): lax.all_to_all(normed, 'lat_lo', split_axis=2, concat_axis=0, tiled=True)  10.3 us
    all_to_all x1, waiting for transfers between devices, local(): lax.all_to_all(normed, 'lat_lo', split_axis=2, concat_axis=0, tiled=True)  9.5 us
    all_to_all x1, waiting for transfers between devices, local(): lax.all_to_all(vertical(taps, w_vert, b_vert), 'lat_lo', split_axis=0, co...  7.88 us
    pallas_call x1, Pallas kernels, horizontal(): pl.pallas_call(horizontal_kernel, out_shape=jax.ShapeDtypeStruct((rows_la...  5.37 us
    all_to_all x1, starting transfers between devices, local(): lax.all_to_all(vertical(taps, w_vert, b_vert), 'lat_lo', split_axis=0, co...  4.98 us
    ppermute x1, waiting for transfers between devices, local(): recv = lax.ppermute(send, 'lat_hi', [(0, 1), (1, 0)])  4.28 us
  transfers between devices with their start and end apart: 3, of which 3 were waited for; matrix products, arithmetic and copies ran while one was open for 2% of the time, Pallas kernels for 0%

profile of v12, /device:TPU:1, one launch (start us, length us, event | category | flops | bytes accessed | tf_op | source)
XLA Modules:
  0.0 87.9 jit_solution(17970958484699743031)
XLA Ops:
  0.0 1.2 %convert_reduce_fusion = f32[32,128]{1,0:T(8,128)S(1)} fusion(bf16[1,64,32,128]{3,2,1,0:T(8,128)(2,1)} %param.7), kind=kLoop, calls=%fused_computation.3 | loop fusion | flops 520192 | bytes 540672 | tf_op jit(solution)/shard_map/reduce_sum | solution.py:13
  1.2 1.3 %fusion.3 = f32[32,128]{1,0:T(8,128)S(1)} fusion(f32[32,128]{1,0:T(8,128)S(1)} %broadcast_multiply_fusion.1, bf16[1,64,32,128]{3,2,1,0:T(8,128)(2,1)} %param.7), kind=kLoop, calls=%fused_computation.11 | loop fusion | flops 1044480 | bytes 557056 | tf_op jit(solution)/shard_map/reduce_sum | solution.py:14
  2.5 2.2 %fusion.19 = bf16[1,64,32,128]{3,1,0,2:T(8,128)(2,1)} fusion(f32[64]{0:T(128)} %param.9, f32[32,128]{1,0:T(8,128)S(1)} %add_rsqrt_fusion, f32[32,128]{1,0:T(8,128)S(1)} %broadcast_multiply_fusion.1, bf16[1,64,32,128]{3,2,1,0:T(8,128)(2,1)} %param.7), kind=kLoop, calls=%fused_computation.34 | loop fusion | flops 1310720 | bytes 1081600 | tf_op jit(solution)/shard_map/convert_element_type | solution.py:15
  4.7 10.3 %all-to-all-start = ((bf16[1,64,32,128]{3,1,0,2:T(8,128)(2,1)}), bf16[1,64,32,128]{3,1,0,2:T(8,128)(2,1)S(1)}, u32[]{:S(2)}, u32[]{:S(2)}) async-start(bf16[1,64,32,128]{3,1,0,2:T(8,128)(2,1)} %fusion.19), calls=%async_computation | async-start | bytes 1048576 | tf_op jit(solution)/shard_map/all_to_all | solution.py:36
  15.0 0.0 copy-start.2
  15.0 9.5 %all-to-all-done = bf16[1,64,32,128]{3,1,0,2:T(8,128)(2,1)S(1)} async-done(((bf16[1,64,32,128]{3,1,0,2:T(8,128)(2,1)}), bf16[1,64,32,128]{3,1,0,2:T(8,128)(2,1)S(1)}, u32[]{:S(2)}, u32[]{:S(2)}) %all-to-all-start) | async-done | bytes 524320 | tf_op jit(solution)/shard_map/all_to_all | solution.py:36
  24.5 10.9 %collective-permute-start = (bf16[2,64,4,128]{3,1,2,0:T(8,128)(2,1)S(1)}, bf16[2,64,4,128]{3,1,2,0:T(8,128)(2,1)S(1)}, u32[]{:S(2)}, u32[]{:S(2)}) collective-permute-start(bf16[2,64,4,128]{3,1,2,0:T(8,128)(2,1)S(1)} %fusion.28), channel_id=1, source_target_pairs={{0,8},{8,0},{1,9},{9,1},{2,10},{10,2},{3,11},{11,3},{4,12},{12,4},... | collective-permute-start | bytes 393224 | tf_op jit(solution)/shard_map/ppermute | solution.py:40
  35.4 4.3 %collective-permute-done = bf16[2,64,4,128]{3,1,2,0:T(8,128)(2,1)S(1)} collective-permute-done((bf16[2,64,4,128]{3,1,2,0:T(8,128)(2,1)S(1)}, bf16[2,64,4,128]{3,1,2,0:T(8,128)(2,1)S(1)}, u32[]{:S(2)}, u32[]{:S(2)}) %collective-permute-start) | collective-permute-done | bytes 131104 | tf_op jit(solution)/shard_map/ppermute | solution.py:40
  39.7 0.1 fusion.20
  39.9 0.0 copy-done.2
  39.9 0.3 fusion.26
  40.3 0.4 convolution_add_fusion.3
  40.6 0.3 convolution_add_fusion.2
  41.0 0.0 copy-start.4
  41.0 0.4 convolution_add_fusion.1
  41.3 0.0 copy-start.3
  41.4 0.0 copy-start.1
  41.4 0.4 fusion
  41.7 0.0 copy-done.4
  41.7 1.2 %fusion.14 = bf16[8,64,4,128]{3,1,2,0:T(8,128)(2,1)} fusion(f32[8,8,8,4,128]{4,2,3,0,1:T(8,128)S(1)} %fusion, f32[64]{0:T(128)S(1)} %copy-done.4), kind=kLoop, calls=%fused_computation.22 | loop fusion | flops 2621440 | bytes 1573120 | tf_op jit(solution)/shard_map/convert_element_type | solution.py:30
  43.0 5.0 %all-to-all-start.1 = ((bf16[8,64,4,128]{3,1,2,0:T(8,128)(2,1)}), bf16[8,64,4,128]{3,1,2,0:T(8,128)(2,1)S(1)}, u32[]{:S(2)}, u32[]{:S(2)}) async-start(bf16[8,64,4,128]{3,1,2,0:T(8,128)(2,1)} %fusion.14), calls=%async_computation.1 | async-start | bytes 1048576 | tf_op jit(solution)/shard_map/all_to_all | solution.py:46
  48.0 0.0 copy-done.3
  48.0 0.1 copy.48
  48.1 0.0 copy-done.1
  48.1 0.3 copy.53
  48.4 1.1 %reshape.103.w_ref = bf16[320,320]{1,0:T(8,128)(2,1)} reshape(bf16[5,64,5,64]{3,2,1,0:T(8,128)(2,1)S(1)} %copy.53) | data formatting | bytes 409600 | tf_op jit(solution)/shard_map/reshape | solution.py:90
  49.5 0.1 pad.8.clone
  49.6 7.9 %all-to-all-done.1 = bf16[8,64,4,128]{3,1,2,0:T(8,128)(2,1)S(1)} async-done(((bf16[8,64,4,128]{3,1,2,0:T(8,128)(2,1)}), bf16[8,64,4,128]{3,1,2,0:T(8,128)(2,1)S(1)}, u32[]{:S(2)}, u32[]{:S(2)}) %all-to-all-start.1) | async-done | bytes 524320 | tf_op jit(solution)/shard_map/all_to_all | solution.py:46
  57.5 1.9 %copy.49 = bf16[1,64,32,128]{2,3,1,0:T(8,128)(2,1)} copy(bf16[1,64,32,128]{3,1,2,0:T(8,128)(2,1)S(1)} %bitcast.90) | data formatting | bytes 1048576 | tf_op jit(solution)/shard_map/all_to_all | solution.py:46
  59.4 1.7 %broadcast_multiply_fusion = bf16[1,64,32,128]{2,3,1,0:T(8,128)(2,1)S(1)} fusion(bf16[1,64,32,128]{2,3,1,0:T(8,128)(2,1)} %copy.49, bf16[32,128]{0,1:T(8,128)(2,1)S(1)} %copy.48), kind=kLoop, calls=%fused_computation.25 | loop fusion | flops 262144 | bytes 1056768 | tf_op jit(solution)/shard_map/mul | solution.py:49
  61.1 0.1 fusion.39
  61.2 0.9 copy.51
  62.0 0.7 maximum_bitcast_fusion.1.edges
  62.8 12.5 %shard_map.73 = bf16[2,64,2,32]{3,2,1,0:T(2,128)(2,1)} custom-call(bf16[2,64,2,32]{3,2,1,0:T(2,128)(2,1)} %maximum_bitcast_fusion.1.edges), custom_call_target="tpu_custom_call" | custom-call | tf_op jit(solution)/shard_map/pallas_call | solution.py:142
  75.3 0.8 fusion.40
  76.1 0.5 copy.52
  76.6 0.5 copy.50
  77.1 0.7 maximum_bitcast_fusion
  77.8 0.7 pad.4
  78.6 1.3 %copy.65 = bf16[8,8,36,256]{3,1,2,0:T(8,128)(2,1)} copy(bf16[8,8,36,256]{3,2,1,0:T(8,128)(2,1)S(1)} %bitcast.89) | data formatting | bytes 2359296
  79.8 0.0 copy-start
  79.8 0.0 copy-start.5
  79.8 5.4 %shard_map.74 = f32[32,64,128]{2,1,0:T(8,128)} custom-call(bf16[64,9216]{1,0:T(8,128)(2,1)} %bitcast.91, bf16[320,320]{1,0:T(8,128)(2,1)} %reshape.103.w_ref), custom_call_target="tpu_custom_call" | custom-call | flops 1677721600 | bytes 2433024 | tf_op jit(solution)/shard_map/pallas_call | solution.py:91
  85.2 0.0 copy-done
  85.2 0.0 copy-done.5
  85.2 1.5 %fusion.6 = bf16[1,64,32,128]{3,1,2,0:T(8,128)(2,1)S(1)} fusion(f32[32,64,128]{2,1,0:T(8,128)} %shard_map.74, f32[64]{0:T(128)S(1)} %copy-done.5, f32[32,128]{1,0:T(8,128)S(1)} %get-tuple-element.17, bf16[1,64,32,128]{3,2,1,0:T(8,128)(2,1)S(1)} %copy-done), kind=kLoop, calls=%fused_computation.14 | loop fusion | flops 1310720 | bytes 2113792 | tf_op jit(solution)/shard_map/convert_element_type | solution.py:52
  86.7 1.1 %copy.54 = bf16[1,64,32,128]{3,2,1,0:T(8,128)(2,1)} copy(bf16[1,64,32,128]{3,1,2,0:T(8,128)(2,1)S(1)} %fusion.6) | data formatting | bytes 1048576 | tf_op jit(solution)/shard_map/convert_element_type | solution.py:52
  (6 shorter events, 0.1 us)
Async XLA Ops:
  4.7 19.8 %all-to-all-start = ((bf16[1,64,32,128]{3,1,0,2:T(8,128)(2,1)}), bf16[1,64,32,128]{3,1,0,2:T(8,128)(2,1)S(1)}, u32[]{:S(2)}, u32[]{:S(2)}) async-start(bf16[1,64,32,128]{3,1,0,2:T(8,128)(2,1)} %fusion.19), calls=%async_computation | async-start | bytes 1048576 | tf_op jit(solution)/shard_map/all_to_all | solution.py:36
  15.0 24.9 %copy-start.2 = (bf16[5,8,8,8]{3,2,1,0:T(8,128)(2,1)S(1)}, bf16[5,8,8,8]{3,2,1,0:T(8,128)(2,1)}, u32[]{:S(2)}) copy-start(bf16[5,8,8,8]{3,2,1,0:T(8,128)(2,1)} %param.10) | copy-start | bytes 15364
  24.5 15.2 %collective-permute-start = (bf16[2,64,4,128]{3,1,2,0:T(8,128)(2,1)S(1)}, bf16[2,64,4,128]{3,1,2,0:T(8,128)(2,1)S(1)}, u32[]{:S(2)}, u32[]{:S(2)}) collective-permute-start(bf16[2,64,4,128]{3,1,2,0:T(8,128)(2,1)S(1)} %fusion.28), channel_id=1, source_target_pairs={{0,8},{8,0},{1,9},{9,1},{2,10},{10,2},{3,11},{11,3},{4,12},{12,4},... | collective-permute-start | bytes 393224 | tf_op jit(solution)/shard_map/ppermute | solution.py:40
  41.0 0.8 copy-start.4
  41.3 6.6 %copy-start.3 = (s32[1,32,128]{2,1,0:T(8,128)S(1)}, s32[1,32,128]{2,1,0:T(8,128)}, u32[]{:S(2)}) copy-start(s32[1,32,128]{2,1,0:T(8,128)} %param.8) | copy-start | bytes 49156
  41.4 6.7 %copy-start.1 = (bf16[5,64,5,64]{3,1,2,0:T(8,128)(2,1)S(1)}, bf16[5,64,5,64]{3,1,2,0:T(8,128)(2,1)}, u32[]{:S(2)}) copy-start(bf16[5,64,5,64]{3,1,2,0:T(8,128)(2,1)} %param.12) | copy-start | bytes 614404
  43.0 14.5 %all-to-all-start.1 = ((bf16[8,64,4,128]{3,1,2,0:T(8,128)(2,1)}), bf16[8,64,4,128]{3,1,2,0:T(8,128)(2,1)S(1)}, u32[]{:S(2)}, u32[]{:S(2)}) async-start(bf16[8,64,4,128]{3,1,2,0:T(8,128)(2,1)} %fusion.14), calls=%async_computation.1 | async-start | bytes 1048576 | tf_op jit(solution)/shard_map/all_to_all | solution.py:46
  79.8 5.4 %copy-start = (bf16[1,64,32,128]{3,2,1,0:T(8,128)(2,1)S(1)}, bf16[1,64,32,128]{3,2,1,0:T(8,128)(2,1)}, u32[]{:S(2)}) copy-start(bf16[1,64,32,128]{3,2,1,0:T(8,128)(2,1)} %param.7) | copy-start | bytes 1572868
  79.8 5.4 %copy-start.5 = (f32[64]{0:T(128)S(1)}, f32[64]{0:T(128)}, u32[]{:S(2)}) copy-start(f32[64]{0:T(128)} %param.13) | copy-start | bytes 772

commit v13 on v5

--- a/solution.py
+++ b/solution.py
@@ -30,6 +30,70 @@
     return jax.nn.gelu(summed).astype(jnp.bfloat16)
 
 
+def relay_kernel(ring, ys, quarter, send_ref, out_ref, relay, send_sems, recv_sems):
+    lon, half, place = (lax.axis_index("lon"), lax.axis_index("lat_hi"), lax.axis_index("lat_lo"))
+    spread = ring // 2
+    z = half * spread + lon // ys
+    y = lon % ys
+
+    def device(step):
+        other = (z + step + ring) % ring
+        return ((other % spread) * ys + y, other // spread, place)
+
+    ahead, behind = device(quarter), device(-quarter)
+    mesh_ids = pl.DeviceIdType.MESH
+    barrier = pltpu.get_barrier_semaphore()
+    for neighbour in (ahead, behind):
+        pl.semaphore_signal(barrier, inc=1, device_id=neighbour, device_id_type=mesh_ids)
+    pl.semaphore_wait(barrier, 2)
+
+    def copy(src, dst, index, target):
+        return pltpu.make_async_remote_copy(
+            src_ref=src,
+            dst_ref=dst,
+            send_sem=send_sems.at[index],
+            recv_sem=recv_sems.at[index],
+            device_id=target,
+            device_id_type=mesh_ids,
+        )
+
+    first = copy(send_ref.at[0], relay.at[0], 0, ahead)
+    second = copy(send_ref.at[1], relay.at[1], 1, behind)
+    first.start()
+    second.start()
+    first.wait_recv()
+    onward = copy(relay.at[0], out_ref.at[0], 2, ahead)
+    onward.start()
+    second.wait_recv()
+    backward = copy(relay.at[1], out_ref.at[1], 3, behind)
+    backward.start()
+    onward.wait_recv()
+    backward.wait_recv()
+    first.wait_send()
+    second.wait_send()
+    onward.wait_send()
+    backward.wait_send()
+
+
+def across(send):
+    ys = 4
+    spread = lax.axis_size("lon") // ys
+    ring = spread * lax.axis_size("lat_hi")
+    any_spec = pl.BlockSpec(memory_space=pl.ANY)
+    return pl.pallas_call(
+        functools.partial(relay_kernel, ring, ys, ring // 4),
+        out_shape=jax.ShapeDtypeStruct(send.shape, send.dtype),
+        in_specs=[any_spec],
+        out_specs=any_spec,
+        scratch_shapes=[
+            pltpu.VMEM(send.shape, send.dtype),
+            pltpu.SemaphoreType.DMA((4,)),
+            pltpu.SemaphoreType.DMA((4,)),
+        ],
+        compiler_params=pltpu.CompilerParams(collective_id=1, has_side_effects=True),
+    )(send)
+
+
 def local(fields, ocean_mask, norm_gain, w_vert, b_vert, w_horiz, b_horiz):
     normed = normalize(fields, norm_gain)
     reach = w_vert.shape[0] // 2
@@ -37,7 +101,7 @@
     count_lev = columns.shape[0]
     upper = lax.axis_index("lat_hi") == 0
     send = jnp.where(upper, columns[count_lev - reach :], columns[:reach])
-    recv = lax.ppermute(send, "lat_hi", [(0, 1), (1, 0)])
+    recv = across(send)
     zeros = jnp.zeros_like(recv)
     below = jnp.where(upper, zeros, recv)
     above = jnp.where(upper, recv, zeros)

time: 88.8 us -> 99.2 us (1.12)
  Pallas kernels: 17.7 us -> 38.8 us
  starting transfers between devices: 26.3 us -> 17.5 us
  waiting for transfers between devices: 21.8 us -> 17.5 us
  other arithmetic: 8.28 us -> 11.2 us
    pallas_call x0 -> x1, Pallas kernels: none -> 21.1 us  [across(): pl.pallas_call(functools.partial(relay_kernel, ring, ys, ring // 4), out_...]
    ppermute x1 -> x0, starting transfers between devices: 10.9 us -> none  [local(): recv = lax.ppermute(send, 'lat_hi', [(0, 1), (1, 0)])]
    ppermute x1 -> x0, waiting for transfers between devices: 4.28 us -> none  [local(): recv = lax.ppermute(send, 'lat_hi', [(0, 1), (1, 0)])]
    all_to_all x1, starting transfers between devices: 5.12 us -> 7.19 us  [local(): lax.all_to_all(vertical(taps, w_vert, b_vert), 'lat_lo', split_axis=0, co...]
    concatenate x0 -> x1, other arithmetic: none -> 1.41 us  [local(): padded = jnp.concatenate([below, columns, above], axis=0)]
  transfers between devices with their start and end apart: 3 -> 2, of which waited for: 3 -> 2; matrix products, arithmetic and copies ran while one was open for 2% -> 2% of each run, Pallas kernels for 0% -> 0%
where the time goes in v13:
time: 99.2 us; the launch traced here: 98.6 us
  Pallas kernels  38.8 us (39%)
  starting transfers between devices  17.5 us (18%)
  waiting for transfers between devices  17.5 us (18%)
  local copies, waits for them, and re-layouts  11.6 us (12%)
  other arithmetic  11.2 us (11%)
  matrix products  1.74 us (2%)
    pallas_call x1, Pallas kernels, across(): pl.pallas_call(functools.partial(relay_kernel, ring, ys, ring // 4), out_...  21.1 us
    pallas_call x1, Pallas kernels, lon_halo(): pl.pallas_call(functools.partial(halo_kernel, count), out_shape=(jax.Shap...  12.4 us
    all_to_all x1, starting transfers between devices, local(): lax.all_to_all(normed, 'lat_lo', split_axis=2, concat_axis=0, tiled=True)  10.3 us
    all_to_all x1, waiting for transfers between devices, local(): lax.all_to_all(normed, 'lat_lo', split_axis=2, concat_axis=0, tiled=True)  9.5 us
    all_to_all x1, waiting for transfers between devices, local(): lax.all_to_all(vertical(taps, w_vert, b_vert), 'lat_lo', split_axis=0, co...  8.01 us
    all_to_all x1, starting transfers between devices, local(): lax.all_to_all(vertical(taps, w_vert, b_vert), 'lat_lo', split_axis=0, co...  7.19 us
    pallas_call x1, Pallas kernels, horizontal(): pl.pallas_call(horizontal_kernel, out_shape=jax.ShapeDtypeStruct((rows_la...  5.34 us
  transfers between devices with their start and end apart: 2, of which 2 were waited for; matrix products, arithmetic and copies ran while one was open for 2% of the time, Pallas kernels for 0%

profile of v13, /device:TPU:1, one launch (start us, length us, event | category | flops | bytes accessed | tf_op | source)
XLA Modules:
  0.0 98.6 jit_solution(14532296899512100571)
XLA Ops:
  0.0 0.0 copy-start
  0.0 1.3 %convert_reduce_fusion = f32[32,128]{1,0:T(8,128)S(1)} fusion(bf16[1,64,32,128]{3,2,1,0:T(8,128)(2,1)} %param.7), kind=kLoop, calls=%fused_computation.3 | loop fusion | flops 520192 | bytes 540672 | tf_op jit(solution)/shard_map/reduce_sum | solution.py:13
  1.3 1.3 %fusion.3 = f32[32,128]{1,0:T(8,128)S(1)} fusion(f32[32,128]{1,0:T(8,128)S(1)} %broadcast_multiply_fusion, bf16[1,64,32,128]{3,2,1,0:T(8,128)(2,1)} %param.7), kind=kLoop, calls=%fused_computation.11 | loop fusion | flops 1044480 | bytes 557056 | tf_op jit(solution)/shard_map/reduce_sum | solution.py:14
  2.6 0.0 copy-done
  2.6 1.7 %fusion.17 = bf16[1,64,32,128]{3,1,0,2:T(8,128)(2,1)} fusion(f32[64]{0:T(128)} %param.9, f32[32,128]{1,0:T(8,128)S(1)} %add_rsqrt_fusion, f32[32,128]{1,0:T(8,128)S(1)} %broadcast_multiply_fusion, bf16[1,64,32,128]{3,2,1,0:T(8,128)(2,1)S(1)} %copy-done), kind=kLoop, calls=%fused_computation.31 | loop fusion | flops 1310720 | bytes 1081600 | tf_op jit(solution)/shard_map/convert_element_type | solution.py:15
  4.4 10.3 %all-to-all-start = ((bf16[1,64,32,128]{3,1,0,2:T(8,128)(2,1)}), bf16[1,64,32,128]{3,1,0,2:T(8,128)(2,1)S(1)}, u32[]{:S(2)}, u32[]{:S(2)}) async-start(bf16[1,64,32,128]{3,1,0,2:T(8,128)(2,1)} %fusion.17), calls=%async_computation | async-start | bytes 1048576 | tf_op jit(solution)/shard_map/all_to_all | solution.py:100
  14.6 9.5 %all-to-all-done = bf16[1,64,32,128]{3,1,0,2:T(8,128)(2,1)S(1)} async-done(((bf16[1,64,32,128]{3,1,0,2:T(8,128)(2,1)}), bf16[1,64,32,128]{3,1,0,2:T(8,128)(2,1)S(1)}, u32[]{:S(2)}, u32[]{:S(2)}) %all-to-all-start) | async-done | bytes 524320 | tf_op jit(solution)/shard_map/all_to_all | solution.py:100
  24.1 0.4 copy.125
  24.6 0.7 fusion.24.send_ref
  25.3 21.1 %shard_map.73 = bf16[2,64,4,128]{3,2,1,0:T(4,128)(2,1)} custom-call(bf16[2,64,4,128]{3,2,1,0:T(4,128)(2,1)} %fusion.24.send_ref), custom_call_target="tpu_custom_call" | custom-call | tf_op jit(solution)/shard_map/pallas_call | solution.py:83
  46.4 1.0 %broadcast_select_fusion = (bf16[2,64,4,128]{3,2,1,0:T(4,128)(2,1)S(1)}, bf16[2,64,4,128]{3,2,1,0:T(4,128)(2,1)S(1)}) fusion(bf16[2,64,4,128]{3,2,1,0:T(4,128)(2,1)} %shard_map.73, pred[]{:T(512)S(6)} %eq.3), kind=kLoop, calls=%fused_computation.43 | loop fusion | flops 131072 | bytes 393217 | tf_op jit(solution)/shard_map/jit(_where)/select_n | solution.py:107
  47.4 0.0 copy-start.2
  47.5 1.4 %pad_maximum_fusion = (bf16[8,64,4,128]{3,2,1,0:T(4,128)(2,1)S(1)}, bf16[8,64,4,128]{3,2,1,0:T(4,128)(2,1)S(1)}, bf16[8,64,4,128]{3,2,1,0:T(4,128)(2,1)S(1)}, bf16[8,64,4,128]{3,2,1,0:T(4,128)(2,1)S(1)}) fusion(bf16[2,64,4,128]{3,2,1,0:T(4,128)(2,1)S(1)} %get-tuple-element.20, bf16[8,64,4,128]{3,2,1,0:T(4,128)(2,1)S(1)} %bitcast.85, ...), kind=kLoop, calls=%fused_computation.32 | loop fusion | flops 1048576 | bytes 2883584 | tf_op jit(solution)/shard_map/concatenate | solution.py:108
  48.9 0.0 copy-done.2
  48.9 0.3 fusion.22
  49.2 0.3 convolution_add_fusion.3
  49.6 0.3 convolution_add_fusion.2
  50.0 0.3 convolution_add_fusion.1
  50.3 0.0 copy-start.4
  50.3 0.3 fusion
  50.7 0.3 copy-done.4
  51.0 0.0 copy-start.1
  51.0 1.2 %fusion.14 = bf16[8,64,4,128]{3,1,2,0:T(8,128)(2,1)} fusion(f32[8,8,8,4,128]{4,2,3,0,1:T(8,128)S(1)} %fusion, f32[64]{0:T(128)S(1)} %copy-done.4), kind=kLoop, calls=%fused_computation.22 | loop fusion | flops 2621440 | bytes 1573120 | tf_op jit(solution)/shard_map/convert_element_type | solution.py:30
  52.2 0.0 copy-start.3
  52.2 7.2 %all-to-all-start.1 = ((bf16[8,64,4,128]{3,1,2,0:T(8,128)(2,1)}), bf16[8,64,4,128]{3,1,2,0:T(8,128)(2,1)S(1)}, u32[]{:S(2)}, u32[]{:S(2)}) async-start(bf16[8,64,4,128]{3,1,2,0:T(8,128)(2,1)} %fusion.14), calls=%async_computation.1 | async-start | bytes 1048576 | tf_op jit(solution)/shard_map/all_to_all | solution.py:110
  59.4 0.0 copy-done.1
  59.4 0.3 copy.93
  59.7 1.1 %reshape.115.w_ref = bf16[320,320]{1,0:T(8,128)(2,1)} reshape(bf16[5,64,5,64]{3,2,1,0:T(8,128)(2,1)S(1)} %copy.93) | data formatting | bytes 409600 | tf_op jit(solution)/shard_map/reshape | solution.py:154
  60.8 0.1 pad.8.clone
  60.9 0.0 copy-done.3
  60.9 8.0 %all-to-all-done.1 = bf16[8,64,4,128]{3,1,2,0:T(8,128)(2,1)S(1)} async-done(((bf16[8,64,4,128]{3,1,2,0:T(8,128)(2,1)}), bf16[8,64,4,128]{3,1,2,0:T(8,128)(2,1)S(1)}, u32[]{:S(2)}, u32[]{:S(2)}) %all-to-all-start.1) | async-done | bytes 524320 | tf_op jit(solution)/shard_map/all_to_all | solution.py:110
  68.9 0.3 copy_multiply_fusion
  69.2 0.2 fusion.35
  69.4 0.6 copy.85
  70.0 0.7 copy.87.left_edge
  70.7 0.6 copy.86
  71.4 0.7 copy.88.right_edge
  72.1 12.4 %shard_map.74 = (bf16[64,64]{1,0:T(8,128)(2,1)}, bf16[64,64]{1,0:T(8,128)(2,1)}) custom-call(bf16[64,64]{1,0:T(8,128)(2,1)} %copy.87.left_edge, bf16[64,64]{1,0:T(8,128)(2,1)} %copy.88.right_edge), custom_call_target="tpu_custom_call" | custom-call | tf_op jit(solution)/shard_map/pallas_call | solution.py:208
  84.4 0.8 copy.89
  85.2 0.9 copy.91
  86.2 0.8 copy.90
  87.0 0.9 copy.92
  87.9 0.7 maximum_bitcast_fusion
  88.6 0.7 pad.4
  89.3 1.3 %copy.105 = bf16[8,8,36,256]{3,1,2,0:T(8,128)(2,1)} copy(bf16[8,8,36,256]{3,2,1,0:T(8,128)(2,1)S(1)} %bitcast.87) | data formatting | bytes 2359296
  90.6 0.0 copy-start.5
  90.6 5.3 %shard_map.75 = f32[32,64,128]{2,1,0:T(8,128)} custom-call(bf16[64,9216]{1,0:T(8,128)(2,1)} %bitcast.94, bf16[320,320]{1,0:T(8,128)(2,1)} %reshape.115.w_ref), custom_call_target="tpu_custom_call" | custom-call | flops 1677721600 | bytes 2433024 | tf_op jit(solution)/shard_map/pallas_call | solution.py:155
  95.9 0.0 copy-done.5
  96.0 1.5 %fusion.6 = bf16[1,64,32,128]{3,1,2,0:T(8,128)(2,1)S(1)} fusion(f32[32,64,128]{2,1,0:T(8,128)} %shard_map.75, f32[64]{0:T(128)S(1)} %copy-done.5, f32[32,128]{1,0:T(8,128)S(1)} %get-tuple-element.22, bf16[1,64,32,128]{3,2,1,0:T(8,128)(2,1)S(1)} %copy-done), kind=kLoop, calls=%fused_computation.14 | loop fusion | flops 1310720 | bytes 2113792 | tf_op jit(solution)/shard_map/convert_element_type | solution.py:116
  97.5 1.1 %copy.94 = bf16[1,64,32,128]{3,2,1,0:T(8,128)(2,1)} copy(bf16[1,64,32,128]{3,1,2,0:T(8,128)(2,1)S(1)} %fusion.6) | data formatting | bytes 1048576 | tf_op jit(solution)/shard_map/convert_element_type | solution.py:116
  (4 shorter events, 0.0 us)
Async XLA Ops:
  0.0 2.6 %copy-start = (bf16[1,64,32,128]{3,2,1,0:T(8,128)(2,1)S(1)}, bf16[1,64,32,128]{3,2,1,0:T(8,128)(2,1)}, u32[]{:S(2)}) copy-start(bf16[1,64,32,128]{3,2,1,0:T(8,128)(2,1)} %param.7) | copy-start | bytes 1572868
  4.4 19.8 %all-to-all-start = ((bf16[1,64,32,128]{3,1,0,2:T(8,128)(2,1)}), bf16[1,64,32,128]{3,1,0,2:T(8,128)(2,1)S(1)}, u32[]{:S(2)}, u32[]{:S(2)}) async-start(bf16[1,64,32,128]{3,1,0,2:T(8,128)(2,1)} %fusion.17), calls=%async_computation | async-start | bytes 1048576 | tf_op jit(solution)/shard_map/all_to_all | solution.py:100
  47.4 1.4 %copy-start.2 = (bf16[5,8,8,8]{3,2,1,0:T(8,128)(2,1)S(1)}, bf16[5,8,8,8]{3,2,1,0:T(8,128)(2,1)}, u32[]{:S(2)}) copy-start(bf16[5,8,8,8]{3,2,1,0:T(8,128)(2,1)} %param.10) | copy-start | bytes 15364
  50.3 0.7 copy-start.4
  51.0 8.4 %copy-start.1 = (bf16[5,64,5,64]{3,1,2,0:T(8,128)(2,1)S(1)}, bf16[5,64,5,64]{3,1,2,0:T(8,128)(2,1)}, u32[]{:S(2)}) copy-start(bf16[5,64,5,64]{3,1,2,0:T(8,128)(2,1)} %param.12) | copy-start | bytes 614404
  52.2 8.7 %copy-start.3 = (s32[1,32,128]{2,1,0:T(8,128)S(1)}, s32[1,32,128]{2,1,0:T(8,128)}, u32[]{:S(2)}) copy-start(s32[1,32,128]{2,1,0:T(8,128)} %param.8) | copy-start | bytes 49156
  52.2 16.7 %all-to-all-start.1 = ((bf16[8,64,4,128]{3,1,2,0:T(8,128)(2,1)}), bf16[8,64,4,128]{3,1,2,0:T(8,128)(2,1)S(1)}, u32[]{:S(2)}, u32[]{:S(2)}) async-start(bf16[8,64,4,128]{3,1,2,0:T(8,128)(2,1)} %fusion.14), calls=%async_computation.1 | async-start | bytes 1048576 | tf_op jit(solution)/shard_map/all_to_all | solution.py:110
  90.6 5.3 %copy-start.5 = (f32[64]{0:T(128)S(1)}, f32[64]{0:T(128)}, u32[]{:S(2)}) copy-start(f32[64]{0:T(128)} %param.13) | copy-start | bytes 772

commit v14 on v5

--- a/solution.py
+++ b/solution.py
@@ -55,7 +55,7 @@
 
 
 def horizontal_kernel(x_ref, w_ref, o_ref):
-    rows, channels, cols_lon = o_ref.shape
+    channels, rows, cols_lon = o_ref.shape
     taps = w_ref.shape[0] // channels
     segment = x_ref.shape[1] // (rows + taps - 1)
     chunk = 8
@@ -74,7 +74,7 @@
             piece = partial[col_tap * channels : (col_tap + 1) * channels]
             total = total + pltpu.roll(piece, chunk * segment - col_tap, 1)
         for row in range(chunk):
-            o_ref[start + row] = total[:, row * segment : row * segment + cols_lon]
+            o_ref[:, start + row, :] = total[:, row * segment : row * segment + cols_lon]
 
 
 def horizontal(masked, w_horiz):
@@ -90,7 +90,7 @@
     weights = jnp.transpose(w_horiz, (2, 1, 0, 3)).reshape(col_taps * channels, row_taps * channels)
     conv = pl.pallas_call(
         horizontal_kernel,
-        out_shape=jax.ShapeDtypeStruct((rows_lat, channels, cols_lon), jnp.float32),
+        out_shape=jax.ShapeDtypeStruct((channels, rows_lat, cols_lon), jnp.float32),
         in_specs=[pl.BlockSpec(memory_space=pltpu.VMEM)] * 2,
         out_specs=pl.BlockSpec(memory_space=pltpu.VMEM),
         cost_estimate=pl.CostEstimate(
@@ -99,7 +99,7 @@
             transcendentals=0,
         ),
     )(wide, weights)
-    return jnp.transpose(conv, (1, 0, 2))[None]
+    return conv[None]
 
 
 def halo_kernel(count, left_edge, right_edge, from_left, from_right, send_sems, recv_sems):

time: 88.8 us -> 88.8 us (level)
    convert_element_type x1, other arithmetic: 1.75 us -> 0.86 us  [normalize(): ((values - center) * lax.rsqrt(spread + 1e-05) * norm_gain[None, :, None,...]
where the time goes in v14:
time: 88.8 us; the launch traced here: 88 us
  starting transfers between devices  26.3 us (30%)
  waiting for transfers between devices  21.8 us (25%)
  Pallas kernels  18.1 us (20%)
  local copies, waits for them, and re-layouts  11.8 us (13%)
  other arithmetic  7.98 us (9%)
  matrix products  1.75 us (2%)
    pallas_call x1, Pallas kernels, lon_halo(): pl.pallas_call(functools.partial(halo_kernel, count), out_shape=(jax.Shap...  12.4 us
    ppermute x1, starting transfers between devices, local(): recv = lax.ppermute(send, 'lat_hi', [(0, 1), (1, 0)])  10.9 us
    all_to_all x1, starting transfers between devices, local(): lax.all_to_all(normed, 'lat_lo', split_axis=2, concat_axis=0, tiled=True)  10.3 us
    all_to_all x1, waiting for transfers between devices, local(): lax.all_to_all(normed, 'lat_lo', split_axis=2, concat_axis=0, tiled=True)  9.5 us
    all_to_all x1, waiting for transfers between devices, local(): lax.all_to_all(vertical(taps, w_vert, b_vert), 'lat_lo', split_axis=0, co...  8.01 us
    pallas_call x1, Pallas kernels, horizontal(): pl.pallas_call(horizontal_kernel, out_shape=jax.ShapeDtypeStruct((channel...  5.77 us
    all_to_all x1, starting transfers between devices, local(): lax.all_to_all(vertical(taps, w_vert, b_vert), 'lat_lo', split_axis=0, co...  5.12 us
    ppermute x1, waiting for transfers between devices, local(): recv = lax.ppermute(send, 'lat_hi', [(0, 1), (1, 0)])  4.28 us
  transfers between devices with their start and end apart: 3, of which 3 were waited for; matrix products, arithmetic and copies ran while one was open for 2% of the time, Pallas kernels for 0%

profile of v14, /device:TPU:1, one launch (start us, length us, event | category | flops | bytes accessed | tf_op | source)
XLA Modules:
  0.0 88.0 jit_solution(3459596545829315106)
XLA Ops:
  0.0 0.0 copy-start
  0.0 1.2 %convert_reduce_fusion = f32[32,128]{1,0:T(8,128)S(1)} fusion(bf16[1,64,32,128]{3,2,1,0:T(8,128)(2,1)} %param.7), kind=kLoop, calls=%fused_computation.3 | loop fusion | flops 520192 | bytes 540672 | tf_op jit(solution)/shard_map/reduce_sum | solution.py:13
  1.2 1.2 %fusion.3 = f32[32,128]{1,0:T(8,128)S(1)} fusion(bf16[1,64,32,128]{3,2,1,0:T(8,128)(2,1)} %param.7, f32[32,128]{1,0:T(8,128)S(1)} %broadcast_multiply_fusion), kind=kLoop, calls=%fused_computation.11 | loop fusion | flops 1044480 | bytes 557056 | tf_op jit(solution)/shard_map/reduce_sum | solution.py:14
  2.4 0.0 copy-done
  2.5 0.9 fusion.5
  3.3 1.0 %copy.36 = bf16[1,64,32,128]{3,1,0,2:T(8,128)(2,1)} copy(bf16[1,64,32,128]{3,2,1,0:T(8,128)(2,1)S(1)} %fusion.5) | data formatting | bytes 1048576 | tf_op jit(solution)/shard_map/convert_element_type | solution.py:15
  4.3 10.3 %all-to-all-start = ((bf16[1,64,32,128]{3,1,0,2:T(8,128)(2,1)}), bf16[1,64,32,128]{3,1,0,2:T(8,128)(2,1)S(1)}, u32[]{:S(2)}, u32[]{:S(2)}) async-start(bf16[1,64,32,128]{3,1,0,2:T(8,128)(2,1)} %copy.36), calls=%async_computation | async-start | bytes 1048576 | tf_op jit(solution)/shard_map/all_to_all | solution.py:36
  14.6 9.5 %all-to-all-done = bf16[1,64,32,128]{3,1,0,2:T(8,128)(2,1)S(1)} async-done(((bf16[1,64,32,128]{3,1,0,2:T(8,128)(2,1)}), bf16[1,64,32,128]{3,1,0,2:T(8,128)(2,1)S(1)}, u32[]{:S(2)}, u32[]{:S(2)}) %all-to-all-start) | async-done | bytes 524320 | tf_op jit(solution)/shard_map/all_to_all | solution.py:36
  24.1 10.9 %collective-permute-start = (bf16[2,64,4,128]{3,1,2,0:T(8,128)(2,1)S(1)}, bf16[2,64,4,128]{3,1,2,0:T(8,128)(2,1)S(1)}, u32[]{:S(2)}, u32[]{:S(2)}) collective-permute-start(bf16[2,64,4,128]{3,1,2,0:T(8,128)(2,1)S(1)} %fusion.27), channel_id=1, source_target_pairs={{0,8},{8,0},{1,9},{9,1},{2,10},{10,2},{3,11},{11,3},{4,12},{12,4},... | collective-permute-start | bytes 393224 | tf_op jit(solution)/shard_map/ppermute | solution.py:40
  35.1 4.3 %collective-permute-done = bf16[2,64,4,128]{3,1,2,0:T(8,128)(2,1)S(1)} collective-permute-done((bf16[2,64,4,128]{3,1,2,0:T(8,128)(2,1)S(1)}, bf16[2,64,4,128]{3,1,2,0:T(8,128)(2,1)S(1)}, u32[]{:S(2)}, u32[]{:S(2)}) %collective-permute-start) | collective-permute-done | bytes 131104 | tf_op jit(solution)/shard_map/ppermute | solution.py:40
  39.4 0.0 copy-start.2
  39.4 0.1 fusion.19
  39.5 0.7 copy-done.2
  40.3 0.3 fusion.25
  40.6 0.4 convolution_add_fusion.3
  41.0 0.3 convolution_add_fusion.2
  41.3 0.4 convolution_add_fusion.1
  41.7 0.0 copy-start.4
  41.7 0.4 fusion
  42.1 0.3 copy-done.4
  42.3 0.0 copy-start.1
  42.3 1.2 %fusion.14 = bf16[8,64,4,128]{3,1,2,0:T(8,128)(2,1)} fusion(f32[8,8,8,4,128]{4,2,3,0,1:T(8,128)S(1)} %fusion, f32[64]{0:T(128)S(1)} %copy-done.4), kind=kLoop, calls=%fused_computation.22 | loop fusion | flops 2621440 | bytes 1573120 | tf_op jit(solution)/shard_map/convert_element_type | solution.py:30
  43.6 0.0 copy-start.3
  43.6 5.1 %all-to-all-start.1 = ((bf16[8,64,4,128]{3,1,2,0:T(8,128)(2,1)}), bf16[8,64,4,128]{3,1,2,0:T(8,128)(2,1)S(1)}, u32[]{:S(2)}, u32[]{:S(2)}) async-start(bf16[8,64,4,128]{3,1,2,0:T(8,128)(2,1)} %fusion.14), calls=%async_computation.1 | async-start | bytes 1048576 | tf_op jit(solution)/shard_map/all_to_all | solution.py:46
  48.7 0.0 copy-done.1
  48.7 0.3 copy.57
  49.0 1.1 %reshape.115.w_ref = bf16[320,320]{1,0:T(8,128)(2,1)} reshape(bf16[5,64,5,64]{3,2,1,0:T(8,128)(2,1)S(1)} %copy.57) | data formatting | bytes 409600 | tf_op jit(solution)/shard_map/reshape | solution.py:90
  50.1 0.1 pad.8.clone
  50.2 0.0 copy-done.3
  50.2 8.0 %all-to-all-done.1 = bf16[8,64,4,128]{3,1,2,0:T(8,128)(2,1)S(1)} async-done(((bf16[8,64,4,128]{3,1,2,0:T(8,128)(2,1)}), bf16[8,64,4,128]{3,1,2,0:T(8,128)(2,1)S(1)}, u32[]{:S(2)}, u32[]{:S(2)}) %all-to-all-start.1) | async-done | bytes 524320 | tf_op jit(solution)/shard_map/all_to_all | solution.py:46
  58.2 0.3 copy_multiply_fusion
  58.5 0.2 fusion.38
  58.7 0.6 copy.49
  59.3 0.7 copy.51.left_edge
  60.0 0.6 copy.50
  60.7 0.7 copy.52.right_edge
  61.4 12.4 %shard_map.73 = (bf16[64,64]{1,0:T(8,128)(2,1)}, bf16[64,64]{1,0:T(8,128)(2,1)}) custom-call(bf16[64,64]{1,0:T(8,128)(2,1)} %copy.51.left_edge, bf16[64,64]{1,0:T(8,128)(2,1)} %copy.52.right_edge), custom_call_target="tpu_custom_call" | custom-call | tf_op jit(solution)/shard_map/pallas_call | solution.py:144
  73.7 0.8 copy.53
  74.5 0.9 %copy.55 = bf16[1,64,32,2]{3,2,1,0:T(8,128)(2,1)S(1)} copy(bf16[1,64,32,2]{1,3,2,0:T(2,128)(2,1)S(1)} %bitcast.92) | data formatting | bytes 16384 | tf_op jit(solution)/shard_map/reshape | solution.py:152
  75.5 0.8 copy.54
  76.3 0.9 %copy.56 = bf16[1,64,32,2]{3,2,1,0:T(8,128)(2,1)S(1)} copy(bf16[1,64,32,2]{1,3,2,0:T(2,128)(2,1)S(1)} %bitcast.93) | data formatting | bytes 16384 | tf_op jit(solution)/shard_map/reshape | solution.py:152
  77.2 0.7 maximum_bitcast_fusion
  77.9 0.7 pad.4
  78.7 1.3 %copy.68 = bf16[8,8,36,256]{3,1,2,0:T(8,128)(2,1)} copy(bf16[8,8,36,256]{3,2,1,0:T(8,128)(2,1)S(1)} %bitcast.86) | data formatting | bytes 2359296
  79.9 0.0 copy-start.5
  79.9 5.8 %shard_map.74 = f32[64,32,128]{2,1,0:T(8,128)} custom-call(bf16[64,9216]{1,0:T(8,128)(2,1)} %bitcast.88, bf16[320,320]{1,0:T(8,128)(2,1)} %reshape.115.w_ref), custom_call_target="tpu_custom_call" | custom-call | flops 1677721600 | bytes 2433024 | tf_op jit(solution)/shard_map/pallas_call | solution.py:91
  85.7 0.0 copy-done.5
  85.7 2.3 %fusion.6 = bf16[1,64,32,128]{3,2,1,0:T(8,128)(2,1)} fusion(bf16[1,64,32,128]{3,2,1,0:T(8,128)(2,1)S(1)} %copy-done, f32[64,32,128]{2,1,0:T(8,128)} %shard_map.74, f32[64]{0:T(128)S(1)} %copy-done.5, f32[32,128]{1,0:T(8,128)S(1)} %get-tuple-element.19), kind=kLoop, calls=%fused_computation.14 | loop fusion | flops 1310720 | bytes 2113792 | tf_op jit(solution)/shard_map/convert_element_type | solution.py:52
  (6 shorter events, 0.1 us)
Async XLA Ops:
  0.0 2.4 %copy-start = (bf16[1,64,32,128]{3,2,1,0:T(8,128)(2,1)S(1)}, bf16[1,64,32,128]{3,2,1,0:T(8,128)(2,1)}, u32[]{:S(2)}) copy-start(bf16[1,64,32,128]{3,2,1,0:T(8,128)(2,1)} %param.7) | copy-start | bytes 1572868
  4.3 19.8 %all-to-all-start = ((bf16[1,64,32,128]{3,1,0,2:T(8,128)(2,1)}), bf16[1,64,32,128]{3,1,0,2:T(8,128)(2,1)S(1)}, u32[]{:S(2)}, u32[]{:S(2)}) async-start(bf16[1,64,32,128]{3,1,0,2:T(8,128)(2,1)} %copy.36), calls=%async_computation | async-start | bytes 1048576 | tf_op jit(solution)/shard_map/all_to_all | solution.py:36
  24.1 15.2 %collective-permute-start = (bf16[2,64,4,128]{3,1,2,0:T(8,128)(2,1)S(1)}, bf16[2,64,4,128]{3,1,2,0:T(8,128)(2,1)S(1)}, u32[]{:S(2)}, u32[]{:S(2)}) collective-permute-start(bf16[2,64,4,128]{3,1,2,0:T(8,128)(2,1)S(1)} %fusion.27), channel_id=1, source_target_pairs={{0,8},{8,0},{1,9},{9,1},{2,10},{10,2},{3,11},{11,3},{4,12},{12,4},... | collective-permute-start | bytes 393224 | tf_op jit(solution)/shard_map/ppermute | solution.py:40
  39.4 0.9 %copy-start.2 = (bf16[5,8,8,8]{3,2,1,0:T(8,128)(2,1)S(1)}, bf16[5,8,8,8]{3,2,1,0:T(8,128)(2,1)}, u32[]{:S(2)}) copy-start(bf16[5,8,8,8]{3,2,1,0:T(8,128)(2,1)} %param.10) | copy-start | bytes 15364
  41.7 0.7 copy-start.4
  42.3 6.4 %copy-start.1 = (bf16[5,64,5,64]{3,1,2,0:T(8,128)(2,1)S(1)}, bf16[5,64,5,64]{3,1,2,0:T(8,128)(2,1)}, u32[]{:S(2)}) copy-start(bf16[5,64,5,64]{3,1,2,0:T(8,128)(2,1)} %param.12) | copy-start | bytes 614404
  43.6 6.6 %copy-start.3 = (s32[1,32,128]{2,1,0:T(8,128)S(1)}, s32[1,32,128]{2,1,0:T(8,128)}, u32[]{:S(2)}) copy-start(s32[1,32,128]{2,1,0:T(8,128)} %param.8) | copy-start | bytes 49156
  43.6 14.6 %all-to-all-start.1 = ((bf16[8,64,4,128]{3,1,2,0:T(8,128)(2,1)}), bf16[8,64,4,128]{3,1,2,0:T(8,128)(2,1)S(1)}, u32[]{:S(2)}, u32[]{:S(2)}) async-start(bf16[8,64,4,128]{3,1,2,0:T(8,128)(2,1)} %fusion.14), calls=%async_computation.1 | async-start | bytes 1048576 | tf_op jit(solution)/shard_map/all_to_all | solution.py:46
  79.9 5.8 %copy-start.5 = (f32[64]{0:T(128)S(1)}, f32[64]{0:T(128)}, u32[]{:S(2)}) copy-start(f32[64]{0:T(128)} %param.13) | copy-start | bytes 772

commit v15 on v8

--- a/solution.py
+++ b/solution.py
@@ -9,23 +9,26 @@
 
 
 def normalize_kernel(x_ref, g_ref, o_ref):
-    values = x_ref[...].astype(jnp.float32)
-    channels = values.shape[1]
-    center = jnp.sum(values, axis=1, keepdims=True) / channels
-    spread = jnp.sum((values - center) ** 2, axis=1, keepdims=True) / channels
-    scale = lax.rsqrt(spread + 1e-05)
-    o_ref[...] = ((values - center) * scale * g_ref[...]).astype(o_ref.dtype)
+    rows, channels, _ = o_ref.shape
+    gain = g_ref[...]
+    for row in range(rows):
+        values = x_ref[0, :, row, :].astype(jnp.float32)
+        center = jnp.sum(values, axis=0, keepdims=True) / channels
+        offset = values - center
+        spread = jnp.sum(offset * offset, axis=0, keepdims=True) / channels
+        o_ref[row] = (offset * lax.rsqrt(spread + 1e-05) * gain).astype(o_ref.dtype)
 
 
 def normalize(block, norm_gain):
+    _, channels, rows_lat, cols_lon = block.shape
     vmem = pl.BlockSpec(memory_space=pltpu.VMEM)
-    gain = jnp.broadcast_to(norm_gain[None, :, None, None], (1, norm_gain.shape[0], 1, block.shape[3]))
-    return pl.pallas_call(
+    normed = pl.pallas_call(
         normalize_kernel,
-        out_shape=jax.ShapeDtypeStruct(block.shape, jnp.bfloat16),
+        out_shape=jax.ShapeDtypeStruct((rows_lat, channels, cols_lon), jnp.bfloat16),
         in_specs=[vmem, vmem],
         out_specs=vmem,
-    )(block, gain)
+    )(block, norm_gain[:, None])
+    return jnp.transpose(normed, (1, 0, 2))[None]
 
 
 def vertical(taps, w_vert, b_vert):

time: 90.1 us -> 88.8 us (0.986)
  local copies, waits for them, and re-layouts: 15.4 us -> 13.3 us
    pallas_call x1 -> x0, local copies, waits for them, and re-layouts: 2.03 us -> none  [normalize(): pl.pallas_call(normalize_kernel, out_shape=jax.ShapeDtypeStruct(block.sha...]
where the time goes in v15:
time: 88.8 us; the launch traced here: 88 us
  starting transfers between devices  26.3 us (30%)
  waiting for transfers between devices  21.8 us (25%)
  Pallas kernels  20.7 us (23%)
  local copies, waits for them, and re-layouts  13.3 us (15%)
  other arithmetic  3.95 us (4%)
  matrix products  1.75 us (2%)
    pallas_call x1, Pallas kernels, lon_halo(): pl.pallas_call(functools.partial(halo_kernel, count), out_shape=(jax.Shap...  12.4 us
    ppermute x1, starting transfers between devices, local(): recv = lax.ppermute(send, 'lat_hi', [(0, 1), (1, 0)])  10.9 us
    all_to_all x1, starting transfers between devices, local(): lax.all_to_all(normed, 'lat_lo', split_axis=2, concat_axis=0, tiled=True)  10.3 us
    all_to_all x1, waiting for transfers between devices, local(): lax.all_to_all(normed, 'lat_lo', split_axis=2, concat_axis=0, tiled=True)  9.5 us
    all_to_all x1, waiting for transfers between devices, local(): lax.all_to_all(vertical(taps, w_vert, b_vert), 'lat_lo', split_axis=0, co...  8.01 us
    pallas_call x1, Pallas kernels, horizontal(): pl.pallas_call(horizontal_kernel, out_shape=jax.ShapeDtypeStruct((rows_la...  5.34 us
    all_to_all x1, starting transfers between devices, local(): lax.all_to_all(vertical(taps, w_vert, b_vert), 'lat_lo', split_axis=0, co...  5.12 us
    ppermute x1, waiting for transfers between devices, local(): recv = lax.ppermute(send, 'lat_hi', [(0, 1), (1, 0)])  4.28 us
  transfers between devices with their start and end apart: 3, of which 3 were waited for; matrix products, arithmetic and copies ran while one was open for 2% of the time, Pallas kernels for 0%

profile of v15, /device:TPU:1, one launch (start us, length us, event | category | flops | bytes accessed | tf_op | source)
XLA Modules:
  0.0 88.0 jit_solution(16135235058416345386)
XLA Ops:
  0.0 1.3 %copy.42.g_ref = f32[64,1]{1,0:T(8,128)} copy(f32[64,1]{0,1:T(1,128)} %bitcast.105) | data formatting | bytes 512 | tf_op jit(solution)/shard_map/broadcast_in_dim | solution.py:30
  1.3 3.0 %shard_map.73 = bf16[32,64,128]{2,1,0:T(8,128)(2,1)} custom-call(bf16[1,64,32,128]{3,2,1,0:T(8,128)(2,1)} %x_ref.1, f32[64,1]{1,0:T(8,128)} %copy.42.g_ref), custom_call_target="tpu_custom_call" | custom-call | tf_op jit(solution)/shard_map/pallas_call | solution.py:25
  4.4 10.3 %all-to-all-start = ((bf16[1,64,32,128]{3,1,0,2:T(8,128)(2,1)}), bf16[1,64,32,128]{3,1,0,2:T(8,128)(2,1)S(1)}, u32[]{:S(2)}, u32[]{:S(2)}) async-start(bf16[1,64,32,128]{3,1,0,2:T(8,128)(2,1)} %bitcast.98), calls=%async_computation | async-start | bytes 1048576 | tf_op jit(solution)/shard_map/all_to_all | solution.py:50
  14.6 9.5 %all-to-all-done = bf16[1,64,32,128]{3,1,0,2:T(8,128)(2,1)S(1)} async-done(((bf16[1,64,32,128]{3,1,0,2:T(8,128)(2,1)}), bf16[1,64,32,128]{3,1,0,2:T(8,128)(2,1)S(1)}, u32[]{:S(2)}, u32[]{:S(2)}) %all-to-all-start) | async-done | bytes 524320 | tf_op jit(solution)/shard_map/all_to_all | solution.py:50
  24.2 10.9 %collective-permute-start = (bf16[2,64,4,128]{3,1,2,0:T(8,128)(2,1)S(1)}, bf16[2,64,4,128]{3,1,2,0:T(8,128)(2,1)S(1)}, u32[]{:S(2)}, u32[]{:S(2)}) collective-permute-start(bf16[2,64,4,128]{3,1,2,0:T(8,128)(2,1)S(1)} %fusion.22), channel_id=1, source_target_pairs={{0,8},{8,0},{1,9},{9,1},{2,10},{10,2},{3,11},{11,3},{4,12},{12,4},... | collective-permute-start | bytes 393224 | tf_op jit(solution)/shard_map/ppermute | solution.py:54
  35.1 4.3 %collective-permute-done = bf16[2,64,4,128]{3,1,2,0:T(8,128)(2,1)S(1)} collective-permute-done((bf16[2,64,4,128]{3,1,2,0:T(8,128)(2,1)S(1)}, bf16[2,64,4,128]{3,1,2,0:T(8,128)(2,1)S(1)}, u32[]{:S(2)}, u32[]{:S(2)}) %collective-permute-start) | collective-permute-done | bytes 131104 | tf_op jit(solution)/shard_map/ppermute | solution.py:54
  39.4 0.0 copy-start.2
  39.4 0.1 fusion.14
  39.6 0.7 copy-done.2
  40.3 0.3 fusion.20
  40.7 0.3 convolution_add_fusion.3
  41.0 0.3 convolution_add_fusion.2
  41.4 0.4 convolution_add_fusion.1
  41.7 0.0 copy-start.4
  41.8 0.4 fusion
  42.1 0.3 copy-done.4
  42.4 0.0 copy-start.1
  42.4 1.2 %fusion.8 = bf16[8,64,4,128]{3,1,2,0:T(8,128)(2,1)} fusion(f32[8,8,8,4,128]{4,2,3,0,1:T(8,128)S(1)} %fusion, f32[64]{0:T(128)S(1)} %copy-done.4), kind=kLoop, calls=%fused_computation.13 | loop fusion | flops 2621440 | bytes 1573120 | tf_op jit(solution)/shard_map/convert_element_type | solution.py:44
  43.6 0.0 copy-start.3
  43.6 5.1 %all-to-all-start.1 = ((bf16[8,64,4,128]{3,1,2,0:T(8,128)(2,1)}), bf16[8,64,4,128]{3,1,2,0:T(8,128)(2,1)S(1)}, u32[]{:S(2)}, u32[]{:S(2)}) async-start(bf16[8,64,4,128]{3,1,2,0:T(8,128)(2,1)} %fusion.8), calls=%async_computation.1 | async-start | bytes 1048576 | tf_op jit(solution)/shard_map/all_to_all | solution.py:60
  48.8 0.0 copy-done.1
  48.8 0.3 copy.64
  49.1 1.1 %reshape.90.w_ref = bf16[320,320]{1,0:T(8,128)(2,1)} reshape(bf16[5,64,5,64]{3,2,1,0:T(8,128)(2,1)S(1)} %copy.64) | data formatting | bytes 409600 | tf_op jit(solution)/shard_map/reshape | solution.py:104
  50.2 0.1 pad.8.clone
  50.2 0.0 copy-done.3
  50.3 8.0 %all-to-all-done.1 = bf16[8,64,4,128]{3,1,2,0:T(8,128)(2,1)S(1)} async-done(((bf16[8,64,4,128]{3,1,2,0:T(8,128)(2,1)}), bf16[8,64,4,128]{3,1,2,0:T(8,128)(2,1)S(1)}, u32[]{:S(2)}, u32[]{:S(2)}) %all-to-all-start.1) | async-done | bytes 524320 | tf_op jit(solution)/shard_map/all_to_all | solution.py:60
  58.3 0.3 copy_multiply_fusion
  58.6 0.2 fusion.33
  58.8 0.6 copy.56
  59.4 0.7 copy.58.left_edge
  60.1 0.6 copy.57
  60.7 0.7 copy.59.right_edge
  61.4 12.4 %shard_map.74 = (bf16[64,64]{1,0:T(8,128)(2,1)}, bf16[64,64]{1,0:T(8,128)(2,1)}) custom-call(bf16[64,64]{1,0:T(8,128)(2,1)} %copy.58.left_edge, bf16[64,64]{1,0:T(8,128)(2,1)} %copy.59.right_edge), custom_call_target="tpu_custom_call" | custom-call | tf_op jit(solution)/shard_map/pallas_call | solution.py:158
  73.8 0.8 copy.60
  74.6 0.9 %copy.62 = bf16[1,64,32,2]{3,2,1,0:T(8,128)(2,1)S(1)} copy(bf16[1,64,32,2]{1,3,2,0:T(2,128)(2,1)S(1)} %bitcast.103) | data formatting | bytes 16384 | tf_op jit(solution)/shard_map/reshape | solution.py:166
  75.5 0.8 copy.61
  76.3 0.9 %copy.63 = bf16[1,64,32,2]{3,2,1,0:T(8,128)(2,1)S(1)} copy(bf16[1,64,32,2]{1,3,2,0:T(2,128)(2,1)S(1)} %bitcast.104) | data formatting | bytes 16384 | tf_op jit(solution)/shard_map/reshape | solution.py:166
  77.3 0.7 maximum_bitcast_fusion
  78.0 0.7 pad.4
  78.7 1.3 %copy.76 = bf16[8,8,36,256]{3,1,2,0:T(8,128)(2,1)} copy(bf16[8,8,36,256]{3,2,1,0:T(8,128)(2,1)S(1)} %bitcast.96) | data formatting | bytes 2359296
  80.0 0.0 copy-start
  80.0 0.0 copy-start.5
  80.0 5.3 %shard_map.75 = f32[32,64,128]{2,1,0:T(8,128)} custom-call(bf16[64,9216]{1,0:T(8,128)(2,1)} %bitcast.99, bf16[320,320]{1,0:T(8,128)(2,1)} %reshape.90.w_ref), custom_call_target="tpu_custom_call" | custom-call | flops 1677721600 | bytes 2433024 | tf_op jit(solution)/shard_map/pallas_call | solution.py:105
  85.3 0.0 copy-done
  85.3 0.0 copy-done.5
  85.3 1.5 %fusion.9 = bf16[1,64,32,128]{3,1,2,0:T(8,128)(2,1)S(1)} fusion(f32[32,64,128]{2,1,0:T(8,128)} %shard_map.75, bf16[1,64,32,128]{3,2,1,0:T(8,128)(2,1)S(1)} %copy-done, f32[64]{0:T(128)S(1)} %copy-done.5, f32[32,128]{1,0:T(8,128)S(1)} %get-tuple-element.19), kind=kLoop, calls=%fused_computation.16 | loop fusion | flops 1310720 | bytes 2113792 | tf_op jit(solution)/shard_map/convert_element_type | solution.py:66
  86.9 1.1 %copy.65 = bf16[1,64,32,128]{3,2,1,0:T(8,128)(2,1)} copy(bf16[1,64,32,128]{3,1,2,0:T(8,128)(2,1)S(1)} %fusion.9) | data formatting | bytes 1048576 | tf_op jit(solution)/shard_map/convert_element_type | solution.py:66
  (4 shorter events, 0.0 us)
Async XLA Ops:
  4.4 19.8 %all-to-all-start = ((bf16[1,64,32,128]{3,1,0,2:T(8,128)(2,1)}), bf16[1,64,32,128]{3,1,0,2:T(8,128)(2,1)S(1)}, u32[]{:S(2)}, u32[]{:S(2)}) async-start(bf16[1,64,32,128]{3,1,0,2:T(8,128)(2,1)} %bitcast.98), calls=%async_computation | async-start | bytes 1048576 | tf_op jit(solution)/shard_map/all_to_all | solution.py:50
  24.2 15.2 %collective-permute-start = (bf16[2,64,4,128]{3,1,2,0:T(8,128)(2,1)S(1)}, bf16[2,64,4,128]{3,1,2,0:T(8,128)(2,1)S(1)}, u32[]{:S(2)}, u32[]{:S(2)}) collective-permute-start(bf16[2,64,4,128]{3,1,2,0:T(8,128)(2,1)S(1)} %fusion.22), channel_id=1, source_target_pairs={{0,8},{8,0},{1,9},{9,1},{2,10},{10,2},{3,11},{11,3},{4,12},{12,4},... | collective-permute-start | bytes 393224 | tf_op jit(solution)/shard_map/ppermute | solution.py:54
  39.4 0.9 %copy-start.2 = (bf16[5,8,8,8]{3,2,1,0:T(8,128)(2,1)S(1)}, bf16[5,8,8,8]{3,2,1,0:T(8,128)(2,1)}, u32[]{:S(2)}) copy-start(bf16[5,8,8,8]{3,2,1,0:T(8,128)(2,1)} %param.10) | copy-start | bytes 15364
  41.7 0.7 copy-start.4
  42.4 6.4 %copy-start.1 = (bf16[5,64,5,64]{3,1,2,0:T(8,128)(2,1)S(1)}, bf16[5,64,5,64]{3,1,2,0:T(8,128)(2,1)}, u32[]{:S(2)}) copy-start(bf16[5,64,5,64]{3,1,2,0:T(8,128)(2,1)} %param.12) | copy-start | bytes 614404
  43.6 6.6 %copy-start.3 = (s32[1,32,128]{2,1,0:T(8,128)S(1)}, s32[1,32,128]{2,1,0:T(8,128)}, u32[]{:S(2)}) copy-start(s32[1,32,128]{2,1,0:T(8,128)} %param.8) | copy-start | bytes 49156
  43.6 14.6 %all-to-all-start.1 = ((bf16[8,64,4,128]{3,1,2,0:T(8,128)(2,1)}), bf16[8,64,4,128]{3,1,2,0:T(8,128)(2,1)S(1)}, u32[]{:S(2)}, u32[]{:S(2)}) async-start(bf16[8,64,4,128]{3,1,2,0:T(8,128)(2,1)} %fusion.8), calls=%async_computation.1 | async-start | bytes 1048576 | tf_op jit(solution)/shard_map/all_to_all | solution.py:60
  80.0 5.3 %copy-start = (bf16[1,64,32,128]{3,2,1,0:T(8,128)(2,1)S(1)}, bf16[1,64,32,128]{3,2,1,0:T(8,128)(2,1)}, u32[]{:S(2)}) copy-start(bf16[1,64,32,128]{3,2,1,0:T(8,128)(2,1)} %x_ref.1) | copy-start | bytes 1572868
  80.0 5.3 %copy-start.5 = (f32[64]{0:T(128)S(1)}, f32[64]{0:T(128)}, u32[]{:S(2)}) copy-start(f32[64]{0:T(128)} %param.13) | copy-start | bytes 772

commit v16 on v15

--- a/solution.py
+++ b/solution.py
@@ -9,8 +9,11 @@
 
 
 def normalize_kernel(x_ref, g_ref, o_ref):
-    rows, channels, _ = o_ref.shape
-    gain = g_ref[...]
+    rows, channels, cols_lon = o_ref.shape
+    channel = lax.broadcasted_iota(jnp.int32, (channels, cols_lon), 0)
+    gain = jnp.zeros((channels, cols_lon), jnp.float32)
+    for index in range(channels):
+        gain = jnp.where(channel == index, g_ref[index], gain)
     for row in range(rows):
         values = x_ref[0, :, row, :].astype(jnp.float32)
         center = jnp.sum(values, axis=0, keepdims=True) / channels
@@ -25,9 +28,9 @@
     normed = pl.pallas_call(
         normalize_kernel,
         out_shape=jax.ShapeDtypeStruct((rows_lat, channels, cols_lon), jnp.bfloat16),
-        in_specs=[vmem, vmem],
+        in_specs=[vmem, pl.BlockSpec(memory_space=pltpu.SMEM)],
         out_specs=vmem,
-    )(block, norm_gain[:, None])
+    )(block, norm_gain)
     return jnp.transpose(normed, (1, 0, 2))[None]
 
 

time: 88.8 us -> 87.4 us (0.984)
  local copies, waits for them, and re-layouts: 13.3 us -> 12 us
    broadcast_in_dim x1 -> x0, local copies, waits for them, and re-layouts: 1.34 us -> none  [normalize(): norm_gain[:, None]]
where the time goes in v16:
time: 87.4 us; the launch traced here: 86.7 us
  starting transfers between devices  26.3 us (30%)
  waiting for transfers between devices  21.8 us (25%)
  Pallas kernels  20.8 us (24%)
  local copies, waits for them, and re-layouts  12 us (14%)
  other arithmetic  3.95 us (5%)
  matrix products  1.75 us (2%)
    pallas_call x1, Pallas kernels, lon_halo(): pl.pallas_call(functools.partial(halo_kernel, count), out_shape=(jax.Shap...  12.4 us
    ppermute x1, starting transfers between devices, local(): recv = lax.ppermute(send, 'lat_hi', [(0, 1), (1, 0)])  10.9 us
    all_to_all x1, starting transfers between devices, local(): lax.all_to_all(normed, 'lat_lo', split_axis=2, concat_axis=0, tiled=True)  10.3 us
    all_to_all x1, waiting for transfers between devices, local(): lax.all_to_all(normed, 'lat_lo', split_axis=2, concat_axis=0, tiled=True)  9.5 us
    all_to_all x1, waiting for transfers between devices, local(): lax.all_to_all(vertical(taps, w_vert, b_vert), 'lat_lo', split_axis=0, co...  8.01 us
    pallas_call x1, Pallas kernels, horizontal(): pl.pallas_call(horizontal_kernel, out_shape=jax.ShapeDtypeStruct((rows_la...  5.34 us
    all_to_all x1, starting transfers between devices, local(): lax.all_to_all(vertical(taps, w_vert, b_vert), 'lat_lo', split_axis=0, co...  5.12 us
    ppermute x1, waiting for transfers between devices, local(): recv = lax.ppermute(send, 'lat_hi', [(0, 1), (1, 0)])  4.28 us
  transfers between devices with their start and end apart: 3, of which 3 were waited for; matrix products, arithmetic and copies ran while one was open for 2% of the time, Pallas kernels for 0%

profile of v16, /device:TPU:1, one launch (start us, length us, event | category | flops | bytes accessed | tf_op | source)
XLA Modules:
  0.0 86.7 jit_solution(1310174396883034062)
XLA Ops:
  0.0 3.1 %shard_map.73 = bf16[32,64,128]{2,1,0:T(8,128)(2,1)} custom-call(bf16[1,64,32,128]{3,2,1,0:T(8,128)(2,1)} %x_ref.1, f32[64]{0:T(128)} %g_ref.1), custom_call_target="tpu_custom_call" | custom-call | tf_op jit(solution)/shard_map/pallas_call | solution.py:28
  3.1 10.3 %all-to-all-start = ((bf16[1,64,32,128]{3,1,0,2:T(8,128)(2,1)}), bf16[1,64,32,128]{3,1,0,2:T(8,128)(2,1)S(1)}, u32[]{:S(2)}, u32[]{:S(2)}) async-start(bf16[1,64,32,128]{3,1,0,2:T(8,128)(2,1)} %bitcast.97), calls=%async_computation | async-start | bytes 1048576 | tf_op jit(solution)/shard_map/all_to_all | solution.py:53
  13.3 9.5 %all-to-all-done = bf16[1,64,32,128]{3,1,0,2:T(8,128)(2,1)S(1)} async-done(((bf16[1,64,32,128]{3,1,0,2:T(8,128)(2,1)}), bf16[1,64,32,128]{3,1,0,2:T(8,128)(2,1)S(1)}, u32[]{:S(2)}, u32[]{:S(2)}) %all-to-all-start) | async-done | bytes 524320 | tf_op jit(solution)/shard_map/all_to_all | solution.py:53
  22.9 10.9 %collective-permute-start = (bf16[2,64,4,128]{3,1,2,0:T(8,128)(2,1)S(1)}, bf16[2,64,4,128]{3,1,2,0:T(8,128)(2,1)S(1)}, u32[]{:S(2)}, u32[]{:S(2)}) collective-permute-start(bf16[2,64,4,128]{3,1,2,0:T(8,128)(2,1)S(1)} %fusion.22), channel_id=1, source_target_pairs={{0,8},{8,0},{1,9},{9,1},{2,10},{10,2},{3,11},{11,3},{4,12},{12,4},... | collective-permute-start | bytes 393224 | tf_op jit(solution)/shard_map/ppermute | solution.py:57
  33.8 4.3 %collective-permute-done = bf16[2,64,4,128]{3,1,2,0:T(8,128)(2,1)S(1)} collective-permute-done((bf16[2,64,4,128]{3,1,2,0:T(8,128)(2,1)S(1)}, bf16[2,64,4,128]{3,1,2,0:T(8,128)(2,1)S(1)}, u32[]{:S(2)}, u32[]{:S(2)}) %collective-permute-start) | collective-permute-done | bytes 131104 | tf_op jit(solution)/shard_map/ppermute | solution.py:57
  38.1 0.0 copy-start.2
  38.1 0.1 fusion.14
  38.3 0.7 copy-done.2
  39.0 0.3 fusion.20
  39.4 0.3 convolution_add_fusion.3
  39.7 0.3 convolution_add_fusion.2
  40.1 0.4 convolution_add_fusion.1
  40.4 0.0 copy-start.4
  40.4 0.4 fusion
  40.8 0.3 copy-done.4
  41.1 0.0 copy-start.1
  41.1 1.2 %fusion.8 = bf16[8,64,4,128]{3,1,2,0:T(8,128)(2,1)} fusion(f32[8,8,8,4,128]{4,2,3,0,1:T(8,128)S(1)} %fusion, f32[64]{0:T(128)S(1)} %copy-done.4), kind=kLoop, calls=%fused_computation.13 | loop fusion | flops 2621440 | bytes 1573120 | tf_op jit(solution)/shard_map/convert_element_type | solution.py:47
  42.3 0.0 copy-start.3
  42.3 5.1 %all-to-all-start.1 = ((bf16[8,64,4,128]{3,1,2,0:T(8,128)(2,1)}), bf16[8,64,4,128]{3,1,2,0:T(8,128)(2,1)S(1)}, u32[]{:S(2)}, u32[]{:S(2)}) async-start(bf16[8,64,4,128]{3,1,2,0:T(8,128)(2,1)} %fusion.8), calls=%async_computation.1 | async-start | bytes 1048576 | tf_op jit(solution)/shard_map/all_to_all | solution.py:63
  47.5 0.0 copy-done.1
  47.5 0.3 copy.61
  47.8 1.1 %reshape.90.w_ref = bf16[320,320]{1,0:T(8,128)(2,1)} reshape(bf16[5,64,5,64]{3,2,1,0:T(8,128)(2,1)S(1)} %copy.61) | data formatting | bytes 409600 | tf_op jit(solution)/shard_map/reshape | solution.py:107
  48.9 0.1 pad.8.clone
  48.9 0.0 copy-done.3
  48.9 8.0 %all-to-all-done.1 = bf16[8,64,4,128]{3,1,2,0:T(8,128)(2,1)S(1)} async-done(((bf16[8,64,4,128]{3,1,2,0:T(8,128)(2,1)}), bf16[8,64,4,128]{3,1,2,0:T(8,128)(2,1)S(1)}, u32[]{:S(2)}, u32[]{:S(2)}) %all-to-all-start.1) | async-done | bytes 524320 | tf_op jit(solution)/shard_map/all_to_all | solution.py:63
  57.0 0.3 copy_multiply_fusion
  57.3 0.2 fusion.33
  57.5 0.6 copy.53
  58.1 0.7 copy.55.left_edge
  58.8 0.6 copy.54
  59.4 0.7 copy.56.right_edge
  60.1 12.4 %shard_map.74 = (bf16[64,64]{1,0:T(8,128)(2,1)}, bf16[64,64]{1,0:T(8,128)(2,1)}) custom-call(bf16[64,64]{1,0:T(8,128)(2,1)} %copy.55.left_edge, bf16[64,64]{1,0:T(8,128)(2,1)} %copy.56.right_edge), custom_call_target="tpu_custom_call" | custom-call | tf_op jit(solution)/shard_map/pallas_call | solution.py:161
  72.5 0.8 copy.57
  73.3 0.9 %copy.59 = bf16[1,64,32,2]{3,2,1,0:T(8,128)(2,1)S(1)} copy(bf16[1,64,32,2]{1,3,2,0:T(2,128)(2,1)S(1)} %bitcast.102) | data formatting | bytes 16384 | tf_op jit(solution)/shard_map/reshape | solution.py:169
  74.2 0.8 copy.58
  75.0 0.9 %copy.60 = bf16[1,64,32,2]{3,2,1,0:T(8,128)(2,1)S(1)} copy(bf16[1,64,32,2]{1,3,2,0:T(2,128)(2,1)S(1)} %bitcast.103) | data formatting | bytes 16384 | tf_op jit(solution)/shard_map/reshape | solution.py:169
  76.0 0.7 maximum_bitcast_fusion
  76.7 0.7 pad.4
  77.4 1.3 %copy.73 = bf16[8,8,36,256]{3,1,2,0:T(8,128)(2,1)} copy(bf16[8,8,36,256]{3,2,1,0:T(8,128)(2,1)S(1)} %bitcast.95) | data formatting | bytes 2359296
  78.7 0.0 copy-start
  78.7 0.0 copy-start.5
  78.7 5.3 %shard_map.75 = f32[32,64,128]{2,1,0:T(8,128)} custom-call(bf16[64,9216]{1,0:T(8,128)(2,1)} %bitcast.98, bf16[320,320]{1,0:T(8,128)(2,1)} %reshape.90.w_ref), custom_call_target="tpu_custom_call" | custom-call | flops 1677721600 | bytes 2433024 | tf_op jit(solution)/shard_map/pallas_call | solution.py:108
  84.0 0.0 copy-done
  84.0 0.0 copy-done.5
  84.0 1.5 %fusion.9 = bf16[1,64,32,128]{3,1,2,0:T(8,128)(2,1)S(1)} fusion(f32[32,64,128]{2,1,0:T(8,128)} %shard_map.75, bf16[1,64,32,128]{3,2,1,0:T(8,128)(2,1)S(1)} %copy-done, f32[64]{0:T(128)S(1)} %copy-done.5, f32[32,128]{1,0:T(8,128)S(1)} %get-tuple-element.19), kind=kLoop, calls=%fused_computation.16 | loop fusion | flops 1310720 | bytes 2113792 | tf_op jit(solution)/shard_map/convert_element_type | solution.py:69
  85.5 1.1 %copy.62 = bf16[1,64,32,128]{3,2,1,0:T(8,128)(2,1)} copy(bf16[1,64,32,128]{3,1,2,0:T(8,128)(2,1)S(1)} %fusion.9) | data formatting | bytes 1048576 | tf_op jit(solution)/shard_map/convert_element_type | solution.py:69
  (4 shorter events, 0.0 us)
Async XLA Ops:
  3.1 19.8 %all-to-all-start = ((bf16[1,64,32,128]{3,1,0,2:T(8,128)(2,1)}), bf16[1,64,32,128]{3,1,0,2:T(8,128)(2,1)S(1)}, u32[]{:S(2)}, u32[]{:S(2)}) async-start(bf16[1,64,32,128]{3,1,0,2:T(8,128)(2,1)} %bitcast.97), calls=%async_computation | async-start | bytes 1048576 | tf_op jit(solution)/shard_map/all_to_all | solution.py:53
  22.9 15.2 %collective-permute-start = (bf16[2,64,4,128]{3,1,2,0:T(8,128)(2,1)S(1)}, bf16[2,64,4,128]{3,1,2,0:T(8,128)(2,1)S(1)}, u32[]{:S(2)}, u32[]{:S(2)}) collective-permute-start(bf16[2,64,4,128]{3,1,2,0:T(8,128)(2,1)S(1)} %fusion.22), channel_id=1, source_target_pairs={{0,8},{8,0},{1,9},{9,1},{2,10},{10,2},{3,11},{11,3},{4,12},{12,4},... | collective-permute-start | bytes 393224 | tf_op jit(solution)/shard_map/ppermute | solution.py:57
  38.1 0.9 %copy-start.2 = (bf16[5,8,8,8]{3,2,1,0:T(8,128)(2,1)S(1)}, bf16[5,8,8,8]{3,2,1,0:T(8,128)(2,1)}, u32[]{:S(2)}) copy-start(bf16[5,8,8,8]{3,2,1,0:T(8,128)(2,1)} %param.10) | copy-start | bytes 15364
  40.4 0.7 copy-start.4
  41.1 6.4 %copy-start.1 = (bf16[5,64,5,64]{3,1,2,0:T(8,128)(2,1)S(1)}, bf16[5,64,5,64]{3,1,2,0:T(8,128)(2,1)}, u32[]{:S(2)}) copy-start(bf16[5,64,5,64]{3,1,2,0:T(8,128)(2,1)} %param.12) | copy-start | bytes 614404
  42.3 6.6 %copy-start.3 = (s32[1,32,128]{2,1,0:T(8,128)S(1)}, s32[1,32,128]{2,1,0:T(8,128)}, u32[]{:S(2)}) copy-start(s32[1,32,128]{2,1,0:T(8,128)} %param.8) | copy-start | bytes 49156
  42.3 14.6 %all-to-all-start.1 = ((bf16[8,64,4,128]{3,1,2,0:T(8,128)(2,1)}), bf16[8,64,4,128]{3,1,2,0:T(8,128)(2,1)S(1)}, u32[]{:S(2)}, u32[]{:S(2)}) async-start(bf16[8,64,4,128]{3,1,2,0:T(8,128)(2,1)} %fusion.8), calls=%async_computation.1 | async-start | bytes 1048576 | tf_op jit(solution)/shard_map/all_to_all | solution.py:63
  78.7 5.3 %copy-start = (bf16[1,64,32,128]{3,2,1,0:T(8,128)(2,1)S(1)}, bf16[1,64,32,128]{3,2,1,0:T(8,128)(2,1)}, u32[]{:S(2)}) copy-start(bf16[1,64,32,128]{3,2,1,0:T(8,128)(2,1)} %x_ref.1) | copy-start | bytes 1572868
  78.7 5.3 %copy-start.5 = (f32[64]{0:T(128)S(1)}, f32[64]{0:T(128)}, u32[]{:S(2)}) copy-start(f32[64]{0:T(128)} %param.13) | copy-start | bytes 772

commit v17 on v4

--- a/solution.py
+++ b/solution.py
@@ -1,3 +1,5 @@
+import functools
+
 import jax
 from jax.experimental import pallas as pl
 from jax.experimental.pallas import tpu as pltpu
@@ -6,13 +8,30 @@
 from jax.sharding import PartitionSpec as P
 
 
+def normalize_kernel(x_ref, g_ref, o_ref):
+    rows, channels, cols_lon = o_ref.shape
+    channel = lax.broadcasted_iota(jnp.int32, (channels, cols_lon), 0)
+    gain = jnp.zeros((channels, cols_lon), jnp.float32)
+    for index in range(channels):
+        gain = jnp.where(channel == index, g_ref[index], gain)
+    for row in range(rows):
+        values = x_ref[0, :, row, :].astype(jnp.float32)
+        center = jnp.sum(values, axis=0, keepdims=True) / channels
+        offset = values - center
+        spread = jnp.sum(offset * offset, axis=0, keepdims=True) / channels
+        o_ref[row] = (offset * lax.rsqrt(spread + 1e-05) * gain).astype(o_ref.dtype)
+
+
 def normalize(block, norm_gain):
-    values = block.astype(jnp.float32)
-    center = jnp.mean(values, axis=1, keepdims=True)
-    spread = jnp.mean((values - center) ** 2, axis=1, keepdims=True)
-    return ((values - center) * lax.rsqrt(spread + 1e-05) * norm_gain[None, :, None, None]).astype(
-        jnp.bfloat16
-    )
+    _, channels, rows_lat, cols_lon = block.shape
+    vmem = pl.BlockSpec(memory_space=pltpu.VMEM)
+    normed = pl.pallas_call(
+        normalize_kernel,
+        out_shape=jax.ShapeDtypeStruct((rows_lat, channels, cols_lon), jnp.bfloat16),
+        in_specs=[vmem, pl.BlockSpec(memory_space=pltpu.SMEM)],
+        out_specs=vmem,
+    )(block, norm_gain)
+    return jnp.transpose(normed, (1, 0, 2))[None]
 
 
 def vertical(taps, w_vert, b_vert):
@@ -52,16 +71,85 @@
     )
 
 
-def horizontal_kernel(x_ref, w_ref, o_ref):
+def horizontal_kernel(
+    count, x_ref, w_ref, o_ref, wide, edges, from_left, from_right, send_sems, recv_sems
+):
+    me = lax.axis_index("lon")
+    right, left = lax.rem(me + 1, count), lax.rem(me + count - 1, count)
+    rest = (lax.axis_index("lat_hi"), lax.axis_index("lat_lo"))
+    mesh_ids = pl.DeviceIdType.MESH
+    barrier = pltpu.get_barrier_semaphore()
+    for neighbour in (left, right):
+        pl.semaphore_signal(barrier, inc=1, device_id=(neighbour,) + rest, device_id_type=mesh_ids)
+
     rows, channels, cols_lon = o_ref.shape
     taps = w_ref.shape[0] // channels
-    segment = x_ref.shape[1] // (rows + taps - 1)
+    reach = taps // 2
+    segment = 2 * cols_lon
+    lane = lax.broadcasted_iota(jnp.int32, (channels, cols_lon), 1)
+    packed = jnp.zeros((channels, cols_lon), x_ref.dtype)
+    for row in range(rows):
+        line = x_ref[row]
+        start = 2 * reach * row
+        packed = jnp.where(
+            jnp.logical_and(lane >= start, lane < start + reach),
+            pltpu.roll(line, start, 1),
+            packed,
+        )
+        packed = jnp.where(
+            jnp.logical_and(lane >= start + reach, lane < start + 2 * reach),
+            pltpu.roll(line, (start + 2 * reach) % cols_lon, 1),
+            packed,
+        )
+    edges[...] = packed
+
+    pl.semaphore_wait(barrier, 2)
+    to_right = pltpu.make_async_remote_copy(
+        src_ref=edges,
+        dst_ref=from_left,
+        send_sem=send_sems.at[0],
+        recv_sem=recv_sems.at[0],
+        device_id=(right,) + rest,
+        device_id_type=mesh_ids,
+    )
+    to_left = pltpu.make_async_remote_copy(
+        src_ref=edges,
+        dst_ref=from_right,
+        send_sem=send_sems.at[1],
+        recv_sem=recv_sems.at[1],
+        device_id=(left,) + rest,
+        device_id_type=mesh_ids,
+    )
+    to_right.start()
+    to_left.start()
+    to_right.wait()
+    to_left.wait()
+
+    left_halo, right_halo = from_left[...], from_right[...]
+    blank = jnp.zeros((channels, cols_lon), x_ref.dtype)
+    for padded_row in range(rows + 2 * reach):
+        row = padded_row - reach
+        base = padded_row * segment
+        if row < 0 or row >= rows:
+            wide[:, base : base + cols_lon] = blank
+            wide[:, base + cols_lon : base + segment] = blank
+            continue
+        start = 2 * reach * row
+        shifted = pltpu.roll(x_ref[row], reach, 1)
+        wide[:, base : base + cols_lon] = jnp.where(
+            lane < reach, pltpu.roll(left_halo, (cols_lon - start - reach) % cols_lon, 1), shifted
+        )
+        tail = pltpu.roll(right_halo, (reach - start) % cols_lon, 1)
+        wide[:, base + cols_lon : base + segment] = jnp.where(
+            lane < reach, shifted, jnp.where(lane < 2 * reach, tail, blank)
+        )
+
     chunk = 8
     weights = w_ref[...]
     for start in range(0, rows, chunk):
         window = jnp.concatenate(
             [
-                x_ref[:, (start + row_tap) * segment : (start + row_tap + chunk) * segment]
+                wide[:, (start + row_tap) * segment : (start + row_tap + chunk) * segment]
                 for row_tap in range(taps)
             ],
             axis=0,
@@ -77,37 +165,34 @@
 
 def horizontal(masked, w_horiz):
     row_taps, channels, col_taps, _ = w_horiz.shape
-    reach_row, reach_col = row_taps // 2, col_taps // 2
+    reach_row = row_taps // 2
     _, _, rows_lat, cols_lon = masked.shape
-    before, after = lon_halo(masked, reach_col)
+    count = lax.axis_size("lon")
     segment = 2 * cols_lon
-    gap = jnp.zeros(masked.shape[:3] + (segment - cols_lon - 2 * reach_col,), masked.dtype)
-    wide = jnp.concatenate([before, masked, after, gap], axis=3)[0]
-    wide = jnp.pad(wide, ((0, 0), (reach_row, reach_row), (0, 0)))
-    wide = wide.reshape(channels, (rows_lat + 2 * reach_row) * segment)
+    rows_major = jnp.transpose(masked[0], (1, 0, 2))
     weights = jnp.transpose(w_horiz, (2, 1, 0, 3)).reshape(col_taps * channels, row_taps * channels)
+    vmem = pl.BlockSpec(memory_space=pltpu.VMEM)
     conv = pl.pallas_call(
-        horizontal_kernel,
+        functools.partial(horizontal_kernel, count),
         out_shape=jax.ShapeDtypeStruct((rows_lat, channels, cols_lon), jnp.float32),
-        in_specs=[pl.BlockSpec(memory_space=pltpu.VMEM)] * 2,
-        out_specs=pl.BlockSpec(memory_space=pltpu.VMEM),
+        in_specs=[vmem, vmem],
+        out_specs=vmem,
+        scratch_shapes=[
+            pltpu.VMEM((channels, (rows_lat + 2 * reach_row) * segment), masked.dtype),
+            pltpu.VMEM((channels, cols_lon), masked.dtype),
+            pltpu.VMEM((channels, cols_lon), masked.dtype),
+            pltpu.VMEM((channels, cols_lon), masked.dtype),
+            pltpu.SemaphoreType.DMA((2,)),
+            pltpu.SemaphoreType.DMA((2,)),
+        ],
+        compiler_params=pltpu.CompilerParams(collective_id=0, has_side_effects=True),
         cost_estimate=pl.CostEstimate(
             flops=2 * rows_lat * segment * weights.shape[0] * weights.shape[1],
-            bytes_accessed=wide.size * 2 + weights.size * 2 + rows_lat * channels * cols_lon * 4,
+            bytes_accessed=masked.size * 2 + weights.size * 2 + rows_lat * channels * cols_lon * 4,
             transcendentals=0,
         ),
-    )(wide, weights)
+    )(rows_major, weights)
     return jnp.transpose(conv, (1, 0, 2))[None]
-
-
-def lon_halo(block, width):
-    devices = lax.axis_size("lon")
-    length = block.shape[-1]
-    up = [(i, (i + 1) % devices) for i in range(devices)]
-    down = [(j, i) for i, j in up]
-    before = lax.ppermute(block[..., length - width :], "lon", up)
-    after = lax.ppermute(block[..., :width], "lon", down)
-    return before, after
 
 
 def solution(mesh):

time: 96.9 us -> 79.1 us (0.82)
  the two profiles are of different devices: /device:TPU:24 before, /device:TPU:1 now
where the time goes in v17:
time: 79.1 us; the launch traced here: 78.5 us
  starting transfers between devices  26.3 us (33%)
  waiting for transfers between devices  21.8 us (28%)
  Pallas kernels  20.4 us (26%)
  local copies, waits for them, and re-layouts  4.22 us (5%)
  other arithmetic  3.8 us (5%)
  matrix products  1.75 us (2%)
    pallas_call x1, Pallas kernels, horizontal(): pl.pallas_call(functools.partial(horizontal_kernel, count), out_shape=jax...  17.3 us
    ppermute x1, starting transfers between devices, local(): recv = lax.ppermute(send, 'lat_hi', [(0, 1), (1, 0)])  10.9 us
    all_to_all x1, starting transfers between devices, local(): lax.all_to_all(normed, 'lat_lo', split_axis=2, concat_axis=0, tiled=True)  10.3 us
    all_to_all x1, waiting for transfers between devices, local(): lax.all_to_all(normed, 'lat_lo', split_axis=2, concat_axis=0, tiled=True)  9.5 us
    all_to_all x1, waiting for transfers between devices, local(): lax.all_to_all(vertical(taps, w_vert, b_vert), 'lat_lo', split_axis=0, co...  8.07 us
    all_to_all x1, starting transfers between devices, local(): lax.all_to_all(vertical(taps, w_vert, b_vert), 'lat_lo', split_axis=0, co...  5.11 us
    ppermute x1, waiting for transfers between devices, local(): recv = lax.ppermute(send, 'lat_hi', [(0, 1), (1, 0)])  4.28 us
    pallas_call x1, Pallas kernels, normalize(): pl.pallas_call(normalize_kernel, out_shape=jax.ShapeDtypeStruct((rows_lat...  3.06 us
  transfers between devices with their start and end apart: 3, of which 3 were waited for; matrix products, arithmetic and copies ran while one was open for 2% of the time, Pallas kernels for 0%

profile of v17, /device:TPU:1, one launch (start us, length us, event | category | flops | bytes accessed | tf_op | source)
XLA Modules:
  0.0 78.5 jit_solution(10595631127473794482)
XLA Ops:
  0.0 3.1 %shard_map.73 = bf16[32,64,128]{2,1,0:T(8,128)(2,1)} custom-call(bf16[1,64,32,128]{3,2,1,0:T(8,128)(2,1)} %x_ref.1, f32[64]{0:T(128)} %g_ref.1), custom_call_target="tpu_custom_call" | custom-call | tf_op jit(solution)/shard_map/pallas_call | solution.py:28
  3.1 10.3 %all-to-all-start = ((bf16[1,64,32,128]{3,1,0,2:T(8,128)(2,1)}), bf16[1,64,32,128]{3,1,0,2:T(8,128)(2,1)S(1)}, u32[]{:S(2)}, u32[]{:S(2)}) async-start(bf16[1,64,32,128]{3,1,0,2:T(8,128)(2,1)} %bitcast.89), calls=%async_computation | async-start | bytes 1048576 | tf_op jit(solution)/shard_map/all_to_all | solution.py:53
  13.3 9.5 %all-to-all-done = bf16[1,64,32,128]{3,1,0,2:T(8,128)(2,1)S(1)} async-done(((bf16[1,64,32,128]{3,1,0,2:T(8,128)(2,1)}), bf16[1,64,32,128]{3,1,0,2:T(8,128)(2,1)S(1)}, u32[]{:S(2)}, u32[]{:S(2)}) %all-to-all-start) | async-done | bytes 524320 | tf_op jit(solution)/shard_map/all_to_all | solution.py:53
  22.9 10.9 %collective-permute-start = (bf16[2,64,4,128]{3,1,2,0:T(8,128)(2,1)S(1)}, bf16[2,64,4,128]{3,1,2,0:T(8,128)(2,1)S(1)}, u32[]{:S(2)}, u32[]{:S(2)}) collective-permute-start(bf16[2,64,4,128]{3,1,2,0:T(8,128)(2,1)S(1)} %fusion.22), channel_id=1, source_target_pairs={{0,8},{8,0},{1,9},{9,1},{2,10},{10,2},{3,11},{11,3},{4,12},{12,4},... | collective-permute-start | bytes 393224 | tf_op jit(solution)/shard_map/ppermute | solution.py:57
  33.8 4.3 %collective-permute-done = bf16[2,64,4,128]{3,1,2,0:T(8,128)(2,1)S(1)} collective-permute-done((bf16[2,64,4,128]{3,1,2,0:T(8,128)(2,1)S(1)}, bf16[2,64,4,128]{3,1,2,0:T(8,128)(2,1)S(1)}, u32[]{:S(2)}, u32[]{:S(2)}) %collective-permute-start) | collective-permute-done | bytes 131104 | tf_op jit(solution)/shard_map/ppermute | solution.py:57
  38.1 0.0 copy-start.2
  38.1 0.1 fusion.14
  38.3 0.7 copy-done.2
  39.0 0.3 fusion.20
  39.4 0.4 convolution_add_fusion.3
  39.7 0.3 convolution_add_fusion.2
  40.1 0.4 convolution_add_fusion.1
  40.4 0.0 copy-start.4
  40.4 0.4 fusion
  40.8 0.3 copy-done.4
  41.1 1.2 %fusion.8 = bf16[8,64,4,128]{3,1,2,0:T(8,128)(2,1)} fusion(f32[8,8,8,4,128]{4,2,3,0,1:T(8,128)S(1)} %fusion, f32[64]{0:T(128)S(1)} %copy-done.4), kind=kLoop, calls=%fused_computation.13 | loop fusion | flops 2621440 | bytes 1573120 | tf_op jit(solution)/shard_map/convert_element_type | solution.py:47
  42.3 0.0 copy-start.1
  42.3 5.1 %all-to-all-start.1 = ((bf16[8,64,4,128]{3,1,2,0:T(8,128)(2,1)}), bf16[8,64,4,128]{3,1,2,0:T(8,128)(2,1)S(1)}, u32[]{:S(2)}, u32[]{:S(2)}) async-start(bf16[8,64,4,128]{3,1,2,0:T(8,128)(2,1)} %fusion.8), calls=%async_computation.1 | async-start | bytes 1048576 | tf_op jit(solution)/shard_map/all_to_all | solution.py:63
  47.4 0.0 copy-done.1
  47.5 0.3 copy.43
  47.8 0.0 copy-start.3
  47.8 1.1 %reshape.62.w_ref = bf16[320,320]{1,0:T(8,128)(2,1)} reshape(bf16[5,64,5,64]{3,2,1,0:T(8,128)(2,1)S(1)} %copy.43) | data formatting | bytes 409600 | tf_op jit(solution)/shard_map/reshape | solution.py:173
  48.9 0.0 copy-done.3
  48.9 8.1 %all-to-all-done.1 = bf16[8,64,4,128]{3,1,2,0:T(8,128)(2,1)S(1)} async-done(((bf16[8,64,4,128]{3,1,2,0:T(8,128)(2,1)}), bf16[8,64,4,128]{3,1,2,0:T(8,128)(2,1)S(1)}, u32[]{:S(2)}, u32[]{:S(2)}) %all-to-all-start.1) | async-done | bytes 524320 | tf_op jit(solution)/shard_map/all_to_all | solution.py:63
  57.0 0.9 %bitcast_multiply_fusion = bf16[64,32,128]{2,0,1:T(8,128)(2,1)} fusion(bf16[8,64,4,128]{3,1,2,0:T(8,128)(2,1)S(1)} %all-to-all-done.1, bf16[32,128]{1,0:T(8,128)(2,1)S(1)} %get-tuple-element.14), kind=kLoop, calls=%fused_computation.29 | loop fusion | flops 262144 | bytes 1056768 | tf_op jit(solution)/shard_map/mul | solution.py:66
  57.8 0.0 copy-start
  57.8 17.3 %shard_map.74 = f32[32,64,128]{2,1,0:T(8,128)} custom-call(bf16[32,64,128]{2,1,0:T(8,128)(2,1)} %bitcast.90, bf16[320,320]{1,0:T(8,128)(2,1)} %reshape.62.w_ref), custom_call_target="tpu_custom_call" | custom-call | flops 1677721600 | bytes 1777664 | tf_op jit(solution)/shard_map/pallas_call | solution.py:175
  75.2 0.0 copy-start.5
  75.2 0.0 copy-done
  75.2 0.6 copy-done.5
  75.8 1.5 %fusion.9 = bf16[1,64,32,128]{3,1,2,0:T(8,128)(2,1)S(1)} fusion(f32[32,64,128]{2,1,0:T(8,128)} %shard_map.74, bf16[1,64,32,128]{3,2,1,0:T(8,128)(2,1)S(1)} %copy-done, f32[64]{0:T(128)S(1)} %copy-done.5, f32[32,128]{1,0:T(8,128)S(1)} %get-tuple-element.13), kind=kLoop, calls=%fused_computation.15 | loop fusion | flops 1310720 | bytes 2113792 | tf_op jit(solution)/shard_map/convert_element_type | solution.py:69
  77.4 1.1 %copy.44 = bf16[1,64,32,128]{3,2,1,0:T(8,128)(2,1)} copy(bf16[1,64,32,128]{3,1,2,0:T(8,128)(2,1)S(1)} %fusion.9) | data formatting | bytes 1048576 | tf_op jit(solution)/shard_map/convert_element_type | solution.py:69
  (3 shorter events, 0.0 us)
Async XLA Ops:
  3.1 19.8 %all-to-all-start = ((bf16[1,64,32,128]{3,1,0,2:T(8,128)(2,1)}), bf16[1,64,32,128]{3,1,0,2:T(8,128)(2,1)S(1)}, u32[]{:S(2)}, u32[]{:S(2)}) async-start(bf16[1,64,32,128]{3,1,0,2:T(8,128)(2,1)} %bitcast.89), calls=%async_computation | async-start | bytes 1048576 | tf_op jit(solution)/shard_map/all_to_all | solution.py:53
  22.9 15.2 %collective-permute-start = (bf16[2,64,4,128]{3,1,2,0:T(8,128)(2,1)S(1)}, bf16[2,64,4,128]{3,1,2,0:T(8,128)(2,1)S(1)}, u32[]{:S(2)}, u32[]{:S(2)}) collective-permute-start(bf16[2,64,4,128]{3,1,2,0:T(8,128)(2,1)S(1)} %fusion.22), channel_id=1, source_target_pairs={{0,8},{8,0},{1,9},{9,1},{2,10},{10,2},{3,11},{11,3},{4,12},{12,4},... | collective-permute-start | bytes 393224 | tf_op jit(solution)/shard_map/ppermute | solution.py:57
  38.1 0.9 %copy-start.2 = (bf16[5,8,8,8]{3,2,1,0:T(8,128)(2,1)S(1)}, bf16[5,8,8,8]{3,2,1,0:T(8,128)(2,1)}, u32[]{:S(2)}) copy-start(bf16[5,8,8,8]{3,2,1,0:T(8,128)(2,1)} %param.10) | copy-start | bytes 15364
  40.4 0.7 copy-start.4
  42.3 5.1 %copy-start.1 = (bf16[5,64,5,64]{3,1,2,0:T(8,128)(2,1)S(1)}, bf16[5,64,5,64]{3,1,2,0:T(8,128)(2,1)}, u32[]{:S(2)}) copy-start(bf16[5,64,5,64]{3,1,2,0:T(8,128)(2,1)} %param.12) | copy-start | bytes 614404
  42.3 14.6 %all-to-all-start.1 = ((bf16[8,64,4,128]{3,1,2,0:T(8,128)(2,1)}), bf16[8,64,4,128]{3,1,2,0:T(8,128)(2,1)S(1)}, u32[]{:S(2)}, u32[]{:S(2)}) async-start(bf16[8,64,4,128]{3,1,2,0:T(8,128)(2,1)} %fusion.8), calls=%async_computation.1 | async-start | bytes 1048576 | tf_op jit(solution)/shard_map/all_to_all | solution.py:63
  47.8 1.1 %copy-start.3 = (s32[1,32,128]{2,1,0:T(8,128)S(1)}, s32[1,32,128]{2,1,0:T(8,128)}, u32[]{:S(2)}) copy-start(s32[1,32,128]{2,1,0:T(8,128)} %param.8) | copy-start | bytes 49156
  57.8 17.4 %copy-start = (bf16[1,64,32,128]{3,2,1,0:T(8,128)(2,1)S(1)}, bf16[1,64,32,128]{3,2,1,0:T(8,128)(2,1)}, u32[]{:S(2)}) copy-start(bf16[1,64,32,128]{3,2,1,0:T(8,128)(2,1)} %x_ref.1) | copy-start | bytes 1572868
  75.2 0.7 copy-start.5

commit v18 on v17

--- a/solution.py
+++ b/solution.py
@@ -64,15 +64,12 @@
         vertical(taps, w_vert, b_vert), "lat_lo", split_axis=0, concat_axis=2, tiled=True
     )
     masked = mixed * ocean_mask[:, None].astype(jnp.bfloat16)
-    conv = horizontal(masked, w_horiz)
-    ocean = ocean_mask[:, None].astype(jnp.float32)
-    return (fields.astype(jnp.float32) + ocean * (conv + b_horiz[None, :, None, None])).astype(
-        jnp.bfloat16
-    )
+    return horizontal(masked, w_horiz, fields, ocean_mask, b_horiz)
 
 
 def horizontal_kernel(
-    count, x_ref, w_ref, o_ref, wide, edges, from_left, from_right, send_sems, recv_sems
+    count, x_ref, w_ref, f_ref, m_ref, b_ref, o_ref, wide, edges, from_left, from_right, send_sems,
+    recv_sems,
 ):
     me = lax.axis_index("lon")
     right, left = lax.rem(me + 1, count), lax.rem(me + count - 1, count)
@@ -82,7 +79,7 @@
     for neighbour in (left, right):
         pl.semaphore_signal(barrier, inc=1, device_id=(neighbour,) + rest, device_id_type=mesh_ids)
 
-    rows, channels, cols_lon = o_ref.shape
+    rows, channels, cols_lon = x_ref.shape
     taps = w_ref.shape[0] // channels
     reach = taps // 2
     segment = 2 * cols_lon
@@ -144,6 +141,10 @@
             lane < reach, shifted, jnp.where(lane < 2 * reach, tail, blank)
         )
 
+    channel = lax.broadcasted_iota(jnp.int32, (channels, cols_lon), 0)
+    bias = jnp.zeros((channels, cols_lon), jnp.float32)
+    for index in range(channels):
+        bias = jnp.where(channel == index, b_ref[index], bias)
     chunk = 8
     weights = w_ref[...]
     for start in range(0, rows, chunk):
@@ -160,10 +161,14 @@
             piece = partial[col_tap * channels : (col_tap + 1) * channels]
             total = total + pltpu.roll(piece, chunk * segment - col_tap, 1)
         for row in range(chunk):
-            o_ref[start + row] = total[:, row * segment : row * segment + cols_lon]
-
-
-def horizontal(masked, w_horiz):
+            line = start + row
+            conv = total[:, row * segment : row * segment + cols_lon]
+            ocean = m_ref[0, line : line + 1, :].astype(jnp.float32)
+            base = f_ref[0, :, line, :].astype(jnp.float32)
+            o_ref[0, :, line, :] = (base + ocean * (conv + bias)).astype(o_ref.dtype)
+
+
+def horizontal(masked, w_horiz, fields, ocean_mask, b_horiz):
     row_taps, channels, col_taps, _ = w_horiz.shape
     reach_row = row_taps // 2
     _, _, rows_lat, cols_lon = masked.shape
@@ -172,10 +177,10 @@
     rows_major = jnp.transpose(masked[0], (1, 0, 2))
     weights = jnp.transpose(w_horiz, (2, 1, 0, 3)).reshape(col_taps * channels, row_taps * channels)
     vmem = pl.BlockSpec(memory_space=pltpu.VMEM)
-    conv = pl.pallas_call(
+    return pl.pallas_call(
         functools.partial(horizontal_kernel, count),
-        out_shape=jax.ShapeDtypeStruct((rows_lat, channels, cols_lon), jnp.float32),
-        in_specs=[vmem, vmem],
+        out_shape=jax.ShapeDtypeStruct(fields.shape, fields.dtype),
+        in_specs=[vmem] * 4 + [pl.BlockSpec(memory_space=pltpu.SMEM)],
         out_specs=vmem,
         scratch_shapes=[
             pltpu.VMEM((channels, (rows_lat + 2 * reach_row) * segment), masked.dtype),
@@ -191,8 +196,7 @@
             bytes_accessed=masked.size * 2 + weights.size * 2 + rows_lat * channels * cols_lon * 4,
             transcendentals=0,
         ),
-    )(rows_major, weights)
-    return jnp.transpose(conv, (1, 0, 2))[None]
+    )(rows_major, weights, fields, ocean_mask, b_horiz)
 
 
 def solution(mesh):

time: 79.1 us -> 78.4 us (level)
  other arithmetic: 3.8 us -> 2.29 us
  Pallas kernels: 20.4 us -> 21.2 us
    convert_element_type x2 -> x1, other arithmetic: 1.52 us -> 0.01 us  [local(): masked = mixed * ocean_mask[:, None].astype(jnp.bfloat16)]
    unnamed x12 -> x9, local copies, waits for them, and re-layouts: 1.68 us -> 2.91 us
    convert_element_type x1 -> x0, local copies, waits for them, and re-layouts: 1.14 us -> none  [local(): (fields.astype(jnp.float32) + ocean * (conv + b_horiz[None, :, None, None...]
    pallas_call x1, Pallas kernels: 17.3 us -> 18.1 us  [horizontal(): pl.pallas_call(functools.partial(horizontal_kernel, count), out_shape=jax...]
where the time goes in v18:
time: 78.4 us; the launch traced here: 77.8 us
  starting transfers between devices  26.3 us (34%)
  waiting for transfers between devices  21.9 us (28%)
  Pallas kernels  21.2 us (27%)
  local copies, waits for them, and re-layouts  4.28 us (5%)
  other arithmetic  2.29 us (3%)
  matrix products  1.75 us (2%)
    pallas_call x1, Pallas kernels, horizontal(): pl.pallas_call(functools.partial(horizontal_kernel, count), out_shape=jax...  18.1 us
    ppermute x1, starting transfers between devices, local(): recv = lax.ppermute(send, 'lat_hi', [(0, 1), (1, 0)])  10.9 us
    all_to_all x1, starting transfers between devices, local(): lax.all_to_all(normed, 'lat_lo', split_axis=2, concat_axis=0, tiled=True)  10.3 us
    all_to_all x1, waiting for transfers between devices, local(): lax.all_to_all(normed, 'lat_lo', split_axis=2, concat_axis=0, tiled=True)  9.5 us
    all_to_all x1, waiting for transfers between devices, local(): lax.all_to_all(vertical(taps, w_vert, b_vert), 'lat_lo', split_axis=0, co...  8.1 us
    all_to_all x1, starting transfers between devices, local(): lax.all_to_all(vertical(taps, w_vert, b_vert), 'lat_lo', split_axis=0, co...  5.11 us
    ppermute x1, waiting for transfers between devices, local(): recv = lax.ppermute(send, 'lat_hi', [(0, 1), (1, 0)])  4.28 us
    pallas_call x1, Pallas kernels, normalize(): pl.pallas_call(normalize_kernel, out_shape=jax.ShapeDtypeStruct((rows_lat...  3.06 us
  transfers between devices with their start and end apart: 3, of which 3 were waited for; matrix products, arithmetic and copies ran while one was open for 2% of the time, Pallas kernels for 0%

profile of v18, /device:TPU:1, one launch (start us, length us, event | category | flops | bytes accessed | tf_op | source)
XLA Modules:
  0.0 77.8 jit_solution(4562186094198263795)
XLA Ops:
  0.0 3.1 %shard_map.73 = bf16[32,64,128]{2,1,0:T(8,128)(2,1)} custom-call(bf16[1,64,32,128]{3,2,1,0:T(8,128)(2,1)} %f_ref.1, f32[64]{0:T(128)} %g_ref.1), custom_call_target="tpu_custom_call" | custom-call | tf_op jit(solution)/shard_map/pallas_call | solution.py:28
  3.1 10.3 %all-to-all-start = ((bf16[1,64,32,128]{3,1,0,2:T(8,128)(2,1)}), bf16[1,64,32,128]{3,1,0,2:T(8,128)(2,1)S(1)}, u32[]{:S(2)}, u32[]{:S(2)}) async-start(bf16[1,64,32,128]{3,1,0,2:T(8,128)(2,1)} %bitcast.81), calls=%async_computation | async-start | bytes 1048576 | tf_op jit(solution)/shard_map/all_to_all | solution.py:53
  13.3 9.5 %all-to-all-done = bf16[1,64,32,128]{3,1,0,2:T(8,128)(2,1)S(1)} async-done(((bf16[1,64,32,128]{3,1,0,2:T(8,128)(2,1)}), bf16[1,64,32,128]{3,1,0,2:T(8,128)(2,1)S(1)}, u32[]{:S(2)}, u32[]{:S(2)}) %all-to-all-start) | async-done | bytes 524320 | tf_op jit(solution)/shard_map/all_to_all | solution.py:53
  22.9 10.9 %collective-permute-start = (bf16[2,64,4,128]{3,1,2,0:T(8,128)(2,1)S(1)}, bf16[2,64,4,128]{3,1,2,0:T(8,128)(2,1)S(1)}, u32[]{:S(2)}, u32[]{:S(2)}) collective-permute-start(bf16[2,64,4,128]{3,1,2,0:T(8,128)(2,1)S(1)} %fusion.21), channel_id=1, source_target_pairs={{0,8},{8,0},{1,9},{9,1},{2,10},{10,2},{3,11},{11,3},{4,12},{12,4},... | collective-permute-start | bytes 393224 | tf_op jit(solution)/shard_map/ppermute | solution.py:57
  33.8 4.3 %collective-permute-done = bf16[2,64,4,128]{3,1,2,0:T(8,128)(2,1)S(1)} collective-permute-done((bf16[2,64,4,128]{3,1,2,0:T(8,128)(2,1)S(1)}, bf16[2,64,4,128]{3,1,2,0:T(8,128)(2,1)S(1)}, u32[]{:S(2)}, u32[]{:S(2)}) %collective-permute-start) | collective-permute-done | bytes 131104 | tf_op jit(solution)/shard_map/ppermute | solution.py:57
  38.1 0.0 copy-start.1
  38.1 0.1 fusion.13
  38.3 0.7 copy-done.1
  39.0 0.3 fusion.19
  39.4 0.4 convolution_add_fusion.3
  39.7 0.3 convolution_add_fusion.2
  40.1 0.4 convolution_add_fusion.1
  40.4 0.0 copy-start.3
  40.4 0.4 fusion
  40.8 0.3 copy-done.3
  41.1 1.2 %fusion.8 = bf16[8,64,4,128]{3,1,2,0:T(8,128)(2,1)} fusion(f32[8,8,8,4,128]{4,2,3,0,1:T(8,128)S(1)} %fusion, f32[64]{0:T(128)S(1)} %copy-done.3), kind=kLoop, calls=%fused_computation.13 | loop fusion | flops 2621440 | bytes 1573120 | tf_op jit(solution)/shard_map/convert_element_type | solution.py:47
  42.3 0.0 copy-start
  42.3 5.1 %all-to-all-start.1 = ((bf16[8,64,4,128]{3,1,2,0:T(8,128)(2,1)}), bf16[8,64,4,128]{3,1,2,0:T(8,128)(2,1)S(1)}, u32[]{:S(2)}, u32[]{:S(2)}) async-start(bf16[8,64,4,128]{3,1,2,0:T(8,128)(2,1)} %fusion.8), calls=%async_computation.1 | async-start | bytes 1048576 | tf_op jit(solution)/shard_map/all_to_all | solution.py:63
  47.4 0.0 copy-done
  47.5 0.3 copy.38
  47.8 0.0 copy-start.2
  47.8 1.1 %reshape.47.w_ref = bf16[320,320]{1,0:T(8,128)(2,1)} reshape(bf16[5,64,5,64]{3,2,1,0:T(8,128)(2,1)S(1)} %copy.38) | data formatting | bytes 409600 | tf_op jit(solution)/shard_map/reshape | solution.py:178
  48.8 0.0 copy-done.2
  48.9 8.1 %all-to-all-done.1 = bf16[8,64,4,128]{3,1,2,0:T(8,128)(2,1)S(1)} async-done(((bf16[8,64,4,128]{3,1,2,0:T(8,128)(2,1)}), bf16[8,64,4,128]{3,1,2,0:T(8,128)(2,1)S(1)}, u32[]{:S(2)}, u32[]{:S(2)}) %all-to-all-start.1) | async-done | bytes 524320 | tf_op jit(solution)/shard_map/all_to_all | solution.py:63
  57.0 0.9 %bitcast_multiply_fusion = bf16[64,32,128]{2,0,1:T(8,128)(2,1)} fusion(bf16[8,64,4,128]{3,1,2,0:T(8,128)(2,1)S(1)} %all-to-all-done.1, bf16[32,128]{1,0:T(8,128)(2,1)S(1)} %convert_bitcast_fusion), kind=kLoop, calls=%fused_computation.27 | loop fusion | flops 262144 | bytes 1056768 | tf_op jit(solution)/shard_map/mul | solution.py:66
  57.8 18.1 %shard_map.74 = bf16[1,64,32,128]{3,2,1,0:T(8,128)(2,1)} custom-call(bf16[32,64,128]{2,1,0:T(8,128)(2,1)} %bitcast.82, bf16[320,320]{1,0:T(8,128)(2,1)} %reshape.47.w_ref, bf16[1,64,32,128]{3,2,1,0:T(8,128)(2,1)} %f_ref.1, s32[1,32,128]{2,1,0:T(8,128)} %m_ref.1, f32[64]{0:T(128)} %b_ref.1), custom_call_target="tpu_custom_call" | custom-call | flops 1677721600 | bytes 1777664 | tf_op jit(solution)/shard_map/pallas_call | solution.py:180
  76.0 1.9 %copy.61 = bf16[1,64,32,128]{3,2,1,0:T(8,128)(2,1)} copy(bf16[1,64,32,128]{3,2,1,0:T(8,128)(2,1)} %shard_map.74) | data formatting | bytes 1048576
  (3 shorter events, 0.0 us)
Async XLA Ops:
  3.1 19.8 %all-to-all-start = ((bf16[1,64,32,128]{3,1,0,2:T(8,128)(2,1)}), bf16[1,64,32,128]{3,1,0,2:T(8,128)(2,1)S(1)}, u32[]{:S(2)}, u32[]{:S(2)}) async-start(bf16[1,64,32,128]{3,1,0,2:T(8,128)(2,1)} %bitcast.81), calls=%async_computation | async-start | bytes 1048576 | tf_op jit(solution)/shard_map/all_to_all | solution.py:53
  22.9 15.2 %collective-permute-start = (bf16[2,64,4,128]{3,1,2,0:T(8,128)(2,1)S(1)}, bf16[2,64,4,128]{3,1,2,0:T(8,128)(2,1)S(1)}, u32[]{:S(2)}, u32[]{:S(2)}) collective-permute-start(bf16[2,64,4,128]{3,1,2,0:T(8,128)(2,1)S(1)} %fusion.21), channel_id=1, source_target_pairs={{0,8},{8,0},{1,9},{9,1},{2,10},{10,2},{3,11},{11,3},{4,12},{12,4},... | collective-permute-start | bytes 393224 | tf_op jit(solution)/shard_map/ppermute | solution.py:57
  38.1 0.9 %copy-start.1 = (bf16[5,8,8,8]{3,2,1,0:T(8,128)(2,1)S(1)}, bf16[5,8,8,8]{3,2,1,0:T(8,128)(2,1)}, u32[]{:S(2)}) copy-start(bf16[5,8,8,8]{3,2,1,0:T(8,128)(2,1)} %param.10) | copy-start | bytes 15364
  40.4 0.7 copy-start.3
  42.3 5.1 %copy-start = (bf16[5,64,5,64]{3,1,2,0:T(8,128)(2,1)S(1)}, bf16[5,64,5,64]{3,1,2,0:T(8,128)(2,1)}, u32[]{:S(2)}) copy-start(bf16[5,64,5,64]{3,1,2,0:T(8,128)(2,1)} %param.12) | copy-start | bytes 614404
  42.3 14.6 %all-to-all-start.1 = ((bf16[8,64,4,128]{3,1,2,0:T(8,128)(2,1)}), bf16[8,64,4,128]{3,1,2,0:T(8,128)(2,1)S(1)}, u32[]{:S(2)}, u32[]{:S(2)}) async-start(bf16[8,64,4,128]{3,1,2,0:T(8,128)(2,1)} %fusion.8), calls=%async_computation.1 | async-start | bytes 1048576 | tf_op jit(solution)/shard_map/all_to_all | solution.py:63
  47.8 1.1 %copy-start.2 = (s32[1,32,128]{2,1,0:T(8,128)S(1)}, s32[1,32,128]{2,1,0:T(8,128)}, u32[]{:S(2)}) copy-start(s32[1,32,128]{2,1,0:T(8,128)} %m_ref.1) | copy-start | bytes 49156

commit v19 on v18

--- a/solution.py
+++ b/solution.py
@@ -63,8 +63,7 @@
     mixed = lax.all_to_all(
         vertical(taps, w_vert, b_vert), "lat_lo", split_axis=0, concat_axis=2, tiled=True
     )
-    masked = mixed * ocean_mask[:, None].astype(jnp.bfloat16)
-    return horizontal(masked, w_horiz, fields, ocean_mask, b_horiz)
+    return horizontal(mixed, w_horiz, fields, ocean_mask, b_horiz)
 
 
 def horizontal_kernel(
@@ -85,8 +84,11 @@
     segment = 2 * cols_lon
     lane = lax.broadcasted_iota(jnp.int32, (channels, cols_lon), 1)
     packed = jnp.zeros((channels, cols_lon), x_ref.dtype)
+    def masked_row(row):
+        return x_ref[row] * m_ref[0, row : row + 1, :].astype(x_ref.dtype)
+
     for row in range(rows):
-        line = x_ref[row]
+        line = masked_row(row)
         start = 2 * reach * row
         packed = jnp.where(
             jnp.logical_and(lane >= start, lane < start + reach),
@@ -132,7 +134,7 @@
             wide[:, base + cols_lon : base + segment] = blank
             continue
         start = 2 * reach * row
-        shifted = pltpu.roll(x_ref[row], reach, 1)
+        shifted = pltpu.roll(masked_row(row), reach, 1)
         wide[:, base : base + cols_lon] = jnp.where(
             lane < reach, pltpu.roll(left_halo, (cols_lon - start - reach) % cols_lon, 1), shifted
         )

time: 78.4 us -> 78.4 us (level)
  other arithmetic: 2.29 us -> 1.42 us
  local copies, waits for them, and re-layouts: 4.28 us -> 5.07 us
    mul x1 -> x0, other arithmetic: 0.87 us -> none  [local(): masked = mixed * ocean_mask[:, None].astype(jnp.bfloat16)]
    unnamed x9, local copies, waits for them, and re-layouts: 2.91 us -> 3.69 us
where the time goes in v19:
time: 78.4 us; the launch traced here: 77.7 us
  starting transfers between devices  26.3 us (34%)
  waiting for transfers between devices  21.9 us (28%)
  Pallas kernels  21.2 us (27%)
  local copies, waits for them, and re-layouts  5.07 us (6%)
  matrix products  1.75 us (2%)
  other arithmetic  1.42 us (2%)
    pallas_call x1, Pallas kernels, horizontal(): pl.pallas_call(functools.partial(horizontal_kernel, count), out_shape=jax...  18.1 us
    ppermute x1, starting transfers between devices, local(): recv = lax.ppermute(send, 'lat_hi', [(0, 1), (1, 0)])  10.9 us
    all_to_all x1, starting transfers between devices, local(): lax.all_to_all(normed, 'lat_lo', split_axis=2, concat_axis=0, tiled=True)  10.3 us
    all_to_all x1, waiting for transfers between devices, local(): lax.all_to_all(normed, 'lat_lo', split_axis=2, concat_axis=0, tiled=True)  9.5 us
    all_to_all x1, waiting for transfers between devices, local(): lax.all_to_all(vertical(taps, w_vert, b_vert), 'lat_lo', split_axis=0, co...  8.12 us
    all_to_all x1, starting transfers between devices, local(): lax.all_to_all(vertical(taps, w_vert, b_vert), 'lat_lo', split_axis=0, co...  5.11 us
    ppermute x1, waiting for transfers between devices, local(): recv = lax.ppermute(send, 'lat_hi', [(0, 1), (1, 0)])  4.28 us
    unnamed x9, local copies, waits for them, and re-layouts  3.69 us
  transfers between devices with their start and end apart: 3, of which 3 were waited for; matrix products, arithmetic and copies ran while one was open for 2% of the time, Pallas kernels for 0%

profile of v19, /device:TPU:1, one launch (start us, length us, event | category | flops | bytes accessed | tf_op | source)
XLA Modules:
  0.0 77.7 jit_solution(13915358840850611841)
XLA Ops:
  0.0 3.1 %shard_map.73 = bf16[32,64,128]{2,1,0:T(8,128)(2,1)} custom-call(bf16[1,64,32,128]{3,2,1,0:T(8,128)(2,1)} %f_ref.1, f32[64]{0:T(128)} %g_ref.1), custom_call_target="tpu_custom_call" | custom-call | tf_op jit(solution)/shard_map/pallas_call | solution.py:28
  3.1 10.3 %all-to-all-start = ((bf16[1,64,32,128]{3,1,0,2:T(8,128)(2,1)}), bf16[1,64,32,128]{3,1,0,2:T(8,128)(2,1)S(1)}, u32[]{:S(2)}, u32[]{:S(2)}) async-start(bf16[1,64,32,128]{3,1,0,2:T(8,128)(2,1)} %bitcast.79), calls=%async_computation | async-start | bytes 1048576 | tf_op jit(solution)/shard_map/all_to_all | solution.py:53
  13.3 9.5 %all-to-all-done = bf16[1,64,32,128]{3,1,0,2:T(8,128)(2,1)S(1)} async-done(((bf16[1,64,32,128]{3,1,0,2:T(8,128)(2,1)}), bf16[1,64,32,128]{3,1,0,2:T(8,128)(2,1)S(1)}, u32[]{:S(2)}, u32[]{:S(2)}) %all-to-all-start) | async-done | bytes 524320 | tf_op jit(solution)/shard_map/all_to_all | solution.py:53
  22.9 10.9 %collective-permute-start = (bf16[2,64,4,128]{3,1,2,0:T(8,128)(2,1)S(1)}, bf16[2,64,4,128]{3,1,2,0:T(8,128)(2,1)S(1)}, u32[]{:S(2)}, u32[]{:S(2)}) collective-permute-start(bf16[2,64,4,128]{3,1,2,0:T(8,128)(2,1)S(1)} %fusion.21), channel_id=1, source_target_pairs={{0,8},{8,0},{1,9},{9,1},{2,10},{10,2},{3,11},{11,3},{4,12},{12,4},... | collective-permute-start | bytes 393224 | tf_op jit(solution)/shard_map/ppermute | solution.py:57
  33.8 4.3 %collective-permute-done = bf16[2,64,4,128]{3,1,2,0:T(8,128)(2,1)S(1)} collective-permute-done((bf16[2,64,4,128]{3,1,2,0:T(8,128)(2,1)S(1)}, bf16[2,64,4,128]{3,1,2,0:T(8,128)(2,1)S(1)}, u32[]{:S(2)}, u32[]{:S(2)}) %collective-permute-start) | collective-permute-done | bytes 131104 | tf_op jit(solution)/shard_map/ppermute | solution.py:57
  38.1 0.0 copy-start.2
  38.1 0.1 fusion.13
  38.3 0.7 copy-done.2
  39.0 0.3 fusion.19
  39.4 0.4 convolution_add_fusion.3
  39.7 0.3 convolution_add_fusion.2
  40.1 0.4 convolution_add_fusion.1
  40.4 0.0 copy-start.3
  40.4 0.4 fusion
  40.8 0.3 copy-done.3
  41.1 1.2 %fusion.8 = bf16[8,64,4,128]{3,1,2,0:T(8,128)(2,1)} fusion(f32[8,8,8,4,128]{4,2,3,0,1:T(8,128)S(1)} %fusion, f32[64]{0:T(128)S(1)} %copy-done.3), kind=kLoop, calls=%fused_computation.13 | loop fusion | flops 2621440 | bytes 1573120 | tf_op jit(solution)/shard_map/convert_element_type | solution.py:47
  42.3 0.0 copy-start.1
  42.3 5.1 %all-to-all-start.1 = ((bf16[8,64,4,128]{3,1,2,0:T(8,128)(2,1)}), bf16[8,64,4,128]{3,1,2,0:T(8,128)(2,1)S(1)}, u32[]{:S(2)}, u32[]{:S(2)}) async-start(bf16[8,64,4,128]{3,1,2,0:T(8,128)(2,1)} %fusion.8), calls=%async_computation.1 | async-start | bytes 1048576 | tf_op jit(solution)/shard_map/all_to_all | solution.py:63
  47.4 0.0 copy-done.1
  47.5 0.3 copy.38
  47.8 1.1 %reshape.34.w_ref = bf16[320,320]{1,0:T(8,128)(2,1)} reshape(bf16[5,64,5,64]{3,2,1,0:T(8,128)(2,1)S(1)} %copy.38) | data formatting | bytes 409600 | tf_op jit(solution)/shard_map/reshape | solution.py:180
  48.8 8.1 %all-to-all-done.1 = bf16[8,64,4,128]{3,1,2,0:T(8,128)(2,1)S(1)} async-done(((bf16[8,64,4,128]{3,1,2,0:T(8,128)(2,1)}), bf16[8,64,4,128]{3,1,2,0:T(8,128)(2,1)S(1)}, u32[]{:S(2)}, u32[]{:S(2)}) %all-to-all-start.1) | async-done | bytes 524320 | tf_op jit(solution)/shard_map/all_to_all | solution.py:63
  57.0 0.0 copy-start
  57.0 0.8 %copy-done = bf16[8,64,4,128]{3,1,2,0:T(8,128)(2,1)} copy-done((bf16[8,64,4,128]{3,1,2,0:T(8,128)(2,1)}, bf16[8,64,4,128]{3,1,2,0:T(8,128)(2,1)S(1)}, u32[]{:S(2)}) %copy-start) | copy-done | bytes 524312
  57.7 18.1 %shard_map.74 = bf16[1,64,32,128]{3,2,1,0:T(8,128)(2,1)} custom-call(bf16[32,64,128]{2,1,0:T(8,128)(2,1)} %bitcast.80, bf16[320,320]{1,0:T(8,128)(2,1)} %reshape.34.w_ref, bf16[1,64,32,128]{3,2,1,0:T(8,128)(2,1)} %f_ref.1, s32[1,32,128]{2,1,0:T(8,128)} %m_ref.1, f32[64]{0:T(128)} %b_ref.1), custom_call_target="tpu_custom_call" | custom-call | flops 1677721600 | bytes 1777664 | tf_op jit(solution)/shard_map/pallas_call | solution.py:182
  75.9 1.9 %copy.61 = bf16[1,64,32,128]{3,2,1,0:T(8,128)(2,1)} copy(bf16[1,64,32,128]{3,2,1,0:T(8,128)(2,1)} %shard_map.74) | data formatting | bytes 1048576
  (2 shorter events, 0.0 us)
Async XLA Ops:
  3.1 19.8 %all-to-all-start = ((bf16[1,64,32,128]{3,1,0,2:T(8,128)(2,1)}), bf16[1,64,32,128]{3,1,0,2:T(8,128)(2,1)S(1)}, u32[]{:S(2)}, u32[]{:S(2)}) async-start(bf16[1,64,32,128]{3,1,0,2:T(8,128)(2,1)} %bitcast.79), calls=%async_computation | async-start | bytes 1048576 | tf_op jit(solution)/shard_map/all_to_all | solution.py:53
  22.9 15.2 %collective-permute-start = (bf16[2,64,4,128]{3,1,2,0:T(8,128)(2,1)S(1)}, bf16[2,64,4,128]{3,1,2,0:T(8,128)(2,1)S(1)}, u32[]{:S(2)}, u32[]{:S(2)}) collective-permute-start(bf16[2,64,4,128]{3,1,2,0:T(8,128)(2,1)S(1)} %fusion.21), channel_id=1, source_target_pairs={{0,8},{8,0},{1,9},{9,1},{2,10},{10,2},{3,11},{11,3},{4,12},{12,4},... | collective-permute-start | bytes 393224 | tf_op jit(solution)/shard_map/ppermute | solution.py:57
  38.1 0.9 %copy-start.2 = (bf16[5,8,8,8]{3,2,1,0:T(8,128)(2,1)S(1)}, bf16[5,8,8,8]{3,2,1,0:T(8,128)(2,1)}, u32[]{:S(2)}) copy-start(bf16[5,8,8,8]{3,2,1,0:T(8,128)(2,1)} %param.10) | copy-start | bytes 15364
  40.4 0.7 copy-start.3
  42.3 5.1 %copy-start.1 = (bf16[5,64,5,64]{3,1,2,0:T(8,128)(2,1)S(1)}, bf16[5,64,5,64]{3,1,2,0:T(8,128)(2,1)}, u32[]{:S(2)}) copy-start(bf16[5,64,5,64]{3,1,2,0:T(8,128)(2,1)} %param.12) | copy-start | bytes 614404
  42.3 14.6 %all-to-all-start.1 = ((bf16[8,64,4,128]{3,1,2,0:T(8,128)(2,1)}), bf16[8,64,4,128]{3,1,2,0:T(8,128)(2,1)S(1)}, u32[]{:S(2)}, u32[]{:S(2)}) async-start(bf16[8,64,4,128]{3,1,2,0:T(8,128)(2,1)} %fusion.8), calls=%async_computation.1 | async-start | bytes 1048576 | tf_op jit(solution)/shard_map/all_to_all | solution.py:63
  57.0 0.8 %copy-start = (bf16[8,64,4,128]{3,1,2,0:T(8,128)(2,1)}, bf16[8,64,4,128]{3,1,2,0:T(8,128)(2,1)S(1)}, u32[]{:S(2)}) copy-start(bf16[8,64,4,128]{3,1,2,0:T(8,128)(2,1)S(1)} %all-to-all-done.1) | copy-start | bytes 1572868

commit v20 on v18

--- a/solution.py
+++ b/solution.py
@@ -47,6 +47,36 @@
     return jax.nn.gelu(summed).astype(jnp.bfloat16)
 
 
+def partner_kernel(halves, send_ref, out_ref, send_sem, recv_sem):
+    partner = (lax.axis_index("lon"), halves - 1 - lax.axis_index("lat_hi"), lax.axis_index("lat_lo"))
+    mesh_ids = pl.DeviceIdType.MESH
+    barrier = pltpu.get_barrier_semaphore()
+    pl.semaphore_signal(barrier, inc=1, device_id=partner, device_id_type=mesh_ids)
+    pl.semaphore_wait(barrier, 1)
+    swap = pltpu.make_async_remote_copy(
+        src_ref=send_ref,
+        dst_ref=out_ref,
+        send_sem=send_sem.at[0],
+        recv_sem=recv_sem.at[0],
+        device_id=partner,
+        device_id_type=mesh_ids,
+    )
+    swap.start()
+    swap.wait()
+
+
+def across(send):
+    any_spec = pl.BlockSpec(memory_space=pl.ANY)
+    return pl.pallas_call(
+        functools.partial(partner_kernel, lax.axis_size("lat_hi")),
+        out_shape=jax.ShapeDtypeStruct(send.shape, send.dtype),
+        in_specs=[any_spec],
+        out_specs=any_spec,
+        scratch_shapes=[pltpu.SemaphoreType.DMA((1,)), pltpu.SemaphoreType.DMA((1,))],
+        compiler_params=pltpu.CompilerParams(collective_id=1, has_side_effects=True),
+    )(send)
+
+
 def local(fields, ocean_mask, norm_gain, w_vert, b_vert, w_horiz, b_horiz):
     normed = normalize(fields, norm_gain)
     reach = w_vert.shape[0] // 2
@@ -54,7 +84,7 @@
     count_lev = columns.shape[0]
     upper = lax.axis_index("lat_hi") == 0
     send = jnp.where(upper, columns[count_lev - reach :], columns[:reach])
-    recv = lax.ppermute(send, "lat_hi", [(0, 1), (1, 0)])
+    recv = across(send)
     zeros = jnp.zeros_like(recv)
     below = jnp.where(upper, zeros, recv)
     above = jnp.where(upper, recv, zeros)

time: 78.4 us -> 80.2 us (1.023)
  Pallas kernels: 21.2 us -> 35.6 us
  starting transfers between devices: 26.3 us -> 15.4 us
  waiting for transfers between devices: 21.9 us -> 17.6 us
  other arithmetic: 2.29 us -> 5.26 us
    pallas_call x0 -> x1, Pallas kernels: none -> 14.4 us  [across(): pl.pallas_call(functools.partial(partner_kernel, lax.axis_size('lat_hi'))...]
    ppermute x1 -> x0, starting transfers between devices: 10.9 us -> none  [local(): recv = lax.ppermute(send, 'lat_hi', [(0, 1), (1, 0)])]
    ppermute x1 -> x0, waiting for transfers between devices: 4.28 us -> none  [local(): recv = lax.ppermute(send, 'lat_hi', [(0, 1), (1, 0)])]
    concatenate x0 -> x1, other arithmetic: none -> 1.41 us  [local(): padded = jnp.concatenate([below, columns, above], axis=0)]
    select_n x1, other arithmetic: 0.02 us -> 1.01 us  [local(): above = jnp.where(upper, recv, zeros)]
  transfers between devices with their start and end apart: 3 -> 2, of which waited for: 3 -> 2; matrix products, arithmetic and copies ran while one was open for 2% -> 2% of each run, Pallas kernels for 0% -> 0%
where the time goes in v20:
time: 80.2 us; the launch traced here: 79.6 us
  Pallas kernels  35.6 us (44%)
  waiting for transfers between devices  17.6 us (22%)
  starting transfers between devices  15.4 us (19%)
  other arithmetic  5.26 us (7%)
  local copies, waits for them, and re-layouts  3.98 us (5%)
  matrix products  1.74 us (2%)
    pallas_call x1, Pallas kernels, horizontal(): pl.pallas_call(functools.partial(horizontal_kernel, count), out_shape=jax...  18.1 us
    pallas_call x1, Pallas kernels, across(): pl.pallas_call(functools.partial(partner_kernel, lax.axis_size('lat_hi'))...  14.4 us
    all_to_all x1, starting transfers between devices, local(): lax.all_to_all(normed, 'lat_lo', split_axis=2, concat_axis=0, tiled=True)  10.3 us
    all_to_all x1, waiting for transfers between devices, local(): lax.all_to_all(normed, 'lat_lo', split_axis=2, concat_axis=0, tiled=True)  9.5 us
    all_to_all x1, waiting for transfers between devices, local(): lax.all_to_all(vertical(taps, w_vert, b_vert), 'lat_lo', split_axis=0, co...  8.08 us
    all_to_all x1, starting transfers between devices, local(): lax.all_to_all(vertical(taps, w_vert, b_vert), 'lat_lo', split_axis=0, co...  5.11 us
    pallas_call x1, Pallas kernels, normalize(): pl.pallas_call(normalize_kernel, out_shape=jax.ShapeDtypeStruct((rows_lat...  3.06 us
    unnamed x9, local copies, waits for them, and re-layouts  2.18 us
  transfers between devices with their start and end apart: 2, of which 2 were waited for; matrix products, arithmetic and copies ran while one was open for 2% of the time, Pallas kernels for 0%

profile of v20, /device:TPU:1, one launch (start us, length us, event | category | flops | bytes accessed | tf_op | source)
XLA Modules:
  0.0 79.6 jit_solution(1763646336784501447)
XLA Ops:
  0.0 3.1 %shard_map.73 = bf16[32,64,128]{2,1,0:T(8,128)(2,1)} custom-call(bf16[1,64,32,128]{3,2,1,0:T(8,128)(2,1)} %f_ref.1, f32[64]{0:T(128)} %g_ref.1), custom_call_target="tpu_custom_call" | custom-call | tf_op jit(solution)/shard_map/pallas_call | solution.py:28
  3.1 10.3 %all-to-all-start = ((bf16[1,64,32,128]{3,1,0,2:T(8,128)(2,1)}), bf16[1,64,32,128]{3,1,0,2:T(8,128)(2,1)S(1)}, u32[]{:S(2)}, u32[]{:S(2)}) async-start(bf16[1,64,32,128]{3,1,0,2:T(8,128)(2,1)} %bitcast.79), calls=%async_computation | async-start | bytes 1048576 | tf_op jit(solution)/shard_map/all_to_all | solution.py:83
  13.3 9.5 %all-to-all-done = bf16[1,64,32,128]{3,1,0,2:T(8,128)(2,1)S(1)} async-done(((bf16[1,64,32,128]{3,1,0,2:T(8,128)(2,1)}), bf16[1,64,32,128]{3,1,0,2:T(8,128)(2,1)S(1)}, u32[]{:S(2)}, u32[]{:S(2)}) %all-to-all-start) | async-done | bytes 524320 | tf_op jit(solution)/shard_map/all_to_all | solution.py:83
  22.8 0.4 copy.70
  23.2 0.7 fusion.17.send_ref
  24.0 14.4 %shard_map.74 = bf16[2,64,4,128]{3,2,1,0:T(4,128)(2,1)} custom-call(bf16[2,64,4,128]{3,2,1,0:T(4,128)(2,1)} %fusion.17.send_ref), custom_call_target="tpu_custom_call" | custom-call | tf_op jit(solution)/shard_map/pallas_call | solution.py:70
  38.4 1.0 %broadcast_select_fusion = (bf16[2,64,4,128]{3,2,1,0:T(4,128)(2,1)S(1)}, bf16[2,64,4,128]{3,2,1,0:T(4,128)(2,1)S(1)}) fusion(bf16[2,64,4,128]{3,2,1,0:T(4,128)(2,1)} %shard_map.74, pred[]{:T(512)S(6)} %eq.3), kind=kLoop, calls=%fused_computation.32 | loop fusion | flops 131072 | bytes 393217 | tf_op jit(solution)/shard_map/jit(_where)/select_n | solution.py:90
  39.4 0.0 copy-start.1
  39.4 1.4 %pad_maximum_fusion = (bf16[8,64,4,128]{3,2,1,0:T(4,128)(2,1)S(1)}, bf16[8,64,4,128]{3,2,1,0:T(4,128)(2,1)S(1)}, bf16[8,64,4,128]{3,2,1,0:T(4,128)(2,1)S(1)}, bf16[8,64,4,128]{3,2,1,0:T(4,128)(2,1)S(1)}) fusion(bf16[2,64,4,128]{3,2,1,0:T(4,128)(2,1)S(1)} %get-tuple-element.14, bf16[8,64,4,128]{3,2,1,0:T(4,128)(2,1)S(1)} %bitcast.76, ...), kind=kLoop, calls=%fused_computation.21 | loop fusion | flops 1048576 | bytes 2883584 | tf_op jit(solution)/shard_map/concatenate | solution.py:91
  40.8 0.0 copy-done.1
  40.8 0.3 fusion.15
  41.2 0.3 convolution_add_fusion.3
  41.5 0.3 convolution_add_fusion.2
  41.9 0.3 convolution_add_fusion.1
  42.2 0.0 copy-start.3
  42.3 0.3 fusion
  42.6 0.3 copy-done.3
  42.9 1.2 %fusion.8 = bf16[8,64,4,128]{3,1,2,0:T(8,128)(2,1)} fusion(f32[8,8,8,4,128]{4,2,3,0,1:T(8,128)S(1)} %fusion, f32[64]{0:T(128)S(1)} %copy-done.3), kind=kLoop, calls=%fused_computation.13 | loop fusion | flops 2621440 | bytes 1573120 | tf_op jit(solution)/shard_map/convert_element_type | solution.py:47
  44.1 0.0 copy-start
  44.1 5.1 %all-to-all-start.1 = ((bf16[8,64,4,128]{3,1,2,0:T(8,128)(2,1)}), bf16[8,64,4,128]{3,1,2,0:T(8,128)(2,1)S(1)}, u32[]{:S(2)}, u32[]{:S(2)}) async-start(bf16[8,64,4,128]{3,1,2,0:T(8,128)(2,1)} %fusion.8), calls=%async_computation.1 | async-start | bytes 1048576 | tf_op jit(solution)/shard_map/all_to_all | solution.py:93
  49.3 0.0 copy-done
  49.3 0.3 copy.45
  49.6 0.0 copy-start.2
  49.6 1.1 %reshape.47.w_ref = bf16[320,320]{1,0:T(8,128)(2,1)} reshape(bf16[5,64,5,64]{3,2,1,0:T(8,128)(2,1)S(1)} %copy.45) | data formatting | bytes 409600 | tf_op jit(solution)/shard_map/reshape | solution.py:208
  50.7 0.0 copy-done.2
  50.7 8.1 %all-to-all-done.1 = bf16[8,64,4,128]{3,1,2,0:T(8,128)(2,1)S(1)} async-done(((bf16[8,64,4,128]{3,1,2,0:T(8,128)(2,1)}), bf16[8,64,4,128]{3,1,2,0:T(8,128)(2,1)S(1)}, u32[]{:S(2)}, u32[]{:S(2)}) %all-to-all-start.1) | async-done | bytes 524320 | tf_op jit(solution)/shard_map/all_to_all | solution.py:93
  58.8 0.9 %bitcast_multiply_fusion = bf16[64,32,128]{2,0,1:T(8,128)(2,1)} fusion(bf16[8,64,4,128]{3,1,2,0:T(8,128)(2,1)S(1)} %all-to-all-done.1, bf16[32,128]{1,0:T(8,128)(2,1)S(1)} %convert_bitcast_fusion), kind=kLoop, calls=%fused_computation.23 | loop fusion | flops 262144 | bytes 1056768 | tf_op jit(solution)/shard_map/mul | solution.py:96
  59.6 18.1 %shard_map.75 = bf16[1,64,32,128]{3,2,1,0:T(8,128)(2,1)} custom-call(bf16[32,64,128]{2,1,0:T(8,128)(2,1)} %bitcast.84, bf16[320,320]{1,0:T(8,128)(2,1)} %reshape.47.w_ref, bf16[1,64,32,128]{3,2,1,0:T(8,128)(2,1)} %f_ref.1, s32[1,32,128]{2,1,0:T(8,128)} %m_ref.1, f32[64]{0:T(128)} %b_ref.1), custom_call_target="tpu_custom_call" | custom-call | flops 1677721600 | bytes 1777664 | tf_op jit(solution)/shard_map/pallas_call | solution.py:210
  77.8 1.9 %copy.72 = bf16[1,64,32,128]{3,2,1,0:T(8,128)(2,1)} copy(bf16[1,64,32,128]{3,2,1,0:T(8,128)(2,1)} %shard_map.75) | data formatting | bytes 1048576
  (1 shorter events, 0.0 us)
Async XLA Ops:
  3.1 19.8 %all-to-all-start = ((bf16[1,64,32,128]{3,1,0,2:T(8,128)(2,1)}), bf16[1,64,32,128]{3,1,0,2:T(8,128)(2,1)S(1)}, u32[]{:S(2)}, u32[]{:S(2)}) async-start(bf16[1,64,32,128]{3,1,0,2:T(8,128)(2,1)} %bitcast.79), calls=%async_computation | async-start | bytes 1048576 | tf_op jit(solution)/shard_map/all_to_all | solution.py:83
  39.4 1.4 %copy-start.1 = (bf16[5,8,8,8]{3,2,1,0:T(8,128)(2,1)S(1)}, bf16[5,8,8,8]{3,2,1,0:T(8,128)(2,1)}, u32[]{:S(2)}) copy-start(bf16[5,8,8,8]{3,2,1,0:T(8,128)(2,1)} %param.10) | copy-start | bytes 15364
  42.2 0.7 copy-start.3
  44.1 5.1 %copy-start = (bf16[5,64,5,64]{3,1,2,0:T(8,128)(2,1)S(1)}, bf16[5,64,5,64]{3,1,2,0:T(8,128)(2,1)}, u32[]{:S(2)}) copy-start(bf16[5,64,5,64]{3,1,2,0:T(8,128)(2,1)} %param.12) | copy-start | bytes 614404
  44.1 14.6 %all-to-all-start.1 = ((bf16[8,64,4,128]{3,1,2,0:T(8,128)(2,1)}), bf16[8,64,4,128]{3,1,2,0:T(8,128)(2,1)S(1)}, u32[]{:S(2)}, u32[]{:S(2)}) async-start(bf16[8,64,4,128]{3,1,2,0:T(8,128)(2,1)} %fusion.8), calls=%async_computation.1 | async-start | bytes 1048576 | tf_op jit(solution)/shard_map/all_to_all | solution.py:93
  49.6 1.1 %copy-start.2 = (s32[1,32,128]{2,1,0:T(8,128)S(1)}, s32[1,32,128]{2,1,0:T(8,128)}, u32[]{:S(2)}) copy-start(s32[1,32,128]{2,1,0:T(8,128)} %m_ref.1) | copy-start | bytes 49156

commit v21 on v18

--- a/solution.py
+++ b/solution.py
@@ -37,12 +37,11 @@
 def vertical(taps, w_vert, b_vert):
     count_lev, channels, rows_lat, cols_lon = taps[0].shape
     groups, width_in, width_out = (w_vert.shape[1], w_vert.shape[2], w_vert.shape[3])
-    summed = jnp.zeros((count_lev, groups, width_out, rows_lat, cols_lon), jnp.float32)
-    for tap_index in range(len(taps)):
-        grouped = taps[tap_index].reshape(count_lev, groups, width_in, rows_lat, cols_lon)
-        summed = summed + jnp.einsum(
-            "gio,ngiab->ngoab", w_vert[tap_index], grouped, preferred_element_type=jnp.float32
-        )
+    stacked = jnp.stack(
+        [tap.reshape(count_lev, groups, width_in, rows_lat, cols_lon) for tap in taps], axis=2
+    ).reshape(count_lev, groups, len(taps) * width_in, rows_lat, cols_lon)
+    weights = jnp.transpose(w_vert, (1, 0, 2, 3)).reshape(groups, len(taps) * width_in, width_out)
+    summed = jnp.einsum("gjo,ngjab->ngoab", weights, stacked, preferred_element_type=jnp.float32)
     summed = summed.reshape(count_lev, channels, rows_lat, cols_lon) + b_vert[None, :, None, None]
     return jax.nn.gelu(summed).astype(jnp.bfloat16)
 

time: 78.4 us -> 76.4 us (0.974)
  waiting for transfers between devices: 21.9 us -> 20.7 us
  matrix products: 1.75 us -> 0.65 us
    ppermute x1, waiting for transfers between devices: 4.28 us -> 3.12 us  [local(): recv = lax.ppermute(send, 'lat_hi', [(0, 1), (1, 0)])]
    dot_general x5 -> x1, matrix products: 1.75 us -> 0.65 us  [vertical(): jnp.einsum('gjo,ngjab->ngoab', weights, stacked, preferred_element_type=j...]
    transpose x0 -> x1, local copies, waits for them, and re-layouts: none -> 1.03 us  [vertical(): jnp.transpose(w_vert, (1, 0, 2, 3))]
    unnamed x9 -> x8, local copies, waits for them, and re-layouts: 2.91 us -> 1.97 us
  transfers between devices with their start and end apart: 3 -> 3, of which waited for: 3 -> 3; matrix products, arithmetic and copies ran while one was open for 2% -> 3% of each run, Pallas kernels for 0% -> 0%
where the time goes in v21:
time: 76.4 us; the launch traced here: 75.8 us
  starting transfers between devices  26.2 us (34%)
  Pallas kernels  21.2 us (28%)
  waiting for transfers between devices  20.7 us (27%)
  local copies, waits for them, and re-layouts  4.51 us (6%)
  other arithmetic  2.43 us (3%)
    pallas_call x1, Pallas kernels, horizontal(): pl.pallas_call(functools.partial(horizontal_kernel, count), out_shape=jax...  18.1 us
    ppermute x1, starting transfers between devices, local(): recv = lax.ppermute(send, 'lat_hi', [(0, 1), (1, 0)])  10.9 us
    all_to_all x1, starting transfers between devices, local(): lax.all_to_all(normed, 'lat_lo', split_axis=2, concat_axis=0, tiled=True)  10.3 us
    all_to_all x1, waiting for transfers between devices, local(): lax.all_to_all(normed, 'lat_lo', split_axis=2, concat_axis=0, tiled=True)  9.5 us
    all_to_all x1, waiting for transfers between devices, local(): lax.all_to_all(vertical(taps, w_vert, b_vert), 'lat_lo', split_axis=0, co...  8.11 us
    all_to_all x1, starting transfers between devices, local(): lax.all_to_all(vertical(taps, w_vert, b_vert), 'lat_lo', split_axis=0, co...  4.98 us
    ppermute x1, waiting for transfers between devices, local(): recv = lax.ppermute(send, 'lat_hi', [(0, 1), (1, 0)])  3.12 us
    pallas_call x1, Pallas kernels, normalize(): pl.pallas_call(normalize_kernel, out_shape=jax.ShapeDtypeStruct((rows_lat...  3.06 us
  transfers between devices with their start and end apart: 3, of which 3 were waited for; matrix products, arithmetic and copies ran while one was open for 3% of the time, Pallas kernels for 0%

profile of v21, /device:TPU:1, one launch (start us, length us, event | category | flops | bytes accessed | tf_op | source)
XLA Modules:
  0.0 75.8 jit_solution(972074207205973044)
XLA Ops:
  0.0 3.1 %shard_map.73 = bf16[32,64,128]{2,1,0:T(8,128)(2,1)} custom-call(bf16[1,64,32,128]{3,2,1,0:T(8,128)(2,1)} %f_ref.1, f32[64]{0:T(128)} %g_ref.1), custom_call_target="tpu_custom_call" | custom-call | tf_op jit(solution)/shard_map/pallas_call | solution.py:28
  3.1 10.3 %all-to-all-start = ((bf16[1,64,32,128]{3,1,0,2:T(8,128)(2,1)}), bf16[1,64,32,128]{3,1,0,2:T(8,128)(2,1)S(1)}, u32[]{:S(2)}, u32[]{:S(2)}) async-start(bf16[1,64,32,128]{3,1,0,2:T(8,128)(2,1)} %bitcast.63), calls=%async_computation | async-start | bytes 1048576 | tf_op jit(solution)/shard_map/all_to_all | solution.py:52
  13.3 9.5 %all-to-all-done = bf16[1,64,32,128]{3,1,0,2:T(8,128)(2,1)S(1)} async-done(((bf16[1,64,32,128]{3,1,0,2:T(8,128)(2,1)}), bf16[1,64,32,128]{3,1,0,2:T(8,128)(2,1)S(1)}, u32[]{:S(2)}, u32[]{:S(2)}) %all-to-all-start) | async-done | bytes 524320 | tf_op jit(solution)/shard_map/all_to_all | solution.py:52
  22.9 10.9 %collective-permute-start = (bf16[2,64,4,128]{3,1,2,0:T(8,128)(2,1)S(1)}, bf16[2,64,4,128]{3,1,2,0:T(8,128)(2,1)S(1)}, u32[]{:S(2)}, u32[]{:S(2)}) collective-permute-start(bf16[2,64,4,128]{3,1,2,0:T(8,128)(2,1)S(1)} %fusion.24), channel_id=1, source_target_pairs={{0,8},{8,0},{1,9},{9,1},{2,10},{10,2},{3,11},{11,3},{4,12},{12,4},... | collective-permute-start | bytes 393224 | tf_op jit(solution)/shard_map/ppermute | solution.py:56
  33.8 1.0 %copy.28 = bf16[8,5,8,8]{2,1,3,0:T(8,128)(2,1)S(1)} copy(bf16[8,5,8,8]{3,2,0,1:T(8,128)(2,1)} %bitcast.66) | data formatting | bytes 10240 | tf_op jit(solution)/shard_map/transpose | solution.py:43
  34.8 0.1 reshape.36
  35.0 3.1 %collective-permute-done = bf16[2,64,4,128]{3,1,2,0:T(8,128)(2,1)S(1)} collective-permute-done((bf16[2,64,4,128]{3,1,2,0:T(8,128)(2,1)S(1)}, bf16[2,64,4,128]{3,1,2,0:T(8,128)(2,1)S(1)}, u32[]{:S(2)}, u32[]{:S(2)}) %collective-permute-start) | collective-permute-done | bytes 131104 | tf_op jit(solution)/shard_map/ppermute | solution.py:56
  38.2 0.1 fusion.23
  38.3 0.1 constant_dynamic-update-slice_fusion
  38.3 0.1 fusion.16
  38.4 0.0 copy-start.2
  38.5 0.1 fusion.21
  38.5 0.0 copy-start
  38.5 0.7 fusion.3
  39.2 0.0 copy-done.2
  39.2 0.0 copy-start.1
  39.2 1.2 %fusion.13 = bf16[8,64,4,128]{3,1,2,0:T(8,128)(2,1)} fusion(f32[8,8,8,4,128]{4,2,3,0,1:T(8,128)S(1)} %fusion.3, f32[64]{0:T(128)S(1)} %copy-done.2), kind=kLoop, calls=%fused_computation.12 | loop fusion | flops 2621440 | bytes 1573120 | tf_op jit(solution)/shard_map/convert_element_type | solution.py:46
  40.4 5.0 %all-to-all-start.1 = ((bf16[8,64,4,128]{3,1,2,0:T(8,128)(2,1)}), bf16[8,64,4,128]{3,1,2,0:T(8,128)(2,1)S(1)}, u32[]{:S(2)}, u32[]{:S(2)}) async-start(bf16[8,64,4,128]{3,1,2,0:T(8,128)(2,1)} %fusion.13), calls=%async_computation.1 | async-start | bytes 1048576 | tf_op jit(solution)/shard_map/all_to_all | solution.py:62
  45.4 0.0 copy-done
  45.4 0.3 copy.30
  45.7 1.1 %reshape.35.w_ref = bf16[320,320]{1,0:T(8,128)(2,1)} reshape(bf16[5,64,5,64]{3,2,1,0:T(8,128)(2,1)S(1)} %copy.30) | data formatting | bytes 409600 | tf_op jit(solution)/shard_map/reshape | solution.py:177
  46.8 0.0 copy-done.1
  46.8 8.1 %all-to-all-done.1 = bf16[8,64,4,128]{3,1,2,0:T(8,128)(2,1)S(1)} async-done(((bf16[8,64,4,128]{3,1,2,0:T(8,128)(2,1)}), bf16[8,64,4,128]{3,1,2,0:T(8,128)(2,1)S(1)}, u32[]{:S(2)}, u32[]{:S(2)}) %all-to-all-start.1) | async-done | bytes 524320 | tf_op jit(solution)/shard_map/all_to_all | solution.py:62
  54.9 0.9 %bitcast_multiply_fusion = bf16[64,32,128]{2,0,1:T(8,128)(2,1)} fusion(bf16[8,64,4,128]{3,1,2,0:T(8,128)(2,1)S(1)} %all-to-all-done.1, bf16[32,128]{1,0:T(8,128)(2,1)S(1)} %convert_bitcast_fusion), kind=kLoop, calls=%fused_computation.30 | loop fusion | flops 262144 | bytes 1056768 | tf_op jit(solution)/shard_map/mul | solution.py:65
  55.8 18.1 %shard_map.74 = bf16[1,64,32,128]{3,2,1,0:T(8,128)(2,1)} custom-call(bf16[32,64,128]{2,1,0:T(8,128)(2,1)} %bitcast.64, bf16[320,320]{1,0:T(8,128)(2,1)} %reshape.35.w_ref, bf16[1,64,32,128]{3,2,1,0:T(8,128)(2,1)} %f_ref.1, s32[1,32,128]{2,1,0:T(8,128)} %m_ref.1, f32[64]{0:T(128)} %b_ref.1), custom_call_target="tpu_custom_call" | custom-call | flops 1677721600 | bytes 1777664 | tf_op jit(solution)/shard_map/pallas_call | solution.py:179
  74.0 1.9 %copy.44 = bf16[1,64,32,128]{3,2,1,0:T(8,128)(2,1)} copy(bf16[1,64,32,128]{3,2,1,0:T(8,128)(2,1)} %shard_map.74) | data formatting | bytes 1048576
  (4 shorter events, 0.1 us)
Async XLA Ops:
  3.1 19.8 %all-to-all-start = ((bf16[1,64,32,128]{3,1,0,2:T(8,128)(2,1)}), bf16[1,64,32,128]{3,1,0,2:T(8,128)(2,1)S(1)}, u32[]{:S(2)}, u32[]{:S(2)}) async-start(bf16[1,64,32,128]{3,1,0,2:T(8,128)(2,1)} %bitcast.63), calls=%async_computation | async-start | bytes 1048576 | tf_op jit(solution)/shard_map/all_to_all | solution.py:52
  22.9 15.2 %collective-permute-start = (bf16[2,64,4,128]{3,1,2,0:T(8,128)(2,1)S(1)}, bf16[2,64,4,128]{3,1,2,0:T(8,128)(2,1)S(1)}, u32[]{:S(2)}, u32[]{:S(2)}) collective-permute-start(bf16[2,64,4,128]{3,1,2,0:T(8,128)(2,1)S(1)} %fusion.24), channel_id=1, source_target_pairs={{0,8},{8,0},{1,9},{9,1},{2,10},{10,2},{3,11},{11,3},{4,12},{12,4},... | collective-permute-start | bytes 393224 | tf_op jit(solution)/shard_map/ppermute | solution.py:56
  38.4 0.8 %copy-start.2 = (f32[64]{0:T(128)S(1)}, f32[64]{0:T(128)}, u32[]{:S(2)}) copy-start(f32[64]{0:T(128)} %param.11) | copy-start | bytes 772
  38.5 6.9 %copy-start = (bf16[5,64,5,64]{3,1,2,0:T(8,128)(2,1)S(1)}, bf16[5,64,5,64]{3,1,2,0:T(8,128)(2,1)}, u32[]{:S(2)}) copy-start(bf16[5,64,5,64]{3,1,2,0:T(8,128)(2,1)} %param.12) | copy-start | bytes 614404
  39.2 7.6 %copy-start.1 = (s32[1,32,128]{2,1,0:T(8,128)S(1)}, s32[1,32,128]{2,1,0:T(8,128)}, u32[]{:S(2)}) copy-start(s32[1,32,128]{2,1,0:T(8,128)} %m_ref.1) | copy-start | bytes 49156
  40.4 14.5 %all-to-all-start.1 = ((bf16[8,64,4,128]{3,1,2,0:T(8,128)(2,1)}), bf16[8,64,4,128]{3,1,2,0:T(8,128)(2,1)S(1)}, u32[]{:S(2)}, u32[]{:S(2)}) async-start(bf16[8,64,4,128]{3,1,2,0:T(8,128)(2,1)} %fusion.13), calls=%async_computation.1 | async-start | bytes 1048576 | tf_op jit(solution)/shard_map/all_to_all | solution.py:62

commit v22 on v21

--- a/solution.py
+++ b/solution.py
@@ -14,12 +14,12 @@
     gain = jnp.zeros((channels, cols_lon), jnp.float32)
     for index in range(channels):
         gain = jnp.where(channel == index, g_ref[index], gain)
+    values = x_ref[0].astype(jnp.float32)
+    center = jnp.sum(values, axis=0) / channels
+    offset = values - center[None]
+    scale = lax.rsqrt(jnp.sum(offset * offset, axis=0) / channels + 1e-05)
     for row in range(rows):
-        values = x_ref[0, :, row, :].astype(jnp.float32)
-        center = jnp.sum(values, axis=0, keepdims=True) / channels
-        offset = values - center
-        spread = jnp.sum(offset * offset, axis=0, keepdims=True) / channels
-        o_ref[row] = (offset * lax.rsqrt(spread + 1e-05) * gain).astype(o_ref.dtype)
+        o_ref[row] = (offset[:, row, :] * scale[row : row + 1, :] * gain).astype(o_ref.dtype)
 
 
 def normalize(block, norm_gain):

time: 76.4 us -> 76.2 us (level)
  no operation moved by 1% of the time
where the time goes in v22:
time: 76.2 us; the launch traced here: 75.6 us
  starting transfers between devices  26.2 us (34%)
  Pallas kernels  21 us (28%)
  waiting for transfers between devices  20.7 us (27%)
  local copies, waits for them, and re-layouts  4.51 us (6%)
  other arithmetic  2.43 us (3%)
    pallas_call x1, Pallas kernels, horizontal(): pl.pallas_call(functools.partial(horizontal_kernel, count), out_shape=jax...  18.2 us
    ppermute x1, starting transfers between devices, local(): recv = lax.ppermute(send, 'lat_hi', [(0, 1), (1, 0)])  10.9 us
    all_to_all x1, starting transfers between devices, local(): lax.all_to_all(normed, 'lat_lo', split_axis=2, concat_axis=0, tiled=True)  10.3 us
    all_to_all x1, waiting for transfers between devices, local(): lax.all_to_all(normed, 'lat_lo', split_axis=2, concat_axis=0, tiled=True)  9.5 us
    all_to_all x1, waiting for transfers between devices, local(): lax.all_to_all(vertical(taps, w_vert, b_vert), 'lat_lo', split_axis=0, co...  8.11 us
    all_to_all x1, starting transfers between devices, local(): lax.all_to_all(vertical(taps, w_vert, b_vert), 'lat_lo', split_axis=0, co...  4.98 us
    ppermute x1, waiting for transfers between devices, local(): recv = lax.ppermute(send, 'lat_hi', [(0, 1), (1, 0)])  3.12 us
    pallas_call x1, Pallas kernels, normalize(): pl.pallas_call(normalize_kernel, out_shape=jax.ShapeDtypeStruct((rows_lat...  2.85 us
  transfers between devices with their start and end apart: 3, of which 3 were waited for; matrix products, arithmetic and copies ran while one was open for 3% of the time, Pallas kernels for 0%

profile of v22, /device:TPU:1, one launch (start us, length us, event | category | flops | bytes accessed | tf_op | source)
XLA Modules:
  0.0 75.6 jit_solution(11255519893995191057)
XLA Ops:
  0.0 2.9 %shard_map.73 = bf16[32,64,128]{2,1,0:T(8,128)(2,1)} custom-call(bf16[1,64,32,128]{3,2,1,0:T(8,128)(2,1)} %f_ref.1, f32[64]{0:T(128)} %g_ref.1), custom_call_target="tpu_custom_call" | custom-call | tf_op jit(solution)/shard_map/pallas_call | solution.py:28
  2.9 10.3 %all-to-all-start = ((bf16[1,64,32,128]{3,1,0,2:T(8,128)(2,1)}), bf16[1,64,32,128]{3,1,0,2:T(8,128)(2,1)S(1)}, u32[]{:S(2)}, u32[]{:S(2)}) async-start(bf16[1,64,32,128]{3,1,0,2:T(8,128)(2,1)} %bitcast.63), calls=%async_computation | async-start | bytes 1048576 | tf_op jit(solution)/shard_map/all_to_all | solution.py:52
  13.1 9.5 %all-to-all-done = bf16[1,64,32,128]{3,1,0,2:T(8,128)(2,1)S(1)} async-done(((bf16[1,64,32,128]{3,1,0,2:T(8,128)(2,1)}), bf16[1,64,32,128]{3,1,0,2:T(8,128)(2,1)S(1)}, u32[]{:S(2)}, u32[]{:S(2)}) %all-to-all-start) | async-done | bytes 524320 | tf_op jit(solution)/shard_map/all_to_all | solution.py:52
  22.6 10.9 %collective-permute-start = (bf16[2,64,4,128]{3,1,2,0:T(8,128)(2,1)S(1)}, bf16[2,64,4,128]{3,1,2,0:T(8,128)(2,1)S(1)}, u32[]{:S(2)}, u32[]{:S(2)}) collective-permute-start(bf16[2,64,4,128]{3,1,2,0:T(8,128)(2,1)S(1)} %fusion.24), channel_id=1, source_target_pairs={{0,8},{8,0},{1,9},{9,1},{2,10},{10,2},{3,11},{11,3},{4,12},{12,4},... | collective-permute-start | bytes 393224 | tf_op jit(solution)/shard_map/ppermute | solution.py:56
  33.6 1.0 %copy.28 = bf16[8,5,8,8]{2,1,3,0:T(8,128)(2,1)S(1)} copy(bf16[8,5,8,8]{3,2,0,1:T(8,128)(2,1)} %bitcast.66) | data formatting | bytes 10240 | tf_op jit(solution)/shard_map/transpose | solution.py:43
  34.6 0.1 reshape.36
  34.8 3.1 %collective-permute-done = bf16[2,64,4,128]{3,1,2,0:T(8,128)(2,1)S(1)} collective-permute-done((bf16[2,64,4,128]{3,1,2,0:T(8,128)(2,1)S(1)}, bf16[2,64,4,128]{3,1,2,0:T(8,128)(2,1)S(1)}, u32[]{:S(2)}, u32[]{:S(2)}) %collective-permute-start) | collective-permute-done | bytes 131104 | tf_op jit(solution)/shard_map/ppermute | solution.py:56
  38.0 0.1 fusion.23
  38.0 0.1 constant_dynamic-update-slice_fusion
  38.1 0.1 fusion.16
  38.2 0.0 copy-start.2
  38.2 0.1 fusion.21
  38.3 0.0 copy-start
  38.3 0.7 fusion.3
  39.0 0.0 copy-done.2
  39.0 0.0 copy-start.1
  39.0 1.2 %fusion.13 = bf16[8,64,4,128]{3,1,2,0:T(8,128)(2,1)} fusion(f32[8,8,8,4,128]{4,2,3,0,1:T(8,128)S(1)} %fusion.3, f32[64]{0:T(128)S(1)} %copy-done.2), kind=kLoop, calls=%fused_computation.12 | loop fusion | flops 2621440 | bytes 1573120 | tf_op jit(solution)/shard_map/convert_element_type | solution.py:46
  40.2 5.0 %all-to-all-start.1 = ((bf16[8,64,4,128]{3,1,2,0:T(8,128)(2,1)}), bf16[8,64,4,128]{3,1,2,0:T(8,128)(2,1)S(1)}, u32[]{:S(2)}, u32[]{:S(2)}) async-start(bf16[8,64,4,128]{3,1,2,0:T(8,128)(2,1)} %fusion.13), calls=%async_computation.1 | async-start | bytes 1048576 | tf_op jit(solution)/shard_map/all_to_all | solution.py:62
  45.2 0.0 copy-done
  45.2 0.3 copy.30
  45.5 1.1 %reshape.35.w_ref = bf16[320,320]{1,0:T(8,128)(2,1)} reshape(bf16[5,64,5,64]{3,2,1,0:T(8,128)(2,1)S(1)} %copy.30) | data formatting | bytes 409600 | tf_op jit(solution)/shard_map/reshape | solution.py:177
  46.6 0.0 copy-done.1
  46.6 8.1 %all-to-all-done.1 = bf16[8,64,4,128]{3,1,2,0:T(8,128)(2,1)S(1)} async-done(((bf16[8,64,4,128]{3,1,2,0:T(8,128)(2,1)}), bf16[8,64,4,128]{3,1,2,0:T(8,128)(2,1)S(1)}, u32[]{:S(2)}, u32[]{:S(2)}) %all-to-all-start.1) | async-done | bytes 524320 | tf_op jit(solution)/shard_map/all_to_all | solution.py:62
  54.7 0.9 %bitcast_multiply_fusion = bf16[64,32,128]{2,0,1:T(8,128)(2,1)} fusion(bf16[8,64,4,128]{3,1,2,0:T(8,128)(2,1)S(1)} %all-to-all-done.1, bf16[32,128]{1,0:T(8,128)(2,1)S(1)} %convert_bitcast_fusion), kind=kLoop, calls=%fused_computation.30 | loop fusion | flops 262144 | bytes 1056768 | tf_op jit(solution)/shard_map/mul | solution.py:65
  55.6 18.2 %shard_map.74 = bf16[1,64,32,128]{3,2,1,0:T(8,128)(2,1)} custom-call(bf16[32,64,128]{2,1,0:T(8,128)(2,1)} %bitcast.64, bf16[320,320]{1,0:T(8,128)(2,1)} %reshape.35.w_ref, bf16[1,64,32,128]{3,2,1,0:T(8,128)(2,1)} %f_ref.1, s32[1,32,128]{2,1,0:T(8,128)} %m_ref.1, f32[64]{0:T(128)} %b_ref.1), custom_call_target="tpu_custom_call" | custom-call | flops 1677721600 | bytes 1777664 | tf_op jit(solution)/shard_map/pallas_call | solution.py:179
  73.8 1.9 %copy.44 = bf16[1,64,32,128]{3,2,1,0:T(8,128)(2,1)} copy(bf16[1,64,32,128]{3,2,1,0:T(8,128)(2,1)} %shard_map.74) | data formatting | bytes 1048576
  (4 shorter events, 0.1 us)
Async XLA Ops:
  2.9 19.8 %all-to-all-start = ((bf16[1,64,32,128]{3,1,0,2:T(8,128)(2,1)}), bf16[1,64,32,128]{3,1,0,2:T(8,128)(2,1)S(1)}, u32[]{:S(2)}, u32[]{:S(2)}) async-start(bf16[1,64,32,128]{3,1,0,2:T(8,128)(2,1)} %bitcast.63), calls=%async_computation | async-start | bytes 1048576 | tf_op jit(solution)/shard_map/all_to_all | solution.py:52
  22.6 15.2 %collective-permute-start = (bf16[2,64,4,128]{3,1,2,0:T(8,128)(2,1)S(1)}, bf16[2,64,4,128]{3,1,2,0:T(8,128)(2,1)S(1)}, u32[]{:S(2)}, u32[]{:S(2)}) collective-permute-start(bf16[2,64,4,128]{3,1,2,0:T(8,128)(2,1)S(1)} %fusion.24), channel_id=1, source_target_pairs={{0,8},{8,0},{1,9},{9,1},{2,10},{10,2},{3,11},{11,3},{4,12},{12,4},... | collective-permute-start | bytes 393224 | tf_op jit(solution)/shard_map/ppermute | solution.py:56
  38.2 0.8 %copy-start.2 = (f32[64]{0:T(128)S(1)}, f32[64]{0:T(128)}, u32[]{:S(2)}) copy-start(f32[64]{0:T(128)} %param.11) | copy-start | bytes 772
  38.3 6.9 %copy-start = (bf16[5,64,5,64]{3,1,2,0:T(8,128)(2,1)S(1)}, bf16[5,64,5,64]{3,1,2,0:T(8,128)(2,1)}, u32[]{:S(2)}) copy-start(bf16[5,64,5,64]{3,1,2,0:T(8,128)(2,1)} %param.12) | copy-start | bytes 614404
  39.0 7.6 %copy-start.1 = (s32[1,32,128]{2,1,0:T(8,128)S(1)}, s32[1,32,128]{2,1,0:T(8,128)}, u32[]{:S(2)}) copy-start(s32[1,32,128]{2,1,0:T(8,128)} %m_ref.1) | copy-start | bytes 49156
  40.2 14.5 %all-to-all-start.1 = ((bf16[8,64,4,128]{3,1,2,0:T(8,128)(2,1)}), bf16[8,64,4,128]{3,1,2,0:T(8,128)(2,1)S(1)}, u32[]{:S(2)}, u32[]{:S(2)}) async-start(bf16[8,64,4,128]{3,1,2,0:T(8,128)(2,1)} %fusion.13), calls=%async_computation.1 | async-start | bytes 1048576 | tf_op jit(solution)/shard_map/all_to_all | solution.py:62

commit v23 on v22

--- a/solution.py
+++ b/solution.py
@@ -62,8 +62,7 @@
     mixed = lax.all_to_all(
         vertical(taps, w_vert, b_vert), "lat_lo", split_axis=0, concat_axis=2, tiled=True
     )
-    masked = mixed * ocean_mask[:, None].astype(jnp.bfloat16)
-    return horizontal(masked, w_horiz, fields, ocean_mask, b_horiz)
+    return horizontal(mixed, w_horiz, fields, ocean_mask, b_horiz)
 
 
 def horizontal_kernel(
@@ -84,8 +83,11 @@
     segment = 2 * cols_lon
     lane = lax.broadcasted_iota(jnp.int32, (channels, cols_lon), 1)
     packed = jnp.zeros((channels, cols_lon), x_ref.dtype)
+    def masked_row(row):
+        return x_ref[row] * m_ref[0, row : row + 1, :].astype(x_ref.dtype)
+
     for row in range(rows):
-        line = x_ref[row]
+        line = masked_row(row)
         start = 2 * reach * row
         packed = jnp.where(
             jnp.logical_and(lane >= start, lane < start + reach),
@@ -131,7 +133,7 @@
             wide[:, base + cols_lon : base + segment] = blank
             continue
         start = 2 * reach * row
-        shifted = pltpu.roll(x_ref[row], reach, 1)
+        shifted = pltpu.roll(masked_row(row), reach, 1)
         wide[:, base : base + cols_lon] = jnp.where(
             lane < reach, pltpu.roll(left_halo, (cols_lon - start - reach) % cols_lon, 1), shifted
         )

time: 76.2 us -> 76.1 us (level)
  other arithmetic: 2.43 us -> 1.56 us
  local copies, waits for them, and re-layouts: 4.51 us -> 5.29 us
    mul x1 -> x0, other arithmetic: 0.87 us -> none  [local(): masked = mixed * ocean_mask[:, None].astype(jnp.bfloat16)]
    unnamed x8, local copies, waits for them, and re-layouts: 1.97 us -> 2.76 us
where the time goes in v23:
time: 76.1 us; the launch traced here: 75.5 us
  starting transfers between devices  26.2 us (34%)
  Pallas kernels  21 us (28%)
  waiting for transfers between devices  20.7 us (27%)
  local copies, waits for them, and re-layouts  5.29 us (7%)
  other arithmetic  1.56 us (2%)
    pallas_call x1, Pallas kernels, horizontal(): pl.pallas_call(functools.partial(horizontal_kernel, count), out_shape=jax...  18.1 us
    ppermute x1, starting transfers between devices, local(): recv = lax.ppermute(send, 'lat_hi', [(0, 1), (1, 0)])  10.9 us
    all_to_all x1, starting transfers between devices, local(): lax.all_to_all(normed, 'lat_lo', split_axis=2, concat_axis=0, tiled=True)  10.3 us
    all_to_all x1, waiting for transfers between devices, local(): lax.all_to_all(normed, 'lat_lo', split_axis=2, concat_axis=0, tiled=True)  9.5 us
    all_to_all x1, waiting for transfers between devices, local(): lax.all_to_all(vertical(taps, w_vert, b_vert), 'lat_lo', split_axis=0, co...  8.11 us
    all_to_all x1, starting transfers between devices, local(): lax.all_to_all(vertical(taps, w_vert, b_vert), 'lat_lo', split_axis=0, co...  4.98 us
    ppermute x1, waiting for transfers between devices, local(): recv = lax.ppermute(send, 'lat_hi', [(0, 1), (1, 0)])  3.12 us
    pallas_call x1, Pallas kernels, normalize(): pl.pallas_call(normalize_kernel, out_shape=jax.ShapeDtypeStruct((rows_lat...  2.85 us
  transfers between devices with their start and end apart: 3, of which 3 were waited for; matrix products, arithmetic and copies ran while one was open for 3% of the time, Pallas kernels for 0%

profile of v23, /device:TPU:1, one launch (start us, length us, event | category | flops | bytes accessed | tf_op | source)
XLA Modules:
  0.0 75.5 jit_solution(6726000942122778228)
XLA Ops:
  0.0 2.9 %shard_map.73 = bf16[32,64,128]{2,1,0:T(8,128)(2,1)} custom-call(bf16[1,64,32,128]{3,2,1,0:T(8,128)(2,1)} %f_ref.1, f32[64]{0:T(128)} %g_ref.1), custom_call_target="tpu_custom_call" | custom-call | tf_op jit(solution)/shard_map/pallas_call | solution.py:28
  2.9 10.3 %all-to-all-start = ((bf16[1,64,32,128]{3,1,0,2:T(8,128)(2,1)}), bf16[1,64,32,128]{3,1,0,2:T(8,128)(2,1)S(1)}, u32[]{:S(2)}, u32[]{:S(2)}) async-start(bf16[1,64,32,128]{3,1,0,2:T(8,128)(2,1)} %bitcast.61), calls=%async_computation | async-start | bytes 1048576 | tf_op jit(solution)/shard_map/all_to_all | solution.py:52
  13.1 9.5 %all-to-all-done = bf16[1,64,32,128]{3,1,0,2:T(8,128)(2,1)S(1)} async-done(((bf16[1,64,32,128]{3,1,0,2:T(8,128)(2,1)}), bf16[1,64,32,128]{3,1,0,2:T(8,128)(2,1)S(1)}, u32[]{:S(2)}, u32[]{:S(2)}) %all-to-all-start) | async-done | bytes 524320 | tf_op jit(solution)/shard_map/all_to_all | solution.py:52
  22.6 10.9 %collective-permute-start = (bf16[2,64,4,128]{3,1,2,0:T(8,128)(2,1)S(1)}, bf16[2,64,4,128]{3,1,2,0:T(8,128)(2,1)S(1)}, u32[]{:S(2)}, u32[]{:S(2)}) collective-permute-start(bf16[2,64,4,128]{3,1,2,0:T(8,128)(2,1)S(1)} %fusion.24), channel_id=1, source_target_pairs={{0,8},{8,0},{1,9},{9,1},{2,10},{10,2},{3,11},{11,3},{4,12},{12,4},... | collective-permute-start | bytes 393224 | tf_op jit(solution)/shard_map/ppermute | solution.py:56
  33.6 1.0 %copy.28 = bf16[8,5,8,8]{2,1,3,0:T(8,128)(2,1)S(1)} copy(bf16[8,5,8,8]{3,2,0,1:T(8,128)(2,1)} %bitcast.64) | data formatting | bytes 10240 | tf_op jit(solution)/shard_map/transpose | solution.py:43
  34.6 0.1 reshape.23
  34.8 3.1 %collective-permute-done = bf16[2,64,4,128]{3,1,2,0:T(8,128)(2,1)S(1)} collective-permute-done((bf16[2,64,4,128]{3,1,2,0:T(8,128)(2,1)S(1)}, bf16[2,64,4,128]{3,1,2,0:T(8,128)(2,1)S(1)}, u32[]{:S(2)}, u32[]{:S(2)}) %collective-permute-start) | collective-permute-done | bytes 131104 | tf_op jit(solution)/shard_map/ppermute | solution.py:56
  38.0 0.1 fusion.23
  38.0 0.1 constant_dynamic-update-slice_fusion
  38.1 0.1 fusion.16
  38.2 0.0 copy-start.2
  38.2 0.1 fusion.21
  38.3 0.0 copy-start.1
  38.3 0.7 fusion.3
  39.0 0.0 copy-done.2
  39.0 1.2 %fusion.13 = bf16[8,64,4,128]{3,1,2,0:T(8,128)(2,1)} fusion(f32[8,8,8,4,128]{4,2,3,0,1:T(8,128)S(1)} %fusion.3, f32[64]{0:T(128)S(1)} %copy-done.2), kind=kLoop, calls=%fused_computation.12 | loop fusion | flops 2621440 | bytes 1573120 | tf_op jit(solution)/shard_map/convert_element_type | solution.py:46
  40.2 5.0 %all-to-all-start.1 = ((bf16[8,64,4,128]{3,1,2,0:T(8,128)(2,1)}), bf16[8,64,4,128]{3,1,2,0:T(8,128)(2,1)S(1)}, u32[]{:S(2)}, u32[]{:S(2)}) async-start(bf16[8,64,4,128]{3,1,2,0:T(8,128)(2,1)} %fusion.13), calls=%async_computation.1 | async-start | bytes 1048576 | tf_op jit(solution)/shard_map/all_to_all | solution.py:62
  45.2 0.0 copy-done.1
  45.2 0.3 copy.30
  45.5 1.1 %reshape.22.w_ref = bf16[320,320]{1,0:T(8,128)(2,1)} reshape(bf16[5,64,5,64]{3,2,1,0:T(8,128)(2,1)S(1)} %copy.30) | data formatting | bytes 409600 | tf_op jit(solution)/shard_map/reshape | solution.py:179
  46.6 8.1 %all-to-all-done.1 = bf16[8,64,4,128]{3,1,2,0:T(8,128)(2,1)S(1)} async-done(((bf16[8,64,4,128]{3,1,2,0:T(8,128)(2,1)}), bf16[8,64,4,128]{3,1,2,0:T(8,128)(2,1)S(1)}, u32[]{:S(2)}, u32[]{:S(2)}) %all-to-all-start.1) | async-done | bytes 524320 | tf_op jit(solution)/shard_map/all_to_all | solution.py:62
  54.7 0.0 copy-start
  54.7 0.8 %copy-done = bf16[8,64,4,128]{3,1,2,0:T(8,128)(2,1)} copy-done((bf16[8,64,4,128]{3,1,2,0:T(8,128)(2,1)}, bf16[8,64,4,128]{3,1,2,0:T(8,128)(2,1)S(1)}, u32[]{:S(2)}) %copy-start) | copy-done | bytes 524312
  55.5 18.1 %shard_map.74 = bf16[1,64,32,128]{3,2,1,0:T(8,128)(2,1)} custom-call(bf16[32,64,128]{2,1,0:T(8,128)(2,1)} %bitcast.62, bf16[320,320]{1,0:T(8,128)(2,1)} %reshape.22.w_ref, bf16[1,64,32,128]{3,2,1,0:T(8,128)(2,1)} %f_ref.1, s32[1,32,128]{2,1,0:T(8,128)} %m_ref.1, f32[64]{0:T(128)} %b_ref.1), custom_call_target="tpu_custom_call" | custom-call | flops 1677721600 | bytes 1777664 | tf_op jit(solution)/shard_map/pallas_call | solution.py:181
  73.7 1.9 %copy.44 = bf16[1,64,32,128]{3,2,1,0:T(8,128)(2,1)} copy(bf16[1,64,32,128]{3,2,1,0:T(8,128)(2,1)} %shard_map.74) | data formatting | bytes 1048576
  (3 shorter events, 0.1 us)
Async XLA Ops:
  2.9 19.8 %all-to-all-start = ((bf16[1,64,32,128]{3,1,0,2:T(8,128)(2,1)}), bf16[1,64,32,128]{3,1,0,2:T(8,128)(2,1)S(1)}, u32[]{:S(2)}, u32[]{:S(2)}) async-start(bf16[1,64,32,128]{3,1,0,2:T(8,128)(2,1)} %bitcast.61), calls=%async_computation | async-start | bytes 1048576 | tf_op jit(solution)/shard_map/all_to_all | solution.py:52
  22.6 15.2 %collective-permute-start = (bf16[2,64,4,128]{3,1,2,0:T(8,128)(2,1)S(1)}, bf16[2,64,4,128]{3,1,2,0:T(8,128)(2,1)S(1)}, u32[]{:S(2)}, u32[]{:S(2)}) collective-permute-start(bf16[2,64,4,128]{3,1,2,0:T(8,128)(2,1)S(1)} %fusion.24), channel_id=1, source_target_pairs={{0,8},{8,0},{1,9},{9,1},{2,10},{10,2},{3,11},{11,3},{4,12},{12,4},... | collective-permute-start | bytes 393224 | tf_op jit(solution)/shard_map/ppermute | solution.py:56
  38.2 0.8 %copy-start.2 = (f32[64]{0:T(128)S(1)}, f32[64]{0:T(128)}, u32[]{:S(2)}) copy-start(f32[64]{0:T(128)} %param.11) | copy-start | bytes 772
  38.3 6.9 %copy-start.1 = (bf16[5,64,5,64]{3,1,2,0:T(8,128)(2,1)S(1)}, bf16[5,64,5,64]{3,1,2,0:T(8,128)(2,1)}, u32[]{:S(2)}) copy-start(bf16[5,64,5,64]{3,1,2,0:T(8,128)(2,1)} %param.12) | copy-start | bytes 614404
  40.2 14.5 %all-to-all-start.1 = ((bf16[8,64,4,128]{3,1,2,0:T(8,128)(2,1)}), bf16[8,64,4,128]{3,1,2,0:T(8,128)(2,1)S(1)}, u32[]{:S(2)}, u32[]{:S(2)}) async-start(bf16[8,64,4,128]{3,1,2,0:T(8,128)(2,1)} %fusion.13), calls=%async_computation.1 | async-start | bytes 1048576 | tf_op jit(solution)/shard_map/all_to_all | solution.py:62
  54.7 0.8 %copy-start = (bf16[8,64,4,128]{3,1,2,0:T(8,128)(2,1)}, bf16[8,64,4,128]{3,1,2,0:T(8,128)(2,1)S(1)}, u32[]{:S(2)}) copy-start(bf16[8,64,4,128]{3,1,2,0:T(8,128)(2,1)S(1)} %all-to-all-done.1) | copy-start | bytes 1572868

commit v24 on v23

--- a/solution.py
+++ b/solution.py
@@ -146,7 +146,7 @@
     bias = jnp.zeros((channels, cols_lon), jnp.float32)
     for index in range(channels):
         bias = jnp.where(channel == index, b_ref[index], bias)
-    chunk = 8
+    chunk = 16
     weights = w_ref[...]
     for start in range(0, rows, chunk):
         window = jnp.concatenate(

time: 76.1 us -> 76.1 us (level)
  no operation moved by 1% of the time
where the time goes in v24:
time: 76.1 us; the launch traced here: 75.6 us
  starting transfers between devices  26.2 us (34%)
  Pallas kernels  21 us (28%)
  waiting for transfers between devices  20.7 us (27%)
  local copies, waits for them, and re-layouts  5.29 us (7%)
  other arithmetic  1.56 us (2%)
    pallas_call x1, Pallas kernels, horizontal(): pl.pallas_call(functools.partial(horizontal_kernel, count), out_shape=jax...  18.2 us
    ppermute x1, starting transfers between devices, local(): recv = lax.ppermute(send, 'lat_hi', [(0, 1), (1, 0)])  10.9 us
    all_to_all x1, starting transfers between devices, local(): lax.all_to_all(normed, 'lat_lo', split_axis=2, concat_axis=0, tiled=True)  10.3 us
    all_to_all x1, waiting for transfers between devices, local(): lax.all_to_all(normed, 'lat_lo', split_axis=2, concat_axis=0, tiled=True)  9.5 us
    all_to_all x1, waiting for transfers between devices, local(): lax.all_to_all(vertical(taps, w_vert, b_vert), 'lat_lo', split_axis=0, co...  8.11 us
    all_to_all x1, starting transfers between devices, local(): lax.all_to_all(vertical(taps, w_vert, b_vert), 'lat_lo', split_axis=0, co...  4.98 us
    ppermute x1, waiting for transfers between devices, local(): recv = lax.ppermute(send, 'lat_hi', [(0, 1), (1, 0)])  3.12 us
    pallas_call x1, Pallas kernels, normalize(): pl.pallas_call(normalize_kernel, out_shape=jax.ShapeDtypeStruct((rows_lat...  2.85 us
  transfers between devices with their start and end apart: 3, of which 3 were waited for; matrix products, arithmetic and copies ran while one was open for 3% of the time, Pallas kernels for 0%

profile of v24, /device:TPU:1, one launch (start us, length us, event | category | flops | bytes accessed | tf_op | source)
XLA Modules:
  0.0 75.6 jit_solution(6883439529663319500)
XLA Ops:
  0.0 2.9 %shard_map.73 = bf16[32,64,128]{2,1,0:T(8,128)(2,1)} custom-call(bf16[1,64,32,128]{3,2,1,0:T(8,128)(2,1)} %f_ref.1, f32[64]{0:T(128)} %g_ref.1), custom_call_target="tpu_custom_call" | custom-call | tf_op jit(solution)/shard_map/pallas_call | solution.py:28
  2.9 10.3 %all-to-all-start = ((bf16[1,64,32,128]{3,1,0,2:T(8,128)(2,1)}), bf16[1,64,32,128]{3,1,0,2:T(8,128)(2,1)S(1)}, u32[]{:S(2)}, u32[]{:S(2)}) async-start(bf16[1,64,32,128]{3,1,0,2:T(8,128)(2,1)} %bitcast.61), calls=%async_computation | async-start | bytes 1048576 | tf_op jit(solution)/shard_map/all_to_all | solution.py:52
  13.1 9.5 %all-to-all-done = bf16[1,64,32,128]{3,1,0,2:T(8,128)(2,1)S(1)} async-done(((bf16[1,64,32,128]{3,1,0,2:T(8,128)(2,1)}), bf16[1,64,32,128]{3,1,0,2:T(8,128)(2,1)S(1)}, u32[]{:S(2)}, u32[]{:S(2)}) %all-to-all-start) | async-done | bytes 524320 | tf_op jit(solution)/shard_map/all_to_all | solution.py:52
  22.6 10.9 %collective-permute-start = (bf16[2,64,4,128]{3,1,2,0:T(8,128)(2,1)S(1)}, bf16[2,64,4,128]{3,1,2,0:T(8,128)(2,1)S(1)}, u32[]{:S(2)}, u32[]{:S(2)}) collective-permute-start(bf16[2,64,4,128]{3,1,2,0:T(8,128)(2,1)S(1)} %fusion.24), channel_id=1, source_target_pairs={{0,8},{8,0},{1,9},{9,1},{2,10},{10,2},{3,11},{11,3},{4,12},{12,4},... | collective-permute-start | bytes 393224 | tf_op jit(solution)/shard_map/ppermute | solution.py:56
  33.6 1.0 %copy.28 = bf16[8,5,8,8]{2,1,3,0:T(8,128)(2,1)S(1)} copy(bf16[8,5,8,8]{3,2,0,1:T(8,128)(2,1)} %bitcast.64) | data formatting | bytes 10240 | tf_op jit(solution)/shard_map/transpose | solution.py:43
  34.6 0.1 reshape.23
  34.8 3.1 %collective-permute-done = bf16[2,64,4,128]{3,1,2,0:T(8,128)(2,1)S(1)} collective-permute-done((bf16[2,64,4,128]{3,1,2,0:T(8,128)(2,1)S(1)}, bf16[2,64,4,128]{3,1,2,0:T(8,128)(2,1)S(1)}, u32[]{:S(2)}, u32[]{:S(2)}) %collective-permute-start) | collective-permute-done | bytes 131104 | tf_op jit(solution)/shard_map/ppermute | solution.py:56
  38.0 0.1 fusion.23
  38.0 0.1 constant_dynamic-update-slice_fusion
  38.1 0.1 fusion.16
  38.2 0.0 copy-start.2
  38.2 0.1 fusion.21
  38.3 0.0 copy-start.1
  38.3 0.7 fusion.3
  39.0 0.0 copy-done.2
  39.0 1.2 %fusion.13 = bf16[8,64,4,128]{3,1,2,0:T(8,128)(2,1)} fusion(f32[8,8,8,4,128]{4,2,3,0,1:T(8,128)S(1)} %fusion.3, f32[64]{0:T(128)S(1)} %copy-done.2), kind=kLoop, calls=%fused_computation.12 | loop fusion | flops 2621440 | bytes 1573120 | tf_op jit(solution)/shard_map/convert_element_type | solution.py:46
  40.2 5.0 %all-to-all-start.1 = ((bf16[8,64,4,128]{3,1,2,0:T(8,128)(2,1)}), bf16[8,64,4,128]{3,1,2,0:T(8,128)(2,1)S(1)}, u32[]{:S(2)}, u32[]{:S(2)}) async-start(bf16[8,64,4,128]{3,1,2,0:T(8,128)(2,1)} %fusion.13), calls=%async_computation.1 | async-start | bytes 1048576 | tf_op jit(solution)/shard_map/all_to_all | solution.py:62
  45.2 0.0 copy-done.1
  45.2 0.3 copy.30
  45.5 1.1 %reshape.22.w_ref = bf16[320,320]{1,0:T(8,128)(2,1)} reshape(bf16[5,64,5,64]{3,2,1,0:T(8,128)(2,1)S(1)} %copy.30) | data formatting | bytes 409600 | tf_op jit(solution)/shard_map/reshape | solution.py:179
  46.6 8.1 %all-to-all-done.1 = bf16[8,64,4,128]{3,1,2,0:T(8,128)(2,1)S(1)} async-done(((bf16[8,64,4,128]{3,1,2,0:T(8,128)(2,1)}), bf16[8,64,4,128]{3,1,2,0:T(8,128)(2,1)S(1)}, u32[]{:S(2)}, u32[]{:S(2)}) %all-to-all-start.1) | async-done | bytes 524320 | tf_op jit(solution)/shard_map/all_to_all | solution.py:62
  54.7 0.0 copy-start
  54.7 0.8 %copy-done = bf16[8,64,4,128]{3,1,2,0:T(8,128)(2,1)} copy-done((bf16[8,64,4,128]{3,1,2,0:T(8,128)(2,1)}, bf16[8,64,4,128]{3,1,2,0:T(8,128)(2,1)S(1)}, u32[]{:S(2)}) %copy-start) | copy-done | bytes 524312
  55.5 18.2 %shard_map.74 = bf16[1,64,32,128]{3,2,1,0:T(8,128)(2,1)} custom-call(bf16[32,64,128]{2,1,0:T(8,128)(2,1)} %bitcast.62, bf16[320,320]{1,0:T(8,128)(2,1)} %reshape.22.w_ref, bf16[1,64,32,128]{3,2,1,0:T(8,128)(2,1)} %f_ref.1, s32[1,32,128]{2,1,0:T(8,128)} %m_ref.1, f32[64]{0:T(128)} %b_ref.1), custom_call_target="tpu_custom_call" | custom-call | flops 1677721600 | bytes 1777664 | tf_op jit(solution)/shard_map/pallas_call | solution.py:181
  73.7 1.9 %copy.44 = bf16[1,64,32,128]{3,2,1,0:T(8,128)(2,1)} copy(bf16[1,64,32,128]{3,2,1,0:T(8,128)(2,1)} %shard_map.74) | data formatting | bytes 1048576
  (3 shorter events, 0.1 us)
Async XLA Ops:
  2.9 19.8 %all-to-all-start = ((bf16[1,64,32,128]{3,1,0,2:T(8,128)(2,1)}), bf16[1,64,32,128]{3,1,0,2:T(8,128)(2,1)S(1)}, u32[]{:S(2)}, u32[]{:S(2)}) async-start(bf16[1,64,32,128]{3,1,0,2:T(8,128)(2,1)} %bitcast.61), calls=%async_computation | async-start | bytes 1048576 | tf_op jit(solution)/shard_map/all_to_all | solution.py:52
  22.6 15.2 %collective-permute-start = (bf16[2,64,4,128]{3,1,2,0:T(8,128)(2,1)S(1)}, bf16[2,64,4,128]{3,1,2,0:T(8,128)(2,1)S(1)}, u32[]{:S(2)}, u32[]{:S(2)}) collective-permute-start(bf16[2,64,4,128]{3,1,2,0:T(8,128)(2,1)S(1)} %fusion.24), channel_id=1, source_target_pairs={{0,8},{8,0},{1,9},{9,1},{2,10},{10,2},{3,11},{11,3},{4,12},{12,4},... | collective-permute-start | bytes 393224 | tf_op jit(solution)/shard_map/ppermute | solution.py:56
  38.2 0.8 %copy-start.2 = (f32[64]{0:T(128)S(1)}, f32[64]{0:T(128)}, u32[]{:S(2)}) copy-start(f32[64]{0:T(128)} %param.11) | copy-start | bytes 772
  38.3 6.9 %copy-start.1 = (bf16[5,64,5,64]{3,1,2,0:T(8,128)(2,1)S(1)}, bf16[5,64,5,64]{3,1,2,0:T(8,128)(2,1)}, u32[]{:S(2)}) copy-start(bf16[5,64,5,64]{3,1,2,0:T(8,128)(2,1)} %param.12) | copy-start | bytes 614404
  40.2 14.5 %all-to-all-start.1 = ((bf16[8,64,4,128]{3,1,2,0:T(8,128)(2,1)}), bf16[8,64,4,128]{3,1,2,0:T(8,128)(2,1)S(1)}, u32[]{:S(2)}, u32[]{:S(2)}) async-start(bf16[8,64,4,128]{3,1,2,0:T(8,128)(2,1)} %fusion.13), calls=%async_computation.1 | async-start | bytes 1048576 | tf_op jit(solution)/shard_map/all_to_all | solution.py:62
  54.7 0.8 %copy-start = (bf16[8,64,4,128]{3,1,2,0:T(8,128)(2,1)}, bf16[8,64,4,128]{3,1,2,0:T(8,128)(2,1)S(1)}, u32[]{:S(2)}) copy-start(bf16[8,64,4,128]{3,1,2,0:T(8,128)(2,1)S(1)} %all-to-all-done.1) | copy-start | bytes 1572868

commit v25 on v23

--- a/solution.py
+++ b/solution.py
@@ -166,7 +166,7 @@
             conv = total[:, row * segment : row * segment + cols_lon]
             ocean = m_ref[0, line : line + 1, :].astype(jnp.float32)
             base = f_ref[0, :, line, :].astype(jnp.float32)
-            o_ref[0, :, line, :] = (base + ocean * (conv + bias)).astype(o_ref.dtype)
+            o_ref[line] = (base + ocean * (conv + bias)).astype(o_ref.dtype)
 
 
 def horizontal(masked, w_horiz, fields, ocean_mask, b_horiz):
@@ -178,9 +178,9 @@
     rows_major = jnp.transpose(masked[0], (1, 0, 2))
     weights = jnp.transpose(w_horiz, (2, 1, 0, 3)).reshape(col_taps * channels, row_taps * channels)
     vmem = pl.BlockSpec(memory_space=pltpu.VMEM)
-    return pl.pallas_call(
+    updated = pl.pallas_call(
         functools.partial(horizontal_kernel, count),
-        out_shape=jax.ShapeDtypeStruct(fields.shape, fields.dtype),
+        out_shape=jax.ShapeDtypeStruct((rows_lat, channels, cols_lon), fields.dtype),
         in_specs=[vmem] * 4 + [pl.BlockSpec(memory_space=pltpu.SMEM)],
         out_specs=vmem,
         scratch_shapes=[
@@ -198,6 +198,7 @@
             transcendentals=0,
         ),
     )(rows_major, weights, fields, ocean_mask, b_horiz)
+    return jnp.transpose(updated, (1, 0, 2))[None]
 
 
 def solution(mesh):

time: 76.1 us -> 75.8 us (level)
    broadcast_in_dim x0 -> x1, local copies, waits for them, and re-layouts: none -> 2.18 us  [horizontal(): return jnp.transpose(updated, (1, 0, 2))[None]]
    unnamed x8 -> x7, local copies, waits for them, and re-layouts: 2.76 us -> 0.89 us
where the time goes in v25:
time: 75.8 us; the launch traced here: 75.2 us
  starting transfers between devices  26.2 us (35%)
  waiting for transfers between devices  20.7 us (27%)
  Pallas kernels  20.4 us (27%)
  local copies, waits for them, and re-layouts  5.6 us (7%)
  other arithmetic  1.56 us (2%)
    pallas_call x1, Pallas kernels, horizontal(): pl.pallas_call(functools.partial(horizontal_kernel, count), out_shape=jax...  17.5 us
    ppermute x1, starting transfers between devices, local(): recv = lax.ppermute(send, 'lat_hi', [(0, 1), (1, 0)])  10.9 us
    all_to_all x1, starting transfers between devices, local(): lax.all_to_all(normed, 'lat_lo', split_axis=2, concat_axis=0, tiled=True)  10.3 us
    all_to_all x1, waiting for transfers between devices, local(): lax.all_to_all(normed, 'lat_lo', split_axis=2, concat_axis=0, tiled=True)  9.5 us
    all_to_all x1, waiting for transfers between devices, local(): lax.all_to_all(vertical(taps, w_vert, b_vert), 'lat_lo', split_axis=0, co...  8.11 us
    all_to_all x1, starting transfers between devices, local(): lax.all_to_all(vertical(taps, w_vert, b_vert), 'lat_lo', split_axis=0, co...  4.98 us
    ppermute x1, waiting for transfers between devices, local(): recv = lax.ppermute(send, 'lat_hi', [(0, 1), (1, 0)])  3.12 us
    pallas_call x1, Pallas kernels, normalize(): pl.pallas_call(normalize_kernel, out_shape=jax.ShapeDtypeStruct((rows_lat...  2.85 us
  transfers between devices with their start and end apart: 3, of which 3 were waited for; matrix products, arithmetic and copies ran while one was open for 3% of the time, Pallas kernels for 0%

profile of v25, /device:TPU:1, one launch (start us, length us, event | category | flops | bytes accessed | tf_op | source)
XLA Modules:
  0.0 75.2 jit_solution(16582817542485451118)
XLA Ops:
  0.0 2.9 %shard_map.73 = bf16[32,64,128]{2,1,0:T(8,128)(2,1)} custom-call(bf16[1,64,32,128]{3,2,1,0:T(8,128)(2,1)} %f_ref.1, f32[64]{0:T(128)} %g_ref.1), custom_call_target="tpu_custom_call" | custom-call | tf_op jit(solution)/shard_map/pallas_call | solution.py:28
  2.9 10.3 %all-to-all-start = ((bf16[1,64,32,128]{3,1,0,2:T(8,128)(2,1)}), bf16[1,64,32,128]{3,1,0,2:T(8,128)(2,1)S(1)}, u32[]{:S(2)}, u32[]{:S(2)}) async-start(bf16[1,64,32,128]{3,1,0,2:T(8,128)(2,1)} %bitcast.64), calls=%async_computation | async-start | bytes 1048576 | tf_op jit(solution)/shard_map/all_to_all | solution.py:52
  13.1 9.5 %all-to-all-done = bf16[1,64,32,128]{3,1,0,2:T(8,128)(2,1)S(1)} async-done(((bf16[1,64,32,128]{3,1,0,2:T(8,128)(2,1)}), bf16[1,64,32,128]{3,1,0,2:T(8,128)(2,1)S(1)}, u32[]{:S(2)}, u32[]{:S(2)}) %all-to-all-start) | async-done | bytes 524320 | tf_op jit(solution)/shard_map/all_to_all | solution.py:52
  22.6 10.9 %collective-permute-start = (bf16[2,64,4,128]{3,1,2,0:T(8,128)(2,1)S(1)}, bf16[2,64,4,128]{3,1,2,0:T(8,128)(2,1)S(1)}, u32[]{:S(2)}, u32[]{:S(2)}) collective-permute-start(bf16[2,64,4,128]{3,1,2,0:T(8,128)(2,1)S(1)} %fusion.24), channel_id=1, source_target_pairs={{0,8},{8,0},{1,9},{9,1},{2,10},{10,2},{3,11},{11,3},{4,12},{12,4},... | collective-permute-start | bytes 393224 | tf_op jit(solution)/shard_map/ppermute | solution.py:56
  33.6 1.0 %copy.31 = bf16[8,5,8,8]{2,1,3,0:T(8,128)(2,1)S(1)} copy(bf16[8,5,8,8]{3,2,0,1:T(8,128)(2,1)} %bitcast.68) | data formatting | bytes 10240 | tf_op jit(solution)/shard_map/transpose | solution.py:43
  34.6 0.1 reshape.23
  34.8 3.1 %collective-permute-done = bf16[2,64,4,128]{3,1,2,0:T(8,128)(2,1)S(1)} collective-permute-done((bf16[2,64,4,128]{3,1,2,0:T(8,128)(2,1)S(1)}, bf16[2,64,4,128]{3,1,2,0:T(8,128)(2,1)S(1)}, u32[]{:S(2)}, u32[]{:S(2)}) %collective-permute-start) | collective-permute-done | bytes 131104 | tf_op jit(solution)/shard_map/ppermute | solution.py:56
  38.0 0.1 fusion.23
  38.0 0.1 constant_dynamic-update-slice_fusion
  38.1 0.1 fusion.16
  38.2 0.0 copy-start.2
  38.2 0.1 fusion.21
  38.3 0.0 copy-start.1
  38.3 0.7 fusion.3
  39.0 0.0 copy-done.2
  39.0 1.2 %fusion.13 = bf16[8,64,4,128]{3,1,2,0:T(8,128)(2,1)} fusion(f32[8,8,8,4,128]{4,2,3,0,1:T(8,128)S(1)} %fusion.3, f32[64]{0:T(128)S(1)} %copy-done.2), kind=kLoop, calls=%fused_computation.12 | loop fusion | flops 2621440 | bytes 1573120 | tf_op jit(solution)/shard_map/convert_element_type | solution.py:46
  40.2 5.0 %all-to-all-start.1 = ((bf16[8,64,4,128]{3,1,2,0:T(8,128)(2,1)}), bf16[8,64,4,128]{3,1,2,0:T(8,128)(2,1)S(1)}, u32[]{:S(2)}, u32[]{:S(2)}) async-start(bf16[8,64,4,128]{3,1,2,0:T(8,128)(2,1)} %fusion.13), calls=%async_computation.1 | async-start | bytes 1048576 | tf_op jit(solution)/shard_map/all_to_all | solution.py:62
  45.2 0.0 copy-done.1
  45.2 0.3 copy.33
  45.5 1.1 %reshape.22.w_ref = bf16[320,320]{1,0:T(8,128)(2,1)} reshape(bf16[5,64,5,64]{3,2,1,0:T(8,128)(2,1)S(1)} %copy.33) | data formatting | bytes 409600 | tf_op jit(solution)/shard_map/reshape | solution.py:179
  46.6 8.1 %all-to-all-done.1 = bf16[8,64,4,128]{3,1,2,0:T(8,128)(2,1)S(1)} async-done(((bf16[8,64,4,128]{3,1,2,0:T(8,128)(2,1)}), bf16[8,64,4,128]{3,1,2,0:T(8,128)(2,1)S(1)}, u32[]{:S(2)}, u32[]{:S(2)}) %all-to-all-start.1) | async-done | bytes 524320 | tf_op jit(solution)/shard_map/all_to_all | solution.py:62
  54.7 0.0 copy-start
  54.7 0.8 %copy-done = bf16[8,64,4,128]{3,1,2,0:T(8,128)(2,1)} copy-done((bf16[8,64,4,128]{3,1,2,0:T(8,128)(2,1)}, bf16[8,64,4,128]{3,1,2,0:T(8,128)(2,1)S(1)}, u32[]{:S(2)}) %copy-start) | copy-done | bytes 524312
  55.5 17.5 %shard_map.74 = bf16[32,64,128]{2,1,0:T(8,128)(2,1)} custom-call(bf16[32,64,128]{2,1,0:T(8,128)(2,1)} %bitcast.65, bf16[320,320]{1,0:T(8,128)(2,1)} %reshape.22.w_ref, bf16[1,64,32,128]{3,2,1,0:T(8,128)(2,1)} %f_ref.1, s32[1,32,128]{2,1,0:T(8,128)} %m_ref.1, f32[64]{0:T(128)} %b_ref.1), custom_call_target="tpu_custom_call" | custom-call | flops 1677721600 | bytes 1777664 | tf_op jit(solution)/shard_map/pallas_call | solution.py:181
  73.1 2.2 %copy.34 = bf16[1,64,32,128]{3,2,1,0:T(8,128)(2,1)} copy(bf16[1,64,32,128]{3,1,2,0:T(8,128)(2,1)} %bitcast.66) | data formatting | bytes 1048576 | tf_op jit(solution)/shard_map/broadcast_in_dim | solution.py:201
  (3 shorter events, 0.1 us)
Async XLA Ops:
  2.9 19.8 %all-to-all-start = ((bf16[1,64,32,128]{3,1,0,2:T(8,128)(2,1)}), bf16[1,64,32,128]{3,1,0,2:T(8,128)(2,1)S(1)}, u32[]{:S(2)}, u32[]{:S(2)}) async-start(bf16[1,64,32,128]{3,1,0,2:T(8,128)(2,1)} %bitcast.64), calls=%async_computation | async-start | bytes 1048576 | tf_op jit(solution)/shard_map/all_to_all | solution.py:52
  22.6 15.2 %collective-permute-start = (bf16[2,64,4,128]{3,1,2,0:T(8,128)(2,1)S(1)}, bf16[2,64,4,128]{3,1,2,0:T(8,128)(2,1)S(1)}, u32[]{:S(2)}, u32[]{:S(2)}) collective-permute-start(bf16[2,64,4,128]{3,1,2,0:T(8,128)(2,1)S(1)} %fusion.24), channel_id=1, source_target_pairs={{0,8},{8,0},{1,9},{9,1},{2,10},{10,2},{3,11},{11,3},{4,12},{12,4},... | collective-permute-start | bytes 393224 | tf_op jit(solution)/shard_map/ppermute | solution.py:56
  38.2 0.8 %copy-start.2 = (f32[64]{0:T(128)S(1)}, f32[64]{0:T(128)}, u32[]{:S(2)}) copy-start(f32[64]{0:T(128)} %param.11) | copy-start | bytes 772
  38.3 6.9 %copy-start.1 = (bf16[5,64,5,64]{3,1,2,0:T(8,128)(2,1)S(1)}, bf16[5,64,5,64]{3,1,2,0:T(8,128)(2,1)}, u32[]{:S(2)}) copy-start(bf16[5,64,5,64]{3,1,2,0:T(8,128)(2,1)} %param.12) | copy-start | bytes 614404
  40.2 14.5 %all-to-all-start.1 = ((bf16[8,64,4,128]{3,1,2,0:T(8,128)(2,1)}), bf16[8,64,4,128]{3,1,2,0:T(8,128)(2,1)S(1)}, u32[]{:S(2)}, u32[]{:S(2)}) async-start(bf16[8,64,4,128]{3,1,2,0:T(8,128)(2,1)} %fusion.13), calls=%async_computation.1 | async-start | bytes 1048576 | tf_op jit(solution)/shard_map/all_to_all | solution.py:62
  54.7 0.8 %copy-start = (bf16[8,64,4,128]{3,1,2,0:T(8,128)(2,1)}, bf16[8,64,4,128]{3,1,2,0:T(8,128)(2,1)S(1)}, u32[]{:S(2)}) copy-start(bf16[8,64,4,128]{3,1,2,0:T(8,128)(2,1)S(1)} %all-to-all-done.1) | copy-start | bytes 1572868
